TPU v7x, 512 devices: a whole 4x4x16 slice. The times are simulated.
512 devices in a mesh: axial: 64 (over z, x), azim: 8 (over y, core).
Axes of the slice: x: 4, y: 4, z: 16, core: 2. Of those that a mesh axis runs over, the one named last changes fastest.
Arguments:
- state: float32 [14, 512, 64, 128], P(None, 'axial', 'azim'), may hold values from -18 to 18, as said below
- diff_coef: float32 [10], replicated, may hold values from 0.1 to 1
- parcel_state: float32 [8, 1048576], P(None, ('axial', 'azim')), may hold values from -6 to 6, as said below
- parcel_cell: int32 [1048576], P(('axial', 'azim')), may hold values from 0 to 8191
- parcel_dest: int32 [1048576], P(('axial', 'azim')), may hold values from 0 to 4, as said below
- live_count: int32 [512], P(('axial', 'azim')), may hold values from 256 to 2048, as said below
Outputs:
- scalars_new: float32 [10, 512, 64, 128], P(None, 'axial', 'azim')
- velocity_new: float32 [3, 512, 64, 128], P(None, 'axial', 'azim')
- kept_parcels: float32 [8, 1048576], P(None, ('axial', 'azim'))
- arrived: float32 [4, 8, 32768], P(None, None, ('axial', 'azim'))
Inputs may be any that keep to these rules, and one draw needn't show every extreme that they name: `state`: component 0 (density) lies in [0.5, 2] and components 5 to 13 (species fractions) in [0, 1]. `parcel_state`: row 0 (mass) lies in [0.2, 2], rows 5 to 7 (offsets) in [0, 1]. Live parcels of a box fill its first live_count slots; boxes at axial index 0 are full. `parcel_dest`: among the live parcels of one box at most 64 have any one destination 1 to 4, and in every box one destination has exactly 64. Entries of slots that are not live are ignored. `parcel_cell`: x * 8 * 128 + y * 128 + z for box-local cell (x, y, z).
All inputs are finite; a program needn't handle non-finite values. Where the computation divides by a largest or mean magnitude, that divisor is 1e-20 or more.
Results may differ from a plain program's by a relative error of at most 0.0003.
Values sent between devices are 32-bit elements; how exact they have to be, the bound alone decides.
A program may use at most 64 MiB of HBM per device.

v0:
```python
import jax
import jax.numpy as jnp
from jax import lax
from jax.sharding import PartitionSpec as P

CAP = 64
ITERS = 4


CFL = 0.4
SHIFT_PRESSURE = 0.25
EVAP = 8.0
RELAX = 4.0
DRAG = 6.0
LATENT = 0.5
HEAT_CAP = 0.8
HIGHEST = lax.Precision.HIGHEST


def extended(block, sides, width):
    for axis, dim in sides:
        count = lax.axis_size(axis)
        forward = [(i, i + 1) for i in range(count - 1)]
        forward.append((count - 1, 0))
        backward = [(target, source) for source, target in forward]
        low = lax.ppermute(
            lax.slice_in_dim(block, block.shape[dim] - width, None, axis=dim), axis, forward
        )
        high = lax.ppermute(lax.slice_in_dim(block, 0, width, axis=dim), axis, backward)
        block = jnp.concatenate([low, block, high], axis=dim)
    return block


def shifted_2(shard, axis, by):
    length = lax.axis_size(axis)
    pairs = [(i, i + by) for i in range(length) if 0 <= i + by < length]
    return lax.ppermute(shard, axis, pairs)


def shifted_3(shard, axis, by):
    length = lax.axis_size(axis)
    return lax.ppermute(shard, axis, [(i, (i + by) % length) for i in range(length)])


def shifted(padded, rim_width, direction, step_by):
    selector = []
    total_dims = padded.ndim
    for dim_index in range(total_dims):
        extent = padded.shape[dim_index]
        if dim_index == total_dims - 3 + direction:
            selector.append(slice(rim_width + step_by, extent - rim_width + step_by))
        elif dim_index >= total_dims - 3:
            selector.append(slice(rim_width, extent - rim_width))
        else:
            selector.append(slice(None))
    return padded[tuple(selector)]


def clear_ends(padded, rim_width, axial_dim):
    extent = padded.shape[axial_dim]
    at_first = lax.axis_index("axial") == 0
    at_last = lax.axis_index("axial") == lax.axis_size("axial") - 1
    shape_list = [1] * padded.ndim
    shape_list[axial_dim] = extent
    position = lax.broadcasted_iota(jnp.int32, tuple(shape_list), axial_dim)
    dropped = at_first & (position < rim_width) | at_last & (position >= extent - rim_width)
    return jnp.where(dropped, jnp.float32(0.0), padded)


def radial_pad(values, rim_width, radial_mode):
    return jnp.pad(
        values, [(0, 0)] * (values.ndim - 1) + [(rim_width, rim_width)], mode=radial_mode
    )


def transport(scalar_pad, vel_pad, density_pad, density_rim, diffusion, step_size):
    center = shifted(scalar_pad, 2, 0, 0)
    density = shifted(density_pad, density_rim, 0, 0)
    change = jnp.zeros_like(center)
    for direction in range(3):
        carried = vel_pad[direction] * scalar_pad
        advect = (
            -shifted(carried, 2, direction, 2)
            + 8.0 * shifted(carried, 2, direction, 1)
            - 8.0 * shifted(carried, 2, direction, -1)
            + shifted(carried, 2, direction, -2)
        ) / 12.0
        upper_flux = (
            0.5
            * diffusion
            * (density + shifted(density_pad, density_rim, direction, 1))
            * (shifted(scalar_pad, 2, direction, 1) - center)
        )
        lower_flux = (
            0.5
            * diffusion
            * (density + shifted(density_pad, density_rim, direction, -1))
            * (center - shifted(scalar_pad, 2, direction, -1))
        )
        change = change - advect + upper_flux - lower_flux
    return center + step_size * change


def evaporate(attrs, gas_values, alive_mask, step_size):
    parcel_mass = attrs[0]
    parcel_temp = attrs[1]
    parcel_vel = attrs[2:5]
    offsets = attrs[5:8]
    gas_heat = gas_values[3]
    gas_fuel = gas_values[4]
    evap_rate = EVAP * jax.nn.softplus(gas_heat - parcel_temp) * (1.0 - gas_fuel)
    new_mass = parcel_mass * jnp.exp(-step_size * evap_rate)
    lost_mass = parcel_mass - new_mass
    new_temp = parcel_temp + step_size * RELAX * (gas_heat - parcel_temp)
    new_vel = parcel_vel + step_size * DRAG * (gas_values[0:3] - parcel_vel)
    new_offsets = offsets + step_size * new_vel
    heat_source = -LATENT * lost_mass - HEAT_CAP * new_mass * (new_temp - parcel_temp)
    new_attrs = (
        jnp.concatenate([new_mass[None], new_temp[None], new_vel, new_offsets], axis=0)
        * alive_mask[None]
    )
    sources = jnp.stack([heat_source * alive_mask, lost_mass * alive_mask])
    return (new_attrs, sources)


def pressure_pad(values):
    padded = extended(values, (("axial", 0), ("azim", 1)), 1)
    return radial_pad(clear_ends(padded, 1, 0), 1, "constant")


def operate(values):
    padded = pressure_pad(values)
    beside = shifted(padded, 1, 0, 1) + shifted(padded, 1, 0, -1)
    beside = beside + shifted(padded, 1, 1, 1) + shifted(padded, 1, 1, -1)
    beside = beside + shifted(padded, 1, 2, 1) + shifted(padded, 1, 2, -1)
    return (6.0 + SHIFT_PRESSURE) * values - beside


def squares(residual):
    return lax.psum(jnp.sum(residual * residual), ("axial", "azim"))


def solve_pressure(divergence):
    pressure = jnp.zeros_like(divergence)
    residual = divergence
    search = divergence
    norm_now = squares(residual)
    for iteration in range(ITERS):
        image = operate(search)
        alpha = norm_now / lax.psum(jnp.sum(search * image), ("axial", "azim"))
        pressure = pressure + alpha * search
        residual = residual - alpha * image
        norm_next = squares(residual)
        search = residual + norm_next / norm_now * search
        norm_now = norm_next
    return pressure


def along_axial(buffer, step_by):
    return shifted_2(buffer, "axial", step_by)


def along_azim(buffer, step_by):
    return shifted_3(buffer, "azim", step_by)


def on_device(state, diff_coef, parcel_state, parcel_cell, parcel_dest, live_count):
    velocity = state[1:4]
    fastest = lax.pmax(jnp.max(jnp.abs(velocity)), ("axial", "azim"))
    step_size = CFL / (fastest + 1e-06)
    whole_pad = extended(state, (("axial", 1), ("azim", 2)), 2)
    whole_pad = radial_pad(clear_ends(whole_pad, 2, 1), 2, "edge")
    moving = whole_pad[1:]
    density_pad = whole_pad[0]
    density_rim = 2
    vel_pad = moving[0:3]
    transported = transport(
        moving[3:], vel_pad, density_pad, density_rim, diff_coef[:, None, None, None], step_size
    )
    npar_local = parcel_cell.shape[0]
    block_rows = 512
    cells_x, cells_y, cells_z = (state.shape[1], state.shape[2], state.shape[3])
    plane_count = cells_x * cells_y
    gas_table = jnp.transpose(state[1:6].reshape(5, plane_count, cells_z), (1, 0, 2)).reshape(
        plane_count, 5 * cells_z
    )
    live_now = live_count[0]

    def one_block(block_index, carried_pair):
        deposit, updated = carried_pair
        first_slot = block_index * block_rows
        cell_ids = lax.dynamic_slice_in_dim(parcel_cell, first_slot, block_rows)
        attrs = lax.dynamic_slice_in_dim(parcel_state, first_slot, block_rows, 1)
        alive_mask = (first_slot + jnp.arange(block_rows) < live_now).astype(jnp.float32)
        plane_ids = cell_ids // cells_z
        radial_ids = cell_ids % cells_z
        plane_hot = (plane_ids[:, None] == jnp.arange(plane_count)[None, :]).astype(jnp.float32)
        radial_hot = (radial_ids[:, None] == jnp.arange(cells_z)[None, :]).astype(jnp.float32)
        gas_rows = jnp.dot(plane_hot, gas_table, precision=HIGHEST).reshape(block_rows, 5, cells_z)
        gas_values = jnp.sum(gas_rows * radial_hot[:, None, :], axis=2).T
        new_attrs, sources = evaporate(attrs, gas_values, alive_mask, step_size)
        spread = (sources.T[:, :, None] * radial_hot[:, None, :]).reshape(block_rows, 2 * cells_z)
        deposit = deposit + lax.dot_general(
            plane_hot, spread, (((0,), (0,)), ((), ())), precision=HIGHEST
        )
        updated = lax.dynamic_update_slice_in_dim(updated, new_attrs, first_slot, 1)
        return (deposit, updated)

    initial = (jnp.zeros((plane_count, 2 * cells_z), jnp.float32), jnp.zeros_like(parcel_state))
    block_count = npar_local // block_rows
    deposit, updated = lax.fori_loop(0, block_count, one_block, initial)
    deposit = jnp.transpose(deposit.reshape(cells_x, cells_y, 2, cells_z), (2, 0, 1, 3))
    scalars_new = jnp.concatenate(
        [transported[:2] + deposit / state[0][None], transported[2:]], axis=0
    )
    slot_alive = jnp.arange(npar_local) < live_now
    stacked = jnp.stack([(parcel_dest == d + 1) & slot_alive for d in range(4)]).astype(jnp.int32)
    ranks = jnp.cumsum(stacked, axis=1) - 1
    mover = jnp.sum(stacked, axis=0) > 0
    target = jnp.where(mover, jnp.sum(stacked * (jnp.arange(4)[:, None] * CAP + ranks), axis=0), -1)
    select = (target[:, None] == jnp.arange(4 * CAP)[None, :]).astype(jnp.float32)
    buffers = jnp.transpose(
        jnp.dot(updated, select, precision=HIGHEST).reshape(updated.shape[0], 4, CAP), (1, 0, 2)
    )
    arrived = jnp.stack(
        [
            along_axial(buffers[0], -1),
            along_axial(buffers[1], 1),
            along_azim(buffers[2], -1),
            along_azim(buffers[3], 1),
        ]
    )
    kept_parcels = jnp.where((parcel_dest == 0)[None], updated, jnp.float32(0.0))
    divergence = jnp.zeros_like(state[0])
    for direction in range(3):
        divergence = divergence + 0.5 * (
            shifted(vel_pad[direction], 2, direction, 1)
            - shifted(vel_pad[direction], 2, direction, -1)
        )
    pressure = solve_pressure(divergence)
    padded_pressure = pressure_pad(pressure)
    velocity_new = jnp.stack(
        [
            velocity[d]
            - 0.5 * (shifted(padded_pressure, 1, d, 1) - shifted(padded_pressure, 1, d, -1))
            for d in range(3)
        ]
    )
    return (scalars_new, velocity_new, kept_parcels, arrived)


def solution(mesh):
    in_specs = (
        P(None, "axial", "azim", None),
        P(),
        P(None, ("axial", "azim")),
        P(("axial", "azim")),
        P(("axial", "azim")),
        P(("axial", "azim")),
    )
    out_specs = (
        P(None, "axial", "azim", None),
        P(None, "axial", "azim", None),
        P(None, ("axial", "azim")),
        P(None, None, ("axial", "azim")),
    )
    return jax.shard_map(
        on_device, mesh=mesh, in_specs=in_specs, out_specs=out_specs, check_vma=False
    )
```

profile of v0, /device:TPU:6, one launch (start us, length us, event | category | flops | bytes accessed | tf_op | source)
XLA Modules:
  0.0 980.9 jit_solution(4990811178400912499)
XLA Ops:
  1.6 3.7 collective-permute-start
  9.9 109.5 %pmax.7 = f32[]{:T(128)} all-reduce(f32[]{:T(128)} %abs_reduce_fusion), channel_id=1, replica_groups=mesh['axial'=64,'azim'=8] {'axial','azim'}, use_global_device_ids=true, to_apply=%region_1.0 | all-reduce | flops 1 | bytes 8 | tf_op jit(solution)/shard_map/pmax | solution.py:169
  121.0 31.7 %while.18 = (s32[]{:T(128)}, f32[64,256]{1,0:T(8,128)S(1)}, f32[8,2048]{1,0:T(8,128)S(1)}, s32[2048]{0:T(1024)}, s32[]{:T(128)}, /*index=5*/f32[8,2048]{1,0:T(8,...) while((s32[]{:T(128)}, f32[64,256]{1,0:T(8,128)S(1)}, ...), condition=%wide.region_4.5_spmd.clone, body=%wide.region_2.4_spmd.clone.sunk | while | flops 353384960 | bytes 5411153 | solution.py:211
  157.7 3.1 collective-permute-done.2
  169.7 2.7 collective-permute-start.5
  172.5 5.2 collective-permute-start.4
  177.7 2.9 collective-permute-start.26
  180.7 3.4 collective-permute-start.25
  185.5 2.9 collective-permute-done.6
  189.3 99.4 %all-reduce.5 = (f32[]{:T(128)}, f32[]{:T(128)}) all-reduce(f32[]{:T(128)} %get-tuple-element.277, f32[]{:T(128)} %get-tuple-element.276), channel_id=1, replica_groups=mesh['axial'=64,'azim'=8] {'axial','azim'}, use_global_device_ids=true, to_apply=%region_6.7 | all-reduce | flops 2 | bytes 16 | tf_op jit(solution)/shard_map/psum | solution.py:140
  291.2 99.3 %psum.58 = f32[]{:T(128)} all-reduce(f32[]{:T(128)} %multiply_reduce_fusion.5), channel_id=1, replica_groups=mesh['axial'=64,'azim'=8] {'axial','azim'}, use_global_device_ids=true, to_apply=%region_10.11 | all-reduce | flops 1 | bytes 8 | tf_op jit(solution)/shard_map/psum | solution.py:140
  393.8 6.0 collective-permute-start.8
  406.3 104.1 %psum.59 = f32[]{:T(128)} all-reduce(f32[]{:T(128)} %get-tuple-element.311), channel_id=1, replica_groups=mesh['axial'=64,'azim'=8] {'axial','azim'}, use_global_device_ids=true, to_apply=%region_12.13 | all-reduce | flops 1 | bytes 8 | tf_op jit(solution)/shard_map/psum | solution.py:150
  512.3 100.9 %psum.60 = f32[]{:T(128)} all-reduce(f32[]{:T(128)} %get-tuple-element.309), channel_id=1, replica_groups=mesh['axial'=64,'azim'=8] {'axial','azim'}, use_global_device_ids=true, to_apply=%region_14.15 | all-reduce | flops 1 | bytes 8 | tf_op jit(solution)/shard_map/psum | solution.py:140
  616.6 6.2 collective-permute-start.12
  624.4 4.0 pad_maximum_fusion
  629.3 104.4 %psum.61 = f32[]{:T(128)} all-reduce(f32[]{:T(128)} %get-tuple-element.307), channel_id=1, replica_groups=mesh['axial'=64,'azim'=8] {'axial','azim'}, use_global_device_ids=true, to_apply=%region_16.17 | all-reduce | flops 1 | bytes 8 | tf_op jit(solution)/shard_map/psum | solution.py:150
  735.6 4.4 slice_multiply_fusion.2
  740.0 100.2 %psum.62 = f32[]{:T(128)} all-reduce(f32[]{:T(128)} %multiply_reduce_fusion.1), channel_id=1, replica_groups=mesh['axial'=64,'azim'=8] {'axial','azim'}, use_global_device_ids=true, to_apply=%region_18.19 | all-reduce | flops 1 | bytes 8 | tf_op jit(solution)/shard_map/psum | solution.py:140
  843.6 6.0 collective-permute-start.16
  851.7 8.5 fusion.19
  861.0 104.1 %psum.63 = f32[]{:T(128)} all-reduce(f32[]{:T(128)} %fusion.68), channel_id=1, replica_groups=mesh['axial'=64,'azim'=8] {'axial','azim'}, use_global_device_ids=true, to_apply=%region_20.21 | all-reduce | flops 1 | bytes 8 | tf_op jit(solution)/shard_map/psum | solution.py:150
  968.4 6.0 collective-permute-start.20
  977.1 2.9 collective-permute-done.22
  (193 shorter events, 78.4 us)
Async XLA Ops:
  1.6 152.9 %collective-permute-start = (f32[14,2,8,128]{3,2,1,0:T(8,128)S(1)}, f32[14,2,8,128]{3,2,1,0:T(8,128)S(1)}, u32[]{:S(2)}, u32[]{:S(2)}) collective-permute-start(f32[14,2,8,128]{3,2,1,0:T(8,128)S(1)} %get-tuple-element.333), channel_id=1, source_target_pairs={{0,8},{8,16},{16,24},{24,32},{32,40},{40,48},{48,56},{56,64},{64,7... | collective-permute-start | bytes 344072 | tf_op jit(solution)/shard_map/ppermute | solution.py:26
  5.4 149.3 %collective-permute-start.1 = (f32[14,2,8,128]{3,2,1,0:T(8,128)S(1)}, f32[14,2,8,128]{3,2,1,0:T(8,128)S(1)}, u32[]{:S(2)}, u32[]{:S(2)}) collective-permute-start(f32[14,2,8,128]{3,2,1,0:T(8,128)S(1)} %get-tuple-element.332), channel_id=1, source_target_pairs={{8,0},{16,8},{24,16},{32,24},{40,32},{48,40},{56,48},{64,56},{72,6... | collective-permute-start | bytes 344072 | tf_op jit(solution)/shard_map/ppermute | solution.py:29
  154.8 6.1 collective-permute-start.2
  169.7 14.4 %collective-permute-start.5 = (f32[1,8,128]{2,1,0:T(8,128)S(1)}, f32[1,8,128]{2,1,0:T(8,128)S(1)}, u32[]{:S(2)}, u32[]{:S(2)}) collective-permute-start(f32[1,8,128]{2,1,0:T(8,128)S(1)} %get-tuple-element.359), channel_id=1, source_target_pairs={{8,0},{16,8},{24,16},{32,24},{40,32},{48,40},{56,48},{64,56},{72,6... | collective-permute-start | bytes 12296 | tf_op jit(solution)/shard_map/ppermute | solution.py:29
  172.5 11.6 %collective-permute-start.4 = (f32[1,8,128]{2,1,0:T(8,128)S(1)}, f32[1,8,128]{2,1,0:T(8,128)S(1)}, u32[]{:S(2)}, u32[]{:S(2)}) collective-permute-start(f32[1,8,128]{2,1,0:T(8,128)S(1)} %get-tuple-element.358), channel_id=1, source_target_pairs={{0,8},{8,16},{16,24},{24,32},{32,40},{40,48},{48,56},{56,64},{64,7... | collective-permute-start | bytes 12296 | tf_op jit(solution)/shard_map/ppermute | solution.py:26
  177.7 438.9 %collective-permute-start.27 = (f32[8,64]{1,0:T(8,128)S(1)}, f32[8,64]{1,0:T(8,128)S(1)}, u32[]{:S(2)}, u32[]{:S(2)}) collective-permute-start(f32[8,64]{1,0:T(8,128)S(1)} %get-tuple-element.361), channel_id=1, source_target_pairs={{0,1},{1,2},{2,3},{3,4},{4,5},{5,6},{6,7},{7,0},{8,9},{9,10},{10,1... | collective-permute-start | bytes 6152 | tf_op jit(solution)/shard_map/ppermute | solution.py:42
  177.7 445.1 %collective-permute-start.26 = (f32[8,64]{1,0:T(8,128)S(1)}, f32[8,64]{1,0:T(8,128)S(1)}, u32[]{:S(2)}, u32[]{:S(2)}) collective-permute-start(f32[8,64]{1,0:T(8,128)S(1)} %get-tuple-element.362), channel_id=1, source_target_pairs={{0,7},{1,0},{2,1},{3,2},{4,3},{5,4},{6,5},{7,6},{8,15},{9,8},{10,9... | collective-permute-start | bytes 6152 | tf_op jit(solution)/shard_map/ppermute | solution.py:42
  180.7 442.1 %collective-permute-start.25 = (f32[8,64]{1,0:T(8,128)S(1)}, f32[8,64]{1,0:T(8,128)S(1)}, u32[]{:S(2)}, u32[]{:S(2)}) collective-permute-start(f32[8,64]{1,0:T(8,128)S(1)} %get-tuple-element.363), channel_id=1, source_target_pairs={{0,8},{8,16},{16,24},{24,32},{32,40},{40,48},{48,56},{56,64},{64,7... | collective-permute-start | bytes 6152 | tf_op jit(solution)/shard_map/ppermute | solution.py:37
  184.2 4.3 collective-permute-start.6
  391.8 8.0 collective-permute-start.9
  393.8 7.3 collective-permute-start.8
  401.1 4.3 collective-permute-start.10
  402.5 220.4 %collective-permute-start.24 = (f32[8,64]{1,0:T(8,128)S(1)}, f32[8,64]{1,0:T(8,128)S(1)}, u32[]{:S(2)}, u32[]{:S(2)}) collective-permute-start(f32[8,64]{1,0:T(8,128)S(1)} %get-tuple-element.360), channel_id=1, source_target_pairs={{8,0},{16,8},{24,16},{32,24},{40,32},{48,40},{56,48},{64,56},{72,6... | collective-permute-start | bytes 6152 | tf_op jit(solution)/shard_map/ppermute | solution.py:37
  614.6 8.8 collective-permute-start.13
  616.6 7.3 collective-permute-start.12
  623.9 4.5 collective-permute-start.15
  624.0 4.5 collective-permute-start.14
  841.7 9.5 collective-permute-start.17
  843.6 7.6 collective-permute-start.16
  851.2 9.0 collective-permute-start.19
  851.2 9.0 collective-permute-start.18
  966.5 8.8 collective-permute-start.21
  968.4 7.3 collective-permute-start.20
  975.8 4.3 collective-permute-start.22
  (14 other events, 552.0 us)
where the time goes:
time: 989 us; the launch traced here: 981 us
  blocking collectives  822 us (83%)
  starting transfers between devices  57.1 us (6%)
  other arithmetic  56.8 us (6%)
  waiting for transfers between devices  15.5 us (2%)
  between operations  11.8 us (1%)
  local copies, waits for them, and re-layouts  11 us (1%)
    psum x4, blocking collectives, squares(): return lax.psum(jnp.sum(residual * residual), ('axial', 'azim'))  400 us
    psum x3, blocking collectives, solve_pressure(): alpha = norm_now / lax.psum(jnp.sum(search * image), ('axial', 'azim'))  313 us
    pmax x1, blocking collectives, on_device(): fastest = lax.pmax(jnp.max(jnp.abs(velocity)), ('axial', 'azim'))  110 us
    ppermute x12, starting transfers between devices, extended(): lax.ppermute(lax.slice_in_dim(block, block.shape[dim] - width, None, axis...  36.2 us
  transfers between devices with their start and end apart: 28, of which 11 were waited for; matrix products, arithmetic and copies ran while one was open for 6% of the time, Pallas kernels for 0%

commit v1 on v0

--- a/solution.py
+++ b/solution.py
@@ -136,24 +136,77 @@
     return (6.0 + SHIFT_PRESSURE) * values - beside
 
 
-def squares(residual):
-    return lax.psum(jnp.sum(residual * residual), ("axial", "azim"))
+def neighbour_sum(padded):
+    beside = shifted(padded, 1, 0, 1) + shifted(padded, 1, 0, -1)
+    beside = beside + shifted(padded, 1, 1, 1) + shifted(padded, 1, 1, -1)
+    return beside + shifted(padded, 1, 2, 1) + shifted(padded, 1, 2, -1)
 
 
 def solve_pressure(divergence):
-    pressure = jnp.zeros_like(divergence)
-    residual = divergence
-    search = divergence
-    norm_now = squares(residual)
+    half_width = 6.0
+    basis = [divergence]
+    padded_basis = []
+    for j in range(ITERS):
+        padded = pressure_pad(basis[j])
+        padded_basis.append(padded)
+        scaled = neighbour_sum(padded) * (-1.0 / half_width)
+        if j == 0:
+            basis.append(scaled)
+        else:
+            basis.append(2.0 * scaled - basis[j - 1])
+    size = ITERS + 1
+    pairs = [(i, j) for i in range(size) for j in range(i, size)]
+    local = jnp.stack([jnp.sum(basis[i] * basis[j]) for i, j in pairs])
+    total = lax.psum(local, ("axial", "azim"))
+    gram = [[None] * size for _ in range(size)]
+    for n, (i, j) in enumerate(pairs):
+        gram[i][j] = total[n]
+        gram[j][i] = total[n]
+    shift = 6.0 + SHIFT_PRESSURE
+
+    def apply_a(c):
+        out = [shift * c[j] for j in range(size)]
+        for j in range(size - 1):
+            if j == 0:
+                out[1] = out[1] + half_width * c[0]
+            else:
+                out[j + 1] = out[j + 1] + 0.5 * half_width * c[j]
+                out[j - 1] = out[j - 1] + 0.5 * half_width * c[j]
+        return out
+
+    def inner(a, b):
+        acc = None
+        for i in range(size):
+            for j in range(size):
+                if isinstance(a[i], float) and a[i] == 0.0:
+                    continue
+                if isinstance(b[j], float) and b[j] == 0.0:
+                    continue
+                term = a[i] * gram[i][j] * b[j]
+                acc = term if acc is None else acc + term
+        return acc
+
+    zero = 0.0
+    solution_c = [zero] * size
+    residual = [1.0] + [zero] * (size - 1)
+    search = list(residual)
+    norm_now = inner(residual, residual)
     for iteration in range(ITERS):
-        image = operate(search)
-        alpha = norm_now / lax.psum(jnp.sum(search * image), ("axial", "azim"))
-        pressure = pressure + alpha * search
-        residual = residual - alpha * image
-        norm_next = squares(residual)
-        search = residual + norm_next / norm_now * search
+        image = apply_a(search)
+        alpha = norm_now / inner(search, image)
+        solution_c = [solution_c[j] + alpha * search[j] for j in range(size)]
+        residual = [residual[j] - alpha * image[j] for j in range(size)]
+        if iteration == ITERS - 1:
+            break
+        norm_next = inner(residual, residual)
+        search = [residual[j] + norm_next / norm_now * search[j] for j in range(size)]
         norm_now = norm_next
-    return pressure
+    pressure = solution_c[0] * basis[0]
+    padded_pressure = solution_c[0] * padded_basis[0]
+    for j in range(1, ITERS):
+        pressure = pressure + solution_c[j] * basis[j]
+        padded_pressure = padded_pressure + solution_c[j] * padded_basis[j]
+    return pressure, padded_pressure
 
 
 def along_axial(buffer, step_by):
@@ -237,8 +290,7 @@
             shifted(vel_pad[direction], 2, direction, 1)
             - shifted(vel_pad[direction], 2, direction, -1)
         )
-    pressure = solve_pressure(divergence)
-    padded_pressure = pressure_pad(pressure)
+    pressure, padded_pressure = solve_pressure(divergence)
     velocity_new = jnp.stack(
         [
             velocity[d]

time: 989 us -> 448 us (0.45)
  blocking collectives: 822 us -> 214 us
  between operations: 11.8 us -> 93.8 us
  other arithmetic: 56.8 us -> 37.4 us
    psum x7 -> x1, blocking collectives: 713 us -> 105 us  [solve_pressure(): total = lax.psum(local, ('axial', 'azim'))]
    ppermute x12 -> x10, starting transfers between devices: 36.2 us -> 27.7 us  [extended(): lax.ppermute(lax.slice_in_dim(block, block.shape[dim] - width, None, axis...]
  transfers between devices with their start and end apart: 28 -> 24, of which waited for: 11 -> 13; matrix products, arithmetic and copies ran while one was open for 6% -> 11% of each run, Pallas kernels for 0% -> 0%
where the time goes in v1:
time: 448 us; the launch traced here: 443 us
  blocking collectives  214 us (48%)
  between operations  93.8 us (21%)
  starting transfers between devices  50.6 us (11%)
  other arithmetic  37.4 us (8%)
  local copies, waits for them, and re-layouts  20.3 us (5%)
  waiting for transfers between devices  20.2 us (5%)
  matrix products  6.24 us (1%)
    pmax x1, blocking collectives, on_device(): fastest = lax.pmax(jnp.max(jnp.abs(velocity)), ('axial', 'azim'))  110 us
    psum x1, blocking collectives, solve_pressure(): total = lax.psum(local, ('axial', 'azim'))  105 us
    ppermute x10, starting transfers between devices, extended(): lax.ppermute(lax.slice_in_dim(block, block.shape[dim] - width, None, axis...  27.7 us
    ppermute x10, waiting for transfers between devices, extended(): lax.ppermute(lax.slice_in_dim(block, block.shape[dim] - width, None, axis...  15.3 us
    ppermute x10, starting transfers between devices, extended(): lax.ppermute(lax.slice_in_dim(block, 0, width, axis=dim), axis, backward)  14.1 us
    mul x8, other arithmetic, evaporate(): sources = jnp.stack([heat_source * alive_mask, lost_mass * alive_mask])  11.7 us
    another operation x1, local copies, waits for them, and re-layouts, solve_pressure(): local = jnp.stack([jnp.sum(basis[i] * basis[j]) for i, j in pairs])  9.33 us
  transfers between devices with their start and end apart: 24, of which 13 were waited for; matrix products, arithmetic and copies ran while one was open for 11% of the time, Pallas kernels for 0%

profile of v1, /device:TPU:6, one launch (start us, length us, event | category | flops | bytes accessed | tf_op | source)
XLA Modules:
  0.0 443.3 jit_solution(8661759650428608741)
XLA Ops:
  1.6 3.7 collective-permute-start
  5.4 2.1 collective-permute-start.1
  9.9 109.5 %pmax.7 = f32[]{:T(128)} all-reduce(f32[]{:T(128)} %abs_reduce_fusion), channel_id=1, replica_groups=mesh['axial'=64,'azim'=8] {'axial','azim'}, use_global_device_ids=true, to_apply=%region_1.0 | all-reduce | flops 1 | bytes 8 | tf_op jit(solution)/shard_map/pmax | solution.py:222
  121.0 31.6 %while.18 = (s32[]{:T(128)}, f32[64,256]{1,0:T(8,128)S(1)}, f32[8,2048]{1,0:T(8,128)S(1)}, s32[2048]{0:T(1024)}, s32[]{:T(128)}, /*index=5*/f32[8,2048]{1,0:T(8,...) while((s32[]{:T(128)}, f32[64,256]{1,0:T(8,128)S(1)}, ...), condition=%wide.region_4.5_spmd.clone, body=%wide.region_2.4_spmd.clone.sunk | while | flops 353384960 | bytes 5411153 | solution.py:264
  155.4 2.9 collective-permute-start.22
  158.4 3.9 collective-permute-start.21
  163.7 2.4 collective-permute-done.3
  166.1 3.1 collective-permute-done.2
  169.6 1.6 fusion.79
  171.1 2.7 copy.247
  176.7 1.9 collective-permute-start.5
  178.6 6.0 %collective-permute-start.4 = (f32[1,8,128]{2,1,0:T(8,128)S(1)}, f32[1,8,128]{2,1,0:T(8,128)S(1)}, u32[]{:S(2)}, u32[]{:S(2)}) collective-permute-start(f32[1,8,128]{2,1,0:T(8,128)S(1)} %get-tuple-element.356), channel_id=1, source_target_pairs={{0,8},{8,16},{16,24},{24,32},{32,40},{40,48},{48,56},{56,64},{64,7... | collective-permute-start | bytes 12296 | tf_op jit(solution)/shard_map/ppermute | solution.py:26
  187.3 1.9 collective-permute-start.20
  190.4 1.9 collective-permute-start.9
  192.4 6.3 %collective-permute-start.8 = (f32[1,8,128]{2,1,0:T(8,128)S(1)}, f32[1,8,128]{2,1,0:T(8,128)S(1)}, u32[]{:S(2)}, u32[]{:S(2)}) collective-permute-start(f32[1,8,128]{2,1,0:T(8,128)S(1)} %get-tuple-element.354), channel_id=1, source_target_pairs={{0,8},{8,16},{16,24},{24,32},{32,40},{40,48},{48,56},{56,64},{64,7... | collective-permute-start | bytes 12296 | tf_op jit(solution)/shard_map/ppermute | solution.py:26
  202.7 2.9 collective-permute-done.10
  205.8 3.6 collective-permute-start.13
  209.5 4.3 collective-permute-start.12
  216.5 2.9 collective-permute-done.14
  219.6 3.1 collective-permute-start.17
  222.7 5.3 %collective-permute-start.16 = (f32[1,8,128]{2,1,0:T(8,128)S(1)}, f32[1,8,128]{2,1,0:T(8,128)S(1)}, u32[]{:S(2)}, u32[]{:S(2)}) collective-permute-start(f32[1,8,128]{2,1,0:T(8,128)S(1)} %get-tuple-element.350), channel_id=1, source_target_pairs={{0,8},{8,16},{16,24},{24,32},{32,40},{40,48},{48,56},{56,64},{64,7... | collective-permute-start | bytes 12296 | tf_op jit(solution)/shard_map/ppermute | solution.py:26
  230.9 2.9 collective-permute-done.18
  234.7 9.3 %stack.131 = f32[15]{0:T(128)S(1)} concatenate(f32[1]{0:T(128)} %bitcast.15, f32[1]{0:T(128)} %bitcast.16, f32[1]{0:T(128)} %bitcast.17, f32[1]{0:T(128)} %bitcast.18, f32[1]{0:T(128)} %bitcast.19, f32[1]{0:T(128)} %bitcast.20, f32[1]{0:T(128)} %bitcast.21, f32[1]{0:T(128)} %bitcast.22, f32[1]{0:T(128)} %bitcast.23, f32[1]{0:T(128)} %bitcast.24, f32[1]{0:T(128)} %bitcast.25, ...), dimensions={0} | concatenate | bytes 120 | tf_op jit(solution)/shard_map/stack | solution.py:159
  244.8 104.7 %psum.7 = f32[15]{0:T(128)S(1)} all-reduce(f32[15]{0:T(128)S(1)} %stack.131), channel_id=1, replica_groups=mesh['axial'=64,'azim'=8] {'axial','azim'}, use_global_device_ids=true, to_apply=%region_20.21 | all-reduce | flops 15 | bytes 120 | tf_op jit(solution)/shard_map/psum | solution.py:160
  (167 shorter events, 59.6 us)
Async XLA Ops:
  1.6 161.3 %collective-permute-start = (f32[14,2,8,128]{3,2,1,0:T(8,128)S(1)}, f32[14,2,8,128]{3,2,1,0:T(8,128)S(1)}, u32[]{:S(2)}, u32[]{:S(2)}) collective-permute-start(f32[14,2,8,128]{3,2,1,0:T(8,128)S(1)} %get-tuple-element.335), channel_id=1, source_target_pairs={{0,8},{8,16},{16,24},{24,32},{32,40},{40,48},{48,56},{56,64},{64,7... | collective-permute-start | bytes 344072 | tf_op jit(solution)/shard_map/ppermute | solution.py:26
  5.4 157.7 %collective-permute-start.1 = (f32[14,2,8,128]{3,2,1,0:T(8,128)S(1)}, f32[14,2,8,128]{3,2,1,0:T(8,128)S(1)}, u32[]{:S(2)}, u32[]{:S(2)}) collective-permute-start(f32[14,2,8,128]{3,2,1,0:T(8,128)S(1)} %get-tuple-element.334), channel_id=1, source_target_pairs={{8,0},{16,8},{24,16},{32,24},{40,32},{48,40},{56,48},{64,56},{72,6... | collective-permute-start | bytes 344072 | tf_op jit(solution)/shard_map/ppermute | solution.py:29
  155.4 37.0 %collective-permute-start.23 = (f32[8,64]{1,0:T(8,128)S(1)}, f32[8,64]{1,0:T(8,128)S(1)}, u32[]{:S(2)}, u32[]{:S(2)}) collective-permute-start(f32[8,64]{1,0:T(8,128)S(1)} %get-tuple-element.359), channel_id=1, source_target_pairs={{0,1},{1,2},{2,3},{3,4},{4,5},{5,6},{6,7},{7,0},{8,9},{9,10},{10,1... | collective-permute-start | bytes 6152 | tf_op jit(solution)/shard_map/ppermute | solution.py:42
  155.4 43.3 %collective-permute-start.22 = (f32[8,64]{1,0:T(8,128)S(1)}, f32[8,64]{1,0:T(8,128)S(1)}, u32[]{:S(2)}, u32[]{:S(2)}) collective-permute-start(f32[8,64]{1,0:T(8,128)S(1)} %get-tuple-element.360), channel_id=1, source_target_pairs={{0,7},{1,0},{2,1},{3,2},{4,3},{5,4},{6,5},{7,6},{8,15},{9,8},{10,9... | collective-permute-start | bytes 6152 | tf_op jit(solution)/shard_map/ppermute | solution.py:42
  158.4 40.3 %collective-permute-start.21 = (f32[8,64]{1,0:T(8,128)S(1)}, f32[8,64]{1,0:T(8,128)S(1)}, u32[]{:S(2)}, u32[]{:S(2)}) collective-permute-start(f32[8,64]{1,0:T(8,128)S(1)} %get-tuple-element.361), channel_id=1, source_target_pairs={{0,8},{8,16},{16,24},{24,32},{32,40},{40,48},{48,56},{56,64},{64,7... | collective-permute-start | bytes 6152 | tf_op jit(solution)/shard_map/ppermute | solution.py:37
  163.2 2.9 collective-permute-start.3
  163.2 6.1 %collective-permute-start.2 = (f32[14,12,2,128]{3,2,1,0:T(2,128)S(1)}, f32[14,12,2,128]{3,2,1,0:T(2,128)S(1)}, u32[]{:S(2)}, u32[]{:S(2)}) collective-permute-start(f32[14,12,2,128]{3,2,1,0:T(2,128)S(1)} %get-tuple-element.329), channel_id=1, source_target_pairs={{0,1},{1,2},{2,3},{3,4},{4,5},{5,6},{6,7},{7,0},{8,9},{9,10},{10,1... | collective-permute-start | bytes 516104 | tf_op jit(solution)/shard_map/ppermute | solution.py:26
  176.7 8.0 %collective-permute-start.5 = (f32[1,8,128]{2,1,0:T(8,128)S(1)}, f32[1,8,128]{2,1,0:T(8,128)S(1)}, u32[]{:S(2)}, u32[]{:S(2)}) collective-permute-start(f32[1,8,128]{2,1,0:T(8,128)S(1)} %get-tuple-element.357), channel_id=1, source_target_pairs={{8,0},{16,8},{24,16},{32,24},{40,32},{48,40},{56,48},{64,56},{72,6... | collective-permute-start | bytes 12296 | tf_op jit(solution)/shard_map/ppermute | solution.py:29
  178.6 7.3 %collective-permute-start.4 = (f32[1,8,128]{2,1,0:T(8,128)S(1)}, f32[1,8,128]{2,1,0:T(8,128)S(1)}, u32[]{:S(2)}, u32[]{:S(2)}) collective-permute-start(f32[1,8,128]{2,1,0:T(8,128)S(1)} %get-tuple-element.356), channel_id=1, source_target_pairs={{0,8},{8,16},{16,24},{24,32},{32,40},{40,48},{48,56},{56,64},{64,7... | collective-permute-start | bytes 12296 | tf_op jit(solution)/shard_map/ppermute | solution.py:26
  186.0 1.4 collective-permute-start.7
  186.0 4.3 collective-permute-start.6
  187.3 11.4 %collective-permute-start.20 = (f32[8,64]{1,0:T(8,128)S(1)}, f32[8,64]{1,0:T(8,128)S(1)}, u32[]{:S(2)}, u32[]{:S(2)}) collective-permute-start(f32[8,64]{1,0:T(8,128)S(1)} %get-tuple-element.358), channel_id=1, source_target_pairs={{8,0},{16,8},{24,16},{32,24},{40,32},{48,40},{56,48},{64,56},{72,6... | collective-permute-start | bytes 6152 | tf_op jit(solution)/shard_map/ppermute | solution.py:37
  190.4 8.9 %collective-permute-start.9 = (f32[1,8,128]{2,1,0:T(8,128)S(1)}, f32[1,8,128]{2,1,0:T(8,128)S(1)}, u32[]{:S(2)}, u32[]{:S(2)}) collective-permute-start(f32[1,8,128]{2,1,0:T(8,128)S(1)} %get-tuple-element.355), channel_id=1, source_target_pairs={{8,0},{16,8},{24,16},{32,24},{40,32},{48,40},{56,48},{64,56},{72,6... | collective-permute-start | bytes 12296 | tf_op jit(solution)/shard_map/ppermute | solution.py:29
  192.4 7.6 %collective-permute-start.8 = (f32[1,8,128]{2,1,0:T(8,128)S(1)}, f32[1,8,128]{2,1,0:T(8,128)S(1)}, u32[]{:S(2)}, u32[]{:S(2)}) collective-permute-start(f32[1,8,128]{2,1,0:T(8,128)S(1)} %get-tuple-element.354), channel_id=1, source_target_pairs={{0,8},{8,16},{16,24},{24,32},{32,40},{40,48},{48,56},{56,64},{64,7... | collective-permute-start | bytes 12296 | tf_op jit(solution)/shard_map/ppermute | solution.py:26
  200.0 2.7 collective-permute-start.11
  201.4 4.3 collective-permute-start.10
  205.8 8.9 %collective-permute-start.13 = (f32[1,8,128]{2,1,0:T(8,128)S(1)}, f32[1,8,128]{2,1,0:T(8,128)S(1)}, u32[]{:S(2)}, u32[]{:S(2)}) collective-permute-start(f32[1,8,128]{2,1,0:T(8,128)S(1)} %get-tuple-element.353), channel_id=1, source_target_pairs={{8,0},{16,8},{24,16},{32,24},{40,32},{48,40},{56,48},{64,56},{72,6... | collective-permute-start | bytes 12296 | tf_op jit(solution)/shard_map/ppermute | solution.py:29
  209.5 5.6 %collective-permute-start.12 = (f32[1,8,128]{2,1,0:T(8,128)S(1)}, f32[1,8,128]{2,1,0:T(8,128)S(1)}, u32[]{:S(2)}, u32[]{:S(2)}) collective-permute-start(f32[1,8,128]{2,1,0:T(8,128)S(1)} %get-tuple-element.352), channel_id=1, source_target_pairs={{0,8},{8,16},{16,24},{24,32},{32,40},{40,48},{48,56},{56,64},{64,7... | collective-permute-start | bytes 12296 | tf_op jit(solution)/shard_map/ppermute | solution.py:26
  215.1 1.4 collective-permute-start.15
  215.2 4.3 collective-permute-start.14
  219.6 9.8 %collective-permute-start.17 = (f32[1,8,128]{2,1,0:T(8,128)S(1)}, f32[1,8,128]{2,1,0:T(8,128)S(1)}, u32[]{:S(2)}, u32[]{:S(2)}) collective-permute-start(f32[1,8,128]{2,1,0:T(8,128)S(1)} %get-tuple-element.351), channel_id=1, source_target_pairs={{8,0},{16,8},{24,16},{32,24},{40,32},{48,40},{56,48},{64,56},{72,6... | collective-permute-start | bytes 12296 | tf_op jit(solution)/shard_map/ppermute | solution.py:29
  222.7 6.8 %collective-permute-start.16 = (f32[1,8,128]{2,1,0:T(8,128)S(1)}, f32[1,8,128]{2,1,0:T(8,128)S(1)}, u32[]{:S(2)}, u32[]{:S(2)}) collective-permute-start(f32[1,8,128]{2,1,0:T(8,128)S(1)} %get-tuple-element.350), channel_id=1, source_target_pairs={{0,8},{8,16},{16,24},{24,32},{32,40},{40,48},{48,56},{56,64},{64,7... | collective-permute-start | bytes 12296 | tf_op jit(solution)/shard_map/ppermute | solution.py:26
  229.5 1.4 collective-permute-start.19
  229.5 4.3 collective-permute-start.18
  (7 other events, 487.1 us)

commit v2 on v1

--- a/solution.py
+++ b/solution.py
@@ -2,6 +2,8 @@
 import jax.numpy as jnp
 from jax import lax
 from jax.sharding import PartitionSpec as P
+from jax.experimental import pallas as pl
+from jax.experimental.pallas import tpu as pltpu
 
 CAP = 64
 ITERS = 4
@@ -136,13 +138,79 @@
     return (6.0 + SHIFT_PRESSURE) * values - beside
 
 
+def butterfly_partners():
+    rounds = []
+    for axis in ("azim", "axial"):
+        step = 1
+        while step < lax.axis_size(axis):
+            rounds.append((axis, step))
+            step *= 2
+    return rounds
+
+
+def reduce_kernel(rounds, x_ref, o_ref, send_buf, recv_buf, send_sems, recv_sems):
+    here = {"axial": lax.axis_index("axial"), "azim": lax.axis_index("azim")}
+
+    def partner(axis, step):
+        index = here[axis]
+        other = index + step - 2 * step * ((index // step) % 2)
+        coords = dict(here)
+        coords[axis] = other
+        return (coords["axial"], coords["azim"])
+
+    barrier = pltpu.get_barrier_semaphore()
+    for axis, step in rounds:
+        pl.semaphore_signal(
+            barrier, inc=1, device_id=partner(axis, step), device_id_type=pl.DeviceIdType.MESH
+        )
+    pl.semaphore_wait(barrier, len(rounds))
+    row = lax.broadcasted_iota(jnp.int32, x_ref.shape, 0)
+    lane = lax.broadcasted_iota(jnp.int32, x_ref.shape, 1)
+    is_max = (row == 0) & (lane == 0)
+    acc = x_ref[...]
+    for r, (axis, step) in enumerate(rounds):
+        send_buf[r] = acc
+        copy = pltpu.make_async_remote_copy(
+            src_ref=send_buf.at[r],
+            dst_ref=recv_buf.at[r],
+            send_sem=send_sems.at[r],
+            recv_sem=recv_sems.at[r],
+            device_id=partner(axis, step),
+            device_id_type=pl.DeviceIdType.MESH,
+        )
+        copy.start()
+        copy.wait()
+        other = recv_buf[r]
+        acc = jnp.where(is_max, jnp.maximum(acc, other), acc + other)
+    o_ref[...] = acc
+
+
+def global_reduce(values):
+    rounds = butterfly_partners()
+    tile = jnp.zeros((8, 128), jnp.float32).at[0, : values.shape[0]].set(values)
+    out = pl.pallas_call(
+        lambda *refs: reduce_kernel(rounds, *refs),
+        out_shape=jax.ShapeDtypeStruct((8, 128), jnp.float32),
+        in_specs=[pl.BlockSpec(memory_space=pltpu.VMEM)],
+        out_specs=pl.BlockSpec(memory_space=pltpu.VMEM),
+        scratch_shapes=[
+            pltpu.VMEM((len(rounds), 8, 128), jnp.float32),
+            pltpu.VMEM((len(rounds), 8, 128), jnp.float32),
+            pltpu.SemaphoreType.DMA((len(rounds),)),
+            pltpu.SemaphoreType.DMA((len(rounds),)),
+        ],
+        compiler_params=pltpu.CompilerParams(collective_id=0, has_side_effects=True),
+    )(tile)
+    return out[0, : values.shape[0]]
+
+
 def neighbour_sum(padded):
     beside = shifted(padded, 1, 0, 1) + shifted(padded, 1, 0, -1)
     beside = beside + shifted(padded, 1, 1, 1) + shifted(padded, 1, 1, -1)
     return beside + shifted(padded, 1, 2, 1) + shifted(padded, 1, 2, -1)
 
 
-def solve_pressure(divergence):
+def solve_pressure(divergence, local_fastest):
     half_width = 6.0
     basis = [divergence]
     padded_basis = []
@@ -156,8 +224,10 @@
             basis.append(2.0 * scaled - basis[j - 1])
     size = ITERS + 1
     pairs = [(i, j) for i in range(size) for j in range(i, size)]
-    local = jnp.stack([jnp.sum(basis[i] * basis[j]) for i, j in pairs])
-    total = lax.psum(local, ("axial", "azim"))
+    local = jnp.stack([local_fastest] + [jnp.sum(basis[i] * basis[j]) for i, j in pairs])
+    reduced = global_reduce(local)
+    fastest = reduced[0]
+    total = reduced[1:]
     gram = [[None] * size for _ in range(size)]
     for n, (i, j) in enumerate(pairs):
         gram[i][j] = total[n]
@@ -201,12 +271,10 @@
         norm_next = inner(residual, residual)
         search = [residual[j] + norm_next / norm_now * search[j] for j in range(size)]
         norm_now = norm_next
-    pressure = solution_c[0] * basis[0]
     padded_pressure = solution_c[0] * padded_basis[0]
     for j in range(1, ITERS):
-        pressure = pressure + solution_c[j] * basis[j]
         padded_pressure = padded_pressure + solution_c[j] * padded_basis[j]
-    return pressure, padded_pressure
+    return padded_pressure, fastest
 
 
 def along_axial(buffer, step_by):
@@ -219,14 +287,21 @@
 
 def on_device(state, diff_coef, parcel_state, parcel_cell, parcel_dest, live_count):
     velocity = state[1:4]
-    fastest = lax.pmax(jnp.max(jnp.abs(velocity)), ("axial", "azim"))
-    step_size = CFL / (fastest + 1e-06)
+    local_fastest = jnp.max(jnp.abs(velocity))
     whole_pad = extended(state, (("axial", 1), ("azim", 2)), 2)
     whole_pad = radial_pad(clear_ends(whole_pad, 2, 1), 2, "edge")
     moving = whole_pad[1:]
     density_pad = whole_pad[0]
     density_rim = 2
     vel_pad = moving[0:3]
+    divergence = jnp.zeros_like(state[0])
+    for direction in range(3):
+        divergence = divergence + 0.5 * (
+            shifted(vel_pad[direction], 2, direction, 1)
+            - shifted(vel_pad[direction], 2, direction, -1)
+        )
+    padded_pressure, fastest = solve_pressure(divergence, local_fastest)
+    step_size = CFL / (fastest + 1e-06)
     transported = transport(
         moving[3:], vel_pad, density_pad, density_rim, diff_coef[:, None, None, None], step_size
     )
@@ -284,13 +359,6 @@
         ]
     )
     kept_parcels = jnp.where((parcel_dest == 0)[None], updated, jnp.float32(0.0))
-    divergence = jnp.zeros_like(state[0])
-    for direction in range(3):
-        divergence = divergence + 0.5 * (
-            shifted(vel_pad[direction], 2, direction, 1)
-            - shifted(vel_pad[direction], 2, direction, -1)
-        )
-    pressure, padded_pressure = solve_pressure(divergence)
     velocity_new = jnp.stack(
         [
             velocity[d]

time: 448 us -> 315 us (0.70)
  blocking collectives: 214 us -> 0 us
  Pallas kernels: 0 us -> 39.4 us
  other arithmetic: 37.4 us -> 51.8 us
  waiting for transfers between devices: 20.2 us -> 30.4 us
  local copies, waits for them, and re-layouts: 20.3 us -> 29.9 us
  starting transfers between devices: 50.6 us -> 55.4 us
    pmax x1 -> x0, blocking collectives: 110 us -> none  [on_device(): fastest = lax.pmax(jnp.max(jnp.abs(velocity)), ('axial', 'azim'))]
    psum x1 -> x0, blocking collectives: 105 us -> none  [solve_pressure(): total = lax.psum(local, ('axial', 'azim'))]
    pallas_call x0 -> x1, Pallas kernels: none -> 39.4 us  [global_reduce(): pl.pallas_call(lambda *refs: reduce_kernel(rounds, *refs), out_shape=jax....]
    ppermute x10, starting transfers between devices: 14.1 us -> 26.7 us  [extended(): lax.ppermute(lax.slice_in_dim(block, 0, width, axis=dim), axis, backward)]
    ppermute x10, starting transfers between devices: 27.7 us -> 18.6 us  [extended(): lax.ppermute(lax.slice_in_dim(block, block.shape[dim] - width, None, axis...]
    ppermute x10, waiting for transfers between devices: 15.3 us -> 21.3 us  [extended(): lax.ppermute(lax.slice_in_dim(block, block.shape[dim] - width, None, axis...]
    add x1, other arithmetic: 1.41 us -> 7.39 us  [transport(): return center + step_size * change]
  transfers between devices with their start and end apart: 24 -> 24, of which waited for: 13 -> 14; matrix products, arithmetic and copies ran while one was open for 11% -> 5% of each run, Pallas kernels for 0% -> 0%
where the time goes in v2:
time: 315 us; the launch traced here: 312 us
  between operations  97.3 us (31%)
  starting transfers between devices  55.4 us (18%)
  other arithmetic  51.8 us (16%)
  Pallas kernels  39.4 us (13%)
  waiting for transfers between devices  30.4 us (10%)
  local copies, waits for them, and re-layouts  29.9 us (9%)
  matrix products  7.08 us (2%)
    pallas_call x1, Pallas kernels, global_reduce(): pl.pallas_call(lambda *refs: reduce_kernel(rounds, *refs), out_shape=jax....  39.4 us
    ppermute x10, starting transfers between devices, extended(): lax.ppermute(lax.slice_in_dim(block, 0, width, axis=dim), axis, backward)  26.7 us
    ppermute x10, waiting for transfers between devices, extended(): lax.ppermute(lax.slice_in_dim(block, block.shape[dim] - width, None, axis...  21.3 us
    ppermute x10, starting transfers between devices, extended(): lax.ppermute(lax.slice_in_dim(block, block.shape[dim] - width, None, axis...  18.6 us
    mul x8, other arithmetic, evaporate(): sources = jnp.stack([heat_source * alive_mask, lost_mass * alive_mask])  11.7 us
    another operation x1, local copies, waits for them, and re-layouts, solve_pressure(): jnp.stack([local_fastest] + [jnp.sum(basis[i] * basis[j]) for i, j in pai...  10.2 us
    add x1, other arithmetic, transport(): return center + step_size * change  7.39 us
    ppermute x2, starting transfers between devices, shifted_2(): return lax.ppermute(shard, axis, pairs)  7.16 us
  transfers between devices with their start and end apart: 24, of which 14 were waited for; matrix products, arithmetic and copies ran while one was open for 5% of the time, Pallas kernels for 0%

profile of v2, /device:TPU:6, one launch (start us, length us, event | category | flops | bytes accessed | tf_op | source)
XLA Modules:
  0.0 311.7 jit_solution(7158535999577288016)
XLA Ops:
  1.7 3.7 %collective-permute-start = (f32[14,2,8,128]{3,2,1,0:T(8,128)S(1)}, f32[14,2,8,128]{3,2,1,0:T(8,128)S(1)}, u32[]{:S(2)}, u32[]{:S(2)}) collective-permute-start(f32[14,2,8,128]{3,2,1,0:T(8,128)S(1)} %get-tuple-element.347), channel_id=1, source_target_pairs={{0,8},{8,16},{16,24},{24,32},{32,40},{40,48},{48,56},{56,64},{64,7... | collective-permute-start | bytes 344072 | tf_op jit(solution)/shard_map/ppermute | solution.py:28
  5.4 2.1 collective-permute-start.1
  16.0 2.3 collective-permute-done.3
  18.3 3.1 %collective-permute-done.2 = f32[14,12,2,128]{3,2,1,0:T(2,128)S(1)} collective-permute-done((f32[14,12,2,128]{3,2,1,0:T(2,128)S(1)}, f32[14,12,2,128]{3,2,1,0:T(2,128)S(1)}, u32[]{:S(2)}, u32[]{:S(2)}) %collective-permute-start.2) | collective-permute-done | bytes 172064 | tf_op jit(solution)/shard_map/ppermute | solution.py:28
  23.3 2.7 copy.247
  26.1 2.1 copy.248
  34.0 6.0 %collective-permute-start.4 = (f32[1,8,128]{2,1,0:T(8,128)S(1)}, f32[1,8,128]{2,1,0:T(8,128)S(1)}, u32[]{:S(2)}, u32[]{:S(2)}) collective-permute-start(f32[1,8,128]{2,1,0:T(8,128)S(1)} %get-tuple-element.368), channel_id=1, source_target_pairs={{0,8},{8,16},{16,24},{24,32},{32,40},{40,48},{48,56},{56,64},{64,7... | collective-permute-start | bytes 12296 | tf_op jit(solution)/shard_map/ppermute | solution.py:28
  42.7 2.9 collective-permute-done.6
  45.8 9.1 %collective-permute-start.9 = (f32[1,8,128]{2,1,0:T(8,128)S(1)}, f32[1,8,128]{2,1,0:T(8,128)S(1)}, u32[]{:S(2)}, u32[]{:S(2)}) collective-permute-start(f32[1,8,128]{2,1,0:T(8,128)S(1)} %get-tuple-element.367), channel_id=1, source_target_pairs={{8,0},{16,8},{24,16},{32,24},{40,32},{48,40},{56,48},{64,56},{72,6... | collective-permute-start | bytes 12296 | tf_op jit(solution)/shard_map/ppermute | solution.py:31
  57.1 3.9 %collective-permute-done.8 = f32[1,8,128]{2,1,0:T(8,128)S(1)} collective-permute-done((f32[1,8,128]{2,1,0:T(8,128)S(1)}, f32[1,8,128]{2,1,0:T(8,128)S(1)}, u32[]{:S(2)}, u32[]{:S(2)}) %collective-permute-start.8) | collective-permute-done | bytes 4128 | tf_op jit(solution)/shard_map/ppermute | solution.py:28
  62.4 2.9 collective-permute-done.10
  65.5 7.2 %collective-permute-start.13 = (f32[1,8,128]{2,1,0:T(8,128)S(1)}, f32[1,8,128]{2,1,0:T(8,128)S(1)}, u32[]{:S(2)}, u32[]{:S(2)}) collective-permute-start(f32[1,8,128]{2,1,0:T(8,128)S(1)} %get-tuple-element.365), channel_id=1, source_target_pairs={{8,0},{16,8},{24,16},{32,24},{40,32},{48,40},{56,48},{64,56},{72,6... | collective-permute-start | bytes 12296 | tf_op jit(solution)/shard_map/ppermute | solution.py:31
  75.9 2.3 collective-permute-done.12
  81.2 2.3 collective-permute-done.14
  84.4 5.2 %collective-permute-start.17 = (f32[1,8,128]{2,1,0:T(8,128)S(1)}, f32[1,8,128]{2,1,0:T(8,128)S(1)}, u32[]{:S(2)}, u32[]{:S(2)}) collective-permute-start(f32[1,8,128]{2,1,0:T(8,128)S(1)} %get-tuple-element.363), channel_id=1, source_target_pairs={{8,0},{16,8},{24,16},{32,24},{40,32},{48,40},{56,48},{64,56},{72,6... | collective-permute-start | bytes 12296 | tf_op jit(solution)/shard_map/ppermute | solution.py:31
  89.7 3.0 collective-permute-start.16
  95.9 2.7 slice_multiply_fusion.2
  101.3 10.2 %stack.135 = f32[16]{0:T(128)S(1)} concatenate(f32[1]{0:T(128)} %bitcast, f32[1]{0:T(128)} %bitcast.8, f32[1]{0:T(128)} %bitcast.9, f32[1]{0:T(128)} %bitcast.10, f32[1]{0:T(128)} %bitcast.11, f32[1]{0:T(128)} %bitcast.12, f32[1]{0:T(128)} %bitcast.13, f32[1]{0:T(128)} %bitcast.14, f32[1]{0:T(128)} %bitcast.15, f32[1]{0:T(128)} %bitcast.16, f32[1]{0:T(128)} %bitcast.17, ...), dimensions={0} | concatenate | bytes 128 | tf_op jit(solution)/shard_map/stack | solution.py:227
  112.0 39.4 %shard_map.93 = f32[8,128]{1,0:T(8,128)} custom-call(f32[8,128]{1,0:T(8,128)} %scatter.4.refs_0_), custom_call_target="tpu_custom_call" | custom-call | tf_op jit(solution)/shard_map/pallas_call | solution.py:191
  248.8 7.4 %fusion.19 = f32[10,8,8,128]{3,2,1,0:T(8,128)S(1)} fusion(f32[14,12,12,128]{3,2,1,0:T(8,128)S(1)} %maximum_select_fusion, f32[14,12,12,2]{3,2,1,0:T(8,128)S(1)} %reshape.241, f32[14,12,12,2]{3,2,1,0:T(8,128)} %copy-done, f32[10,12,12,132]{3,2,1,0:T(8,128)} %get-tuple-element.338, f32[10,12,12,132]{3,2,1,0:T(8,128)} %get-tuple-element.337, ...), kind=kLoop, calls=%fused_computation.52 | loop fusion | flops 4259840 | bytes 8863532 | tf_op jit(solution)/shard_map/add | solution.py:103
  257.6 34.0 %while.19 = (s32[]{:T(128)}, f32[64,256]{1,0:T(8,128)S(1)}, f32[8,2048]{1,0:T(8,128)}, s32[2048]{0:T(1024)}, s32[]{:T(128)}, /*index=5*/f32[8,2048]{1,0:T(8,128)...) while((s32[]{:T(128)}, f32[64,256]{1,0:T(8,128)S(1)}, ...), condition=%wide.region_18.19_spmd.clone, body=%wide.region_16.18_spmd.clone.sunk | while | flops 353384960 | bytes 5407057 | solution.py:339
  295.3 2.9 collective-permute-start.22
  298.2 5.2 %collective-permute-start.21 = (f32[8,64]{1,0:T(8,128)S(1)}, f32[8,64]{1,0:T(8,128)S(1)}, u32[]{:S(2)}, u32[]{:S(2)}) collective-permute-start(f32[8,64]{1,0:T(8,128)S(1)} %get-tuple-element.373), channel_id=1, source_target_pairs={{0,8},{8,16},{16,24},{24,32},{32,40},{40,48},{48,56},{56,64},{64,7... | collective-permute-start | bytes 6152 | tf_op jit(solution)/shard_map/ppermute | solution.py:39
  306.9 4.2 %collective-permute-done.20 = f32[8,64]{1,0:T(8,128)S(1)} collective-permute-done((f32[8,64]{1,0:T(8,128)S(1)}, f32[8,64]{1,0:T(8,128)S(1)}, u32[]{:S(2)}, u32[]{:S(2)}) %collective-permute-start.20) | collective-permute-done | bytes 2080 | tf_op jit(solution)/shard_map/ppermute | solution.py:39
  (207 shorter events, 80.8 us)
Async XLA Ops:
  1.7 10.8 %collective-permute-start = (f32[14,2,8,128]{3,2,1,0:T(8,128)S(1)}, f32[14,2,8,128]{3,2,1,0:T(8,128)S(1)}, u32[]{:S(2)}, u32[]{:S(2)}) collective-permute-start(f32[14,2,8,128]{3,2,1,0:T(8,128)S(1)} %get-tuple-element.347), channel_id=1, source_target_pairs={{0,8},{8,16},{16,24},{24,32},{32,40},{40,48},{48,56},{56,64},{64,7... | collective-permute-start | bytes 344072 | tf_op jit(solution)/shard_map/ppermute | solution.py:28
  5.4 8.8 %collective-permute-start.1 = (f32[14,2,8,128]{3,2,1,0:T(8,128)S(1)}, f32[14,2,8,128]{3,2,1,0:T(8,128)S(1)}, u32[]{:S(2)}, u32[]{:S(2)}) collective-permute-start(f32[14,2,8,128]{3,2,1,0:T(8,128)S(1)} %get-tuple-element.346), channel_id=1, source_target_pairs={{8,0},{16,8},{24,16},{32,24},{40,32},{48,40},{56,48},{64,56},{72,6... | collective-permute-start | bytes 344072 | tf_op jit(solution)/shard_map/ppermute | solution.py:31
  14.3 4.0 %collective-permute-start.3 = (f32[14,12,2,128]{3,2,1,0:T(2,128)S(1)}, f32[14,12,2,128]{3,2,1,0:T(2,128)S(1)}, u32[]{:S(2)}, u32[]{:S(2)}) collective-permute-start(f32[14,12,2,128]{3,2,1,0:T(2,128)S(1)} %get-tuple-element.342), channel_id=1, source_target_pairs={{1,0},{2,1},{3,2},{4,3},{5,4},{6,5},{7,6},{0,7},{9,8},{10,9},{11,1... | collective-permute-start | bytes 516104 | tf_op jit(solution)/shard_map/ppermute | solution.py:31
  15.4 6.0 %collective-permute-start.2 = (f32[14,12,2,128]{3,2,1,0:T(2,128)S(1)}, f32[14,12,2,128]{3,2,1,0:T(2,128)S(1)}, u32[]{:S(2)}, u32[]{:S(2)}) collective-permute-start(f32[14,12,2,128]{3,2,1,0:T(2,128)S(1)} %get-tuple-element.341), channel_id=1, source_target_pairs={{0,1},{1,2},{2,3},{3,4},{4,5},{5,6},{6,7},{7,0},{8,9},{9,10},{10,1... | collective-permute-start | bytes 516104 | tf_op jit(solution)/shard_map/ppermute | solution.py:28
  32.1 8.0 %collective-permute-start.5 = (f32[1,8,128]{2,1,0:T(8,128)S(1)}, f32[1,8,128]{2,1,0:T(8,128)S(1)}, u32[]{:S(2)}, u32[]{:S(2)}) collective-permute-start(f32[1,8,128]{2,1,0:T(8,128)S(1)} %get-tuple-element.369), channel_id=1, source_target_pairs={{8,0},{16,8},{24,16},{32,24},{40,32},{48,40},{56,48},{64,56},{72,6... | collective-permute-start | bytes 12296 | tf_op jit(solution)/shard_map/ppermute | solution.py:31
  34.0 7.3 %collective-permute-start.4 = (f32[1,8,128]{2,1,0:T(8,128)S(1)}, f32[1,8,128]{2,1,0:T(8,128)S(1)}, u32[]{:S(2)}, u32[]{:S(2)}) collective-permute-start(f32[1,8,128]{2,1,0:T(8,128)S(1)} %get-tuple-element.368), channel_id=1, source_target_pairs={{0,8},{8,16},{16,24},{24,32},{32,40},{40,48},{48,56},{56,64},{64,7... | collective-permute-start | bytes 12296 | tf_op jit(solution)/shard_map/ppermute | solution.py:28
  41.4 1.4 collective-permute-start.7
  41.4 4.3 %collective-permute-start.6 = (f32[10,1,128]{2,1,0:T(1,128)S(1)}, f32[10,1,128]{2,1,0:T(1,128)S(1)}, u32[]{:S(2)}, u32[]{:S(2)}) collective-permute-start(f32[10,1,128]{2,1,0:T(1,128)S(1)} %get-tuple-element.360), channel_id=1, source_target_pairs={{0,1},{1,2},{2,3},{3,4},{4,5},{5,6},{6,7},{7,0},{8,9},{9,10},{10,1... | collective-permute-start | bytes 15368 | tf_op jit(solution)/shard_map/ppermute | solution.py:28
  45.8 11.3 %collective-permute-start.9 = (f32[1,8,128]{2,1,0:T(8,128)S(1)}, f32[1,8,128]{2,1,0:T(8,128)S(1)}, u32[]{:S(2)}, u32[]{:S(2)}) collective-permute-start(f32[1,8,128]{2,1,0:T(8,128)S(1)} %get-tuple-element.367), channel_id=1, source_target_pairs={{8,0},{16,8},{24,16},{32,24},{40,32},{48,40},{56,48},{64,56},{72,6... | collective-permute-start | bytes 12296 | tf_op jit(solution)/shard_map/ppermute | solution.py:31
  54.9 6.1 %collective-permute-start.8 = (f32[1,8,128]{2,1,0:T(8,128)S(1)}, f32[1,8,128]{2,1,0:T(8,128)S(1)}, u32[]{:S(2)}, u32[]{:S(2)}) collective-permute-start(f32[1,8,128]{2,1,0:T(8,128)S(1)} %get-tuple-element.366), channel_id=1, source_target_pairs={{0,8},{8,16},{16,24},{24,32},{32,40},{40,48},{48,56},{56,64},{64,7... | collective-permute-start | bytes 12296 | tf_op jit(solution)/shard_map/ppermute | solution.py:28
  61.0 1.4 collective-permute-start.11
  61.0 4.3 %collective-permute-start.10 = (f32[10,1,128]{2,1,0:T(1,128)S(1)}, f32[10,1,128]{2,1,0:T(1,128)S(1)}, u32[]{:S(2)}, u32[]{:S(2)}) collective-permute-start(f32[10,1,128]{2,1,0:T(1,128)S(1)} %get-tuple-element.358), channel_id=1, source_target_pairs={{0,1},{1,2},{2,3},{3,4},{4,5},{5,6},{6,7},{7,0},{8,9},{9,10},{10,1... | collective-permute-start | bytes 15368 | tf_op jit(solution)/shard_map/ppermute | solution.py:28
  65.5 10.4 %collective-permute-start.13 = (f32[1,8,128]{2,1,0:T(8,128)S(1)}, f32[1,8,128]{2,1,0:T(8,128)S(1)}, u32[]{:S(2)}, u32[]{:S(2)}) collective-permute-start(f32[1,8,128]{2,1,0:T(8,128)S(1)} %get-tuple-element.365), channel_id=1, source_target_pairs={{8,0},{16,8},{24,16},{32,24},{40,32},{48,40},{56,48},{64,56},{72,6... | collective-permute-start | bytes 12296 | tf_op jit(solution)/shard_map/ppermute | solution.py:31
  72.8 5.5 %collective-permute-start.12 = (f32[1,8,128]{2,1,0:T(8,128)S(1)}, f32[1,8,128]{2,1,0:T(8,128)S(1)}, u32[]{:S(2)}, u32[]{:S(2)}) collective-permute-start(f32[1,8,128]{2,1,0:T(8,128)S(1)} %get-tuple-element.364), channel_id=1, source_target_pairs={{0,8},{8,16},{16,24},{24,32},{32,40},{40,48},{48,56},{56,64},{64,7... | collective-permute-start | bytes 12296 | tf_op jit(solution)/shard_map/ppermute | solution.py:28
  78.9 2.3 collective-permute-start.15
  78.9 4.6 %collective-permute-start.14 = (f32[10,1,128]{2,1,0:T(1,128)}, f32[10,1,128]{2,1,0:T(1,128)}, u32[]{:S(2)}, u32[]{:S(2)}) collective-permute-start(f32[10,1,128]{2,1,0:T(1,128)} %get-tuple-element.356), channel_id=1, source_target_pairs={{0,1},{1,2},{2,3},{3,4},{4,5},{5,6},{6,7},{7,0},{8,9},{9,10},{10,1... | collective-permute-start | bytes 15368 | tf_op jit(solution)/shard_map/ppermute | solution.py:28
  84.4 9.5 %collective-permute-start.17 = (f32[1,8,128]{2,1,0:T(8,128)S(1)}, f32[1,8,128]{2,1,0:T(8,128)S(1)}, u32[]{:S(2)}, u32[]{:S(2)}) collective-permute-start(f32[1,8,128]{2,1,0:T(8,128)S(1)} %get-tuple-element.363), channel_id=1, source_target_pairs={{8,0},{16,8},{24,16},{32,24},{40,32},{48,40},{56,48},{64,56},{72,6... | collective-permute-start | bytes 12296 | tf_op jit(solution)/shard_map/ppermute | solution.py:31
  89.7 5.6 %collective-permute-start.16 = (f32[1,8,128]{2,1,0:T(8,128)S(1)}, f32[1,8,128]{2,1,0:T(8,128)S(1)}, u32[]{:S(2)}, u32[]{:S(2)}) collective-permute-start(f32[1,8,128]{2,1,0:T(8,128)S(1)} %get-tuple-element.362), channel_id=1, source_target_pairs={{0,8},{8,16},{16,24},{24,32},{32,40},{40,48},{48,56},{56,64},{64,7... | collective-permute-start | bytes 12296 | tf_op jit(solution)/shard_map/ppermute | solution.py:28
  95.4 3.3 %collective-permute-start.19 = (f32[10,1,128]{2,1,0:T(1,128)S(1)}, f32[10,1,128]{2,1,0:T(1,128)S(1)}, u32[]{:S(2)}, u32[]{:S(2)}) collective-permute-start(f32[10,1,128]{2,1,0:T(1,128)S(1)} %get-tuple-element.355), channel_id=1, source_target_pairs={{1,0},{2,1},{3,2},{4,3},{5,4},{6,5},{7,6},{0,7},{9,8},{10,9},{11,1... | collective-permute-start | bytes 15368 | tf_op jit(solution)/shard_map/ppermute | solution.py:31
  95.4 4.3 %collective-permute-start.18 = (f32[10,1,128]{2,1,0:T(1,128)S(1)}, f32[10,1,128]{2,1,0:T(1,128)S(1)}, u32[]{:S(2)}, u32[]{:S(2)}) collective-permute-start(f32[10,1,128]{2,1,0:T(1,128)S(1)} %get-tuple-element.354), channel_id=1, source_target_pairs={{0,1},{1,2},{2,3},{3,4},{4,5},{5,6},{6,7},{7,0},{8,9},{9,10},{10,1... | collective-permute-start | bytes 15368 | tf_op jit(solution)/shard_map/ppermute | solution.py:28
  295.2 11.6 %collective-permute-start.23 = (f32[8,64]{1,0:T(8,128)S(1)}, f32[8,64]{1,0:T(8,128)S(1)}, u32[]{:S(2)}, u32[]{:S(2)}) collective-permute-start(f32[8,64]{1,0:T(8,128)S(1)} %get-tuple-element.371), channel_id=1, source_target_pairs={{0,1},{1,2},{2,3},{3,4},{4,5},{5,6},{6,7},{7,0},{8,9},{9,10},{10,1... | collective-permute-start | bytes 6152 | tf_op jit(solution)/shard_map/ppermute | solution.py:44
  295.3 11.6 %collective-permute-start.22 = (f32[8,64]{1,0:T(8,128)S(1)}, f32[8,64]{1,0:T(8,128)S(1)}, u32[]{:S(2)}, u32[]{:S(2)}) collective-permute-start(f32[8,64]{1,0:T(8,128)S(1)} %get-tuple-element.372), channel_id=1, source_target_pairs={{0,7},{1,0},{2,1},{3,2},{4,3},{5,4},{6,5},{7,6},{8,15},{9,8},{10,9... | collective-permute-start | bytes 6152 | tf_op jit(solution)/shard_map/ppermute | solution.py:44
  298.2 8.6 %collective-permute-start.21 = (f32[8,64]{1,0:T(8,128)S(1)}, f32[8,64]{1,0:T(8,128)S(1)}, u32[]{:S(2)}, u32[]{:S(2)}) collective-permute-start(f32[8,64]{1,0:T(8,128)S(1)} %get-tuple-element.373), channel_id=1, source_target_pairs={{0,8},{8,16},{16,24},{24,32},{32,40},{40,48},{48,56},{56,64},{64,7... | collective-permute-start | bytes 6152 | tf_op jit(solution)/shard_map/ppermute | solution.py:39
  303.5 7.6 %collective-permute-start.20 = (f32[8,64]{1,0:T(8,128)S(1)}, f32[8,64]{1,0:T(8,128)S(1)}, u32[]{:S(2)}, u32[]{:S(2)}) collective-permute-start(f32[8,64]{1,0:T(8,128)S(1)} %get-tuple-element.370), channel_id=1, source_target_pairs={{8,0},{16,8},{24,16},{32,24},{40,32},{48,40},{56,48},{64,56},{72,6... | collective-permute-start | bytes 6152 | tf_op jit(solution)/shard_map/ppermute | solution.py:39
  (28 other events, 355.8 us)

commit v3 on v1

--- a/solution.py
+++ b/solution.py
@@ -2,6 +2,8 @@
 import jax.numpy as jnp
 from jax import lax
 from jax.sharding import PartitionSpec as P
+from jax.experimental import pallas as pl
+from jax.experimental.pallas import tpu as pltpu
 
 CAP = 64
 ITERS = 4
@@ -136,34 +138,17 @@
     return (6.0 + SHIFT_PRESSURE) * values - beside
 
 
-def neighbour_sum(padded):
-    beside = shifted(padded, 1, 0, 1) + shifted(padded, 1, 0, -1)
-    beside = beside + shifted(padded, 1, 1, 1) + shifted(padded, 1, 1, -1)
-    return beside + shifted(padded, 1, 2, 1) + shifted(padded, 1, 2, -1)
-
-
-def solve_pressure(divergence):
-    half_width = 6.0
-    basis = [divergence]
-    padded_basis = []
-    for j in range(ITERS):
-        padded = pressure_pad(basis[j])
-        padded_basis.append(padded)
-        scaled = neighbour_sum(padded) * (-1.0 / half_width)
-        if j == 0:
-            basis.append(scaled)
-        else:
-            basis.append(2.0 * scaled - basis[j - 1])
-    size = ITERS + 1
-    pairs = [(i, j) for i in range(size) for j in range(i, size)]
-    local = jnp.stack([jnp.sum(basis[i] * basis[j]) for i, j in pairs])
-    total = lax.psum(local, ("axial", "azim"))
-    gram = [[None] * size for _ in range(size)]
-    for n, (i, j) in enumerate(pairs):
-        gram[i][j] = total[n]
-        gram[j][i] = total[n]
-    shift = 6.0 + SHIFT_PRESSURE
-
+def butterfly_partners():
+    rounds = []
+    for axis in ("azim", "axial"):
+        step = 1
+        while step < lax.axis_size(axis):
+            rounds.append((axis, step))
+            step *= 2
+    return rounds
+
+
+def coefficient_cg(gram, size, shift, half_width):
     def apply_a(c):
         out = [shift * c[j] for j in range(size)]
         for j in range(size - 1):
@@ -186,9 +171,8 @@
                 acc = term if acc is None else acc + term
         return acc
 
-    zero = 0.0
-    solution_c = [zero] * size
-    residual = [1.0] + [zero] * (size - 1)
+    solution_c = [0.0] * size
+    residual = [1.0] + [0.0] * (size - 1)
     search = list(residual)
     norm_now = inner(residual, residual)
     for iteration in range(ITERS):
@@ -201,12 +185,117 @@
         norm_next = inner(residual, residual)
         search = [residual[j] + norm_next / norm_now * search[j] for j in range(size)]
         norm_now = norm_next
-    pressure = solution_c[0] * basis[0]
-    padded_pressure = solution_c[0] * padded_basis[0]
+    return solution_c
+
+
+def reduce_kernel(rounds, shift, half_width, vel_ref, *refs):
+    size = ITERS + 1
+    basis_refs = refs[:size]
+    o_ref, send_buf, recv_buf, send_sems, recv_sems = refs[size:]
+    here = {"axial": lax.axis_index("axial"), "azim": lax.axis_index("azim")}
+
+    def partner(axis, step):
+        index = here[axis]
+        other = index + step - 2 * step * ((index // step) % 2)
+        coords = dict(here)
+        coords[axis] = other
+        return (coords["axial"], coords["azim"])
+
+    barrier = pltpu.get_barrier_semaphore()
+    for axis, step in rounds:
+        pl.semaphore_signal(
+            barrier, inc=1, device_id=partner(axis, step), device_id_type=pl.DeviceIdType.MESH
+        )
+    pl.semaphore_wait(barrier, len(rounds))
+    row = lax.broadcasted_iota(jnp.int32, o_ref.shape, 0)
+    lane = lax.broadcasted_iota(jnp.int32, o_ref.shape, 1)
+    is_max = (row == 0) & (lane == 0)
+
+    def total(x):
+        return jnp.sum(jnp.sum(x, axis=0, keepdims=True), axis=1, keepdims=True)
+
+    basis = [ref[...] for ref in basis_refs]
+    pairs = [(i, j) for i in range(size) for j in range(i, size)]
+    entries = [jnp.max(jnp.max(jnp.abs(vel_ref[...]), axis=0, keepdims=True), axis=1, keepdims=True)]
+    entries += [total(basis[i] * basis[j]) for i, j in pairs]
+    acc = jnp.zeros(o_ref.shape, jnp.float32)
+    for n, entry in enumerate(entries):
+        acc = jnp.where((row == 0) & (lane == n), entry, acc)
+    for r, (axis, step) in enumerate(rounds):
+        send_buf[r] = acc
+        copy = pltpu.make_async_remote_copy(
+            src_ref=send_buf.at[r],
+            dst_ref=recv_buf.at[r],
+            send_sem=send_sems.at[r],
+            recv_sem=recv_sems.at[r],
+            device_id=partner(axis, step),
+            device_id_type=pl.DeviceIdType.MESH,
+        )
+        copy.start()
+        copy.wait()
+        other = recv_buf[r]
+        acc = jnp.where(is_max, jnp.maximum(acc, other), acc + other)
+    first = acc[0:1, :]
+    first_lane = lax.broadcasted_iota(jnp.int32, first.shape, 1)
+
+    def entry_at(n):
+        return jnp.sum(jnp.where(first_lane == n, first, 0.0), axis=1, keepdims=True)
+
+    gram = [[None] * size for _ in range(size)]
+    for n, (i, j) in enumerate(pairs):
+        gram[i][j] = entry_at(n + 1)
+        gram[j][i] = gram[i][j]
+    coefficients = coefficient_cg(gram, size, shift, half_width)
+    out = jnp.where(lane == ITERS, entry_at(0), 0.0)
+    for j in range(ITERS):
+        out = jnp.where((lane == j), coefficients[j], out)
+    o_ref[...] = out
+
+
+def pressure_coefficients(velocity, basis, shift, half_width):
+    rounds = butterfly_partners()
+    flat = [v.reshape(-1, v.shape[-1]) for v in basis]
+    out = pl.pallas_call(
+        lambda *refs: reduce_kernel(rounds, shift, half_width, *refs),
+        out_shape=jax.ShapeDtypeStruct((8, 128), jnp.float32),
+        in_specs=[pl.BlockSpec(memory_space=pltpu.VMEM)] * (1 + len(flat)),
+        out_specs=pl.BlockSpec(memory_space=pltpu.VMEM),
+        scratch_shapes=[
+            pltpu.VMEM((len(rounds), 8, 128), jnp.float32),
+            pltpu.VMEM((len(rounds), 8, 128), jnp.float32),
+            pltpu.SemaphoreType.DMA((len(rounds),)),
+            pltpu.SemaphoreType.DMA((len(rounds),)),
+        ],
+        compiler_params=pltpu.CompilerParams(collective_id=0, has_side_effects=True),
+    )(velocity.reshape(-1, velocity.shape[-1]), *flat)
+    return [out[0, j] for j in range(ITERS)], out[0, ITERS]
+
+
+def neighbour_sum(padded):
+    beside = shifted(padded, 1, 0, 1) + shifted(padded, 1, 0, -1)
+    beside = beside + shifted(padded, 1, 1, 1) + shifted(padded, 1, 1, -1)
+    return beside + shifted(padded, 1, 2, 1) + shifted(padded, 1, 2, -1)
+
+
+def solve_pressure(divergence, velocity):
+    half_width = 6.0
+    basis = [divergence]
+    padded_basis = []
+    for j in range(ITERS):
+        padded = pressure_pad(basis[j])
+        padded_basis.append(padded)
+        scaled = neighbour_sum(padded) * (-1.0 / half_width)
+        if j == 0:
+            basis.append(scaled)
+        else:
+            basis.append(2.0 * scaled - basis[j - 1])
+    coefficients, fastest = pressure_coefficients(
+        velocity, basis, 6.0 + SHIFT_PRESSURE, half_width
+    )
+    padded_pressure = coefficients[0] * padded_basis[0]
     for j in range(1, ITERS):
-        pressure = pressure + solution_c[j] * basis[j]
-        padded_pressure = padded_pressure + solution_c[j] * padded_basis[j]
-    return pressure, padded_pressure
+        padded_pressure = padded_pressure + coefficients[j] * padded_basis[j]
+    return padded_pressure, fastest
 
 
 def along_axial(buffer, step_by):
@@ -219,14 +308,20 @@
 
 def on_device(state, diff_coef, parcel_state, parcel_cell, parcel_dest, live_count):
     velocity = state[1:4]
-    fastest = lax.pmax(jnp.max(jnp.abs(velocity)), ("axial", "azim"))
-    step_size = CFL / (fastest + 1e-06)
     whole_pad = extended(state, (("axial", 1), ("azim", 2)), 2)
     whole_pad = radial_pad(clear_ends(whole_pad, 2, 1), 2, "edge")
     moving = whole_pad[1:]
     density_pad = whole_pad[0]
     density_rim = 2
     vel_pad = moving[0:3]
+    divergence = jnp.zeros_like(state[0])
+    for direction in range(3):
+        divergence = divergence + 0.5 * (
+            shifted(vel_pad[direction], 2, direction, 1)
+            - shifted(vel_pad[direction], 2, direction, -1)
+        )
+    padded_pressure, fastest = solve_pressure(divergence, velocity)
+    step_size = CFL / (fastest + 1e-06)
     transported = transport(
         moving[3:], vel_pad, density_pad, density_rim, diff_coef[:, None, None, None], step_size
     )
@@ -284,13 +379,6 @@
         ]
     )
     kept_parcels = jnp.where((parcel_dest == 0)[None], updated, jnp.float32(0.0))
-    divergence = jnp.zeros_like(state[0])
-    for direction in range(3):
-        divergence = divergence + 0.5 * (
-            shifted(vel_pad[direction], 2, direction, 1)
-            - shifted(vel_pad[direction], 2, direction, -1)
-        )
-    pressure, padded_pressure = solve_pressure(divergence)
     velocity_new = jnp.stack(
         [
             velocity[d]

time: 448 us -> 215 us (0.48)
  blocking collectives: 214 us -> 0 us
  between operations: 93.8 us -> 2.72 us
  Pallas kernels: 0 us -> 41.3 us
  other arithmetic: 37.4 us -> 55.5 us
  waiting for transfers between devices: 20.2 us -> 26.9 us
  starting transfers between devices: 50.6 us -> 55.9 us
    pmax x1 -> x0, blocking collectives: 110 us -> none  [on_device(): fastest = lax.pmax(jnp.max(jnp.abs(velocity)), ('axial', 'azim'))]
    psum x1 -> x0, blocking collectives: 105 us -> none  [solve_pressure(): total = lax.psum(local, ('axial', 'azim'))]
    pallas_call x0 -> x1, Pallas kernels: none -> 41.3 us  [pressure_coefficients(): pl.pallas_call(lambda *refs: reduce_kernel(rounds, shift, half_width, *re...]
    ppermute x10, starting transfers between devices: 14.1 us -> 26.6 us  [extended(): lax.ppermute(lax.slice_in_dim(block, 0, width, axis=dim), axis, backward)]
    ppermute x10, starting transfers between devices: 27.7 us -> 18.1 us  [extended(): lax.ppermute(lax.slice_in_dim(block, block.shape[dim] - width, None, axis...]
    another operation x2 -> x1, local copies, waits for them, and re-layouts: 9.55 us -> 0.22 us  [the longest x1 9.33 us: solve_pressure(): local = jnp.stack([jnp.sum(basis[i] * basis[j]) for i, j in pairs])]
    add x1, other arithmetic: 1.41 us -> 7.81 us  [transport(): return center + step_size * change]
  transfers between devices with their start and end apart: 24 -> 24, of which waited for: 13 -> 13; matrix products, arithmetic and copies ran while one was open for 11% -> 9% of each run, Pallas kernels for 0% -> 0%
where the time goes in v3:
time: 215 us; the launch traced here: 212 us
  starting transfers between devices  55.9 us (26%)
  other arithmetic  55.5 us (26%)
  Pallas kernels  41.3 us (19%)
  waiting for transfers between devices  26.9 us (13%)
  local copies, waits for them, and re-layouts  22.7 us (11%)
  matrix products  6.24 us (3%)
  between operations  2.72 us (1%)
    pallas_call x1, Pallas kernels, pressure_coefficients(): pl.pallas_call(lambda *refs: reduce_kernel(rounds, shift, half_width, *re...  41.3 us
    ppermute x10, starting transfers between devices, extended(): lax.ppermute(lax.slice_in_dim(block, 0, width, axis=dim), axis, backward)  26.6 us
    ppermute x10, starting transfers between devices, extended(): lax.ppermute(lax.slice_in_dim(block, block.shape[dim] - width, None, axis...  18.1 us
    ppermute x10, waiting for transfers between devices, extended(): lax.ppermute(lax.slice_in_dim(block, block.shape[dim] - width, None, axis...  17.1 us
    mul x8, other arithmetic, evaporate(): sources = jnp.stack([heat_source * alive_mask, lost_mass * alive_mask])  11.7 us
    ppermute x2, starting transfers between devices, shifted_2(): return lax.ppermute(shard, axis, pairs)  8.25 us
    add x1, other arithmetic, transport(): return center + step_size * change  7.81 us
    slice x3, local copies, waits for them, and re-layouts, radial_pad(): jnp.pad(values, [(0, 0)] * (values.ndim - 1) + [(rim_width, rim_width)],...  7 us
  transfers between devices with their start and end apart: 24, of which 13 were waited for; matrix products, arithmetic and copies ran while one was open for 9% of the time, Pallas kernels for 0%

profile of v3, /device:TPU:6, one launch (start us, length us, event | category | flops | bytes accessed | tf_op | source)
XLA Modules:
  0.0 211.6 jit_solution(1813822140704896209)
XLA Ops:
  1.7 3.7 %collective-permute-start = (f32[14,2,8,128]{3,2,1,0:T(8,128)S(1)}, f32[14,2,8,128]{3,2,1,0:T(8,128)S(1)}, u32[]{:S(2)}, u32[]{:S(2)}) collective-permute-start(f32[14,2,8,128]{3,2,1,0:T(8,128)S(1)} %get-tuple-element.320), channel_id=1, source_target_pairs={{0,8},{8,16},{16,24},{24,32},{32,40},{40,48},{48,56},{56,64},{64,7... | collective-permute-start | bytes 344072 | tf_op jit(solution)/shard_map/ppermute | solution.py:28
  5.4 2.1 collective-permute-start.1
  11.9 2.3 %collective-permute-done.1 = f32[14,2,8,128]{3,2,1,0:T(8,128)S(1)} collective-permute-done((f32[14,2,8,128]{3,2,1,0:T(8,128)S(1)}, f32[14,2,8,128]{3,2,1,0:T(8,128)S(1)}, u32[]{:S(2)}, u32[]{:S(2)}) %collective-permute-start.1) | collective-permute-done | bytes 114720 | tf_op jit(solution)/shard_map/ppermute | solution.py:31
  16.0 2.3 %collective-permute-done.3 = f32[14,12,2,128]{3,2,1,0:T(2,128)S(1)} collective-permute-done((f32[14,12,2,128]{3,2,1,0:T(2,128)S(1)}, f32[14,12,2,128]{3,2,1,0:T(2,128)S(1)}, u32[]{:S(2)}, u32[]{:S(2)}) %collective-permute-start.3) | collective-permute-done | bytes 172064 | tf_op jit(solution)/shard_map/ppermute | solution.py:31
  18.3 3.1 %collective-permute-done.2 = f32[14,12,2,128]{3,2,1,0:T(2,128)S(1)} collective-permute-done((f32[14,12,2,128]{3,2,1,0:T(2,128)S(1)}, f32[14,12,2,128]{3,2,1,0:T(2,128)S(1)}, u32[]{:S(2)}, u32[]{:S(2)}) %collective-permute-start.2) | collective-permute-done | bytes 172064 | tf_op jit(solution)/shard_map/ppermute | solution.py:28
  23.4 3.4 %copy.262 = f32[14,12,12,1]{2,1,0,3:T(8,128)} copy(f32[14,12,12,1]{3,2,1,0:T(8,128)} %get-tuple-element.313) | data formatting | bytes 16128 | tf_op jit(solution)/shard_map/jit(_pad)/slice | solution.py:73
  35.1 6.0 %collective-permute-start.4 = (f32[1,8,128]{2,1,0:T(8,128)S(1)}, f32[1,8,128]{2,1,0:T(8,128)S(1)}, u32[]{:S(2)}, u32[]{:S(2)}) collective-permute-start(f32[1,8,128]{2,1,0:T(8,128)S(1)} %get-tuple-element.341), channel_id=1, source_target_pairs={{0,8},{8,16},{16,24},{24,32},{32,40},{40,48},{48,56},{56,64},{64,7... | collective-permute-start | bytes 12296 | tf_op jit(solution)/shard_map/ppermute | solution.py:28
  44.3 2.4 %collective-permute-done.6 = f32[10,1,128]{2,1,0:T(1,128)S(1)} collective-permute-done((f32[10,1,128]{2,1,0:T(1,128)S(1)}, f32[10,1,128]{2,1,0:T(1,128)S(1)}, u32[]{:S(2)}, u32[]{:S(2)}) %collective-permute-start.6) | collective-permute-done | bytes 5152 | tf_op jit(solution)/shard_map/ppermute | solution.py:28
  46.9 8.5 %collective-permute-start.9 = (f32[1,8,128]{2,1,0:T(8,128)S(1)}, f32[1,8,128]{2,1,0:T(8,128)S(1)}, u32[]{:S(2)}, u32[]{:S(2)}) collective-permute-start(f32[1,8,128]{2,1,0:T(8,128)S(1)} %get-tuple-element.340), channel_id=1, source_target_pairs={{8,0},{16,8},{24,16},{32,24},{40,32},{48,40},{56,48},{64,56},{72,6... | collective-permute-start | bytes 12296 | tf_op jit(solution)/shard_map/ppermute | solution.py:31
  63.5 2.9 %collective-permute-done.10 = f32[10,1,128]{2,1,0:T(1,128)S(1)} collective-permute-done((f32[10,1,128]{2,1,0:T(1,128)S(1)}, f32[10,1,128]{2,1,0:T(1,128)S(1)}, u32[]{:S(2)}, u32[]{:S(2)}) %collective-permute-start.10) | collective-permute-done | bytes 5152 | tf_op jit(solution)/shard_map/ppermute | solution.py:28
  68.5 7.2 %collective-permute-start.13 = (f32[1,8,128]{2,1,0:T(8,128)}, f32[1,8,128]{2,1,0:T(8,128)}, u32[]{:S(2)}, u32[]{:S(2)}) collective-permute-start(f32[1,8,128]{2,1,0:T(8,128)} %get-tuple-element.338), channel_id=1, source_target_pairs={{8,0},{16,8},{24,16},{32,24},{40,32},{48,40},{56,48},{64,56},{72,6... | collective-permute-start | bytes 12296 | tf_op jit(solution)/shard_map/ppermute | solution.py:31
  79.6 2.1 collective-permute-done.12
  83.0 2.5 %pad_maximum_fusion = f32[14,12,12,132]{3,2,1,0:T(8,128)S(1)} fusion(f32[14,12,12,2]{3,2,1,0:T(8,128)} %copy-done, f32[14,12,12,128]{3,2,1,0:T(8,128)S(1)} %maximum_select_fusion, f32[14,12,12,2]{3,2,1,0:T(8,128)S(1)} %reshape.197), kind=kLoop, calls=%fused_computation.39 | loop fusion | flops 532224 | bytes 2128896 | tf_op jit(solution)/shard_map/jit(_pad)/concatenate | solution.py:73
  88.4 5.1 %collective-permute-start.17 = (f32[1,8,128]{2,1,0:T(8,128)S(1)}, f32[1,8,128]{2,1,0:T(8,128)S(1)}, u32[]{:S(2)}, u32[]{:S(2)}) collective-permute-start(f32[1,8,128]{2,1,0:T(8,128)S(1)} %get-tuple-element.336), channel_id=1, source_target_pairs={{8,0},{16,8},{24,16},{32,24},{40,32},{48,40},{56,48},{64,56},{72,6... | collective-permute-start | bytes 12296 | tf_op jit(solution)/shard_map/ppermute | solution.py:31
  93.5 3.0 %collective-permute-start.16 = (f32[1,8,128]{2,1,0:T(8,128)S(1)}, f32[1,8,128]{2,1,0:T(8,128)S(1)}, u32[]{:S(2)}, u32[]{:S(2)}) collective-permute-start(f32[1,8,128]{2,1,0:T(8,128)S(1)} %get-tuple-element.335), channel_id=1, source_target_pairs={{0,8},{8,16},{16,24},{24,32},{32,40},{40,48},{48,56},{56,64},{64,7... | collective-permute-start | bytes 12296 | tf_op jit(solution)/shard_map/ppermute | solution.py:28
  96.6 2.8 %slice_multiply_fusion.2 = (f32[10,12,12,132]{3,2,1,0:T(8,128)}, f32[10,12,12,132]{3,2,1,0:T(8,128)}, f32[10,12,12,132]{3,2,1,0:T(8,128)}) fusion(f32[14,12,12,132]{3,2,1,0:T(8,128)S(1)} %pad_maximum_fusion, f32[12,12,132]{2,1,0:T(8,128)S(1)} %copy-done.15, f32[12,12,132]{2,1,0:T(8,128)S(1)} %copy-done.13, f32[12,12,132]{2,1,0:T(8,128)S(1)} %copy-done.11), kind=kLoop, calls=%fused_computation.44 | loop fusion | flops 570240 | bytes 3269376 | tf_op jit(solution)/shard_map/mul | solution.py:83
  101.4 2.9 %collective-permute-done.18 = f32[10,1,128]{2,1,0:T(1,128)S(1)} collective-permute-done((f32[10,1,128]{2,1,0:T(1,128)S(1)}, f32[10,1,128]{2,1,0:T(1,128)S(1)}, u32[]{:S(2)}, u32[]{:S(2)}) %collective-permute-start.18) | collective-permute-done | bytes 5152 | tf_op jit(solution)/shard_map/ppermute | solution.py:28
  105.7 41.3 %shard_map.93 = f32[8,128]{1,0:T(8,128)} custom-call(f32[192,128]{1,0:T(8,128)} %bitcast.108, f32[64,128]{1,0:T(8,128)} %bitcast.103, f32[64,128]{1,0:T(8,128)} %fusion.90.refs_2_, f32[64,128]{1,0:T(8,128)} %bitcast.104, f32[64,128]{1,0:T(8,128)} %bitcast.105, f32[64,128]{1,0:T(8,128)} %fusion.61.refs_5_), custom_call_target="tpu_custom_call" | custom-call | tf_op jit(solution)/shard_map/pallas_call | solution.py:258
  149.2 7.8 %fusion.19 = f32[10,8,8,128]{3,2,1,0:T(8,128)S(1)} fusion(f32[14,12,12,128]{3,2,1,0:T(8,128)S(1)} %maximum_select_fusion, f32[14,12,12,2]{3,2,1,0:T(8,128)S(1)} %reshape.197, f32[14,12,12,2]{3,2,1,0:T(8,128)} %copy-done, f32[10,12,12,132]{3,2,1,0:T(8,128)} %get-tuple-element.311, f32[10,12,12,132]{3,2,1,0:T(8,128)} %get-tuple-element.310, ...), kind=kLoop, calls=%fused_computation.52 | loop fusion | flops 4259840 | bytes 8863532 | tf_op jit(solution)/shard_map/add | solution.py:103
  157.8 31.7 %while.18 = (s32[]{:T(128)}, f32[64,256]{1,0:T(8,128)S(1)}, f32[8,2048]{1,0:T(8,128)S(1)}, s32[2048]{0:T(1024)}, s32[]{:T(128)}, /*index=5*/f32[8,2048]{1,0:T(8,...) while((s32[]{:T(128)}, f32[64,256]{1,0:T(8,128)S(1)}, ...), condition=%wide.region_2.3_spmd.clone, body=%wide.region_0.2_spmd.clone.sunk | while | flops 353384960 | bytes 5411153 | solution.py:359
  189.6 2.9 %fusion.45 = f32[10,10,130]{2,1,0:T(8,128)S(1)} fusion(f32[10,10,128]{2,1,0:T(8,128)S(1)} %maximum_select_fusion.1, f32[10,10,128]{2,1,0:T(8,128)S(1)} %copy-done.5, f32[10,10,128]{2,1,0:T(8,128)S(1)} %copy-done.3, f32[10,10,128]{2,1,0:T(8,128)S(1)} %copy-done.7, f32[]{:T(128)} %bitcast.25, f32[]{:T(128)} %bitcast.24, f32[]{:T(128)} %bitcast.23, f32[]{:T(128)} %bitcast.22), kind=kLoop, calls=%fused_computation.112 | loop fusion | flops 91000 | bytes 256816 | tf_op jit(solution)/shard_map/add | solution.py:297
  194.1 2.9 %collective-permute-start.22 = (f32[8,64]{1,0:T(8,128)S(1)}, f32[8,64]{1,0:T(8,128)S(1)}, u32[]{:S(2)}, u32[]{:S(2)}) collective-permute-start(f32[8,64]{1,0:T(8,128)S(1)} %get-tuple-element.345), channel_id=1, source_target_pairs={{0,7},{1,0},{2,1},{3,2},{4,3},{5,4},{6,5},{7,6},{8,15},{9,8},{10,9... | collective-permute-start | bytes 6152 | tf_op jit(solution)/shard_map/ppermute | solution.py:44
  197.1 6.3 %collective-permute-start.21 = (f32[8,64]{1,0:T(8,128)S(1)}, f32[8,64]{1,0:T(8,128)S(1)}, u32[]{:S(2)}, u32[]{:S(2)}) collective-permute-start(f32[8,64]{1,0:T(8,128)S(1)} %get-tuple-element.346), channel_id=1, source_target_pairs={{0,8},{8,16},{16,24},{24,32},{32,40},{40,48},{48,56},{56,64},{64,7... | collective-permute-start | bytes 6152 | tf_op jit(solution)/shard_map/ppermute | solution.py:39
  206.8 4.2 %collective-permute-done.20 = f32[8,64]{1,0:T(8,128)S(1)} collective-permute-done((f32[8,64]{1,0:T(8,128)S(1)}, f32[8,64]{1,0:T(8,128)S(1)}, u32[]{:S(2)}, u32[]{:S(2)}) %collective-permute-start.20) | collective-permute-done | bytes 2080 | tf_op jit(solution)/shard_map/ppermute | solution.py:39
  (212 shorter events, 80.6 us)
Async XLA Ops:
  1.7 10.1 %collective-permute-start = (f32[14,2,8,128]{3,2,1,0:T(8,128)S(1)}, f32[14,2,8,128]{3,2,1,0:T(8,128)S(1)}, u32[]{:S(2)}, u32[]{:S(2)}) collective-permute-start(f32[14,2,8,128]{3,2,1,0:T(8,128)S(1)} %get-tuple-element.320), channel_id=1, source_target_pairs={{0,8},{8,16},{16,24},{24,32},{32,40},{40,48},{48,56},{56,64},{64,7... | collective-permute-start | bytes 344072 | tf_op jit(solution)/shard_map/ppermute | solution.py:28
  5.4 8.8 %collective-permute-start.1 = (f32[14,2,8,128]{3,2,1,0:T(8,128)S(1)}, f32[14,2,8,128]{3,2,1,0:T(8,128)S(1)}, u32[]{:S(2)}, u32[]{:S(2)}) collective-permute-start(f32[14,2,8,128]{3,2,1,0:T(8,128)S(1)} %get-tuple-element.319), channel_id=1, source_target_pairs={{8,0},{16,8},{24,16},{32,24},{40,32},{48,40},{56,48},{64,56},{72,6... | collective-permute-start | bytes 344072 | tf_op jit(solution)/shard_map/ppermute | solution.py:31
  14.3 4.0 %collective-permute-start.3 = (f32[14,12,2,128]{3,2,1,0:T(2,128)S(1)}, f32[14,12,2,128]{3,2,1,0:T(2,128)S(1)}, u32[]{:S(2)}, u32[]{:S(2)}) collective-permute-start(f32[14,12,2,128]{3,2,1,0:T(2,128)S(1)} %get-tuple-element.315), channel_id=1, source_target_pairs={{1,0},{2,1},{3,2},{4,3},{5,4},{6,5},{7,6},{0,7},{9,8},{10,9},{11,1... | collective-permute-start | bytes 516104 | tf_op jit(solution)/shard_map/ppermute | solution.py:31
  15.4 6.0 %collective-permute-start.2 = (f32[14,12,2,128]{3,2,1,0:T(2,128)S(1)}, f32[14,12,2,128]{3,2,1,0:T(2,128)S(1)}, u32[]{:S(2)}, u32[]{:S(2)}) collective-permute-start(f32[14,12,2,128]{3,2,1,0:T(2,128)S(1)} %get-tuple-element.314), channel_id=1, source_target_pairs={{0,1},{1,2},{2,3},{3,4},{4,5},{5,6},{6,7},{7,0},{8,9},{9,10},{10,1... | collective-permute-start | bytes 516104 | tf_op jit(solution)/shard_map/ppermute | solution.py:28
  33.2 8.0 %collective-permute-start.5 = (f32[1,8,128]{2,1,0:T(8,128)S(1)}, f32[1,8,128]{2,1,0:T(8,128)S(1)}, u32[]{:S(2)}, u32[]{:S(2)}) collective-permute-start(f32[1,8,128]{2,1,0:T(8,128)S(1)} %get-tuple-element.342), channel_id=1, source_target_pairs={{8,0},{16,8},{24,16},{32,24},{40,32},{48,40},{56,48},{64,56},{72,6... | collective-permute-start | bytes 12296 | tf_op jit(solution)/shard_map/ppermute | solution.py:31
  35.1 7.3 %collective-permute-start.4 = (f32[1,8,128]{2,1,0:T(8,128)S(1)}, f32[1,8,128]{2,1,0:T(8,128)S(1)}, u32[]{:S(2)}, u32[]{:S(2)}) collective-permute-start(f32[1,8,128]{2,1,0:T(8,128)S(1)} %get-tuple-element.341), channel_id=1, source_target_pairs={{0,8},{8,16},{16,24},{24,32},{32,40},{40,48},{48,56},{56,64},{64,7... | collective-permute-start | bytes 12296 | tf_op jit(solution)/shard_map/ppermute | solution.py:28
  42.5 1.9 collective-permute-start.7
  42.5 4.3 %collective-permute-start.6 = (f32[10,1,128]{2,1,0:T(1,128)S(1)}, f32[10,1,128]{2,1,0:T(1,128)S(1)}, u32[]{:S(2)}, u32[]{:S(2)}) collective-permute-start(f32[10,1,128]{2,1,0:T(1,128)S(1)} %get-tuple-element.333), channel_id=1, source_target_pairs={{0,1},{1,2},{2,3},{3,4},{4,5},{5,6},{6,7},{7,0},{8,9},{9,10},{10,1... | collective-permute-start | bytes 15368 | tf_op jit(solution)/shard_map/ppermute | solution.py:28
  46.9 14.1 %collective-permute-start.9 = (f32[1,8,128]{2,1,0:T(8,128)S(1)}, f32[1,8,128]{2,1,0:T(8,128)S(1)}, u32[]{:S(2)}, u32[]{:S(2)}) collective-permute-start(f32[1,8,128]{2,1,0:T(8,128)S(1)} %get-tuple-element.340), channel_id=1, source_target_pairs={{8,0},{16,8},{24,16},{32,24},{40,32},{48,40},{56,48},{64,56},{72,6... | collective-permute-start | bytes 12296 | tf_op jit(solution)/shard_map/ppermute | solution.py:31
  55.4 6.7 %collective-permute-start.8 = (f32[1,8,128]{2,1,0:T(8,128)S(1)}, f32[1,8,128]{2,1,0:T(8,128)S(1)}, u32[]{:S(2)}, u32[]{:S(2)}) collective-permute-start(f32[1,8,128]{2,1,0:T(8,128)S(1)} %get-tuple-element.339), channel_id=1, source_target_pairs={{0,8},{8,16},{16,24},{24,32},{32,40},{40,48},{48,56},{56,64},{64,7... | collective-permute-start | bytes 12296 | tf_op jit(solution)/shard_map/ppermute | solution.py:28
  62.1 1.4 collective-permute-start.11
  62.1 4.3 %collective-permute-start.10 = (f32[10,1,128]{2,1,0:T(1,128)S(1)}, f32[10,1,128]{2,1,0:T(1,128)S(1)}, u32[]{:S(2)}, u32[]{:S(2)}) collective-permute-start(f32[10,1,128]{2,1,0:T(1,128)S(1)} %get-tuple-element.331), channel_id=1, source_target_pairs={{0,1},{1,2},{2,3},{3,4},{4,5},{5,6},{6,7},{7,0},{8,9},{9,10},{10,1... | collective-permute-start | bytes 15368 | tf_op jit(solution)/shard_map/ppermute | solution.py:28
  68.5 11.1 %collective-permute-start.13 = (f32[1,8,128]{2,1,0:T(8,128)}, f32[1,8,128]{2,1,0:T(8,128)}, u32[]{:S(2)}, u32[]{:S(2)}) collective-permute-start(f32[1,8,128]{2,1,0:T(8,128)} %get-tuple-element.338), channel_id=1, source_target_pairs={{8,0},{16,8},{24,16},{32,24},{40,32},{48,40},{56,48},{64,56},{72,6... | collective-permute-start | bytes 12296 | tf_op jit(solution)/shard_map/ppermute | solution.py:31
  75.7 5.9 %collective-permute-start.12 = (f32[1,8,128]{2,1,0:T(8,128)}, f32[1,8,128]{2,1,0:T(8,128)}, u32[]{:S(2)}, u32[]{:S(2)}) collective-permute-start(f32[1,8,128]{2,1,0:T(8,128)} %get-tuple-element.337), channel_id=1, source_target_pairs={{0,8},{8,16},{16,24},{24,32},{32,40},{40,48},{48,56},{56,64},{64,7... | collective-permute-start | bytes 12296 | tf_op jit(solution)/shard_map/ppermute | solution.py:28
  82.5 3.0 %collective-permute-start.15 = (f32[10,1,128]{2,1,0:T(1,128)S(1)}, f32[10,1,128]{2,1,0:T(1,128)S(1)}, u32[]{:S(2)}, u32[]{:S(2)}) collective-permute-start(f32[10,1,128]{2,1,0:T(1,128)S(1)} %get-tuple-element.330), channel_id=1, source_target_pairs={{1,0},{2,1},{3,2},{4,3},{5,4},{6,5},{7,6},{0,7},{9,8},{10,9},{11,1... | collective-permute-start | bytes 15368 | tf_op jit(solution)/shard_map/ppermute | solution.py:31
  82.6 4.3 %collective-permute-start.14 = (f32[10,1,128]{2,1,0:T(1,128)S(1)}, f32[10,1,128]{2,1,0:T(1,128)S(1)}, u32[]{:S(2)}, u32[]{:S(2)}) collective-permute-start(f32[10,1,128]{2,1,0:T(1,128)S(1)} %get-tuple-element.329), channel_id=1, source_target_pairs={{0,1},{1,2},{2,3},{3,4},{4,5},{5,6},{6,7},{7,0},{8,9},{9,10},{10,1... | collective-permute-start | bytes 15368 | tf_op jit(solution)/shard_map/ppermute | solution.py:28
  88.4 11.0 %collective-permute-start.17 = (f32[1,8,128]{2,1,0:T(8,128)S(1)}, f32[1,8,128]{2,1,0:T(8,128)S(1)}, u32[]{:S(2)}, u32[]{:S(2)}) collective-permute-start(f32[1,8,128]{2,1,0:T(8,128)S(1)} %get-tuple-element.336), channel_id=1, source_target_pairs={{8,0},{16,8},{24,16},{32,24},{40,32},{48,40},{56,48},{64,56},{72,6... | collective-permute-start | bytes 12296 | tf_op jit(solution)/shard_map/ppermute | solution.py:31
  93.5 5.8 %collective-permute-start.16 = (f32[1,8,128]{2,1,0:T(8,128)S(1)}, f32[1,8,128]{2,1,0:T(8,128)S(1)}, u32[]{:S(2)}, u32[]{:S(2)}) collective-permute-start(f32[1,8,128]{2,1,0:T(8,128)S(1)} %get-tuple-element.335), channel_id=1, source_target_pairs={{0,8},{8,16},{16,24},{24,32},{32,40},{40,48},{48,56},{56,64},{64,7... | collective-permute-start | bytes 12296 | tf_op jit(solution)/shard_map/ppermute | solution.py:28
  99.3 2.0 collective-permute-start.19
  100.0 4.3 %collective-permute-start.18 = (f32[10,1,128]{2,1,0:T(1,128)S(1)}, f32[10,1,128]{2,1,0:T(1,128)S(1)}, u32[]{:S(2)}, u32[]{:S(2)}) collective-permute-start(f32[10,1,128]{2,1,0:T(1,128)S(1)} %get-tuple-element.327), channel_id=1, source_target_pairs={{0,1},{1,2},{2,3},{3,4},{4,5},{5,6},{6,7},{7,0},{8,9},{9,10},{10,1... | collective-permute-start | bytes 15368 | tf_op jit(solution)/shard_map/ppermute | solution.py:28
  194.1 12.7 %collective-permute-start.23 = (f32[8,64]{1,0:T(8,128)S(1)}, f32[8,64]{1,0:T(8,128)S(1)}, u32[]{:S(2)}, u32[]{:S(2)}) collective-permute-start(f32[8,64]{1,0:T(8,128)S(1)} %get-tuple-element.344), channel_id=1, source_target_pairs={{0,1},{1,2},{2,3},{3,4},{4,5},{5,6},{6,7},{7,0},{8,9},{9,10},{10,1... | collective-permute-start | bytes 6152 | tf_op jit(solution)/shard_map/ppermute | solution.py:44
  194.1 12.7 %collective-permute-start.22 = (f32[8,64]{1,0:T(8,128)S(1)}, f32[8,64]{1,0:T(8,128)S(1)}, u32[]{:S(2)}, u32[]{:S(2)}) collective-permute-start(f32[8,64]{1,0:T(8,128)S(1)} %get-tuple-element.345), channel_id=1, source_target_pairs={{0,7},{1,0},{2,1},{3,2},{4,3},{5,4},{6,5},{7,6},{8,15},{9,8},{10,9... | collective-permute-start | bytes 6152 | tf_op jit(solution)/shard_map/ppermute | solution.py:44
  197.1 9.7 %collective-permute-start.21 = (f32[8,64]{1,0:T(8,128)S(1)}, f32[8,64]{1,0:T(8,128)S(1)}, u32[]{:S(2)}, u32[]{:S(2)}) collective-permute-start(f32[8,64]{1,0:T(8,128)S(1)} %get-tuple-element.346), channel_id=1, source_target_pairs={{0,8},{8,16},{16,24},{24,32},{32,40},{40,48},{48,56},{56,64},{64,7... | collective-permute-start | bytes 6152 | tf_op jit(solution)/shard_map/ppermute | solution.py:39
  203.4 7.6 %collective-permute-start.20 = (f32[8,64]{1,0:T(8,128)S(1)}, f32[8,64]{1,0:T(8,128)S(1)}, u32[]{:S(2)}, u32[]{:S(2)}) collective-permute-start(f32[8,64]{1,0:T(8,128)S(1)} %get-tuple-element.343), channel_id=1, source_target_pairs={{8,0},{16,8},{24,16},{32,24},{40,32},{48,40},{56,48},{64,56},{72,6... | collective-permute-start | bytes 6152 | tf_op jit(solution)/shard_map/ppermute | solution.py:39
  (31 other events, 414.6 us)

commit v4 on v3

--- a/solution.py
+++ b/solution.py
@@ -277,21 +277,52 @@
     return beside + shifted(padded, 1, 2, 1) + shifted(padded, 1, 2, -1)
 
 
-def solve_pressure(divergence, velocity):
+def axial_valid(values, rim):
+    extent = values.shape[0]
+    inner_x = extent - 2 * rim
+    first = lax.axis_index("axial") * inner_x - rim
+    position = first + lax.broadcasted_iota(jnp.int32, (extent, 1, 1), 0)
+    inside = (position >= 0) & (position < inner_x * lax.axis_size("axial"))
+    return jnp.where(inside, values, jnp.float32(0.0))
+
+
+def crop(values, by):
+    if by == 0:
+        return values
+    return values[by:-by, by:-by]
+
+
+def neighbour_sum_wide(values):
+    padded = jnp.pad(values, [(0, 0), (0, 0), (1, 1)])
+    nx, ny, nz = padded.shape
+
+    def at(dx, dy, dz):
+        return padded[1 + dx : nx - 1 + dx, 1 + dy : ny - 1 + dy, 1 + dz : nz - 1 + dz]
+
+    beside = at(1, 0, 0) + at(-1, 0, 0)
+    beside = beside + at(0, 1, 0) + at(0, -1, 0)
+    return beside + at(0, 0, 1) + at(0, 0, -1)
+
+
+def solve_pressure(wide_velocity, velocity):
     half_width = 6.0
-    basis = [divergence]
-    padded_basis = []
+    u = wide_velocity
+    divergence = 0.5 * (u[0, 2:, 1:-1, 1:-1] - u[0, :-2, 1:-1, 1:-1])
+    divergence = divergence + 0.5 * (u[1, 1:-1, 2:, 1:-1] - u[1, 1:-1, :-2, 1:-1])
+    divergence = divergence + 0.5 * (u[2, 1:-1, 1:-1, 2:] - u[2, 1:-1, 1:-1, :-2])
+    basis = [axial_valid(divergence, ITERS)]
     for j in range(ITERS):
-        padded = pressure_pad(basis[j])
-        padded_basis.append(padded)
-        scaled = neighbour_sum(padded) * (-1.0 / half_width)
+        scaled = neighbour_sum_wide(basis[j]) * (-1.0 / half_width)
         if j == 0:
-            basis.append(scaled)
+            fresh = scaled
         else:
-            basis.append(2.0 * scaled - basis[j - 1])
+            fresh = 2.0 * scaled - crop(basis[j - 1], 2)
+        basis.append(axial_valid(fresh, ITERS - 1 - j))
+    interior = [crop(basis[j], ITERS - j) for j in range(ITERS + 1)]
     coefficients, fastest = pressure_coefficients(
-        velocity, basis, 6.0 + SHIFT_PRESSURE, half_width
-    )
+        velocity, interior, 6.0 + SHIFT_PRESSURE, half_width
+    )
+    padded_basis = [radial_pad(crop(basis[j], ITERS - j - 1), 1, "constant") for j in range(ITERS)]
     padded_pressure = coefficients[0] * padded_basis[0]
     for j in range(1, ITERS):
         padded_pressure = padded_pressure + coefficients[j] * padded_basis[j]
@@ -314,13 +345,9 @@
     density_pad = whole_pad[0]
     density_rim = 2
     vel_pad = moving[0:3]
-    divergence = jnp.zeros_like(state[0])
-    for direction in range(3):
-        divergence = divergence + 0.5 * (
-            shifted(vel_pad[direction], 2, direction, 1)
-            - shifted(vel_pad[direction], 2, direction, -1)
-        )
-    padded_pressure, fastest = solve_pressure(divergence, velocity)
+    wide_velocity = extended(velocity, (("axial", 1), ("azim", 2)), ITERS + 1)
+    wide_velocity = radial_pad(clear_ends(wide_velocity, ITERS + 1, 1), 1, "edge")
+    padded_pressure, fastest = solve_pressure(wide_velocity, velocity)
     step_size = CFL / (fastest + 1e-06)
     transported = transport(
         moving[3:], vel_pad, density_pad, density_rim, diff_coef[:, None, None, None], step_size

time: 215 us -> 147 us (0.68)
  starting transfers between devices: 55.9 us -> 29.4 us
  waiting for transfers between devices: 26.9 us -> 8.26 us
  other arithmetic: 55.5 us -> 39.1 us
  local copies, waits for them, and re-layouts: 22.7 us -> 15.2 us
    ppermute x10 -> x4, starting transfers between devices: 26.6 us -> 9.25 us  [extended(): lax.ppermute(lax.slice_in_dim(block, 0, width, axis=dim), axis, backward)]
    ppermute x10 -> x4, waiting for transfers between devices: 17.1 us -> 3.12 us  [extended(): lax.ppermute(lax.slice_in_dim(block, block.shape[dim] - width, None, axis...]
    ppermute x10 -> x4, starting transfers between devices: 18.1 us -> 8.96 us  [extended(): lax.ppermute(lax.slice_in_dim(block, block.shape[dim] - width, None, axis...]
    add x1, other arithmetic: 7.81 us -> 1.41 us  [transport(): return center + step_size * change]
    ppermute x10 -> x4, waiting for transfers between devices: 5.52 us -> 0.28 us  [extended(): lax.ppermute(lax.slice_in_dim(block, 0, width, axis=dim), axis, backward)]
    unnamed x63 -> x9, local copies, waits for them, and re-layouts: 4.16 us -> 0.09 us
    another operation x4, local copies, waits for them, and re-layouts: 2.77 us -> 0.05 us  [on_device(): jnp.stack([(parcel_dest == d + 1) & slot_alive for d in range(4)])]
    slice x3 -> x4, local copies, waits for them, and re-layouts: 7 us -> 5.97 us  [radial_pad(): jnp.pad(values, [(0, 0)] * (values.ndim - 1) + [(rim_width, rim_width)],...]
  transfers between devices with their start and end apart: 24 -> 12, of which waited for: 13 -> 3; matrix products, arithmetic and copies ran while one was open for 9% -> 33% of each run, Pallas kernels for 0% -> 30%
where the time goes in v4:
time: 147 us; the launch traced here: 144 us
  Pallas kernels  43.2 us (29%)
  other arithmetic  39.1 us (27%)
  starting transfers between devices  29.4 us (20%)
  local copies, waits for them, and re-layouts  15.2 us (10%)
  waiting for transfers between devices  8.26 us (6%)
  matrix products  6.24 us (4%)
  between operations  2.46 us (2%)
    pallas_call x1, Pallas kernels, pressure_coefficients(): pl.pallas_call(lambda *refs: reduce_kernel(rounds, shift, half_width, *re...  43.2 us
    mul x8, other arithmetic, evaporate(): sources = jnp.stack([heat_source * alive_mask, lost_mass * alive_mask])  11.7 us
    ppermute x4, starting transfers between devices, extended(): lax.ppermute(lax.slice_in_dim(block, 0, width, axis=dim), axis, backward)  9.25 us
    ppermute x4, starting transfers between devices, extended(): lax.ppermute(lax.slice_in_dim(block, block.shape[dim] - width, None, axis...  8.96 us
    ppermute x2, starting transfers between devices, shifted_2(): return lax.ppermute(shard, axis, pairs)  8.21 us
    slice x4, local copies, waits for them, and re-layouts, radial_pad(): jnp.pad(values, [(0, 0)] * (values.ndim - 1) + [(rim_width, rim_width)],...  5.97 us
    ppermute x2, waiting for transfers between devices, shifted_2(): return lax.ppermute(shard, axis, pairs)  4.85 us
    add x4, other arithmetic, evaporate(): new_offsets = offsets + step_size * new_vel  3.53 us
  transfers between devices with their start and end apart: 12, of which 3 were waited for; matrix products, arithmetic and copies ran while one was open for 33% of the time, Pallas kernels for 30%

profile of v4, /device:TPU:6, one launch (start us, length us, event | category | flops | bytes accessed | tf_op | source)
XLA Modules:
  0.0 144.4 jit_solution(11396646893465889388)
XLA Ops:
  1.6 3.7 %collective-permute-start = (f32[14,2,8,128]{3,2,1,0:T(8,128)S(1)}, f32[14,2,8,128]{3,2,1,0:T(8,128)S(1)}, u32[]{:S(2)}, u32[]{:S(2)}) collective-permute-start(f32[14,2,8,128]{3,2,1,0:T(8,128)S(1)} %get-tuple-element.316), channel_id=1, source_target_pairs={{0,8},{8,16},{16,24},{24,32},{32,40},{40,48},{48,56},{56,64},{64,7... | collective-permute-start | bytes 344072 | tf_op jit(solution)/shard_map/ppermute | solution.py:28
  5.4 2.1 %collective-permute-start.1 = (f32[14,2,8,128]{3,2,1,0:T(8,128)S(1)}, f32[14,2,8,128]{3,2,1,0:T(8,128)S(1)}, u32[]{:S(2)}, u32[]{:S(2)}) collective-permute-start(f32[14,2,8,128]{3,2,1,0:T(8,128)S(1)} %get-tuple-element.315), channel_id=1, source_target_pairs={{8,0},{16,8},{24,16},{32,24},{40,32},{48,40},{56,48},{64,56},{72,6... | collective-permute-start | bytes 344072 | tf_op jit(solution)/shard_map/ppermute | solution.py:31
  8.4 2.7 %collective-permute-start.5 = (f32[3,5,8,128]{3,2,1,0:T(8,128)S(1)}, f32[3,5,8,128]{3,2,1,0:T(8,128)S(1)}, u32[]{:S(2)}, u32[]{:S(2)}) collective-permute-start(f32[3,5,8,128]{3,2,1,0:T(8,128)S(1)} %get-tuple-element.314), channel_id=1, source_target_pairs={{8,0},{16,8},{24,16},{32,24},{40,32},{48,40},{56,48},{64,56},{72,6... | collective-permute-start | bytes 184328 | tf_op jit(solution)/shard_map/ppermute | solution.py:31
  11.2 5.2 %collective-permute-start.4 = (f32[3,5,8,128]{3,2,1,0:T(8,128)S(1)}, f32[3,5,8,128]{3,2,1,0:T(8,128)S(1)}, u32[]{:S(2)}, u32[]{:S(2)}) collective-permute-start(f32[3,5,8,128]{3,2,1,0:T(8,128)S(1)} %get-tuple-element.313), channel_id=1, source_target_pairs={{0,8},{8,16},{16,24},{24,32},{32,40},{40,48},{48,56},{56,64},{64,7... | collective-permute-start | bytes 184328 | tf_op jit(solution)/shard_map/ppermute | solution.py:28
  22.5 1.4 %collective-permute-start.7 = (f32[3,18,5,128]{3,2,1,0:T(8,128)S(1)}, f32[3,18,5,128]{3,2,1,0:T(8,128)S(1)}, u32[]{:S(2)}, u32[]{:S(2)}) collective-permute-start(f32[3,18,5,128]{3,2,1,0:T(8,128)S(1)} %get-tuple-element.318), channel_id=1, source_target_pairs={{1,0},{2,1},{3,2},{4,3},{5,4},{6,5},{7,6},{0,7},{9,8},{10,9},{11,1... | collective-permute-start | bytes 414728 | tf_op jit(solution)/shard_map/ppermute | solution.py:31
  24.2 3.0 %collective-permute-start.3 = (f32[14,12,2,128]{3,2,1,0:T(2,128)S(1)}, f32[14,12,2,128]{3,2,1,0:T(2,128)}, u32[]{:S(2)}, u32[]{:S(2)}) collective-permute-start(f32[14,12,2,128]{3,2,1,0:T(2,128)S(1)} %get-tuple-element.307), channel_id=1, source_target_pairs={{1,0},{2,1},{3,2},{4,3},{5,4},{6,5},{7,6},{0,7},{9,8},{10,9},{11,1... | collective-permute-start | bytes 516104 | tf_op jit(solution)/shard_map/ppermute | solution.py:31
  27.4 3.1 %collective-permute-done.6 = f32[3,18,5,128]{3,2,1,0:T(8,128)S(1)} collective-permute-done((f32[3,18,5,128]{3,2,1,0:T(8,128)S(1)}, f32[3,18,5,128]{3,2,1,0:T(8,128)S(1)}, u32[]{:S(2)}, u32[]{:S(2)}) %collective-permute-start.6) | collective-permute-done | bytes 138272 | tf_op jit(solution)/shard_map/ppermute | solution.py:28
  32.9 43.2 %shard_map.93 = f32[8,128]{1,0:T(8,128)} custom-call(f32[192,128]{1,0:T(8,128)} %bitcast.107, f32[64,128]{1,0:T(8,128)} %slice_bitcast_fusion.3.refs_1_, f32[64,128]{1,0:T(8,128)} %get-tuple-element.345.refs_2_, f32[64,128]{1,0:T(8,128)} %get-tuple-element.329.refs_3_, f32[64,128]{1,0:T(8,128)} %get-tuple-element.330.refs_4_, ...), custom_call_target="tpu_custom_call" | custom-call | tf_op jit(solution)/shard_map/pallas_call | solution.py:258
  76.1 1.5 %fusion.92 = (f32[1,1]{1,0:T(1,128)}, f32[1,1]{1,0:T(1,128)}, f32[1,1]{1,0:T(1,128)}, f32[1,1]{1,0:T(1,128)}, f32[1,1]{1,0:T(1,128)}) fusion(f32[8,128]{1,0:T(8,128)} %shard_map.93), kind=kLoop, calls=%fused_computation.218 | loop fusion | bytes 40 | tf_op jit(solution)/shard_map/slice | solution.py:271
  78.3 31.6 %while.18 = (s32[]{:T(128)}, f32[64,256]{1,0:T(8,128)S(1)}, f32[8,2048]{1,0:T(8,128)S(1)}, s32[2048]{0:T(1024)}, s32[]{:T(128)}, /*index=5*/f32[8,2048]{1,0:T(8,...) while((s32[]{:T(128)}, f32[64,256]{1,0:T(8,128)S(1)}, ...), condition=%wide.region_2.3_spmd.clone, body=%wide.region_0.2_spmd.clone.sunk | while | flops 353384960 | bytes 5411153 | solution.py:386
  80.3 1.5 %compare_select_fusion.5 = (f32[1,512]{1,0:T(1,128)S(1)}, f32[1,512]{1,0:T(1,128)S(1)}, f32[1,512]{1,0:T(1,128)S(1)}) fusion(s32[]{:T(128)} %get-tuple-element.467, s32[]{:T(128)S(6)} %mul.835, f32[8,2048]{1,0:T(8,128)} %get-tuple-element.468, s32[]{:T(128)S(6)} %select_n.141, s32[]{:T(128)S(6)} %add.689, f32[5,512]{1,0:T(8,128)S(1)} %bitcast.108, ...), kind=kLoop, calls=%fused_computation.19.clone.1 | loop fusion | flops 11776 | bytes 14360 | tf_op jit(solution)/shard_map/while/body/eval_jaxpr/mul | solution.py:124
  81.8 1.4 compare_select_fusion.6
  88.2 1.5 %compare_select_fusion.5 = (f32[1,512]{1,0:T(1,128)S(1)}, f32[1,512]{1,0:T(1,128)S(1)}, f32[1,512]{1,0:T(1,128)S(1)}) fusion(s32[]{:T(128)} %get-tuple-element.467, s32[]{:T(128)S(6)} %mul.835, f32[8,2048]{1,0:T(8,128)} %get-tuple-element.468, s32[]{:T(128)S(6)} %select_n.141, s32[]{:T(128)S(6)} %add.689, f32[5,512]{1,0:T(8,128)S(1)} %bitcast.108, ...), kind=kLoop, calls=%fused_computation.19.clone.1 | loop fusion | flops 11776 | bytes 14360 | tf_op jit(solution)/shard_map/while/body/eval_jaxpr/mul | solution.py:124
  96.1 1.5 %compare_select_fusion.5 = (f32[1,512]{1,0:T(1,128)S(1)}, f32[1,512]{1,0:T(1,128)S(1)}, f32[1,512]{1,0:T(1,128)S(1)}) fusion(s32[]{:T(128)} %get-tuple-element.467, s32[]{:T(128)S(6)} %mul.835, f32[8,2048]{1,0:T(8,128)} %get-tuple-element.468, s32[]{:T(128)S(6)} %select_n.141, s32[]{:T(128)S(6)} %add.689, f32[5,512]{1,0:T(8,128)S(1)} %bitcast.108, ...), kind=kLoop, calls=%fused_computation.19.clone.1 | loop fusion | flops 11776 | bytes 14360 | tf_op jit(solution)/shard_map/while/body/eval_jaxpr/mul | solution.py:124
  104.0 1.5 %compare_select_fusion.5 = (f32[1,512]{1,0:T(1,128)S(1)}, f32[1,512]{1,0:T(1,128)S(1)}, f32[1,512]{1,0:T(1,128)S(1)}) fusion(s32[]{:T(128)} %get-tuple-element.467, s32[]{:T(128)S(6)} %mul.835, f32[8,2048]{1,0:T(8,128)} %get-tuple-element.468, s32[]{:T(128)S(6)} %select_n.141, s32[]{:T(128)S(6)} %add.689, f32[5,512]{1,0:T(8,128)S(1)} %bitcast.108, ...), kind=kLoop, calls=%fused_computation.19.clone.1 | loop fusion | flops 11776 | bytes 14360 | tf_op jit(solution)/shard_map/while/body/eval_jaxpr/mul | solution.py:124
  111.5 2.7 %fusion.43 = f32[10,10,130]{2,1,0:T(8,128)S(1)} fusion(f32[10,10,128]{2,1,0:T(8,128)S(1)} %get-tuple-element.326, f32[10,10,128]{2,1,0:T(8,128)S(1)} %get-tuple-element.327, f32[10,10,128]{2,1,0:T(8,128)S(1)} %get-tuple-element.325, f32[10,10,128]{2,1,0:T(8,128)S(1)} %slice.625, f32[]{:T(128)} %bitcast.26, f32[]{:T(128)} %bitcast.25, f32[]{:T(128)} %bitcast.24, ...), kind=kLoop, calls=%fused_computation.109 | loop fusion | flops 91000 | bytes 256816 | tf_op jit(solution)/shard_map/add | solution.py:328
  114.4 3.0 %collective-permute-start.10 = (f32[8,64]{1,0:T(8,128)S(1)}, f32[8,64]{1,0:T(8,128)S(1)}, u32[]{:S(2)}, u32[]{:S(2)}) collective-permute-start(f32[8,64]{1,0:T(8,128)S(1)} %get-tuple-element.333), channel_id=1, source_target_pairs={{0,7},{1,0},{2,1},{3,2},{4,3},{5,4},{6,5},{7,6},{8,15},{9,8},{10,9... | collective-permute-start | bytes 6152 | tf_op jit(solution)/shard_map/ppermute | solution.py:44
  117.3 6.1 %collective-permute-start.9 = (f32[8,64]{1,0:T(8,128)S(1)}, f32[8,64]{1,0:T(8,128)S(1)}, u32[]{:S(2)}, u32[]{:S(2)}) collective-permute-start(f32[8,64]{1,0:T(8,128)S(1)} %get-tuple-element.334), channel_id=1, source_target_pairs={{0,8},{8,16},{16,24},{24,32},{32,40},{40,48},{48,56},{56,64},{64,7... | collective-permute-start | bytes 6152 | tf_op jit(solution)/shard_map/ppermute | solution.py:39
  123.5 2.1 %collective-permute-start.8 = (f32[8,64]{1,0:T(8,128)S(1)}, f32[8,64]{1,0:T(8,128)S(1)}, u32[]{:S(2)}, u32[]{:S(2)}) collective-permute-start(f32[8,64]{1,0:T(8,128)S(1)} %get-tuple-element.331), channel_id=1, source_target_pairs={{8,0},{16,8},{24,16},{32,24},{40,32},{48,40},{56,48},{64,56},{72,6... | collective-permute-start | bytes 6152 | tf_op jit(solution)/shard_map/ppermute | solution.py:39
  126.2 4.8 %collective-permute-done.8 = f32[8,64]{1,0:T(8,128)S(1)} collective-permute-done((f32[8,64]{1,0:T(8,128)S(1)}, f32[8,64]{1,0:T(8,128)S(1)}, u32[]{:S(2)}, u32[]{:S(2)}) %collective-permute-start.8) | collective-permute-done | bytes 2080 | tf_op jit(solution)/shard_map/ppermute | solution.py:39
  133.0 1.6 %fusion.85 = (f32[14,12,12,1]{3,2,1,0:T(8,128)S(1)}, f32[14,12,12,1]{3,2,1,0:T(8,128)}) fusion(f32[14,12,12,128]{3,2,1,0:T(8,128)S(1)} %maximum_select_fusion), kind=kLoop, calls=%fused_computation.211 | loop fusion | bytes 32256 | tf_op jit(solution)/shard_map/jit(_pad)/slice | solution.py:73
  134.6 2.7 %copy.184 = f32[14,12,12,1]{2,1,0,3:T(8,128)S(1)} copy(f32[14,12,12,1]{3,2,1,0:T(8,128)} %get-tuple-element.305) | data formatting | bytes 16128 | tf_op jit(solution)/shard_map/jit(_pad)/slice | solution.py:73
  137.3 1.4 copy.185
  142.1 1.4 fusion.19
  (133 shorter events, 42.0 us)
Async XLA Ops:
  0.6 19.9 %copy-start.2 = (s32[2048]{0:T(1024)S(1)}, s32[2048]{0:T(1024)}, u32[]{:S(2)}) copy-start(s32[2048]{0:T(1024)} %param.12) | copy-start | bytes 24580
  1.6 22.4 %collective-permute-start = (f32[14,2,8,128]{3,2,1,0:T(8,128)S(1)}, f32[14,2,8,128]{3,2,1,0:T(8,128)S(1)}, u32[]{:S(2)}, u32[]{:S(2)}) collective-permute-start(f32[14,2,8,128]{3,2,1,0:T(8,128)S(1)} %get-tuple-element.316), channel_id=1, source_target_pairs={{0,8},{8,16},{16,24},{24,32},{32,40},{40,48},{48,56},{56,64},{64,7... | collective-permute-start | bytes 344072 | tf_op jit(solution)/shard_map/ppermute | solution.py:28
  5.4 18.7 %collective-permute-start.1 = (f32[14,2,8,128]{3,2,1,0:T(8,128)S(1)}, f32[14,2,8,128]{3,2,1,0:T(8,128)S(1)}, u32[]{:S(2)}, u32[]{:S(2)}) collective-permute-start(f32[14,2,8,128]{3,2,1,0:T(8,128)S(1)} %get-tuple-element.315), channel_id=1, source_target_pairs={{8,0},{16,8},{24,16},{32,24},{40,32},{48,40},{56,48},{64,56},{72,6... | collective-permute-start | bytes 344072 | tf_op jit(solution)/shard_map/ppermute | solution.py:31
  8.4 14.0 %collective-permute-start.5 = (f32[3,5,8,128]{3,2,1,0:T(8,128)S(1)}, f32[3,5,8,128]{3,2,1,0:T(8,128)S(1)}, u32[]{:S(2)}, u32[]{:S(2)}) collective-permute-start(f32[3,5,8,128]{3,2,1,0:T(8,128)S(1)} %get-tuple-element.314), channel_id=1, source_target_pairs={{8,0},{16,8},{24,16},{32,24},{40,32},{48,40},{56,48},{64,56},{72,6... | collective-permute-start | bytes 184328 | tf_op jit(solution)/shard_map/ppermute | solution.py:31
  11.2 11.3 %collective-permute-start.4 = (f32[3,5,8,128]{3,2,1,0:T(8,128)S(1)}, f32[3,5,8,128]{3,2,1,0:T(8,128)S(1)}, u32[]{:S(2)}, u32[]{:S(2)}) collective-permute-start(f32[3,5,8,128]{3,2,1,0:T(8,128)S(1)} %get-tuple-element.313), channel_id=1, source_target_pairs={{0,8},{8,16},{16,24},{24,32},{32,40},{40,48},{48,56},{56,64},{64,7... | collective-permute-start | bytes 184328 | tf_op jit(solution)/shard_map/ppermute | solution.py:28
  17.3 13.3 %copy-start.1 = (f32[3,8,8,128]{3,2,1,0:T(8,128)}, f32[3,8,8,128]{3,2,1,0:T(8,128)S(1)}, u32[]{:S(2)}) copy-start(f32[3,8,8,128]{3,2,1,0:T(8,128)S(1)} %slice.451) | copy-start | bytes 294916
  19.7 4.2 %copy-start = (f32[14,8,8,128]{3,2,1,0:T(8,128)S(1)}, f32[14,8,8,128]{3,2,1,0:T(8,128)}, u32[]{:S(2)}) copy-start(f32[14,8,8,128]{3,2,1,0:T(8,128)} %param.8) | copy-start | bytes 1376260
  22.5 4.9 %collective-permute-start.7 = (f32[3,18,5,128]{3,2,1,0:T(8,128)S(1)}, f32[3,18,5,128]{3,2,1,0:T(8,128)S(1)}, u32[]{:S(2)}, u32[]{:S(2)}) collective-permute-start(f32[3,18,5,128]{3,2,1,0:T(8,128)S(1)} %get-tuple-element.318), channel_id=1, source_target_pairs={{1,0},{2,1},{3,2},{4,3},{5,4},{6,5},{7,6},{0,7},{9,8},{10,9},{11,1... | collective-permute-start | bytes 414728 | tf_op jit(solution)/shard_map/ppermute | solution.py:31
  24.0 6.6 %collective-permute-start.6 = (f32[3,18,5,128]{3,2,1,0:T(8,128)S(1)}, f32[3,18,5,128]{3,2,1,0:T(8,128)S(1)}, u32[]{:S(2)}, u32[]{:S(2)}) collective-permute-start(f32[3,18,5,128]{3,2,1,0:T(8,128)S(1)} %get-tuple-element.317), channel_id=1, source_target_pairs={{0,1},{1,2},{2,3},{3,4},{4,5},{5,6},{6,7},{7,0},{8,9},{9,10},{10,1... | collective-permute-start | bytes 414728 | tf_op jit(solution)/shard_map/ppermute | solution.py:28
  24.2 107.5 %collective-permute-start.3 = (f32[14,12,2,128]{3,2,1,0:T(2,128)S(1)}, f32[14,12,2,128]{3,2,1,0:T(2,128)}, u32[]{:S(2)}, u32[]{:S(2)}) collective-permute-start(f32[14,12,2,128]{3,2,1,0:T(2,128)S(1)} %get-tuple-element.307), channel_id=1, source_target_pairs={{1,0},{2,1},{3,2},{4,3},{5,4},{6,5},{7,6},{0,7},{9,8},{10,9},{11,1... | collective-permute-start | bytes 516104 | tf_op jit(solution)/shard_map/ppermute | solution.py:31
  27.1 104.5 %collective-permute-start.2 = (f32[14,12,2,128]{3,2,1,0:T(2,128)S(1)}, f32[14,12,2,128]{3,2,1,0:T(2,128)}, u32[]{:S(2)}, u32[]{:S(2)}) collective-permute-start(f32[14,12,2,128]{3,2,1,0:T(2,128)S(1)} %get-tuple-element.306), channel_id=1, source_target_pairs={{0,1},{1,2},{2,3},{3,4},{4,5},{5,6},{6,7},{7,0},{8,9},{9,10},{10,1... | collective-permute-start | bytes 516104 | tf_op jit(solution)/shard_map/ppermute | solution.py:28
  111.5 12.0 %collective-permute-start.11 = (f32[8,64]{1,0:T(8,128)S(1)}, f32[8,64]{1,0:T(8,128)S(1)}, u32[]{:S(2)}, u32[]{:S(2)}) collective-permute-start(f32[8,64]{1,0:T(8,128)S(1)} %get-tuple-element.332), channel_id=1, source_target_pairs={{0,1},{1,2},{2,3},{3,4},{4,5},{5,6},{6,7},{7,0},{8,9},{9,10},{10,1... | collective-permute-start | bytes 6152 | tf_op jit(solution)/shard_map/ppermute | solution.py:44
  114.4 11.8 %collective-permute-start.10 = (f32[8,64]{1,0:T(8,128)S(1)}, f32[8,64]{1,0:T(8,128)S(1)}, u32[]{:S(2)}, u32[]{:S(2)}) collective-permute-start(f32[8,64]{1,0:T(8,128)S(1)} %get-tuple-element.333), channel_id=1, source_target_pairs={{0,7},{1,0},{2,1},{3,2},{4,3},{5,4},{6,5},{7,6},{8,15},{9,8},{10,9... | collective-permute-start | bytes 6152 | tf_op jit(solution)/shard_map/ppermute | solution.py:44
  117.3 8.9 %collective-permute-start.9 = (f32[8,64]{1,0:T(8,128)S(1)}, f32[8,64]{1,0:T(8,128)S(1)}, u32[]{:S(2)}, u32[]{:S(2)}) collective-permute-start(f32[8,64]{1,0:T(8,128)S(1)} %get-tuple-element.334), channel_id=1, source_target_pairs={{0,8},{8,16},{16,24},{24,32},{32,40},{40,48},{48,56},{56,64},{64,7... | collective-permute-start | bytes 6152 | tf_op jit(solution)/shard_map/ppermute | solution.py:39
  123.5 7.6 %collective-permute-start.8 = (f32[8,64]{1,0:T(8,128)S(1)}, f32[8,64]{1,0:T(8,128)S(1)}, u32[]{:S(2)}, u32[]{:S(2)}) collective-permute-start(f32[8,64]{1,0:T(8,128)S(1)} %get-tuple-element.331), channel_id=1, source_target_pairs={{8,0},{16,8},{24,16},{32,24},{40,32},{48,40},{56,48},{64,56},{72,6... | collective-permute-start | bytes 6152 | tf_op jit(solution)/shard_map/ppermute | solution.py:39

commit v5 on v4

--- a/solution.py
+++ b/solution.py
@@ -138,14 +138,11 @@
     return (6.0 + SHIFT_PRESSURE) * values - beside
 
 
-def butterfly_partners():
-    rounds = []
-    for axis in ("azim", "axial"):
-        step = 1
-        while step < lax.axis_size(axis):
-            rounds.append((axis, step))
-            step *= 2
-    return rounds
+def reduce_groups():
+    axial = lax.axis_size("axial")
+    along_x = 4 if axial % 4 == 0 else 1
+    groups = [("azim", 1, lax.axis_size("azim")), ("axial", 1, along_x), ("axial", along_x, axial // along_x)]
+    return [group for group in groups if group[2] > 1]
 
 
 def coefficient_cg(gram, size, shift, half_width):
@@ -188,25 +185,35 @@
     return solution_c
 
 
-def reduce_kernel(rounds, shift, half_width, vel_ref, *refs):
+def reduce_kernel(groups, shift, half_width, vel_ref, *refs):
     size = ITERS + 1
     basis_refs = refs[:size]
-    o_ref, send_buf, recv_buf, send_sems, recv_sems = refs[size:]
+    o_ref, slots, send_sems, recv_sems = refs[size:]
     here = {"axial": lax.axis_index("axial"), "azim": lax.axis_index("azim")}
 
-    def partner(axis, step):
+    def member(axis, stride, count, m):
         index = here[axis]
-        other = index + step - 2 * step * ((index // step) % 2)
+        base = index - ((index // stride) % count) * stride
         coords = dict(here)
-        coords[axis] = other
+        coords[axis] = base + m * stride
         return (coords["axial"], coords["azim"])
 
+    def position(axis, stride, count):
+        return (here[axis] // stride) % count
+
     barrier = pltpu.get_barrier_semaphore()
-    for axis, step in rounds:
-        pl.semaphore_signal(
-            barrier, inc=1, device_id=partner(axis, step), device_id_type=pl.DeviceIdType.MESH
-        )
-    pl.semaphore_wait(barrier, len(rounds))
+    greeted = 0
+    for axis, stride, count in groups:
+        mine = position(axis, stride, count)
+        for m in range(1, count):
+            pl.semaphore_signal(
+                barrier,
+                inc=1,
+                device_id=member(axis, stride, count, (mine + m) % count),
+                device_id_type=pl.DeviceIdType.MESH,
+            )
+            greeted += 1
+    pl.semaphore_wait(barrier, greeted)
     row = lax.broadcasted_iota(jnp.int32, o_ref.shape, 0)
     lane = lax.broadcasted_iota(jnp.int32, o_ref.shape, 1)
     is_max = (row == 0) & (lane == 0)
@@ -221,20 +228,45 @@
     acc = jnp.zeros(o_ref.shape, jnp.float32)
     for n, entry in enumerate(entries):
         acc = jnp.where((row == 0) & (lane == n), entry, acc)
-    for r, (axis, step) in enumerate(rounds):
-        send_buf[r] = acc
-        copy = pltpu.make_async_remote_copy(
-            src_ref=send_buf.at[r],
-            dst_ref=recv_buf.at[r],
-            send_sem=send_sems.at[r],
-            recv_sem=recv_sems.at[r],
-            device_id=partner(axis, step),
-            device_id_type=pl.DeviceIdType.MESH,
-        )
-        copy.start()
-        copy.wait()
-        other = recv_buf[r]
-        acc = jnp.where(is_max, jnp.maximum(acc, other), acc + other)
+    offset = 0
+    for axis, stride, count in groups:
+        mine = position(axis, stride, count)
+        slots[offset + mine] = acc
+        copies = []
+        for m in range(1, count):
+            target = (mine + m) % count
+            copy = pltpu.make_async_remote_copy(
+                src_ref=slots.at[offset + mine],
+                dst_ref=slots.at[offset + mine],
+                send_sem=send_sems.at[offset + target],
+                recv_sem=recv_sems.at[offset + mine],
+                device_id=member(axis, stride, count, target),
+                device_id_type=pl.DeviceIdType.MESH,
+            )
+            copy.start()
+            copies.append(copy)
+        for copy in copies:
+            copy.wait_send()
+        for m in range(count):
+            incoming = pltpu.make_async_remote_copy(
+                src_ref=slots.at[offset + m],
+                dst_ref=slots.at[offset + m],
+                send_sem=send_sems.at[offset + m],
+                recv_sem=recv_sems.at[offset + m],
+                device_id=member(axis, stride, count, m),
+                device_id_type=pl.DeviceIdType.MESH,
+            )
+
+            @pl.when(m != mine)
+            def _():
+                incoming.wait_recv()
+
+        combined = slots[offset]
+        for m in range(1, count):
+            other = slots[offset + m]
+            combined = jnp.where(is_max, jnp.maximum(combined, other), combined + other)
+        acc = combined
+        offset += count
     first = acc[0:1, :]
     first_lane = lax.broadcasted_iota(jnp.int32, first.shape, 1)
 
@@ -253,18 +285,18 @@
 
 
 def pressure_coefficients(velocity, basis, shift, half_width):
-    rounds = butterfly_partners()
+    groups = reduce_groups()
+    slot_count = sum(count for _, _, count in groups)
     flat = [v.reshape(-1, v.shape[-1]) for v in basis]
     out = pl.pallas_call(
-        lambda *refs: reduce_kernel(rounds, shift, half_width, *refs),
+        lambda *refs: reduce_kernel(groups, shift, half_width, *refs),
         out_shape=jax.ShapeDtypeStruct((8, 128), jnp.float32),
         in_specs=[pl.BlockSpec(memory_space=pltpu.VMEM)] * (1 + len(flat)),
         out_specs=pl.BlockSpec(memory_space=pltpu.VMEM),
         scratch_shapes=[
-            pltpu.VMEM((len(rounds), 8, 128), jnp.float32),
-            pltpu.VMEM((len(rounds), 8, 128), jnp.float32),
-            pltpu.SemaphoreType.DMA((len(rounds),)),
-            pltpu.SemaphoreType.DMA((len(rounds),)),
+            pltpu.VMEM((slot_count, 8, 128), jnp.float32),
+            pltpu.SemaphoreType.DMA((slot_count,)),
+            pltpu.SemaphoreType.DMA((slot_count,)),
         ],
         compiler_params=pltpu.CompilerParams(collective_id=0, has_side_effects=True),
     )(velocity.reshape(-1, velocity.shape[-1]), *flat)

time: 147 us -> 131 us (0.89)
  Pallas kernels: 43.2 us -> 29.3 us
  starting transfers between devices: 29.4 us -> 27.4 us
    pallas_call x1, Pallas kernels: 43.2 us -> 29.3 us  [pressure_coefficients(): pl.pallas_call(lambda *refs: reduce_kernel(groups, shift, half_width, *re...]
    ppermute x2, starting transfers between devices: 8.21 us -> 6.2 us  [shifted_2(): return lax.ppermute(shard, axis, pairs)]
  transfers between devices with their start and end apart: 12 -> 12, of which waited for: 3 -> 3; matrix products, arithmetic and copies ran while one was open for 33% -> 37% of each run, Pallas kernels for 30% -> 23%
where the time goes in v5:
time: 131 us; the launch traced here: 128 us
  other arithmetic  39.1 us (30%)
  Pallas kernels  29.3 us (22%)
  starting transfers between devices  27.4 us (21%)
  local copies, waits for them, and re-layouts  15.2 us (12%)
  waiting for transfers between devices  8.26 us (6%)
  matrix products  6.24 us (5%)
  between operations  2.46 us (2%)
    pallas_call x1, Pallas kernels, pressure_coefficients(): pl.pallas_call(lambda *refs: reduce_kernel(groups, shift, half_width, *re...  29.3 us
    mul x8, other arithmetic, evaporate(): sources = jnp.stack([heat_source * alive_mask, lost_mass * alive_mask])  11.7 us
    ppermute x4, starting transfers between devices, extended(): lax.ppermute(lax.slice_in_dim(block, 0, width, axis=dim), axis, backward)  9.25 us
    ppermute x4, starting transfers between devices, extended(): lax.ppermute(lax.slice_in_dim(block, block.shape[dim] - width, None, axis...  8.96 us
    ppermute x2, starting transfers between devices, shifted_2(): return lax.ppermute(shard, axis, pairs)  6.2 us
    slice x4, local copies, waits for them, and re-layouts, radial_pad(): jnp.pad(values, [(0, 0)] * (values.ndim - 1) + [(rim_width, rim_width)],...  5.97 us
    ppermute x2, waiting for transfers between devices, shifted_2(): return lax.ppermute(shard, axis, pairs)  4.85 us
    add x4, other arithmetic, evaporate(): new_offsets = offsets + step_size * new_vel  3.53 us
  transfers between devices with their start and end apart: 12, of which 3 were waited for; matrix products, arithmetic and copies ran while one was open for 37% of the time, Pallas kernels for 23%

profile of v5, /device:TPU:6, one launch (start us, length us, event | category | flops | bytes accessed | tf_op | source)
XLA Modules:
  0.0 128.4 jit_solution(7906298685400817566)
XLA Ops:
  1.6 3.7 %collective-permute-start = (f32[14,2,8,128]{3,2,1,0:T(8,128)S(1)}, f32[14,2,8,128]{3,2,1,0:T(8,128)S(1)}, u32[]{:S(2)}, u32[]{:S(2)}) collective-permute-start(f32[14,2,8,128]{3,2,1,0:T(8,128)S(1)} %get-tuple-element.316), channel_id=1, source_target_pairs={{0,8},{8,16},{16,24},{24,32},{32,40},{40,48},{48,56},{56,64},{64,7... | collective-permute-start | bytes 344072 | tf_op jit(solution)/shard_map/ppermute | solution.py:28
  5.4 2.1 %collective-permute-start.1 = (f32[14,2,8,128]{3,2,1,0:T(8,128)S(1)}, f32[14,2,8,128]{3,2,1,0:T(8,128)S(1)}, u32[]{:S(2)}, u32[]{:S(2)}) collective-permute-start(f32[14,2,8,128]{3,2,1,0:T(8,128)S(1)} %get-tuple-element.315), channel_id=1, source_target_pairs={{8,0},{16,8},{24,16},{32,24},{40,32},{48,40},{56,48},{64,56},{72,6... | collective-permute-start | bytes 344072 | tf_op jit(solution)/shard_map/ppermute | solution.py:31
  8.4 2.7 %collective-permute-start.5 = (f32[3,5,8,128]{3,2,1,0:T(8,128)S(1)}, f32[3,5,8,128]{3,2,1,0:T(8,128)S(1)}, u32[]{:S(2)}, u32[]{:S(2)}) collective-permute-start(f32[3,5,8,128]{3,2,1,0:T(8,128)S(1)} %get-tuple-element.314), channel_id=1, source_target_pairs={{8,0},{16,8},{24,16},{32,24},{40,32},{48,40},{56,48},{64,56},{72,6... | collective-permute-start | bytes 184328 | tf_op jit(solution)/shard_map/ppermute | solution.py:31
  11.2 5.2 %collective-permute-start.4 = (f32[3,5,8,128]{3,2,1,0:T(8,128)S(1)}, f32[3,5,8,128]{3,2,1,0:T(8,128)S(1)}, u32[]{:S(2)}, u32[]{:S(2)}) collective-permute-start(f32[3,5,8,128]{3,2,1,0:T(8,128)S(1)} %get-tuple-element.313), channel_id=1, source_target_pairs={{0,8},{8,16},{16,24},{24,32},{32,40},{40,48},{48,56},{56,64},{64,7... | collective-permute-start | bytes 184328 | tf_op jit(solution)/shard_map/ppermute | solution.py:28
  22.5 1.4 %collective-permute-start.7 = (f32[3,18,5,128]{3,2,1,0:T(8,128)S(1)}, f32[3,18,5,128]{3,2,1,0:T(8,128)S(1)}, u32[]{:S(2)}, u32[]{:S(2)}) collective-permute-start(f32[3,18,5,128]{3,2,1,0:T(8,128)S(1)} %get-tuple-element.318), channel_id=1, source_target_pairs={{1,0},{2,1},{3,2},{4,3},{5,4},{6,5},{7,6},{0,7},{9,8},{10,9},{11,1... | collective-permute-start | bytes 414728 | tf_op jit(solution)/shard_map/ppermute | solution.py:31
  24.2 3.0 %collective-permute-start.3 = (f32[14,12,2,128]{3,2,1,0:T(2,128)S(1)}, f32[14,12,2,128]{3,2,1,0:T(2,128)}, u32[]{:S(2)}, u32[]{:S(2)}) collective-permute-start(f32[14,12,2,128]{3,2,1,0:T(2,128)S(1)} %get-tuple-element.307), channel_id=1, source_target_pairs={{1,0},{2,1},{3,2},{4,3},{5,4},{6,5},{7,6},{0,7},{9,8},{10,9},{11,1... | collective-permute-start | bytes 516104 | tf_op jit(solution)/shard_map/ppermute | solution.py:31
  27.4 3.1 %collective-permute-done.6 = f32[3,18,5,128]{3,2,1,0:T(8,128)S(1)} collective-permute-done((f32[3,18,5,128]{3,2,1,0:T(8,128)S(1)}, f32[3,18,5,128]{3,2,1,0:T(8,128)S(1)}, u32[]{:S(2)}, u32[]{:S(2)}) %collective-permute-start.6) | collective-permute-done | bytes 138272 | tf_op jit(solution)/shard_map/ppermute | solution.py:28
  32.9 29.3 %shard_map.93 = f32[8,128]{1,0:T(8,128)} custom-call(f32[192,128]{1,0:T(8,128)} %bitcast.107, f32[64,128]{1,0:T(8,128)} %slice_bitcast_fusion.3.refs_1_, f32[64,128]{1,0:T(8,128)} %get-tuple-element.345.refs_2_, f32[64,128]{1,0:T(8,128)} %get-tuple-element.329.refs_3_, f32[64,128]{1,0:T(8,128)} %get-tuple-element.330.refs_4_, ...), custom_call_target="tpu_custom_call" | custom-call | tf_op jit(solution)/shard_map/pallas_call | solution.py:291
  62.2 1.5 %fusion.92 = (f32[1,1]{1,0:T(1,128)}, f32[1,1]{1,0:T(1,128)}, f32[1,1]{1,0:T(1,128)}, f32[1,1]{1,0:T(1,128)}, f32[1,1]{1,0:T(1,128)}) fusion(f32[8,128]{1,0:T(8,128)} %shard_map.93), kind=kLoop, calls=%fused_computation.218 | loop fusion | bytes 40 | tf_op jit(solution)/shard_map/slice | solution.py:303
  64.4 31.6 %while.18 = (s32[]{:T(128)}, f32[64,256]{1,0:T(8,128)S(1)}, f32[8,2048]{1,0:T(8,128)S(1)}, s32[2048]{0:T(1024)}, s32[]{:T(128)}, /*index=5*/f32[8,2048]{1,0:T(8,...) while((s32[]{:T(128)}, f32[64,256]{1,0:T(8,128)S(1)}, ...), condition=%wide.region_2.3_spmd.clone, body=%wide.region_0.2_spmd.clone.sunk | while | flops 353384960 | bytes 5411153 | solution.py:418
  66.4 1.5 %compare_select_fusion.5 = (f32[1,512]{1,0:T(1,128)S(1)}, f32[1,512]{1,0:T(1,128)S(1)}, f32[1,512]{1,0:T(1,128)S(1)}) fusion(s32[]{:T(128)} %get-tuple-element.467, s32[]{:T(128)S(6)} %mul.835, f32[8,2048]{1,0:T(8,128)} %get-tuple-element.468, s32[]{:T(128)S(6)} %select_n.141, s32[]{:T(128)S(6)} %add.689, f32[5,512]{1,0:T(8,128)S(1)} %bitcast.108, ...), kind=kLoop, calls=%fused_computation.19.clone.1 | loop fusion | flops 11776 | bytes 14360 | tf_op jit(solution)/shard_map/while/body/eval_jaxpr/mul | solution.py:124
  67.9 1.4 %compare_select_fusion.6 = f32[1,512]{1,0:T(1,128)S(1)} fusion(s32[]{:T(128)} %get-tuple-element.467, s32[]{:T(128)S(6)} %mul.835, f32[1,512]{1,0:T(1,128)S(1)} %get-tuple-element.422, f32[8,2048]{1,0:T(8,128)} %get-tuple-element.468, s32[]{:T(128)S(6)} %select_n.141), kind=kLoop, calls=%fused_computation.18.clone.1 | loop fusion | flops 2048 | bytes 6156 | tf_op jit(solution)/shard_map/while/body/eval_jaxpr/mul | solution.py:124
  74.3 1.5 %compare_select_fusion.5 = (f32[1,512]{1,0:T(1,128)S(1)}, f32[1,512]{1,0:T(1,128)S(1)}, f32[1,512]{1,0:T(1,128)S(1)}) fusion(s32[]{:T(128)} %get-tuple-element.467, s32[]{:T(128)S(6)} %mul.835, f32[8,2048]{1,0:T(8,128)} %get-tuple-element.468, s32[]{:T(128)S(6)} %select_n.141, s32[]{:T(128)S(6)} %add.689, f32[5,512]{1,0:T(8,128)S(1)} %bitcast.108, ...), kind=kLoop, calls=%fused_computation.19.clone.1 | loop fusion | flops 11776 | bytes 14360 | tf_op jit(solution)/shard_map/while/body/eval_jaxpr/mul | solution.py:124
  82.2 1.5 %compare_select_fusion.5 = (f32[1,512]{1,0:T(1,128)S(1)}, f32[1,512]{1,0:T(1,128)S(1)}, f32[1,512]{1,0:T(1,128)S(1)}) fusion(s32[]{:T(128)} %get-tuple-element.467, s32[]{:T(128)S(6)} %mul.835, f32[8,2048]{1,0:T(8,128)} %get-tuple-element.468, s32[]{:T(128)S(6)} %select_n.141, s32[]{:T(128)S(6)} %add.689, f32[5,512]{1,0:T(8,128)S(1)} %bitcast.108, ...), kind=kLoop, calls=%fused_computation.19.clone.1 | loop fusion | flops 11776 | bytes 14360 | tf_op jit(solution)/shard_map/while/body/eval_jaxpr/mul | solution.py:124
  90.1 1.5 %compare_select_fusion.5 = (f32[1,512]{1,0:T(1,128)S(1)}, f32[1,512]{1,0:T(1,128)S(1)}, f32[1,512]{1,0:T(1,128)S(1)}) fusion(s32[]{:T(128)} %get-tuple-element.467, s32[]{:T(128)S(6)} %mul.835, f32[8,2048]{1,0:T(8,128)} %get-tuple-element.468, s32[]{:T(128)S(6)} %select_n.141, s32[]{:T(128)S(6)} %add.689, f32[5,512]{1,0:T(8,128)S(1)} %bitcast.108, ...), kind=kLoop, calls=%fused_computation.19.clone.1 | loop fusion | flops 11776 | bytes 14360 | tf_op jit(solution)/shard_map/while/body/eval_jaxpr/mul | solution.py:124
  97.6 2.7 %fusion.43 = f32[10,10,130]{2,1,0:T(8,128)S(1)} fusion(f32[10,10,128]{2,1,0:T(8,128)S(1)} %get-tuple-element.326, f32[10,10,128]{2,1,0:T(8,128)S(1)} %get-tuple-element.327, f32[10,10,128]{2,1,0:T(8,128)S(1)} %get-tuple-element.325, f32[10,10,128]{2,1,0:T(8,128)S(1)} %slice.625, f32[]{:T(128)} %bitcast.26, f32[]{:T(128)} %bitcast.25, f32[]{:T(128)} %bitcast.24, ...), kind=kLoop, calls=%fused_computation.109 | loop fusion | flops 91000 | bytes 256816 | tf_op jit(solution)/shard_map/add | solution.py:360
  100.5 3.0 %collective-permute-start.10 = (f32[8,64]{1,0:T(8,128)S(1)}, f32[8,64]{1,0:T(8,128)S(1)}, u32[]{:S(2)}, u32[]{:S(2)}) collective-permute-start(f32[8,64]{1,0:T(8,128)S(1)} %get-tuple-element.333), channel_id=1, source_target_pairs={{0,7},{1,0},{2,1},{3,2},{4,3},{5,4},{6,5},{7,6},{8,15},{9,8},{10,9... | collective-permute-start | bytes 6152 | tf_op jit(solution)/shard_map/ppermute | solution.py:44
  103.4 4.1 %collective-permute-start.9 = (f32[8,64]{1,0:T(8,128)S(1)}, f32[8,64]{1,0:T(8,128)S(1)}, u32[]{:S(2)}, u32[]{:S(2)}) collective-permute-start(f32[8,64]{1,0:T(8,128)S(1)} %get-tuple-element.334), channel_id=1, source_target_pairs={{0,8},{8,16},{16,24},{24,32},{32,40},{40,48},{48,56},{56,64},{64,7... | collective-permute-start | bytes 6152 | tf_op jit(solution)/shard_map/ppermute | solution.py:39
  107.5 2.1 %collective-permute-start.8 = (f32[8,64]{1,0:T(8,128)S(1)}, f32[8,64]{1,0:T(8,128)S(1)}, u32[]{:S(2)}, u32[]{:S(2)}) collective-permute-start(f32[8,64]{1,0:T(8,128)S(1)} %get-tuple-element.331), channel_id=1, source_target_pairs={{8,0},{16,8},{24,16},{32,24},{40,32},{48,40},{56,48},{64,56},{72,6... | collective-permute-start | bytes 6152 | tf_op jit(solution)/shard_map/ppermute | solution.py:39
  110.3 4.8 %collective-permute-done.8 = f32[8,64]{1,0:T(8,128)S(1)} collective-permute-done((f32[8,64]{1,0:T(8,128)S(1)}, f32[8,64]{1,0:T(8,128)S(1)}, u32[]{:S(2)}, u32[]{:S(2)}) %collective-permute-start.8) | collective-permute-done | bytes 2080 | tf_op jit(solution)/shard_map/ppermute | solution.py:39
  117.1 1.6 %fusion.85 = (f32[14,12,12,1]{3,2,1,0:T(8,128)S(1)}, f32[14,12,12,1]{3,2,1,0:T(8,128)}) fusion(f32[14,12,12,128]{3,2,1,0:T(8,128)S(1)} %maximum_select_fusion), kind=kLoop, calls=%fused_computation.211 | loop fusion | bytes 32256 | tf_op jit(solution)/shard_map/jit(_pad)/slice | solution.py:73
  118.7 2.7 %copy.184 = f32[14,12,12,1]{2,1,0,3:T(8,128)S(1)} copy(f32[14,12,12,1]{3,2,1,0:T(8,128)} %get-tuple-element.305) | data formatting | bytes 16128 | tf_op jit(solution)/shard_map/jit(_pad)/slice | solution.py:73
  121.4 1.4 %copy.185 = f32[14,12,12,1]{2,1,0,3:T(8,128)S(1)} copy(f32[14,12,12,1]{3,2,1,0:T(8,128)S(1)} %get-tuple-element.304) | data formatting | bytes 16128 | tf_op jit(solution)/shard_map/jit(_pad)/slice | solution.py:73
  126.2 1.4 %fusion.19 = f32[10,8,8,128]{3,2,1,0:T(8,128)S(1)} fusion(f32[14,12,12,128]{3,2,1,0:T(8,128)S(1)} %maximum_select_fusion, f32[14,12,12,2]{3,2,1,0:T(8,128)S(1)} %reshape.264, f32[14,12,12,2]{3,2,1,0:T(8,128)S(1)} %reshape.265, f32[10,12,12,132]{3,2,1,0:T(8,128)S(1)} %get-tuple-element.303, f32[10,12,12,132]{3,2,1,0:T(8,128)S(1)} %get-tuple-element.302, ...), kind=kLoop, calls=%fused_computation.53 | loop fusion | flops 4259840 | bytes 10224132 | tf_op jit(solution)/shard_map/add | solution.py:103
  (133 shorter events, 42.0 us)
Async XLA Ops:
  0.6 19.9 %copy-start.2 = (s32[2048]{0:T(1024)S(1)}, s32[2048]{0:T(1024)}, u32[]{:S(2)}) copy-start(s32[2048]{0:T(1024)} %param.12) | copy-start | bytes 24580
  1.6 22.4 %collective-permute-start = (f32[14,2,8,128]{3,2,1,0:T(8,128)S(1)}, f32[14,2,8,128]{3,2,1,0:T(8,128)S(1)}, u32[]{:S(2)}, u32[]{:S(2)}) collective-permute-start(f32[14,2,8,128]{3,2,1,0:T(8,128)S(1)} %get-tuple-element.316), channel_id=1, source_target_pairs={{0,8},{8,16},{16,24},{24,32},{32,40},{40,48},{48,56},{56,64},{64,7... | collective-permute-start | bytes 344072 | tf_op jit(solution)/shard_map/ppermute | solution.py:28
  5.4 18.7 %collective-permute-start.1 = (f32[14,2,8,128]{3,2,1,0:T(8,128)S(1)}, f32[14,2,8,128]{3,2,1,0:T(8,128)S(1)}, u32[]{:S(2)}, u32[]{:S(2)}) collective-permute-start(f32[14,2,8,128]{3,2,1,0:T(8,128)S(1)} %get-tuple-element.315), channel_id=1, source_target_pairs={{8,0},{16,8},{24,16},{32,24},{40,32},{48,40},{56,48},{64,56},{72,6... | collective-permute-start | bytes 344072 | tf_op jit(solution)/shard_map/ppermute | solution.py:31
  8.4 14.0 %collective-permute-start.5 = (f32[3,5,8,128]{3,2,1,0:T(8,128)S(1)}, f32[3,5,8,128]{3,2,1,0:T(8,128)S(1)}, u32[]{:S(2)}, u32[]{:S(2)}) collective-permute-start(f32[3,5,8,128]{3,2,1,0:T(8,128)S(1)} %get-tuple-element.314), channel_id=1, source_target_pairs={{8,0},{16,8},{24,16},{32,24},{40,32},{48,40},{56,48},{64,56},{72,6... | collective-permute-start | bytes 184328 | tf_op jit(solution)/shard_map/ppermute | solution.py:31
  11.2 11.3 %collective-permute-start.4 = (f32[3,5,8,128]{3,2,1,0:T(8,128)S(1)}, f32[3,5,8,128]{3,2,1,0:T(8,128)S(1)}, u32[]{:S(2)}, u32[]{:S(2)}) collective-permute-start(f32[3,5,8,128]{3,2,1,0:T(8,128)S(1)} %get-tuple-element.313), channel_id=1, source_target_pairs={{0,8},{8,16},{16,24},{24,32},{32,40},{40,48},{48,56},{56,64},{64,7... | collective-permute-start | bytes 184328 | tf_op jit(solution)/shard_map/ppermute | solution.py:28
  17.3 13.3 %copy-start.1 = (f32[3,8,8,128]{3,2,1,0:T(8,128)}, f32[3,8,8,128]{3,2,1,0:T(8,128)S(1)}, u32[]{:S(2)}) copy-start(f32[3,8,8,128]{3,2,1,0:T(8,128)S(1)} %slice.451) | copy-start | bytes 294916
  19.7 4.2 %copy-start = (f32[14,8,8,128]{3,2,1,0:T(8,128)S(1)}, f32[14,8,8,128]{3,2,1,0:T(8,128)}, u32[]{:S(2)}) copy-start(f32[14,8,8,128]{3,2,1,0:T(8,128)} %param.8) | copy-start | bytes 1376260
  22.5 4.9 %collective-permute-start.7 = (f32[3,18,5,128]{3,2,1,0:T(8,128)S(1)}, f32[3,18,5,128]{3,2,1,0:T(8,128)S(1)}, u32[]{:S(2)}, u32[]{:S(2)}) collective-permute-start(f32[3,18,5,128]{3,2,1,0:T(8,128)S(1)} %get-tuple-element.318), channel_id=1, source_target_pairs={{1,0},{2,1},{3,2},{4,3},{5,4},{6,5},{7,6},{0,7},{9,8},{10,9},{11,1... | collective-permute-start | bytes 414728 | tf_op jit(solution)/shard_map/ppermute | solution.py:31
  24.0 6.6 %collective-permute-start.6 = (f32[3,18,5,128]{3,2,1,0:T(8,128)S(1)}, f32[3,18,5,128]{3,2,1,0:T(8,128)S(1)}, u32[]{:S(2)}, u32[]{:S(2)}) collective-permute-start(f32[3,18,5,128]{3,2,1,0:T(8,128)S(1)} %get-tuple-element.317), channel_id=1, source_target_pairs={{0,1},{1,2},{2,3},{3,4},{4,5},{5,6},{6,7},{7,0},{8,9},{9,10},{10,1... | collective-permute-start | bytes 414728 | tf_op jit(solution)/shard_map/ppermute | solution.py:28
  24.2 91.6 %collective-permute-start.3 = (f32[14,12,2,128]{3,2,1,0:T(2,128)S(1)}, f32[14,12,2,128]{3,2,1,0:T(2,128)}, u32[]{:S(2)}, u32[]{:S(2)}) collective-permute-start(f32[14,12,2,128]{3,2,1,0:T(2,128)S(1)} %get-tuple-element.307), channel_id=1, source_target_pairs={{1,0},{2,1},{3,2},{4,3},{5,4},{6,5},{7,6},{0,7},{9,8},{10,9},{11,1... | collective-permute-start | bytes 516104 | tf_op jit(solution)/shard_map/ppermute | solution.py:31
  27.1 88.6 %collective-permute-start.2 = (f32[14,12,2,128]{3,2,1,0:T(2,128)S(1)}, f32[14,12,2,128]{3,2,1,0:T(2,128)}, u32[]{:S(2)}, u32[]{:S(2)}) collective-permute-start(f32[14,12,2,128]{3,2,1,0:T(2,128)S(1)} %get-tuple-element.306), channel_id=1, source_target_pairs={{0,1},{1,2},{2,3},{3,4},{4,5},{5,6},{6,7},{7,0},{8,9},{9,10},{10,1... | collective-permute-start | bytes 516104 | tf_op jit(solution)/shard_map/ppermute | solution.py:28
  97.6 9.9 %collective-permute-start.11 = (f32[8,64]{1,0:T(8,128)S(1)}, f32[8,64]{1,0:T(8,128)S(1)}, u32[]{:S(2)}, u32[]{:S(2)}) collective-permute-start(f32[8,64]{1,0:T(8,128)S(1)} %get-tuple-element.332), channel_id=1, source_target_pairs={{0,1},{1,2},{2,3},{3,4},{4,5},{5,6},{6,7},{7,0},{8,9},{9,10},{10,1... | collective-permute-start | bytes 6152 | tf_op jit(solution)/shard_map/ppermute | solution.py:44
  100.5 9.8 %collective-permute-start.10 = (f32[8,64]{1,0:T(8,128)S(1)}, f32[8,64]{1,0:T(8,128)S(1)}, u32[]{:S(2)}, u32[]{:S(2)}) collective-permute-start(f32[8,64]{1,0:T(8,128)S(1)} %get-tuple-element.333), channel_id=1, source_target_pairs={{0,7},{1,0},{2,1},{3,2},{4,3},{5,4},{6,5},{7,6},{8,15},{9,8},{10,9... | collective-permute-start | bytes 6152 | tf_op jit(solution)/shard_map/ppermute | solution.py:44
  103.4 6.9 %collective-permute-start.9 = (f32[8,64]{1,0:T(8,128)S(1)}, f32[8,64]{1,0:T(8,128)S(1)}, u32[]{:S(2)}, u32[]{:S(2)}) collective-permute-start(f32[8,64]{1,0:T(8,128)S(1)} %get-tuple-element.334), channel_id=1, source_target_pairs={{0,8},{8,16},{16,24},{24,32},{32,40},{40,48},{48,56},{56,64},{64,7... | collective-permute-start | bytes 6152 | tf_op jit(solution)/shard_map/ppermute | solution.py:39
  107.5 7.6 %collective-permute-start.8 = (f32[8,64]{1,0:T(8,128)S(1)}, f32[8,64]{1,0:T(8,128)S(1)}, u32[]{:S(2)}, u32[]{:S(2)}) collective-permute-start(f32[8,64]{1,0:T(8,128)S(1)} %get-tuple-element.331), channel_id=1, source_target_pairs={{8,0},{16,8},{24,16},{32,24},{40,32},{48,40},{56,48},{64,56},{72,6... | collective-permute-start | bytes 6152 | tf_op jit(solution)/shard_map/ppermute | solution.py:39

commit v6 on v5

--- a/solution.py
+++ b/solution.py
@@ -385,37 +385,22 @@
         moving[3:], vel_pad, density_pad, density_rim, diff_coef[:, None, None, None], step_size
     )
     npar_local = parcel_cell.shape[0]
-    block_rows = 512
     cells_x, cells_y, cells_z = (state.shape[1], state.shape[2], state.shape[3])
     plane_count = cells_x * cells_y
     gas_table = jnp.transpose(state[1:6].reshape(5, plane_count, cells_z), (1, 0, 2)).reshape(
         plane_count, 5 * cells_z
     )
     live_now = live_count[0]
-
-    def one_block(block_index, carried_pair):
-        deposit, updated = carried_pair
-        first_slot = block_index * block_rows
-        cell_ids = lax.dynamic_slice_in_dim(parcel_cell, first_slot, block_rows)
-        attrs = lax.dynamic_slice_in_dim(parcel_state, first_slot, block_rows, 1)
-        alive_mask = (first_slot + jnp.arange(block_rows) < live_now).astype(jnp.float32)
-        plane_ids = cell_ids // cells_z
-        radial_ids = cell_ids % cells_z
-        plane_hot = (plane_ids[:, None] == jnp.arange(plane_count)[None, :]).astype(jnp.float32)
-        radial_hot = (radial_ids[:, None] == jnp.arange(cells_z)[None, :]).astype(jnp.float32)
-        gas_rows = jnp.dot(plane_hot, gas_table, precision=HIGHEST).reshape(block_rows, 5, cells_z)
-        gas_values = jnp.sum(gas_rows * radial_hot[:, None, :], axis=2).T
-        new_attrs, sources = evaporate(attrs, gas_values, alive_mask, step_size)
-        spread = (sources.T[:, :, None] * radial_hot[:, None, :]).reshape(block_rows, 2 * cells_z)
-        deposit = deposit + lax.dot_general(
-            plane_hot, spread, (((0,), (0,)), ((), ())), precision=HIGHEST
-        )
-        updated = lax.dynamic_update_slice_in_dim(updated, new_attrs, first_slot, 1)
-        return (deposit, updated)
-
-    initial = (jnp.zeros((plane_count, 2 * cells_z), jnp.float32), jnp.zeros_like(parcel_state))
-    block_count = npar_local // block_rows
-    deposit, updated = lax.fori_loop(0, block_count, one_block, initial)
+    alive_mask = (jnp.arange(npar_local) < live_now).astype(jnp.float32)
+    plane_ids = parcel_cell // cells_z
+    radial_ids = parcel_cell % cells_z
+    plane_hot = (plane_ids[:, None] == jnp.arange(plane_count)[None, :]).astype(jnp.float32)
+    radial_hot = (radial_ids[:, None] == jnp.arange(cells_z)[None, :]).astype(jnp.float32)
+    gas_rows = jnp.dot(plane_hot, gas_table, precision=HIGHEST).reshape(npar_local, 5, cells_z)
+    gas_values = jnp.sum(gas_rows * radial_hot[:, None, :], axis=2).T
+    updated, sources = evaporate(parcel_state, gas_values, alive_mask, step_size)
+    spread = (sources.T[:, :, None] * radial_hot[:, None, :]).reshape(npar_local, 2 * cells_z)
+    deposit = lax.dot_general(plane_hot, spread, (((0,), (0,)), ((), ())), precision=HIGHEST)
     deposit = jnp.transpose(deposit.reshape(cells_x, cells_y, 2, cells_z), (2, 0, 1, 3))
     scalars_new = jnp.concatenate(
         [transported[:2] + deposit / state[0][None], transported[2:]], axis=0

time: 131 us -> 96.9 us (0.74); the launches traced: 128 us -> 96.2 us
  other arithmetic: 39.1 us -> 13.7 us
  local copies, waits for them, and re-layouts: 15.2 us -> 10.3 us
  matrix products: 6.24 us -> 4.66 us
  Pallas kernels: 29.3 us -> 27.8 us
  starting transfers between devices: 27.4 us -> 28.9 us
    mul x8 -> x2, other arithmetic: 11.7 us -> 0.13 us  [evaporate(): sources = jnp.stack([heat_source * alive_mask, lost_mass * alive_mask])]
    slice x4 -> x2, local copies, waits for them, and re-layouts: 5.97 us -> 1.41 us  [radial_pad(): jnp.pad(values, [(0, 0)] * (values.ndim - 1) + [(rim_width, rim_width)],...]
    add x4 -> x1, other arithmetic: 3.53 us -> 0.03 us  [evaporate(): new_offsets = offsets + step_size * new_vel]
    mul x4 -> x0, other arithmetic: 2.82 us -> none  [one_block(): sources.T[:, :, None] * radial_hot[:, None, :]]
    convert_element_type x8 -> x1, other arithmetic: 2.71 us -> 0.11 us  [on_device(): (radial_ids[:, None] == jnp.arange(cells_z)[None, :]).astype(jnp.float32)]
    select_n x4 -> x1, other arithmetic: 3.09 us -> 0.71 us  [on_device(): plane_ids = parcel_cell // cells_z]
    dot_general x8 -> x2, matrix products: 5.45 us -> 3.85 us  [the longest x1 2.54 us: on_device(): jnp.dot(plane_hot, gas_table, precision=HIGHEST)]
    ppermute x2, starting transfers between devices: 6.2 us -> 7.74 us  [shifted_2(): return lax.ppermute(shard, axis, pairs)]
  transfers between devices with their start and end apart: 12 -> 12, of which waited for: 3 -> 3; matrix products, arithmetic and copies ran while one was open for 37% -> 20% of each run, Pallas kernels for 23% -> 29%
where the time goes in v6:
time: 96.9 us; the launch traced here: 96.2 us
  starting transfers between devices  28.9 us (30%)
  Pallas kernels  27.8 us (29%)
  other arithmetic  13.7 us (14%)
  local copies, waits for them, and re-layouts  10.3 us (11%)
  waiting for transfers between devices  8.26 us (9%)
  matrix products  4.66 us (5%)
  between operations  2.52 us (3%)
    pallas_call x1, Pallas kernels, pressure_coefficients(): pl.pallas_call(lambda *refs: reduce_kernel(groups, shift, half_width, *re...  27.8 us
    ppermute x4, starting transfers between devices, extended(): lax.ppermute(lax.slice_in_dim(block, 0, width, axis=dim), axis, backward)  9.25 us
    ppermute x4, starting transfers between devices, extended(): lax.ppermute(lax.slice_in_dim(block, block.shape[dim] - width, None, axis...  8.96 us
    ppermute x2, starting transfers between devices, shifted_2(): return lax.ppermute(shard, axis, pairs)  7.74 us
    ppermute x2, waiting for transfers between devices, shifted_2(): return lax.ppermute(shard, axis, pairs)  4.85 us
    ppermute x4, waiting for transfers between devices, extended(): lax.ppermute(lax.slice_in_dim(block, block.shape[dim] - width, None, axis...  3.12 us
    ppermute x2, starting transfers between devices, shifted_3(): lax.ppermute(shard, axis, [(i, (i + by) % length) for i in range(length)])  2.96 us
    add x1, other arithmetic, solve_pressure(): padded_pressure = padded_pressure + coefficients[j] * padded_basis[j]  2.82 us
  transfers between devices with their start and end apart: 12, of which 3 were waited for; matrix products, arithmetic and copies ran while one was open for 20% of the time, Pallas kernels for 29%

profile of v6, /device:TPU:6, one launch (start us, length us, event | category | flops | bytes accessed | tf_op | source)
XLA Modules:
  0.0 96.2 jit_solution(17820783354609801106)
XLA Ops:
  0.6 1.0 %fusion.108 = (f32[14,2,8,128]{3,2,1,0:T(8,128)S(1)}, f32[14,2,8,128]{3,2,1,0:T(8,128)S(1)}) fusion(f32[14,8,8,128]{3,2,1,0:T(8,128)} %param.6), kind=kLoop, calls=%fused_computation.222 | loop fusion | bytes 458752 | tf_op jit(solution)/shard_map/slice | solution.py:31
  1.6 3.7 %collective-permute-start = (f32[14,2,8,128]{3,2,0,1:T(8,128)S(1)}, f32[14,2,8,128]{3,2,0,1:T(8,128)S(1)}, u32[]{:S(2)}, u32[]{:S(2)}) collective-permute-start(f32[14,2,8,128]{3,2,0,1:T(8,128)S(1)} %copy.39), channel_id=1, source_target_pairs={{0,8},{8,16},{16,24},{24,32},{32,40},{40,48},{48,56},{56,64},{64,7... | collective-permute-start | bytes 344072 | tf_op jit(solution)/shard_map/ppermute | solution.py:28
  5.4 2.1 %collective-permute-start.1 = (f32[14,2,8,128]{3,2,0,1:T(8,128)S(1)}, f32[14,2,8,128]{3,2,0,1:T(8,128)S(1)}, u32[]{:S(2)}, u32[]{:S(2)}) collective-permute-start(f32[14,2,8,128]{3,2,0,1:T(8,128)S(1)} %copy.40), channel_id=1, source_target_pairs={{8,0},{16,8},{24,16},{32,24},{40,32},{48,40},{56,48},{64,56},{72,6... | collective-permute-start | bytes 344072 | tf_op jit(solution)/shard_map/ppermute | solution.py:31
  7.5 0.9 fusion.107
  8.4 2.7 %collective-permute-start.5 = (f32[3,5,8,128]{3,2,1,0:T(8,128)S(1)}, f32[3,5,8,128]{3,2,1,0:T(8,128)S(1)}, u32[]{:S(2)}, u32[]{:S(2)}) collective-permute-start(f32[3,5,8,128]{3,2,1,0:T(8,128)S(1)} %get-tuple-element.38), channel_id=1, source_target_pairs={{8,0},{16,8},{24,16},{32,24},{40,32},{48,40},{56,48},{64,56},{72,6... | collective-permute-start | bytes 184328 | tf_op jit(solution)/shard_map/ppermute | solution.py:31
  11.2 5.2 %collective-permute-start.4 = (f32[3,5,8,128]{3,2,1,0:T(8,128)S(1)}, f32[3,5,8,128]{3,2,1,0:T(8,128)S(1)}, u32[]{:S(2)}, u32[]{:S(2)}) collective-permute-start(f32[3,5,8,128]{3,2,1,0:T(8,128)S(1)} %get-tuple-element.37), channel_id=1, source_target_pairs={{0,8},{8,16},{16,24},{24,32},{32,40},{40,48},{48,56},{56,64},{64,7... | collective-permute-start | bytes 184328 | tf_op jit(solution)/shard_map/ppermute | solution.py:28
  16.4 0.9 slice.402
  18.1 0.9 slice_bitcast_fusion
  21.5 1.2 %reduce-window.6 = s32[4,16,128]{2,1,0:T(8,128)S(1)} reduce-window(s32[4,16,128]{2,1,0:T(8,128)S(1)} %fusion.103, s32[]{:T(128)} %constant.41.clone.1), window={size=1x1x128 pad=0_0x0_0x127_0}, to_apply=%region_2.3 | reduce-window | flops 1040384 | bytes 65540 | tf_op jit(solution)/shard_map/reduce-window
  23.3 2.5 %multiply_reduce_fusion = f32[2048,5]{0,1:T(8,128)S(1)} fusion(f32[2048,128]{0,1:T(8,128)S(1)} %fusion.13, s32[2048]{0:T(1024)S(1)} %get-tuple-element.64, f32[8,8,5,128]{3,2,1,0:T(8,128)S(1)} %bitcast.117), kind=kOutput, calls=%fused_computation | convolution fusion | flops 1009375232 | bytes 1261568 | tf_op jit(solution)/shard_map/dot_general | solution.py:399
  25.9 1.4 %collective-permute-start.7 = (f32[3,18,5,128]{3,2,1,0:T(8,128)S(1)}, f32[3,18,5,128]{3,2,1,0:T(8,128)S(1)}, u32[]{:S(2)}, u32[]{:S(2)}) collective-permute-start(f32[3,18,5,128]{3,2,1,0:T(8,128)S(1)} %get-tuple-element.42), channel_id=1, source_target_pairs={{1,0},{2,1},{3,2},{4,3},{5,4},{6,5},{7,6},{0,7},{9,8},{10,9},{11,1... | collective-permute-start | bytes 414728 | tf_op jit(solution)/shard_map/ppermute | solution.py:31
  27.6 3.0 %collective-permute-start.3 = (f32[14,12,2,128]{3,2,0,1:T(2,128)S(1)}, f32[14,12,2,128]{3,2,0,1:T(2,128)S(1)}, u32[]{:S(2)}, u32[]{:S(2)}) collective-permute-start(f32[14,12,2,128]{3,2,0,1:T(2,128)S(1)} %get-tuple-element.31), channel_id=1, source_target_pairs={{1,0},{2,1},{3,2},{4,3},{5,4},{6,5},{7,6},{0,7},{9,8},{10,9},{11,1... | collective-permute-start | bytes 516104 | tf_op jit(solution)/shard_map/ppermute | solution.py:31
  30.8 3.1 %collective-permute-done.6 = f32[3,18,5,128]{3,2,1,0:T(8,128)S(1)} collective-permute-done((f32[3,18,5,128]{3,2,1,0:T(8,128)S(1)}, f32[3,18,5,128]{3,2,1,0:T(8,128)S(1)}, u32[]{:S(2)}, u32[]{:S(2)}) %collective-permute-start.6) | collective-permute-done | bytes 138272 | tf_op jit(solution)/shard_map/ppermute | solution.py:28
  36.3 27.8 %shard_map.93 = f32[8,128]{1,0:T(8,128)} custom-call(f32[192,128]{1,0:T(8,128)} %bitcast.116, f32[64,128]{1,0:T(8,128)} %slice_bitcast_fusion.3.refs_1_, f32[64,128]{1,0:T(8,128)} %get-tuple-element.71.refs_2_, f32[64,128]{1,0:T(8,128)} %get-tuple-element.53.refs_3_, f32[64,128]{1,0:T(8,128)} %get-tuple-element.54.refs_4_, f32[64,128]{1,0:T(8,128)} %get-tuple-element.52.refs_5_), custom_call_target="tpu_custom_call" | custom-call | tf_op jit(solution)/shard_map/pallas_call | solution.py:291
  64.1 1.5 %fusion.111 = (f32[1,1]{1,0:T(1,128)}, f32[1,1]{1,0:T(1,128)}, f32[1,1]{1,0:T(1,128)}, f32[1,1]{1,0:T(1,128)}, f32[1,1]{1,0:T(1,128)}) fusion(f32[8,128]{1,0:T(8,128)} %shard_map.93), kind=kLoop, calls=%fused_computation.225 | loop fusion | bytes 40 | tf_op jit(solution)/shard_map/slice | solution.py:303
  66.3 2.8 %fusion.49 = f32[10,10,130]{2,1,0:T(8,128)S(1)} fusion(f32[10,10,128]{2,1,0:T(8,128)S(1)} %get-tuple-element.50, f32[10,10,128]{2,1,0:T(8,128)S(1)} %get-tuple-element.51, f32[10,10,128]{2,1,0:T(8,128)S(1)} %get-tuple-element.49, f32[10,10,128]{2,1,0:T(8,128)S(1)} %slice.577, f32[]{:T(128)} %bitcast.31, f32[]{:T(128)} %bitcast.30, f32[]{:T(128)} %bitcast.29, ...), kind=kLoop, calls=%fused_computation.89 | loop fusion | flops 91000 | bytes 256816 | tf_op jit(solution)/shard_map/add | solution.py:360
  71.0 2.9 %collective-permute-start.10 = (f32[8,64]{1,0:T(8,128)S(1)}, f32[8,64]{1,0:T(8,128)S(1)}, u32[]{:S(2)}, u32[]{:S(2)}) collective-permute-start(f32[8,64]{1,0:T(8,128)S(1)} %get-tuple-element.57), channel_id=1, source_target_pairs={{0,7},{1,0},{2,1},{3,2},{4,3},{5,4},{6,5},{7,6},{8,15},{9,8},{10,9... | collective-permute-start | bytes 6152 | tf_op jit(solution)/shard_map/ppermute | solution.py:44
  74.0 5.6 %collective-permute-start.9 = (f32[8,64]{1,0:T(8,128)S(1)}, f32[8,64]{1,0:T(8,128)S(1)}, u32[]{:S(2)}, u32[]{:S(2)}) collective-permute-start(f32[8,64]{1,0:T(8,128)S(1)} %get-tuple-element.58), channel_id=1, source_target_pairs={{0,8},{8,16},{16,24},{24,32},{32,40},{40,48},{48,56},{56,64},{64,7... | collective-permute-start | bytes 6152 | tf_op jit(solution)/shard_map/ppermute | solution.py:39
  79.6 2.1 %collective-permute-start.8 = (f32[8,64]{1,0:T(8,128)S(1)}, f32[8,64]{1,0:T(8,128)S(1)}, u32[]{:S(2)}, u32[]{:S(2)}) collective-permute-start(f32[8,64]{1,0:T(8,128)S(1)} %get-tuple-element.55), channel_id=1, source_target_pairs={{8,0},{16,8},{24,16},{32,24},{40,32},{48,40},{56,48},{64,56},{72,6... | collective-permute-start | bytes 6152 | tf_op jit(solution)/shard_map/ppermute | solution.py:39
  82.4 4.8 %collective-permute-done.8 = f32[8,64]{1,0:T(8,128)S(1)} collective-permute-done((f32[8,64]{1,0:T(8,128)S(1)}, f32[8,64]{1,0:T(8,128)S(1)}, u32[]{:S(2)}, u32[]{:S(2)}) %collective-permute-start.8) | collective-permute-done | bytes 2080 | tf_op jit(solution)/shard_map/ppermute | solution.py:39
  88.2 1.2 %slice_reduce_fusion = (f32[14,12,12]{2,0,1:T(8,128)S(1)}, f32[14,12,12]{2,0,1:T(8,128)S(1)}) fusion(f32[14,12,12,128]{3,2,0,1:T(8,128)S(1)} %maximum_select_fusion), kind=kLoop, calls=%fused_computation.10 | loop fusion | bytes 32256 | tf_op jit(solution)/shard_map/jit(_pad)/slice | solution.py:73
  90.2 1.1 %pad_maximum_fusion = f32[14,12,12,132]{3,2,0,1:T(8,128)S(1)} fusion(f32[14,12,12,2]{3,2,0,1:T(8,128)S(1)} %reshape.258, f32[14,12,12,128]{3,2,0,1:T(8,128)S(1)} %maximum_select_fusion, f32[14,12,12,2]{3,2,0,1:T(8,128)S(1)} %reshape.257), kind=kLoop, calls=%fused_computation.1 | loop fusion | flops 532224 | bytes 2128896 | tf_op jit(solution)/shard_map/jit(_pad)/concatenate | solution.py:73
  92.7 1.4 %fusion.22 = f32[10,8,8,128]{3,2,0,1:T(8,128)S(1)} fusion(f32[14,12,12,128]{3,2,0,1:T(8,128)S(1)} %maximum_select_fusion, f32[14,12,12,2]{3,2,0,1:T(8,128)S(1)} %reshape.257, f32[14,12,12,2]{3,2,0,1:T(8,128)S(1)} %reshape.258, f32[10,12,12,132]{3,2,0,1:T(8,128)S(1)} %get-tuple-element.29, f32[10,12,12,132]{3,2,0,1:T(8,128)S(1)} %get-tuple-element.28, ...), kind=kLoop, calls=%fused_computation.30 | loop fusion | flops 4259840 | bytes 10224132 | tf_op jit(solution)/shard_map/add | solution.py:103
  94.1 1.3 %slice_add_fusion.12 = f32[2,8,8,128]{3,2,0,1:T(8,128)S(1)} fusion(f32[10,8,8,128]{3,2,0,1:T(8,128)S(1)} %fusion.22, f32[8,8,128]{2,1,0:T(8,128)S(1)} %slice_bitcast_fusion.4, f32[2048,128]{0,1:T(8,128)S(1)} %fusion.13, f32[2048,2]{0,1:T(2,128)S(1)} %maximum_bitcast_fusion.4, s32[8,8]{1,0:T(8,128)S(1)} %multiply_add_fusion.2, s32[2048]{0:T(1024)S(1)} %get-tuple-element.64), kind=kOutput, calls=%fused_computation.128 | convolution fusion | flops 403341312 | bytes 1237248 | tf_op jit(solution)/shard_map/dot_general | solution.py:403
  (84 shorter events, 12.3 us)
Async XLA Ops:
  0.6 20.8 %copy-start.3 = (s32[2048]{0:T(1024)S(1)}, s32[2048]{0:T(1024)}, u32[]{:S(2)}) copy-start(s32[2048]{0:T(1024)} %param.10) | copy-start | bytes 24580
  1.6 25.7 %collective-permute-start = (f32[14,2,8,128]{3,2,0,1:T(8,128)S(1)}, f32[14,2,8,128]{3,2,0,1:T(8,128)S(1)}, u32[]{:S(2)}, u32[]{:S(2)}) collective-permute-start(f32[14,2,8,128]{3,2,0,1:T(8,128)S(1)} %copy.39), channel_id=1, source_target_pairs={{0,8},{8,16},{16,24},{24,32},{32,40},{40,48},{48,56},{56,64},{64,7... | collective-permute-start | bytes 344072 | tf_op jit(solution)/shard_map/ppermute | solution.py:28
  5.4 22.0 %collective-permute-start.1 = (f32[14,2,8,128]{3,2,0,1:T(8,128)S(1)}, f32[14,2,8,128]{3,2,0,1:T(8,128)S(1)}, u32[]{:S(2)}, u32[]{:S(2)}) collective-permute-start(f32[14,2,8,128]{3,2,0,1:T(8,128)S(1)} %copy.40), channel_id=1, source_target_pairs={{8,0},{16,8},{24,16},{32,24},{40,32},{48,40},{56,48},{64,56},{72,6... | collective-permute-start | bytes 344072 | tf_op jit(solution)/shard_map/ppermute | solution.py:31
  8.4 17.4 %collective-permute-start.5 = (f32[3,5,8,128]{3,2,1,0:T(8,128)S(1)}, f32[3,5,8,128]{3,2,1,0:T(8,128)S(1)}, u32[]{:S(2)}, u32[]{:S(2)}) collective-permute-start(f32[3,5,8,128]{3,2,1,0:T(8,128)S(1)} %get-tuple-element.38), channel_id=1, source_target_pairs={{8,0},{16,8},{24,16},{32,24},{40,32},{48,40},{56,48},{64,56},{72,6... | collective-permute-start | bytes 184328 | tf_op jit(solution)/shard_map/ppermute | solution.py:31
  11.2 14.7 %collective-permute-start.4 = (f32[3,5,8,128]{3,2,1,0:T(8,128)S(1)}, f32[3,5,8,128]{3,2,1,0:T(8,128)S(1)}, u32[]{:S(2)}, u32[]{:S(2)}) collective-permute-start(f32[3,5,8,128]{3,2,1,0:T(8,128)S(1)} %get-tuple-element.37), channel_id=1, source_target_pairs={{0,8},{8,16},{16,24},{24,32},{32,40},{40,48},{48,56},{56,64},{64,7... | collective-permute-start | bytes 184328 | tf_op jit(solution)/shard_map/ppermute | solution.py:28
  17.3 16.6 %copy-start.1 = (f32[3,8,8,128]{3,2,1,0:T(8,128)}, f32[3,8,8,128]{3,2,1,0:T(8,128)S(1)}, u32[]{:S(2)}) copy-start(f32[3,8,8,128]{3,2,1,0:T(8,128)S(1)} %slice.402) | copy-start | bytes 294916
  23.3 4.1 %copy-start = (f32[14,8,8,128]{3,2,1,0:T(8,128)S(1)}, f32[14,8,8,128]{3,2,1,0:T(8,128)}, u32[]{:S(2)}) copy-start(f32[14,8,8,128]{3,2,1,0:T(8,128)} %param.6) | copy-start | bytes 1376260
  25.9 4.9 %collective-permute-start.7 = (f32[3,18,5,128]{3,2,1,0:T(8,128)S(1)}, f32[3,18,5,128]{3,2,1,0:T(8,128)S(1)}, u32[]{:S(2)}, u32[]{:S(2)}) collective-permute-start(f32[3,18,5,128]{3,2,1,0:T(8,128)S(1)} %get-tuple-element.42), channel_id=1, source_target_pairs={{1,0},{2,1},{3,2},{4,3},{5,4},{6,5},{7,6},{0,7},{9,8},{10,9},{11,1... | collective-permute-start | bytes 414728 | tf_op jit(solution)/shard_map/ppermute | solution.py:31
  27.4 6.6 %collective-permute-start.6 = (f32[3,18,5,128]{3,2,1,0:T(8,128)S(1)}, f32[3,18,5,128]{3,2,1,0:T(8,128)S(1)}, u32[]{:S(2)}, u32[]{:S(2)}) collective-permute-start(f32[3,18,5,128]{3,2,1,0:T(8,128)S(1)} %get-tuple-element.41), channel_id=1, source_target_pairs={{0,1},{1,2},{2,3},{3,4},{4,5},{5,6},{6,7},{7,0},{8,9},{9,10},{10,1... | collective-permute-start | bytes 414728 | tf_op jit(solution)/shard_map/ppermute | solution.py:28
  27.6 60.3 %collective-permute-start.3 = (f32[14,12,2,128]{3,2,0,1:T(2,128)S(1)}, f32[14,12,2,128]{3,2,0,1:T(2,128)S(1)}, u32[]{:S(2)}, u32[]{:S(2)}) collective-permute-start(f32[14,12,2,128]{3,2,0,1:T(2,128)S(1)} %get-tuple-element.31), channel_id=1, source_target_pairs={{1,0},{2,1},{3,2},{4,3},{5,4},{6,5},{7,6},{0,7},{9,8},{10,9},{11,1... | collective-permute-start | bytes 516104 | tf_op jit(solution)/shard_map/ppermute | solution.py:31
  30.5 57.3 %collective-permute-start.2 = (f32[14,12,2,128]{3,2,0,1:T(2,128)S(1)}, f32[14,12,2,128]{3,2,0,1:T(2,128)S(1)}, u32[]{:S(2)}, u32[]{:S(2)}) collective-permute-start(f32[14,12,2,128]{3,2,0,1:T(2,128)S(1)} %get-tuple-element.30), channel_id=1, source_target_pairs={{0,1},{1,2},{2,3},{3,4},{4,5},{5,6},{6,7},{7,0},{8,9},{9,10},{10,1... | collective-permute-start | bytes 516104 | tf_op jit(solution)/shard_map/ppermute | solution.py:28
  35.1 34.1 %copy-start.2 = (f32[8,2048]{1,0:T(8,128)S(1)}, f32[8,2048]{1,0:T(8,128)}, u32[]{:S(2)}) copy-start(f32[8,2048]{1,0:T(8,128)} %param.8) | copy-start | bytes 196612
  71.0 8.6 %collective-permute-start.11 = (f32[8,64]{1,0:T(8,128)S(1)}, f32[8,64]{1,0:T(8,128)S(1)}, u32[]{:S(2)}, u32[]{:S(2)}) collective-permute-start(f32[8,64]{1,0:T(8,128)S(1)} %get-tuple-element.56), channel_id=1, source_target_pairs={{0,1},{1,2},{2,3},{3,4},{4,5},{5,6},{6,7},{7,0},{8,9},{9,10},{10,1... | collective-permute-start | bytes 6152 | tf_op jit(solution)/shard_map/ppermute | solution.py:44
  71.0 11.4 %collective-permute-start.10 = (f32[8,64]{1,0:T(8,128)S(1)}, f32[8,64]{1,0:T(8,128)S(1)}, u32[]{:S(2)}, u32[]{:S(2)}) collective-permute-start(f32[8,64]{1,0:T(8,128)S(1)} %get-tuple-element.57), channel_id=1, source_target_pairs={{0,7},{1,0},{2,1},{3,2},{4,3},{5,4},{6,5},{7,6},{8,15},{9,8},{10,9... | collective-permute-start | bytes 6152 | tf_op jit(solution)/shard_map/ppermute | solution.py:44
  74.0 8.4 %collective-permute-start.9 = (f32[8,64]{1,0:T(8,128)S(1)}, f32[8,64]{1,0:T(8,128)S(1)}, u32[]{:S(2)}, u32[]{:S(2)}) collective-permute-start(f32[8,64]{1,0:T(8,128)S(1)} %get-tuple-element.58), channel_id=1, source_target_pairs={{0,8},{8,16},{16,24},{24,32},{32,40},{40,48},{48,56},{56,64},{64,7... | collective-permute-start | bytes 6152 | tf_op jit(solution)/shard_map/ppermute | solution.py:39
  79.6 7.6 %collective-permute-start.8 = (f32[8,64]{1,0:T(8,128)S(1)}, f32[8,64]{1,0:T(8,128)S(1)}, u32[]{:S(2)}, u32[]{:S(2)}) collective-permute-start(f32[8,64]{1,0:T(8,128)S(1)} %get-tuple-element.55), channel_id=1, source_target_pairs={{8,0},{16,8},{24,16},{32,24},{40,32},{48,40},{56,48},{64,56},{72,6... | collective-permute-start | bytes 6152 | tf_op jit(solution)/shard_map/ppermute | solution.py:39

commit v7 on v6

--- a/solution.py
+++ b/solution.py
@@ -31,6 +31,37 @@
         high = lax.ppermute(lax.slice_in_dim(block, 0, width, axis=dim), axis, backward)
         block = jnp.concatenate([low, block, high], axis=dim)
     return block
+
+
+def extended_pair(first, first_width, second, second_width):
+    blocks = [first, second]
+    widths = [first_width, second_width]
+    for axis, dim in (("axial", 1), ("azim", 2)):
+        count = lax.axis_size(axis)
+        forward = [(i, (i + 1) % count) for i in range(count)]
+        backward = [(target, source) for source, target in forward]
+        lows = [
+            lax.slice_in_dim(b, b.shape[dim] - w, None, axis=dim) for b, w in zip(blocks, widths)
+        ]
+        highs = [lax.slice_in_dim(b, 0, w, axis=dim) for b, w in zip(blocks, widths)]
+        sizes = [piece.size for piece in lows]
+
+        def pack(pieces):
+            return jnp.concatenate([p.reshape(-1, p.shape[-1]) for p in pieces], axis=0)
+
+        def unpack(packed, like):
+            rows = [s // like[0].shape[-1] for s in sizes]
+            return [
+                packed[sum(rows[:k]) : sum(rows[: k + 1])].reshape(like[k].shape)
+                for k in range(len(like))
+            ]
+
+        got_low = unpack(lax.ppermute(pack(lows), axis, forward), lows)
+        got_high = unpack(lax.ppermute(pack(highs), axis, backward), highs)
+        blocks = [
+            jnp.concatenate([lo, b, hi], axis=dim) for lo, b, hi in zip(got_low, blocks, got_high)
+        ]
+    return blocks
 
 
 def shifted_2(shard, axis, by):
@@ -371,13 +402,12 @@
 
 def on_device(state, diff_coef, parcel_state, parcel_cell, parcel_dest, live_count):
     velocity = state[1:4]
-    whole_pad = extended(state, (("axial", 1), ("azim", 2)), 2)
+    whole_pad, wide_velocity = extended_pair(state, 2, velocity, ITERS + 1)
     whole_pad = radial_pad(clear_ends(whole_pad, 2, 1), 2, "edge")
     moving = whole_pad[1:]
     density_pad = whole_pad[0]
     density_rim = 2
     vel_pad = moving[0:3]
-    wide_velocity = extended(velocity, (("axial", 1), ("azim", 2)), ITERS + 1)
     wide_velocity = radial_pad(clear_ends(wide_velocity, ITERS + 1, 1), 1, "edge")
     padded_pressure, fastest = solve_pressure(wide_velocity, velocity)
     step_size = CFL / (fastest + 1e-06)

time: 96.9 us -> 107 us (1.10)
  other arithmetic: 13.7 us -> 26 us
  starting transfers between devices: 28.9 us -> 20.3 us
  local copies, waits for them, and re-layouts: 10.3 us -> 15.2 us
  matrix products: 4.66 us -> 5.85 us
    ppermute x8 -> x4, starting transfers between devices: 18.2 us -> 9.88 us  [the longest x2 5.23 us: extended_pair(): got_low = unpack(lax.ppermute(pack(lows), axis, forward), lows)]
    ppermute x8 -> x4, waiting for transfers between devices: 3.4 us -> 6.31 us  [the longest x2 3.17 us: extended_pair(): got_low = unpack(lax.ppermute(pack(lows), axis, forward), lows)]
    unnamed x13 -> x61, local copies, waits for them, and re-layouts: 0.83 us -> 2.91 us
    ppermute x2, waiting for transfers between devices: 4.85 us -> 2.87 us  [shifted_2(): return lax.ppermute(shard, axis, pairs)]
    mul x1, other arithmetic: 0.86 us -> 2.64 us  [transport(): carried = vel_pad[direction] * scalar_pad]
    mul x2, other arithmetic: 0.13 us -> 1.9 us  [evaporate(): sources = jnp.stack([heat_source * alive_mask, lost_mass * alive_mask])]
    concatenate x1, other arithmetic: 1.13 us -> 2.65 us  [radial_pad(): jnp.pad(values, [(0, 0)] * (values.ndim - 1) + [(rim_width, rim_width)],...]
    reshape x0 -> x4, local copies, waits for them, and re-layouts: none -> 1.47 us  [the longest x2 1.43 us: unpack(): packed[sum(rows[:k]):sum(rows[:k + 1])].reshape(like[k].shape)]
  transfers between devices with their start and end apart: 12 -> 8, of which waited for: 3 -> 3; matrix products, arithmetic and copies ran while one was open for 20% -> 13% of each run, Pallas kernels for 29% -> 0%
where the time goes in v7:
time: 107 us
  Pallas kernels  27.3 us (26%)
  other arithmetic  26 us (24%)
  starting transfers between devices  20.3 us (19%)
  local copies, waits for them, and re-layouts  15.2 us (14%)
  waiting for transfers between devices  9.18 us (9%)
  matrix products  5.85 us (5%)
  between operations  2.67 us (2%)
    pallas_call x1, Pallas kernels, pressure_coefficients(): pl.pallas_call(lambda *refs: reduce_kernel(groups, shift, half_width, *re...  27.3 us
    ppermute x2, starting transfers between devices, shifted_2(): return lax.ppermute(shard, axis, pairs)  7.42 us
    ppermute x2, starting transfers between devices, extended_pair(): got_low = unpack(lax.ppermute(pack(lows), axis, forward), lows)  5.23 us
    ppermute x2, starting transfers between devices, extended_pair(): got_high = unpack(lax.ppermute(pack(highs), axis, backward), highs)  4.64 us
    ppermute x2, waiting for transfers between devices, extended_pair(): got_low = unpack(lax.ppermute(pack(lows), axis, forward), lows)  3.17 us
    ppermute x2, waiting for transfers between devices, extended_pair(): got_high = unpack(lax.ppermute(pack(highs), axis, backward), highs)  3.14 us
    dot_general x1, matrix products, on_device(): jnp.dot(plane_hot, gas_table, precision=HIGHEST)  3.05 us
    ppermute x2, starting transfers between devices, shifted_3(): lax.ppermute(shard, axis, [(i, (i + by) % length) for i in range(length)])  2.96 us
  transfers between devices with their start and end apart: 8, of which 3 were waited for; matrix products, arithmetic and copies ran while one was open for 13% of the time, Pallas kernels for 0%

profile of v7, /device:TPU:6, one launch (start us, length us, event | category | flops | bytes accessed | tf_op | source)
XLA Modules:
  0.0 106.5 jit_solution(1361515460474552532)
XLA Ops:
  2.6 2.7 %collective-permute-start.1 = (f32[344,128]{1,0:T(8,128)S(1)}, f32[344,128]{1,0:T(8,128)S(1)}, u32[]{:S(2)}, u32[]{:S(2)}) collective-permute-start(f32[344,128]{1,0:T(8,128)S(1)} %pad_maximum_fusion.9), channel_id=1, source_target_pairs={{8,0},{16,8},{24,16},{32,24},{40,32},{48,40},{56,48},{64,56},{72,6... | collective-permute-start | bytes 528392 | tf_op jit(solution)/shard_map/ppermute | solution.py:60
  5.4 5.2 %collective-permute-start = (f32[344,128]{1,0:T(8,128)S(1)}, f32[344,128]{1,0:T(8,128)S(1)}, u32[]{:S(2)}, u32[]{:S(2)}) collective-permute-start(f32[344,128]{1,0:T(8,128)S(1)} %pad_maximum_fusion.8), channel_id=1, source_target_pairs={{0,8},{8,16},{16,24},{24,32},{32,40},{40,48},{48,56},{56,64},{64,7... | collective-permute-start | bytes 528392 | tf_op jit(solution)/shard_map/ppermute | solution.py:59
  15.9 1.2 %reduce-window.6 = s32[4,16,128]{2,1,0:T(8,128)S(1)} reduce-window(s32[4,16,128]{2,1,0:T(8,128)S(1)} %fusion.102, s32[]{:T(128)} %constant.41.clone.1), window={size=1x1x128 pad=0_0x0_0x127_0}, to_apply=%region_2.3 | reduce-window | flops 1040384 | bytes 65540 | tf_op jit(solution)/shard_map/reduce-window
  18.2 3.0 %multiply_reduce_fusion = f32[2048,5]{0,1:T(8,128)} fusion(f32[2048,128]{0,1:T(8,128)S(1)} %fusion.16, s32[2048]{0:T(1024)S(1)} %get-tuple-element.64, f32[8,8,5,128]{3,2,1,0:T(8,128)S(1)} %bitcast.141), kind=kOutput, calls=%fused_computation | convolution fusion | flops 1009375232 | bytes 1261568 | tf_op jit(solution)/shard_map/dot_general | solution.py:429
  22.2 1.9 %collective-permute-start.3 = (f32[606,128]{1,0:T(8,128)S(1)}, f32[606,128]{1,0:T(8,128)S(1)}, u32[]{:S(2)}, u32[]{:S(2)}) collective-permute-start(f32[606,128]{1,0:T(8,128)S(1)} %pad_maximum_fusion.6), channel_id=1, source_target_pairs={{1,0},{2,1},{3,2},{4,3},{5,4},{6,5},{7,6},{0,7},{9,8},{10,9},{11,1... | collective-permute-start | bytes 930824 | tf_op jit(solution)/shard_map/ppermute | solution.py:60
  25.4 3.1 %collective-permute-done.3 = f32[606,128]{1,0:T(8,128)S(1)} collective-permute-done((f32[606,128]{1,0:T(8,128)S(1)}, f32[606,128]{1,0:T(8,128)S(1)}, u32[]{:S(2)}, u32[]{:S(2)}) %collective-permute-start.3) | collective-permute-done | bytes 310304 | tf_op jit(solution)/shard_map/ppermute | solution.py:60
  28.5 3.2 %collective-permute-done.2 = f32[606,128]{1,0:T(8,128)S(1)} collective-permute-done((f32[606,128]{1,0:T(8,128)S(1)}, f32[606,128]{1,0:T(8,128)S(1)}, u32[]{:S(2)}, u32[]{:S(2)}) %collective-permute-start.2) | collective-permute-done | bytes 310304 | tf_op jit(solution)/shard_map/ppermute | solution.py:59
  32.7 1.2 %slice_reduce_fusion = (f32[14,12,12]{2,0,1:T(8,128)S(1)}, f32[14,12,12]{2,0,1:T(8,128)S(1)}) fusion(f32[14,12,12,128]{3,2,0,1:T(8,128)S(1)} %copy_select_fusion), kind=kLoop, calls=%fused_computation.10 | loop fusion | bytes 32256 | tf_op jit(solution)/shard_map/jit(_pad)/slice | solution.py:104
  34.8 2.7 %pad_maximum_fusion = f32[14,12,12,132]{3,2,0,1:T(8,128)} fusion(f32[14,12,12,2]{3,2,0,1:T(8,128)S(1)} %reshape.322, f32[14,12,12,128]{3,2,0,1:T(8,128)S(1)} %copy_select_fusion, f32[14,12,12,2]{3,2,0,1:T(8,128)S(1)} %reshape.321), kind=kLoop, calls=%fused_computation.1 | loop fusion | flops 532224 | bytes 2128896 | tf_op jit(solution)/shard_map/jit(_pad)/concatenate | solution.py:104
  37.4 1.3 %maximum_bitcast_fusion.2 = (f32[12,12,132]{2,1,0:T(8,128)}, f32[12,12,132]{2,1,0:T(8,128)}, f32[12,12,132]{2,1,0:T(8,128)}, f32[12,12,132]{2,1,0:T(8,128)}) fusion(f32[14,12,12,2]{3,2,0,1:T(8,128)S(1)} %reshape.322, f32[14,12,12,128]{3,2,0,1:T(8,128)S(1)} %copy_select_fusion, f32[14,12,12,2]{3,2,0,1:T(8,128)S(1)} %reshape.321), kind=kLoop, calls=%fused_computation.91 | loop fusion | flops 152064 | bytes 1368576 | tf_op jit(solution)/shard_map/squeeze | solution.py:408
  41.0 1.2 %maximum_select_fusion = f32[3,18,18,128]{3,2,1,0:T(8,128)S(1)} fusion(f32[3,18,5,128]{3,2,1,0:T(8,128)} %reshape.315, f32[3,5,8,128]{3,2,1,0:T(8,128)S(1)} %bitcast.136, f32[3,8,8,128]{3,2,1,0:T(8,128)S(1)} %slice.429, f32[3,5,8,128]{3,2,1,0:T(8,128)} %bitcast.138, f32[3,18,5,128]{3,2,1,0:T(8,128)} %reshape.314, pred[18]{0:T(512)(128)(4,1)S(1)} %and_or_fusion), kind=kLoop, calls=%fused_computation.22 | loop fusion | flops 622080 | bytes 995346 | tf_op jit(solution)/shard_map/jit(_where)/select_n | solution.py:100
  46.5 27.3 %shard_map.93 = f32[8,128]{1,0:T(8,128)} custom-call(f32[192,128]{1,0:T(8,128)} %bitcast.126, f32[64,128]{1,0:T(8,128)} %slice_bitcast_fusion.3.refs_1_, f32[64,128]{1,0:T(8,128)} %get-tuple-element.71.refs_2_, f32[64,128]{1,0:T(8,128)} %get-tuple-element.53.refs_3_, f32[64,128]{1,0:T(8,128)} %get-tuple-element.54.refs_4_, f32[64,128]{1,0:T(8,128)} %get-tuple-element.52.refs_5_), custom_call_target="tpu_custom_call" | custom-call | tf_op jit(solution)/shard_map/pallas_call | solution.py:322
  73.8 1.5 %fusion.109 = (f32[1,1]{1,0:T(1,128)}, f32[1,1]{1,0:T(1,128)}, f32[1,1]{1,0:T(1,128)}, f32[1,1]{1,0:T(1,128)}, f32[1,1]{1,0:T(1,128)}) fusion(f32[8,128]{1,0:T(8,128)} %shard_map.93), kind=kLoop, calls=%fused_computation.229 | loop fusion | bytes 40 | tf_op jit(solution)/shard_map/slice | solution.py:334
  76.0 2.6 %slice_multiply_fusion.2 = (f32[10,12,12,132]{3,2,0,1:T(8,128)S(1)}, f32[10,12,12,132]{3,2,0,1:T(8,128)S(1)}, f32[10,12,12,132]{3,2,0,1:T(8,128)S(1)}) fusion(f32[14,12,12,132]{3,2,0,1:T(8,128)} %pad_maximum_fusion, f32[12,12,132]{2,1,0:T(8,128)} %get-tuple-element.26, f32[12,12,132]{2,1,0:T(8,128)} %get-tuple-element.25, f32[12,12,132]{2,1,0:T(8,128)S(1)} %copy-done.9), kind=kLoop, calls=%fused_computation.9 | loop fusion | flops 570240 | bytes 3269376 | tf_op jit(solution)/shard_map/mul | solution.py:114
  78.8 1.4 %fusion.25 = f32[10,8,8,128]{3,2,0,1:T(8,128)S(1)} fusion(f32[14,12,12,128]{3,2,0,1:T(8,128)S(1)} %copy_select_fusion, f32[14,12,12,2]{3,2,0,1:T(8,128)S(1)} %reshape.321, f32[14,12,12,2]{3,2,0,1:T(8,128)S(1)} %copy-done.1, f32[10,12,12,132]{3,2,0,1:T(8,128)S(1)} %get-tuple-element.29, f32[10,12,12,132]{3,2,0,1:T(8,128)S(1)} %get-tuple-element.28, ...), kind=kLoop, calls=%fused_computation.32 | loop fusion | flops 4259840 | bytes 10224132 | tf_op jit(solution)/shard_map/add | solution.py:134
  80.9 2.9 %fusion.52 = f32[10,10,130]{2,1,0:T(8,128)S(1)} fusion(f32[10,10,128]{2,1,0:T(8,128)S(1)} %get-tuple-element.50, f32[10,10,128]{2,1,0:T(8,128)S(1)} %copy-done.14, f32[10,10,128]{2,1,0:T(8,128)S(1)} %copy-done.13, f32[10,10,128]{2,1,0:T(8,128)S(1)} %copy-done.12, f32[]{:T(128)} %bitcast.43, f32[]{:T(128)} %bitcast.42, f32[]{:T(128)} %bitcast.41, f32[]{:T(128)} %bitcast.40), kind=kLoop, calls=%fused_computation.98 | loop fusion | flops 91000 | bytes 256816 | tf_op jit(solution)/shard_map/add | solution.py:391
  85.0 1.0 compare_select_fusion.2
  86.9 1.3 %broadcast_select_fusion = f32[8,2048]{1,0:T(8,128)} fusion(pred[2048]{0:T(1024)(128)(4,1)} %get-tuple-element.61, f32[2048]{0:T(1024)S(1)} %get-tuple-element.72, f32[3,2048]{1,0:T(4,128)S(1)} %get-tuple-element.18, f32[3,2048]{1,0:T(4,128)S(1)} %get-tuple-element.19, f32[1,2048]{1,0:T(1,128)S(1)} %get-tuple-element.21, f32[1,2048]{1,0:T(1,128)S(1)} %get-tuple-element.22), kind=kLoop, calls=%fused_computation.175 | loop fusion | flops 81920 | bytes 141312 | tf_op jit(solution)/shard_map/jit(_where)/select_n | solution.py:455
  88.2 1.5 %fusion.3 = f32[8,256]{1,0:T(8,128)S(1)} fusion(s32[2048]{0:T(1024)} %bitcast_select_fusion, f32[3,2048]{1,0:T(4,128)S(1)} %get-tuple-element.18, f32[3,2048]{1,0:T(4,128)S(1)} %get-tuple-element.19, f32[1,2048]{1,0:T(1,128)S(1)} %get-tuple-element.21, f32[1,2048]{1,0:T(1,128)S(1)} %get-tuple-element.22, f32[2048]{0:T(1024)S(1)} %get-tuple-element.72), kind=kOutput, calls=%fused_computation.6 | convolution fusion | flops 50921472 | bytes 90112 | tf_op jit(solution)/shard_map/dot_general | solution.py:445
  89.8 2.9 %collective-permute-start.6 = (f32[8,64]{1,0:T(8,128)S(1)}, f32[8,64]{1,0:T(8,128)S(1)}, u32[]{:S(2)}, u32[]{:S(2)}) collective-permute-start(f32[8,64]{1,0:T(8,128)S(1)} %get-tuple-element.57), channel_id=1, source_target_pairs={{0,7},{1,0},{2,1},{3,2},{4,3},{5,4},{6,5},{7,6},{8,15},{9,8},{10,9... | collective-permute-start | bytes 6152 | tf_op jit(solution)/shard_map/ppermute | solution.py:75
  92.8 5.5 %collective-permute-start.5 = (f32[8,64]{1,0:T(8,128)S(1)}, f32[8,64]{1,0:T(8,128)S(1)}, u32[]{:S(2)}, u32[]{:S(2)}) collective-permute-start(f32[8,64]{1,0:T(8,128)S(1)} %get-tuple-element.58), channel_id=1, source_target_pairs={{0,8},{8,16},{16,24},{24,32},{32,40},{40,48},{48,56},{56,64},{64,7... | collective-permute-start | bytes 6152 | tf_op jit(solution)/shard_map/ppermute | solution.py:70
  98.3 1.9 %collective-permute-start.4 = (f32[8,64]{1,0:T(8,128)S(1)}, f32[8,64]{1,0:T(8,128)S(1)}, u32[]{:S(2)}, u32[]{:S(2)}) collective-permute-start(f32[8,64]{1,0:T(8,128)S(1)} %get-tuple-element.55), channel_id=1, source_target_pairs={{8,0},{16,8},{24,16},{32,24},{40,32},{48,40},{56,48},{64,56},{72,6... | collective-permute-start | bytes 6152 | tf_op jit(solution)/shard_map/ppermute | solution.py:70
  100.3 1.3 %fusion.10 = f32[2,8,8,128]{3,2,0,1:T(8,128)S(1)} fusion(f32[2048,128]{0,1:T(8,128)S(1)} %copy-done.4, f32[2048,2]{0,1:T(2,128)S(1)} %maximum_bitcast_fusion.4, s32[8,8]{1,0:T(8,128)S(1)} %copy-done.23, s32[2048]{0:T(1024)S(1)} %get-tuple-element.64, f32[10,8,8,128]{3,2,0,1:T(8,128)S(1)} %copy-done.7, f32[8,8,128]{2,1,0:T(8,128)S(1)} %copy-done.22), kind=kOutput, calls=%fused_computation.16 | convolution fusion | flops 403341312 | bytes 1237248 | tf_op jit(solution)/shard_map/dot_general | solution.py:433
  103.0 2.9 %collective-permute-done.4 = f32[8,64]{1,0:T(8,128)S(1)} collective-permute-done((f32[8,64]{1,0:T(8,128)S(1)}, f32[8,64]{1,0:T(8,128)S(1)}, u32[]{:S(2)}, u32[]{:S(2)}) %collective-permute-start.4) | collective-permute-done | bytes 2080 | tf_op jit(solution)/shard_map/ppermute | solution.py:70
  (141 shorter events, 23.0 us)
Async XLA Ops:
  0.6 12.4 %copy-start.29 = (f32[10]{0:T(128)S(1)}, f32[10]{0:T(128)}, u32[]{:S(2)}) copy-start(f32[10]{0:T(128)} %param.7) | copy-start | bytes 124
  0.6 13.6 %copy-start.24 = (s32[2048]{0:T(1024)S(1)}, s32[2048]{0:T(1024)}, u32[]{:S(2)}) copy-start(s32[2048]{0:T(1024)} %param.9) | copy-start | bytes 24580
  0.7 14.5 %copy-start.25 = (s32[2048]{0:T(1024)S(1)}, s32[2048]{0:T(1024)}, u32[]{:S(2)}) copy-start(s32[2048]{0:T(1024)} %param.10) | copy-start | bytes 24580
  2.6 18.7 %collective-permute-start.1 = (f32[344,128]{1,0:T(8,128)S(1)}, f32[344,128]{1,0:T(8,128)S(1)}, u32[]{:S(2)}, u32[]{:S(2)}) collective-permute-start(f32[344,128]{1,0:T(8,128)S(1)} %pad_maximum_fusion.9), channel_id=1, source_target_pairs={{8,0},{16,8},{24,16},{32,24},{40,32},{48,40},{56,48},{64,56},{72,6... | collective-permute-start | bytes 528392 | tf_op jit(solution)/shard_map/ppermute | solution.py:60
  5.4 15.9 %collective-permute-start = (f32[344,128]{1,0:T(8,128)S(1)}, f32[344,128]{1,0:T(8,128)S(1)}, u32[]{:S(2)}, u32[]{:S(2)}) collective-permute-start(f32[344,128]{1,0:T(8,128)S(1)} %pad_maximum_fusion.8), channel_id=1, source_target_pairs={{0,8},{8,16},{16,24},{24,32},{32,40},{40,48},{48,56},{56,64},{64,7... | collective-permute-start | bytes 528392 | tf_op jit(solution)/shard_map/ppermute | solution.py:59
  11.5 29.6 %copy-start.5 = (f32[3,8,8,128]{3,2,1,0:T(8,128)}, f32[3,8,8,128]{3,2,1,0:T(8,128)S(1)}, u32[]{:S(2)}) copy-start(f32[3,8,8,128]{3,2,1,0:T(8,128)S(1)} %slice.429) | copy-start | bytes 294916
  14.4 7.5 %copy-start.3 = (f32[2048,128]{0,1:T(8,128)}, f32[2048,128]{0,1:T(8,128)S(1)}, u32[]{:S(2)}) copy-start(f32[2048,128]{0,1:T(8,128)S(1)} %fusion.16) | copy-start | bytes 3145732
  18.2 3.8 %copy-start.2 = (f32[14,8,8,128]{3,2,1,0:T(8,128)S(1)}, f32[14,8,8,128]{3,2,1,0:T(8,128)}, u32[]{:S(2)}) copy-start(f32[14,8,8,128]{3,2,1,0:T(8,128)} %param.6) | copy-start | bytes 1376260
  22.2 6.3 %collective-permute-start.3 = (f32[606,128]{1,0:T(8,128)S(1)}, f32[606,128]{1,0:T(8,128)S(1)}, u32[]{:S(2)}, u32[]{:S(2)}) collective-permute-start(f32[606,128]{1,0:T(8,128)S(1)} %pad_maximum_fusion.6), channel_id=1, source_target_pairs={{1,0},{2,1},{3,2},{4,3},{5,4},{6,5},{7,6},{0,7},{9,8},{10,9},{11,1... | collective-permute-start | bytes 930824 | tf_op jit(solution)/shard_map/ppermute | solution.py:60
  24.1 7.5 %collective-permute-start.2 = (f32[606,128]{1,0:T(8,128)S(1)}, f32[606,128]{1,0:T(8,128)S(1)}, u32[]{:S(2)}, u32[]{:S(2)}) collective-permute-start(f32[606,128]{1,0:T(8,128)S(1)} %pad_maximum_fusion.5), channel_id=1, source_target_pairs={{0,1},{1,2},{2,3},{3,4},{4,5},{5,6},{6,7},{7,0},{8,9},{9,10},{10,1... | collective-permute-start | bytes 930824 | tf_op jit(solution)/shard_map/ppermute | solution.py:59
  28.5 5.4 %copy-start.10 = (f32[606,128]{1,0:T(8,128)}, f32[606,128]{1,0:T(8,128)S(1)}, u32[]{:S(2)}) copy-start(f32[606,128]{1,0:T(8,128)S(1)} %collective-permute-done.3) | copy-start | bytes 930820
  42.7 3.1 %copy-start.26 = (pred[8]{0:T(512)(128)(4,1)S(1)}, pred[8]{0:T(512)(128)(4,1)}, u32[]{:S(2)}) copy-start(pred[8]{0:T(512)(128)(4,1)} %compare_and_fusion) | copy-start | bytes 28
  42.7 33.2 %copy-start.9 = (f32[12,12,132]{2,1,0:T(8,128)S(1)}, f32[12,12,132]{2,1,0:T(8,128)}, u32[]{:S(2)}) copy-start(f32[12,12,132]{2,1,0:T(8,128)} %get-tuple-element.24) | copy-start | bytes 228100
  76.0 2.7 %copy-start.1 = (f32[14,12,12,2]{3,2,0,1:T(8,128)S(1)}, f32[14,12,12,2]{3,2,0,1:T(8,128)}, u32[]{:S(2)}) copy-start(f32[14,12,12,2]{3,2,0,1:T(8,128)} %copy-done) | copy-start | bytes 48388
  76.0 2.7 %copy-start.16 = (f32[8,8,128]{2,1,0:T(8,128)S(1)}, f32[8,8,128]{2,1,0:T(8,128)}, u32[]{:S(2)}) copy-start(f32[8,8,128]{2,1,0:T(8,128)} %get-tuple-element.43) | copy-start | bytes 98308
  80.9 19.4 %copy-start.4 = (f32[2048,128]{0,1:T(8,128)S(1)}, f32[2048,128]{0,1:T(8,128)}, u32[]{:S(2)}) copy-start(f32[2048,128]{0,1:T(8,128)} %copy-done.3) | copy-start | bytes 3145732
  80.9 19.4 %copy-start.22 = (f32[8,8,128]{2,1,0:T(8,128)S(1)}, f32[8,8,128]{2,1,0:T(8,128)}, u32[]{:S(2)}) copy-start(f32[8,8,128]{2,1,0:T(8,128)} %slice_bitcast_fusion.4) | copy-start | bytes 98308
  80.9 19.4 %copy-start.23 = (s32[8,8]{1,0:T(8,128)S(1)}, s32[8,8]{1,0:T(8,128)}, u32[]{:S(2)}) copy-start(s32[8,8]{1,0:T(8,128)} %multiply_add_fusion.2) | copy-start | bytes 772
  80.9 19.4 %copy-start.7 = (f32[10,8,8,128]{3,2,0,1:T(8,128)S(1)}, f32[10,8,8,128]{3,2,0,1:T(8,128)}, u32[]{:S(2)}) copy-start(f32[10,8,8,128]{3,2,0,1:T(8,128)} %copy-done.6) | copy-start | bytes 983044
  80.9 20.7 %slice-start = ((f32[10,8,8,128]{3,2,0,1:T(8,128)}), f32[8,8,8,128]{3,2,0,1:T(8,128)S(1)}, s32[]{:S(2)}) async-start(f32[10,8,8,128]{3,2,0,1:T(8,128)} %copy-done.6), calls=%async_computation | async-start | bytes 524288 | tf_op jit(solution)/shard_map/slice | solution.py:436
  89.8 13.2 %collective-permute-start.7 = (f32[8,64]{1,0:T(8,128)S(1)}, f32[8,64]{1,0:T(8,128)S(1)}, u32[]{:S(2)}, u32[]{:S(2)}) collective-permute-start(f32[8,64]{1,0:T(8,128)S(1)} %get-tuple-element.56), channel_id=1, source_target_pairs={{0,1},{1,2},{2,3},{3,4},{4,5},{5,6},{6,7},{7,0},{8,9},{9,10},{10,1... | collective-permute-start | bytes 6152 | tf_op jit(solution)/shard_map/ppermute | solution.py:75
  89.8 13.2 %collective-permute-start.6 = (f32[8,64]{1,0:T(8,128)S(1)}, f32[8,64]{1,0:T(8,128)S(1)}, u32[]{:S(2)}, u32[]{:S(2)}) collective-permute-start(f32[8,64]{1,0:T(8,128)S(1)} %get-tuple-element.57), channel_id=1, source_target_pairs={{0,7},{1,0},{2,1},{3,2},{4,3},{5,4},{6,5},{7,6},{8,15},{9,8},{10,9... | collective-permute-start | bytes 6152 | tf_op jit(solution)/shard_map/ppermute | solution.py:75
  92.8 10.2 %collective-permute-start.5 = (f32[8,64]{1,0:T(8,128)S(1)}, f32[8,64]{1,0:T(8,128)S(1)}, u32[]{:S(2)}, u32[]{:S(2)}) collective-permute-start(f32[8,64]{1,0:T(8,128)S(1)} %get-tuple-element.58), channel_id=1, source_target_pairs={{0,8},{8,16},{16,24},{24,32},{32,40},{40,48},{48,56},{56,64},{64,7... | collective-permute-start | bytes 6152 | tf_op jit(solution)/shard_map/ppermute | solution.py:70
  98.3 7.6 %collective-permute-start.4 = (f32[8,64]{1,0:T(8,128)S(1)}, f32[8,64]{1,0:T(8,128)S(1)}, u32[]{:S(2)}, u32[]{:S(2)}) collective-permute-start(f32[8,64]{1,0:T(8,128)S(1)} %get-tuple-element.55), channel_id=1, source_target_pairs={{8,0},{16,8},{24,16},{32,24},{40,32},{48,40},{56,48},{64,56},{72,6... | collective-permute-start | bytes 6152 | tf_op jit(solution)/shard_map/ppermute | solution.py:70
  (16 other events, 32.9 us)

commit v8 on v6

--- a/solution.py
+++ b/solution.py
@@ -31,6 +31,83 @@
         high = lax.ppermute(lax.slice_in_dim(block, 0, width, axis=dim), axis, backward)
         block = jnp.concatenate([low, block, high], axis=dim)
     return block
+
+
+def exchange_kernel(offsets, *refs):
+    count = len(offsets)
+    sources = refs[:count]
+    outs = refs[count : 2 * count]
+    landing = refs[2 * count : 3 * count]
+    send_sems, recv_sems = refs[3 * count :]
+    axial = lax.axis_index("axial")
+    azim = lax.axis_index("azim")
+
+    def device(step_axial, step_azim):
+        return (
+            (axial + step_axial + lax.axis_size("axial")) % lax.axis_size("axial"),
+            (azim + step_azim + lax.axis_size("azim")) % lax.axis_size("azim"),
+        )
+
+    neighbours = sorted(set(offsets))
+    barrier = pltpu.get_barrier_semaphore()
+    for step in neighbours:
+        pl.semaphore_signal(
+            barrier, inc=1, device_id=device(*step), device_id_type=pl.DeviceIdType.MESH
+        )
+    pl.semaphore_wait(barrier, len(neighbours))
+    copies = []
+    for k, step in enumerate(offsets):
+        copy = pltpu.make_async_remote_copy(
+            src_ref=sources[k],
+            dst_ref=landing[k],
+            send_sem=send_sems.at[k],
+            recv_sem=recv_sems.at[k],
+            device_id=device(*step),
+            device_id_type=pl.DeviceIdType.MESH,
+        )
+        copy.start()
+        copies.append(copy)
+    for k, copy in enumerate(copies):
+        copy.wait()
+        outs[k][...] = landing[k][...]
+
+
+def neighbour_exchange(items):
+    offsets = [step for _, step in items]
+    flat = [a.reshape(-1, a.shape[-1]) for a, _ in items]
+    count = len(flat)
+    outs = pl.pallas_call(
+        lambda *refs: exchange_kernel(offsets, *refs),
+        out_shape=[jax.ShapeDtypeStruct(f.shape, f.dtype) for f in flat],
+        in_specs=[pl.BlockSpec(memory_space=pltpu.VMEM)] * count,
+        out_specs=[pl.BlockSpec(memory_space=pltpu.VMEM)] * count,
+        scratch_shapes=[pltpu.VMEM(f.shape, f.dtype) for f in flat]
+        + [pltpu.SemaphoreType.DMA((count,)), pltpu.SemaphoreType.DMA((count,))],
+        compiler_params=pltpu.CompilerParams(collective_id=1, has_side_effects=True),
+    )(*flat)
+    return [o.reshape(a.shape) for o, (a, _) in zip(outs, items)]
+
+
+def rim_slab(block, width, step_axial, step_azim):
+    def pick(values, dim, step):
+        if step > 0:
+            return lax.slice_in_dim(values, values.shape[dim] - width, None, axis=dim)
+        if step < 0:
+            return lax.slice_in_dim(values, 0, width, axis=dim)
+        return values
+
+    return pick(pick(block, 1, step_axial), 2, step_azim)
+
+
+NEIGHBOURS = [(sa, sz) for sa in (-1, 0, 1) for sz in (-1, 0, 1) if (sa, sz) != (0, 0)]
+
+
+def assemble(block, received):
+    bands = []
+    for pz in (-1, 0, 1):
+        row = [block if (pa, pz) == (0, 0) else received[(pa, pz)] for pa in (-1, 0, 1)]
+        bands.append(jnp.concatenate(row, axis=1))
+    return jnp.concatenate(bands, axis=2)
 
 
 def shifted_2(shard, axis, by):
@@ -371,19 +448,6 @@
 
 def on_device(state, diff_coef, parcel_state, parcel_cell, parcel_dest, live_count):
     velocity = state[1:4]
-    whole_pad = extended(state, (("axial", 1), ("azim", 2)), 2)
-    whole_pad = radial_pad(clear_ends(whole_pad, 2, 1), 2, "edge")
-    moving = whole_pad[1:]
-    density_pad = whole_pad[0]
-    density_rim = 2
-    vel_pad = moving[0:3]
-    wide_velocity = extended(velocity, (("axial", 1), ("azim", 2)), ITERS + 1)
-    wide_velocity = radial_pad(clear_ends(wide_velocity, ITERS + 1, 1), 1, "edge")
-    padded_pressure, fastest = solve_pressure(wide_velocity, velocity)
-    step_size = CFL / (fastest + 1e-06)
-    transported = transport(
-        moving[3:], vel_pad, density_pad, density_rim, diff_coef[:, None, None, None], step_size
-    )
     npar_local = parcel_cell.shape[0]
     cells_x, cells_y, cells_z = (state.shape[1], state.shape[2], state.shape[3])
     plane_count = cells_x * cells_y
@@ -391,13 +455,45 @@
         plane_count, 5 * cells_z
     )
     live_now = live_count[0]
-    alive_mask = (jnp.arange(npar_local) < live_now).astype(jnp.float32)
+    slot_alive = jnp.arange(npar_local) < live_now
+    alive_mask = slot_alive.astype(jnp.float32)
     plane_ids = parcel_cell // cells_z
     radial_ids = parcel_cell % cells_z
     plane_hot = (plane_ids[:, None] == jnp.arange(plane_count)[None, :]).astype(jnp.float32)
     radial_hot = (radial_ids[:, None] == jnp.arange(cells_z)[None, :]).astype(jnp.float32)
     gas_rows = jnp.dot(plane_hot, gas_table, precision=HIGHEST).reshape(npar_local, 5, cells_z)
     gas_values = jnp.sum(gas_rows * radial_hot[:, None, :], axis=2).T
+    stacked = jnp.stack([(parcel_dest == d + 1) & slot_alive for d in range(4)]).astype(jnp.int32)
+    ranks = jnp.cumsum(stacked, axis=1) - 1
+    mover = jnp.sum(stacked, axis=0) > 0
+    target = jnp.where(mover, jnp.sum(stacked * (jnp.arange(4)[:, None] * CAP + ranks), axis=0), -1)
+    select = (target[:, None] == jnp.arange(4 * CAP)[None, :]).astype(jnp.float32)
+    raw = jnp.concatenate([parcel_state, gas_values, alive_mask[None]], axis=0)
+    leaving = jnp.transpose(
+        jnp.dot(raw, select, precision=HIGHEST).reshape(raw.shape[0], 4, CAP), (1, 0, 2)
+    )
+    parcel_steps = [(-1, 0), (1, 0), (0, -1), (0, 1)]
+    items = [(rim_slab(state, 2, sa, sz), (sa, sz)) for sa, sz in NEIGHBOURS]
+    items += [(rim_slab(velocity, ITERS + 1, sa, sz), (sa, sz)) for sa, sz in NEIGHBOURS]
+    items += [(leaving[d], parcel_steps[d]) for d in range(4)]
+    got = neighbour_exchange(items)
+    count = len(NEIGHBOURS)
+    state_rims = {(-sa, -sz): got[k] for k, (sa, sz) in enumerate(NEIGHBOURS)}
+    velocity_rims = {(-sa, -sz): got[count + k] for k, (sa, sz) in enumerate(NEIGHBOURS)}
+    landed = got[2 * count :]
+    whole_pad = assemble(state, state_rims)
+    whole_pad = radial_pad(clear_ends(whole_pad, 2, 1), 2, "edge")
+    moving = whole_pad[1:]
+    density_pad = whole_pad[0]
+    density_rim = 2
+    vel_pad = moving[0:3]
+    wide_velocity = assemble(velocity, velocity_rims)
+    wide_velocity = radial_pad(clear_ends(wide_velocity, ITERS + 1, 1), 1, "edge")
+    padded_pressure, fastest = solve_pressure(wide_velocity, velocity)
+    step_size = CFL / (fastest + 1e-06)
+    transported = transport(
+        moving[3:], vel_pad, density_pad, density_rim, diff_coef[:, None, None, None], step_size
+    )
     updated, sources = evaporate(parcel_state, gas_values, alive_mask, step_size)
     spread = (sources.T[:, :, None] * radial_hot[:, None, :]).reshape(npar_local, 2 * cells_z)
     deposit = lax.dot_general(plane_hot, spread, (((0,), (0,)), ((), ())), precision=HIGHEST)
@@ -405,23 +501,18 @@
     scalars_new = jnp.concatenate(
         [transported[:2] + deposit / state[0][None], transported[2:]], axis=0
     )
-    slot_alive = jnp.arange(npar_local) < live_now
-    stacked = jnp.stack([(parcel_dest == d + 1) & slot_alive for d in range(4)]).astype(jnp.int32)
-    ranks = jnp.cumsum(stacked, axis=1) - 1
-    mover = jnp.sum(stacked, axis=0) > 0
-    target = jnp.where(mover, jnp.sum(stacked * (jnp.arange(4)[:, None] * CAP + ranks), axis=0), -1)
-    select = (target[:, None] == jnp.arange(4 * CAP)[None, :]).astype(jnp.float32)
-    buffers = jnp.transpose(
-        jnp.dot(updated, select, precision=HIGHEST).reshape(updated.shape[0], 4, CAP), (1, 0, 2)
-    )
-    arrived = jnp.stack(
-        [
-            along_axial(buffers[0], -1),
-            along_axial(buffers[1], 1),
-            along_azim(buffers[2], -1),
-            along_azim(buffers[3], 1),
-        ]
-    )
+    at_first = lax.axis_index("axial") == 0
+    at_last = lax.axis_index("axial") == lax.axis_size("axial") - 1
+    arriving = []
+    for d in range(4):
+        payload = landed[d]
+        if d == 0:
+            payload = jnp.where(at_last, jnp.float32(0.0), payload)
+        if d == 1:
+            payload = jnp.where(at_first, jnp.float32(0.0), payload)
+        moved, _ = evaporate(payload[:8], payload[8:13], payload[13], step_size)
+        arriving.append(moved)
+    arrived = jnp.stack(arriving)
     kept_parcels = jnp.where((parcel_dest == 0)[None], updated, jnp.float32(0.0))
     velocity_new = jnp.stack(
         [

time: 96.9 us -> 89.9 us (0.928)
  starting transfers between devices: 28.9 us -> 0 us
  Pallas kernels: 27.8 us -> 47.6 us
  waiting for transfers between devices: 8.26 us -> 0 us
  local copies, waits for them, and re-layouts: 10.3 us -> 18.3 us
  other arithmetic: 13.7 us -> 14.9 us
    ppermute x12 -> x0, starting transfers between devices: 28.9 us -> none  [the longest x4 9.25 us: extended(): lax.ppermute(lax.slice_in_dim(block, 0, width, axis=dim), axis, backward)]
    pallas_call x0 -> x1, Pallas kernels: none -> 17.1 us  [neighbour_exchange(): pl.pallas_call(lambda *refs: exchange_kernel(offsets, *refs), out_shape=[...]
    reshape x2 -> x14, local copies, waits for them, and re-layouts: 0.09 us -> 8.65 us  [the longest x6 4.82 us: neighbour_exchange(): return [o.reshape(a.shape) for o, (a, _) in zip(outs, items)]]
    ppermute x12 -> x0, waiting for transfers between devices: 8.26 us -> none  [the longest x2 4.85 us: shifted_2(): return lax.ppermute(shard, axis, pairs)]
    pallas_call x1, Pallas kernels: 27.8 us -> 30.5 us  [pressure_coefficients(): pl.pallas_call(lambda *refs: reduce_kernel(groups, shift, half_width, *re...]
    slice x4 -> x6, local copies, waits for them, and re-layouts: 2.04 us -> 2.83 us  [pick(): return lax.slice_in_dim(values, values.shape[dim] - width, None, axis=dim)]
  transfers between devices with their start and end apart: 12 -> 0, of which waited for: 3 -> 0; matrix products, arithmetic and copies ran while one was open for 20% -> 0% of each run, Pallas kernels for 29% -> 0%
where the time goes in v8:
time: 89.9 us; the launch traced here: 88.2 us
  Pallas kernels  47.6 us (53%)
  local copies, waits for them, and re-layouts  18.3 us (20%)
  other arithmetic  14.9 us (17%)
  matrix products  4.65 us (5%)
  between operations  2.75 us (3%)
    pallas_call x1, Pallas kernels, pressure_coefficients(): pl.pallas_call(lambda *refs: reduce_kernel(groups, shift, half_width, *re...  30.5 us
    pallas_call x1, Pallas kernels, neighbour_exchange(): pl.pallas_call(lambda *refs: exchange_kernel(offsets, *refs), out_shape=[...  17.1 us
    reshape x6, local copies, waits for them, and re-layouts, neighbour_exchange(): return [o.reshape(a.shape) for o, (a, _) in zip(outs, items)]  4.82 us
    reshape x6, local copies, waits for them, and re-layouts, neighbour_exchange(): flat = [a.reshape(-1, a.shape[-1]) for a, _ in items]  3.74 us
    slice x6, local copies, waits for them, and re-layouts, pick(): return lax.slice_in_dim(values, values.shape[dim] - width, None, axis=dim)  2.83 us
    add x1, other arithmetic, solve_pressure(): padded_pressure = padded_pressure + coefficients[j] * padded_basis[j]  2.77 us
    dot_general x1, matrix products, on_device(): jnp.dot(plane_hot, gas_table, precision=HIGHEST)  2.53 us

profile of v8, /device:TPU:6, one launch (start us, length us, event | category | flops | bytes accessed | tf_op | source)
XLA Modules:
  0.0 88.2 jit_solution(13829655610013760727)
XLA Ops:
  1.3 0.7 broadcast_compare_fusion
  2.1 1.2 %reduce-window.6 = s32[4,16,128]{2,1,0:T(8,128)S(1)} reduce-window(s32[4,16,128]{2,1,0:T(8,128)S(1)} %fusion.130, s32[]{:T(128)} %constant.45.clone.1), window={size=1x1x128 pad=0_0x0_0x127_0}, to_apply=%region_2.3 | reduce-window | flops 1040384 | bytes 65540 | tf_op jit(solution)/shard_map/reduce-window
  3.9 0.7 add_select_fusion.1
  4.9 2.5 %multiply_reduce_fusion = f32[2048,5]{0,1:T(8,128)S(1)} fusion(f32[2048,128]{0,1:T(8,128)S(1)} %fusion.16, s32[2048]{0:T(1024)S(1)} %get-tuple-element.132, f32[8,8,5,128]{3,2,1,0:T(8,128)S(1)} %bitcast.176), kind=kOutput, calls=%fused_computation | convolution fusion | flops 1009375232 | bytes 1261568 | tf_op jit(solution)/shard_map/dot_general | solution.py:464
  7.5 0.8 fusion.3
  13.5 0.7 fusion.137
  14.2 0.8 fusion.138
  15.6 17.1 %shard_map.93 = (f32[56,128]{1,0:T(8,128)}, f32[224,128]{1,0:T(8,128)}, f32[56,128]{1,0:T(8,128)}, f32[224,128]{1,0:T(8,128)}, f32[224,128]{1,0:T(8,128)}, /*ind...) custom-call(f32[56,128]{1,0:T(8,128)} %bitcast.183, ...), custom_call_target="tpu_custom_call" | custom-call | tf_op jit(solution)/shard_map/pallas_call | solution.py:79
  32.7 0.8 reshape.695
  33.5 0.8 reshape.700
  34.4 0.8 reshape.694
  35.2 0.8 reshape.696
  35.9 0.8 reshape.699
  36.7 0.8 reshape.701
  37.5 1.0 %maximum_select_fusion = f32[3,18,18,128]{3,2,1,0:T(8,128)S(1)} fusion(f32[3,5,5,128]{3,2,1,0:T(8,128)S(1)} %reshape.701, f32[3,8,5,128]{3,2,1,0:T(8,128)S(1)} %reshape.700, f32[3,5,5,128]{3,2,1,0:T(8,128)S(1)} %reshape.699, f32[3,5,8,128]{3,2,1,0:T(8,128)} %bitcast.188, f32[3,8,8,128]{3,2,1,0:T(8,128)S(1)} %slice.595, f32[3,5,8,128]{3,2,1,0:T(8,128)} %bitcast.189, ...), kind=kLoop, calls=%fused_computation.22 | loop fusion | flops 1119744 | bytes 995346 | tf_op jit(solution)/shard_map/jit(_where)/select_n | solution.py:146
  41.6 30.5 %shard_map.94 = f32[8,128]{1,0:T(8,128)} custom-call(f32[192,128]{1,0:T(8,128)} %bitcast.171, f32[64,128]{1,0:T(8,128)} %slice_bitcast_fusion.3.refs_1_, f32[64,128]{1,0:T(8,128)} %slice_bitcast_fusion.2.refs_2_, f32[64,128]{1,0:T(8,128)} %get-tuple-element.101.refs_3_, f32[64,128]{1,0:T(8,128)} %get-tuple-element.102.refs_4_, ...), custom_call_target="tpu_custom_call" | custom-call | tf_op jit(solution)/shard_map/pallas_call | solution.py:368
  72.1 1.5 %fusion.140 = (f32[1,1]{1,0:T(1,128)}, f32[1,1]{1,0:T(1,128)}, f32[1,1]{1,0:T(1,128)}, f32[1,1]{1,0:T(1,128)}, f32[1,1]{1,0:T(1,128)}) fusion(f32[8,128]{1,0:T(8,128)} %shard_map.94), kind=kLoop, calls=%fused_computation.287 | loop fusion | bytes 40 | tf_op jit(solution)/shard_map/slice | solution.py:380
  76.0 2.8 %fusion.52 = f32[10,10,130]{2,1,0:T(8,128)S(1)} fusion(f32[10,10,128]{2,1,0:T(8,128)S(1)} %get-tuple-element.98, f32[10,10,128]{2,1,0:T(8,128)S(1)} %get-tuple-element.99, f32[10,10,128]{2,1,0:T(8,128)S(1)} %get-tuple-element.97, f32[10,10,128]{2,1,0:T(8,128)S(1)} %slice.790, f32[]{:T(128)} %bitcast.61, f32[]{:T(128)} %bitcast.60, f32[]{:T(128)} %bitcast.59, ...), kind=kLoop, calls=%fused_computation.90 | loop fusion | flops 91000 | bytes 256816 | tf_op jit(solution)/shard_map/add | solution.py:437
  80.0 1.2 %slice_reduce_fusion = (f32[14,12,12]{2,0,1:T(8,128)S(1)}, f32[14,12,12]{2,0,1:T(8,128)S(1)}) fusion(f32[14,12,12,128]{3,2,0,1:T(8,128)S(1)} %copy_select_fusion), kind=kLoop, calls=%fused_computation.10 | loop fusion | bytes 32256 | tf_op jit(solution)/shard_map/jit(_pad)/slice | solution.py:150
  82.4 1.1 %pad_maximum_fusion = f32[14,12,12,132]{3,2,0,1:T(8,128)S(1)} fusion(f32[14,12,12,2]{3,2,0,1:T(8,128)S(1)} %reshape.708, f32[14,12,12,128]{3,2,0,1:T(8,128)S(1)} %copy_select_fusion, f32[14,12,12,2]{3,2,0,1:T(8,128)S(1)} %reshape.707), kind=kLoop, calls=%fused_computation.1 | loop fusion | flops 532224 | bytes 2128896 | tf_op jit(solution)/shard_map/jit(_pad)/concatenate | solution.py:150
  83.6 1.0 %slice_multiply_fusion.2 = (f32[10,12,12,132]{3,2,0,1:T(8,128)S(1)}, f32[10,12,12,132]{3,2,0,1:T(8,128)S(1)}, f32[10,12,12,132]{3,2,0,1:T(8,128)S(1)}) fusion(f32[14,12,12,132]{3,2,0,1:T(8,128)S(1)} %pad_maximum_fusion, f32[12,12,132]{2,1,0:T(8,128)S(1)} %get-tuple-element.66, f32[12,12,132]{2,1,0:T(8,128)S(1)} %get-tuple-element.65, ...), kind=kLoop, calls=%fused_computation.9 | loop fusion | flops 570240 | bytes 3269376 | tf_op jit(solution)/shard_map/mul | solution.py:160
  84.7 1.4 %fusion.25 = f32[10,8,8,128]{3,2,0,1:T(8,128)S(1)} fusion(f32[14,12,12,128]{3,2,0,1:T(8,128)S(1)} %copy_select_fusion, f32[14,12,12,2]{3,2,0,1:T(8,128)S(1)} %reshape.707, f32[14,12,12,2]{3,2,0,1:T(8,128)S(1)} %reshape.708, f32[10,12,12,132]{3,2,0,1:T(8,128)S(1)} %get-tuple-element.69, f32[10,12,12,132]{3,2,0,1:T(8,128)S(1)} %get-tuple-element.68, ...), kind=kLoop, calls=%fused_computation.32 | loop fusion | flops 4259840 | bytes 10224132 | tf_op jit(solution)/shard_map/add | solution.py:180
  86.1 1.3 %fusion.10 = f32[2,8,8,128]{3,2,0,1:T(8,128)S(1)} fusion(f32[2048,128]{0,1:T(8,128)S(1)} %copy-done.2, f32[2048,2]{0,1:T(2,128)S(1)} %maximum_bitcast_fusion.4, s32[8,8]{1,0:T(8,128)S(1)} %multiply_add_fusion.2, s32[2048]{0:T(1024)S(1)} %get-tuple-element.132, f32[10,8,8,128]{3,2,0,1:T(8,128)S(1)} %fusion.25, f32[8,8,128]{2,1,0:T(8,128)S(1)} %slice_bitcast_fusion.4), kind=kOutput, calls=%fused_computation.16 | convolution fusion | flops 403341312 | bytes 1237248 | tf_op jit(solution)/shard_map/dot_general | solution.py:499
  87.5 0.8 copy.45
  (113 shorter events, 13.7 us)
Async XLA Ops:
  0.6 4.1 %copy-start = (f32[14,8,8,128]{3,2,1,0:T(8,128)S(1)}, f32[14,8,8,128]{3,2,1,0:T(8,128)}, u32[]{:S(2)}) copy-start(f32[14,8,8,128]{3,2,1,0:T(8,128)} %param.6) | copy-start | bytes 1376260
  4.7 2.7 %copy-start.1 = (f32[2048,128]{0,1:T(8,128)}, f32[2048,128]{0,1:T(8,128)S(1)}, u32[]{:S(2)}) copy-start(f32[2048,128]{0,1:T(8,128)S(1)} %fusion.16) | copy-start | bytes 3145732
  4.9 2.6 %copy-start.4 = (f32[8,2048]{1,0:T(8,128)S(1)}, f32[8,2048]{1,0:T(8,128)}, u32[]{:S(2)}) copy-start(f32[8,2048]{1,0:T(8,128)} %param.8) | copy-start | bytes 196612
  37.5 1.3 %copy-start.3 = (f32[3,8,8,128]{3,2,1,0:T(8,128)}, f32[3,8,8,128]{3,2,1,0:T(8,128)S(1)}, u32[]{:S(2)}) copy-start(f32[3,8,8,128]{3,2,1,0:T(8,128)S(1)} %slice.595) | copy-start | bytes 294916
  39.1 35.2 %copy-start.16 = (f32[14,64]{1,0:T(8,128)S(1)}, f32[14,64]{1,0:T(8,128)}, u32[]{:S(2)}) copy-start(f32[14,64]{1,0:T(8,128)} %get-tuple-element.40) | copy-start | bytes 10756
  39.2 35.2 %copy-start.15 = (f32[14,64]{1,0:T(8,128)S(1)}, f32[14,64]{1,0:T(8,128)}, u32[]{:S(2)}) copy-start(f32[14,64]{1,0:T(8,128)} %get-tuple-element.41) | copy-start | bytes 10756
  39.2 35.2 %copy-start.14 = (f32[14,64]{1,0:T(8,128)S(1)}, f32[14,64]{1,0:T(8,128)}, u32[]{:S(2)}) copy-start(f32[14,64]{1,0:T(8,128)} %get-tuple-element.42) | copy-start | bytes 10756
  39.2 35.3 %copy-start.13 = (f32[14,64]{1,0:T(8,128)S(1)}, f32[14,64]{1,0:T(8,128)}, u32[]{:S(2)}) copy-start(f32[14,64]{1,0:T(8,128)} %get-tuple-element.43) | copy-start | bytes 10756
  39.6 40.1 %copy-start.5 = (f32[224,128]{1,0:T(8,128)S(1)}, f32[224,128]{1,0:T(8,128)}, u32[]{:S(2)}) copy-start(f32[224,128]{1,0:T(8,128)} %get-tuple-element.28) | copy-start | bytes 344068
  39.6 40.1 %copy-start.6 = (f32[224,128]{1,0:T(8,128)S(1)}, f32[224,128]{1,0:T(8,128)}, u32[]{:S(2)}) copy-start(f32[224,128]{1,0:T(8,128)} %get-tuple-element.30) | copy-start | bytes 344068
  39.6 40.1 %copy-start.7 = (f32[224,128]{1,0:T(8,128)S(1)}, f32[224,128]{1,0:T(8,128)}, u32[]{:S(2)}) copy-start(f32[224,128]{1,0:T(8,128)} %get-tuple-element.25) | copy-start | bytes 344068
  39.6 40.1 %copy-start.8 = (f32[224,128]{1,0:T(8,128)S(1)}, f32[224,128]{1,0:T(8,128)}, u32[]{:S(2)}) copy-start(f32[224,128]{1,0:T(8,128)} %get-tuple-element.27) | copy-start | bytes 344068
  39.6 40.1 %copy-start.9 = (f32[56,128]{1,0:T(8,128)S(1)}, f32[56,128]{1,0:T(8,128)}, u32[]{:S(2)}) copy-start(f32[56,128]{1,0:T(8,128)} %get-tuple-element.31) | copy-start | bytes 86020
  39.6 40.1 %copy-start.10 = (f32[56,128]{1,0:T(8,128)S(1)}, f32[56,128]{1,0:T(8,128)}, u32[]{:S(2)}) copy-start(f32[56,128]{1,0:T(8,128)} %get-tuple-element.26) | copy-start | bytes 86020
  39.6 40.1 %copy-start.11 = (f32[56,128]{1,0:T(8,128)S(1)}, f32[56,128]{1,0:T(8,128)}, u32[]{:S(2)}) copy-start(f32[56,128]{1,0:T(8,128)} %get-tuple-element.29) | copy-start | bytes 86020
  39.6 40.1 %copy-start.12 = (f32[56,128]{1,0:T(8,128)S(1)}, f32[56,128]{1,0:T(8,128)}, u32[]{:S(2)}) copy-start(f32[56,128]{1,0:T(8,128)} %get-tuple-element.24) | copy-start | bytes 86020
  83.6 1.1 %copy-start.17 = (f32[10]{0:T(128)S(1)}, f32[10]{0:T(128)}, u32[]{:S(2)}) copy-start(f32[10]{0:T(128)} %param.7) | copy-start | bytes 124
  84.7 1.4 %copy-start.2 = (f32[2048,128]{0,1:T(8,128)S(1)}, f32[2048,128]{0,1:T(8,128)}, u32[]{:S(2)}) copy-start(f32[2048,128]{0,1:T(8,128)} %copy-done.1) | copy-start | bytes 3145732

commit v9 on v8

--- a/solution.py
+++ b/solution.py
@@ -262,11 +262,23 @@
     return solution_c
 
 
-def reduce_kernel(groups, shift, half_width, vel_ref, *refs):
+def reduce_kernel(groups, halo_steps, shift, half_width, vel_ref, *refs):
     size = ITERS + 1
+    halos = len(halo_steps)
     basis_refs = refs[:size]
-    o_ref, slots, send_sems, recv_sems = refs[size:]
+    halo_sources = refs[size : size + halos]
+    o_ref = refs[size + halos]
+    halo_outs = refs[size + halos + 1 : size + 2 * halos + 1]
+    slots, send_sems, recv_sems = refs[size + 2 * halos + 1 : size + 2 * halos + 4]
+    halo_landing = refs[size + 2 * halos + 4 : size + 3 * halos + 4]
+    halo_send, halo_recv = refs[size + 3 * halos + 4 :]
     here = {"axial": lax.axis_index("axial"), "azim": lax.axis_index("azim")}
+
+    def neighbour(step_axial, step_azim):
+        return (
+            (here["axial"] + step_axial + lax.axis_size("axial")) % lax.axis_size("axial"),
+            (here["azim"] + step_azim + lax.axis_size("azim")) % lax.axis_size("azim"),
+        )
 
     def member(axis, stride, count, m):
         index = here[axis]
@@ -290,7 +302,24 @@
                 device_id_type=pl.DeviceIdType.MESH,
             )
             greeted += 1
+    for step in sorted(set(halo_steps)):
+        pl.semaphore_signal(
+            barrier, inc=1, device_id=neighbour(*step), device_id_type=pl.DeviceIdType.MESH
+        )
+        greeted += 1
     pl.semaphore_wait(barrier, greeted)
+    halo_copies = []
+    for k, step in enumerate(halo_steps):
+        copy = pltpu.make_async_remote_copy(
+            src_ref=halo_sources[k],
+            dst_ref=halo_landing[k],
+            send_sem=halo_send.at[k],
+            recv_sem=halo_recv.at[k],
+            device_id=neighbour(*step),
+            device_id_type=pl.DeviceIdType.MESH,
+        )
+        copy.start()
+        halo_copies.append(copy)
     row = lax.broadcasted_iota(jnp.int32, o_ref.shape, 0)
     lane = lax.broadcasted_iota(jnp.int32, o_ref.shape, 1)
     is_max = (row == 0) & (lane == 0)
@@ -359,25 +388,36 @@
     for j in range(ITERS):
         out = jnp.where((lane == j), coefficients[j], out)
     o_ref[...] = out
-
-
-def pressure_coefficients(velocity, basis, shift, half_width):
+    for k, copy in enumerate(halo_copies):
+        copy.wait()
+        halo_outs[k][...] = halo_landing[k][...]
+
+
+def pressure_coefficients(velocity, basis, shift, half_width, halo_items):
     groups = reduce_groups()
     slot_count = sum(count for _, _, count in groups)
     flat = [v.reshape(-1, v.shape[-1]) for v in basis]
-    out = pl.pallas_call(
-        lambda *refs: reduce_kernel(groups, shift, half_width, *refs),
-        out_shape=jax.ShapeDtypeStruct((8, 128), jnp.float32),
-        in_specs=[pl.BlockSpec(memory_space=pltpu.VMEM)] * (1 + len(flat)),
-        out_specs=pl.BlockSpec(memory_space=pltpu.VMEM),
+    halo_steps = [step for _, step in halo_items]
+    halo_flat = [a.reshape(-1, a.shape[-1]) for a, _ in halo_items]
+    halos = len(halo_flat)
+    outs = pl.pallas_call(
+        lambda *refs: reduce_kernel(groups, halo_steps, shift, half_width, *refs),
+        out_shape=[jax.ShapeDtypeStruct((8, 128), jnp.float32)]
+        + [jax.ShapeDtypeStruct(f.shape, f.dtype) for f in halo_flat],
+        in_specs=[pl.BlockSpec(memory_space=pltpu.VMEM)] * (1 + len(flat) + halos),
+        out_specs=[pl.BlockSpec(memory_space=pltpu.VMEM)] * (1 + halos),
         scratch_shapes=[
             pltpu.VMEM((slot_count, 8, 128), jnp.float32),
             pltpu.SemaphoreType.DMA((slot_count,)),
             pltpu.SemaphoreType.DMA((slot_count,)),
-        ],
+        ]
+        + [pltpu.VMEM(f.shape, f.dtype) for f in halo_flat]
+        + [pltpu.SemaphoreType.DMA((halos,)), pltpu.SemaphoreType.DMA((halos,))],
         compiler_params=pltpu.CompilerParams(collective_id=0, has_side_effects=True),
-    )(velocity.reshape(-1, velocity.shape[-1]), *flat)
-    return [out[0, j] for j in range(ITERS)], out[0, ITERS]
+    )(velocity.reshape(-1, velocity.shape[-1]), *flat, *halo_flat)
+    out = outs[0]
+    received = [o.reshape(a.shape) for o, (a, _) in zip(outs[1:], halo_items)]
+    return [out[0, j] for j in range(ITERS)], out[0, ITERS], received
 
 
 def neighbour_sum(padded):
@@ -413,7 +453,7 @@
     return beside + at(0, 0, 1) + at(0, 0, -1)
 
 
-def solve_pressure(wide_velocity, velocity):
+def solve_pressure(wide_velocity, velocity, halo_items):
     half_width = 6.0
     u = wide_velocity
     divergence = 0.5 * (u[0, 2:, 1:-1, 1:-1] - u[0, :-2, 1:-1, 1:-1])
@@ -428,14 +468,14 @@
             fresh = 2.0 * scaled - crop(basis[j - 1], 2)
         basis.append(axial_valid(fresh, ITERS - 1 - j))
     interior = [crop(basis[j], ITERS - j) for j in range(ITERS + 1)]
-    coefficients, fastest = pressure_coefficients(
-        velocity, interior, 6.0 + SHIFT_PRESSURE, half_width
+    coefficients, fastest, received = pressure_coefficients(
+        velocity, interior, 6.0 + SHIFT_PRESSURE, half_width, halo_items
     )
     padded_basis = [radial_pad(crop(basis[j], ITERS - j - 1), 1, "constant") for j in range(ITERS)]
     padded_pressure = coefficients[0] * padded_basis[0]
     for j in range(1, ITERS):
         padded_pressure = padded_pressure + coefficients[j] * padded_basis[j]
-    return padded_pressure, fastest
+    return padded_pressure, fastest, received
 
 
 def along_axial(buffer, step_by):
@@ -473,23 +513,28 @@
         jnp.dot(raw, select, precision=HIGHEST).reshape(raw.shape[0], 4, CAP), (1, 0, 2)
     )
     parcel_steps = [(-1, 0), (1, 0), (0, -1), (0, 1)]
-    items = [(rim_slab(state, 2, sa, sz), (sa, sz)) for sa, sz in NEIGHBOURS]
-    items += [(rim_slab(velocity, ITERS + 1, sa, sz), (sa, sz)) for sa, sz in NEIGHBOURS]
+    rim = ITERS + 1
+    items = [(rim_slab(velocity, rim, sa, sz), (sa, sz)) for sa, sz in NEIGHBOURS]
     items += [(leaving[d], parcel_steps[d]) for d in range(4)]
     got = neighbour_exchange(items)
     count = len(NEIGHBOURS)
-    state_rims = {(-sa, -sz): got[k] for k, (sa, sz) in enumerate(NEIGHBOURS)}
-    velocity_rims = {(-sa, -sz): got[count + k] for k, (sa, sz) in enumerate(NEIGHBOURS)}
-    landed = got[2 * count :]
-    whole_pad = assemble(state, state_rims)
+    velocity_rims = {(-sa, -sz): got[k] for k, (sa, sz) in enumerate(NEIGHBOURS)}
+    landed = got[count:]
+    others = jnp.concatenate([state[0:1], state[4:]], axis=0)
+    halo_items = [(rim_slab(others, 2, sa, sz), (sa, sz)) for sa, sz in NEIGHBOURS]
+    wide_raw = assemble(velocity, velocity_rims)
+    wide_velocity = radial_pad(clear_ends(wide_raw, rim, 1), 1, "edge")
+    padded_pressure, fastest, received = solve_pressure(wide_velocity, velocity, halo_items)
+    others_rims = {(-sa, -sz): received[k] for k, (sa, sz) in enumerate(NEIGHBOURS)}
+    others_pad = assemble(others, others_rims)
+    cut = rim - 2
+    velocity_pad2 = wide_raw[:, cut:-cut, cut:-cut]
+    whole_pad = jnp.concatenate([others_pad[0:1], velocity_pad2, others_pad[1:]], axis=0)
     whole_pad = radial_pad(clear_ends(whole_pad, 2, 1), 2, "edge")
     moving = whole_pad[1:]
     density_pad = whole_pad[0]
     density_rim = 2
     vel_pad = moving[0:3]
-    wide_velocity = assemble(velocity, velocity_rims)
-    wide_velocity = radial_pad(clear_ends(wide_velocity, ITERS + 1, 1), 1, "edge")
-    padded_pressure, fastest = solve_pressure(wide_velocity, velocity)
     step_size = CFL / (fastest + 1e-06)
     transported = transport(
         moving[3:], vel_pad, density_pad, density_rim, diff_coef[:, None, None, None], step_size

time: 89.9 us -> 93 us (1.034)
  the two profiles are of different devices: /device:TPU:6 before, /device:TPU:8 now
where the time goes in v9:
time: 93 us; the launch traced here: 92.2 us
  Pallas kernels  45.8 us (49%)
  local copies, waits for them, and re-layouts  22.7 us (24%)
  other arithmetic  16.3 us (18%)
  matrix products  4.54 us (5%)
  between operations  2.81 us (3%)
    pallas_call x1, Pallas kernels, pressure_coefficients(): pl.pallas_call(lambda *refs: reduce_kernel(groups, halo_steps, shift, hal...  26.2 us
    pallas_call x1, Pallas kernels, neighbour_exchange(): pl.pallas_call(lambda *refs: exchange_kernel(offsets, *refs), out_shape=[...  19.6 us
    reshape x6, local copies, waits for them, and re-layouts, neighbour_exchange(): return [o.reshape(a.shape) for o, (a, _) in zip(outs, items)]  4.82 us
    reshape x6, local copies, waits for them, and re-layouts, neighbour_exchange(): flat = [a.reshape(-1, a.shape[-1]) for a, _ in items]  3.72 us
    add x1, other arithmetic, solve_pressure(): padded_pressure = padded_pressure + coefficients[j] * padded_basis[j]  2.69 us
    reshape x4, local copies, waits for them, and re-layouts, pressure_coefficients(): halo_flat = [a.reshape(-1, a.shape[-1]) for a, _ in halo_items]  2.47 us
    dot_general x1, matrix products, on_device(): jnp.dot(plane_hot, gas_table, precision=HIGHEST)  2.43 us
    slice x2, local copies, waits for them, and re-layouts, radial_pad(): jnp.pad(values, [(0, 0)] * (values.ndim - 1) + [(rim_width, rim_width)],...  2.21 us

profile of v9, /device:TPU:8, one launch (start us, length us, event | category | flops | bytes accessed | tf_op | source)
XLA Modules:
  0.0 92.2 jit_solution(9135367092848159858)
XLA Ops:
  1.3 0.7 broadcast_compare_fusion
  2.1 1.2 %reduce-window.6 = s32[4,16,128]{2,1,0:T(8,128)S(1)} reduce-window(s32[4,16,128]{2,1,0:T(8,128)S(1)} %fusion.151, s32[]{:T(128)} %constant.45.clone.1), window={size=1x1x128 pad=0_0x0_0x127_0}, to_apply=%region_2.3 | reduce-window | flops 1040384 | bytes 65540 | tf_op jit(solution)/shard_map/reduce-window
  3.9 0.7 add_select_fusion.1
  4.9 2.4 %multiply_reduce_fusion = f32[2048,5]{0,1:T(8,128)S(1)} fusion(f32[2048,128]{0,1:T(8,128)S(1)} %fusion.31, s32[2048]{0:T(1024)S(1)} %get-tuple-element.136, f32[8,8,5,128]{3,2,1,0:T(8,128)S(1)} %bitcast.171), kind=kOutput, calls=%fused_computation | convolution fusion | flops 1009375232 | bytes 1261568 | tf_op jit(solution)/shard_map/dot_general | solution.py:504
  7.9 0.8 fusion.3
  13.9 19.6 %shard_map.93 = (f32[75,128]{1,0:T(8,128)}, f32[120,128]{1,0:T(8,128)}, f32[75,128]{1,0:T(8,128)}, f32[120,128]{1,0:T(8,128)}, f32[120,128]{1,0:T(8,128)}, /*ind...) custom-call(f32[75,128]{1,0:T(8,128)} %reshape.666.refs_0_, ...), custom_call_target="tpu_custom_call" | custom-call | tf_op jit(solution)/shard_map/pallas_call | solution.py:79
  33.5 0.8 reshape.679
  34.3 0.8 reshape.684
  35.1 0.8 reshape.678
  35.9 0.8 reshape.680
  36.7 0.8 reshape.683
  37.5 0.8 reshape.685
  38.3 1.0 %broadcast_select_fusion = f32[3,18,18,128]{3,2,0,1:T(8,128)S(1)} fusion(pred[18]{0:T(512)(128)(4,1)S(1)} %and_or_fusion, f32[3,5,5,128]{3,2,1,0:T(8,128)S(1)} %reshape.685, f32[3,8,5,128]{3,2,1,0:T(8,128)S(1)} %reshape.684, f32[3,5,5,128]{3,2,1,0:T(8,128)S(1)} %reshape.683, f32[3,5,8,128]{3,2,1,0:T(8,128)} %bitcast.174, f32[3,8,8,128]{3,2,1,0:T(8,128)S(1)} %slice.584, ...), kind=kLoop, calls=%fused_computation.58 | loop fusion | flops 1119744 | bytes 995346 | tf_op jit(solution)/shard_map/jit(_where)/select_n | solution.py:146
  39.4 1.0 %fusion.153 = (f32[3,18,18,1]{3,2,0,1:T(8,128)S(1)}, f32[3,18,18,1]{3,2,0,1:T(8,128)}) fusion(f32[3,18,18,128]{3,2,0,1:T(8,128)S(1)} %broadcast_select_fusion), kind=kLoop, calls=%fused_computation.322 | loop fusion | bytes 15552 | tf_op jit(solution)/shard_map/jit(_pad)/slice | solution.py:150
  40.4 1.1 %fusion.74 = f32[16,16,128]{2,1,0:T(8,128)S(1)} fusion(f32[3,18,18,128]{3,2,0,1:T(8,128)S(1)} %broadcast_select_fusion, f32[3,18,18,1]{3,2,0,1:T(8,128)} %get-tuple-element.73, f32[3,18,18,1]{3,2,0,1:T(8,128)S(1)} %get-tuple-element.72, pred[16]{0:T(512)(128)(4,1)S(1)} %compare_and_fusion.4), kind=kLoop, calls=%fused_computation.134 | loop fusion | flops 294912 | bytes 1986864 | tf_op jit(solution)/shard_map/jit(_where)/select_n | solution.py:435
  49.2 26.2 %shard_map.94 = (f32[8,128]{1,0:T(8,128)}, f32[44,128]{1,0:T(8,128)}, f32[176,128]{1,0:T(8,128)}, f32[44,128]{1,0:T(8,128)}, f32[176,128]{1,0:T(8,128)}, /*index...) custom-call(f32[192,128]{1,0:T(8,128)} %bitcast.166, ...), custom_call_target="tpu_custom_call" | custom-call | tf_op jit(solution)/shard_map/pallas_call | solution.py:403
  75.5 1.5 %fusion.158 = (f32[1,1]{1,0:T(1,128)}, f32[1,1]{1,0:T(1,128)}, f32[1,1]{1,0:T(1,128)}, f32[1,1]{1,0:T(1,128)}, f32[1,1]{1,0:T(1,128)}) fusion(f32[8,128]{1,0:T(8,128)} %get-tuple-element.41), kind=kLoop, calls=%fused_computation.327 | loop fusion | bytes 40 | tf_op jit(solution)/shard_map/slice | solution.py:420
  79.5 2.7 %fusion.67 = f32[10,10,130]{2,1,0:T(8,128)S(1)} fusion(f32[10,10,128]{2,1,0:T(8,128)S(1)} %get-tuple-element.102, f32[10,10,128]{2,1,0:T(8,128)S(1)} %get-tuple-element.103, f32[10,10,128]{2,1,0:T(8,128)S(1)} %get-tuple-element.101, f32[10,10,128]{2,1,0:T(8,128)S(1)} %slice.820, f32[]{:T(128)} %bitcast.53, f32[]{:T(128)} %bitcast.52, f32[]{:T(128)} %bitcast.51, ...), kind=kLoop, calls=%fused_computation.122 | loop fusion | flops 91000 | bytes 256816 | tf_op jit(solution)/shard_map/add | solution.py:477
  83.8 1.2 %slice_reduce_fusion = (f32[14,12,12]{2,0,1:T(8,128)S(1)}, f32[14,12,12]{2,0,1:T(8,128)S(1)}) fusion(f32[14,12,12,128]{3,2,0,1:T(8,128)S(1)} %fusion.5), kind=kLoop, calls=%fused_computation.10 | loop fusion | bytes 32256 | tf_op jit(solution)/shard_map/jit(_pad)/slice | solution.py:150
  86.2 1.1 %pad_maximum_fusion = f32[14,12,12,132]{3,2,0,1:T(8,128)S(1)} fusion(f32[14,12,12,2]{3,2,0,1:T(8,128)S(1)} %reshape.708, f32[14,12,12,128]{3,2,0,1:T(8,128)S(1)} %fusion.5, f32[14,12,12,2]{3,2,0,1:T(8,128)S(1)} %reshape.707), kind=kLoop, calls=%fused_computation.1 | loop fusion | flops 532224 | bytes 2128896 | tf_op jit(solution)/shard_map/jit(_pad)/concatenate | solution.py:150
  87.4 1.0 %slice_multiply_fusion.2 = (f32[10,12,12,132]{3,2,0,1:T(8,128)S(1)}, f32[10,12,12,132]{3,2,0,1:T(8,128)S(1)}, f32[10,12,12,132]{3,2,0,1:T(8,128)S(1)}) fusion(f32[14,12,12,132]{3,2,0,1:T(8,128)S(1)} %pad_maximum_fusion, f32[12,12,132]{2,1,0:T(8,128)S(1)} %get-tuple-element.68, f32[12,12,132]{2,1,0:T(8,128)S(1)} %get-tuple-element.67, ...), kind=kLoop, calls=%fused_computation.9 | loop fusion | flops 570240 | bytes 3269376 | tf_op jit(solution)/shard_map/mul | solution.py:160
  88.7 1.4 %fusion.40 = f32[10,8,8,128]{3,2,0,1:T(8,128)S(1)} fusion(f32[14,12,12,128]{3,2,0,1:T(8,128)S(1)} %fusion.5, f32[14,12,12,2]{3,2,0,1:T(8,128)S(1)} %reshape.707, f32[14,12,12,2]{3,2,0,1:T(8,128)S(1)} %reshape.708, f32[10,12,12,132]{3,2,0,1:T(8,128)S(1)} %get-tuple-element.71, f32[10,12,12,132]{3,2,0,1:T(8,128)S(1)} %get-tuple-element.70, ...), kind=kLoop, calls=%fused_computation.64 | loop fusion | flops 4259840 | bytes 10224132 | tf_op jit(solution)/shard_map/add | solution.py:180
  90.0 1.3 %fusion.25 = f32[2,8,8,128]{3,2,0,1:T(8,128)S(1)} fusion(f32[2048,128]{0,1:T(8,128)S(1)} %fusion.31, f32[2048,2]{0,1:T(2,128)S(1)} %maximum_bitcast_fusion.4, s32[8,8]{1,0:T(8,128)S(1)} %multiply_add_fusion.2, s32[2048]{0:T(1024)S(1)} %get-tuple-element.136, f32[10,8,8,128]{3,2,0,1:T(8,128)S(1)} %fusion.40, f32[8,8,128]{2,1,0:T(8,128)S(1)} %get-tuple-element.77), kind=kOutput, calls=%fused_computation.35 | convolution fusion | flops 403341312 | bytes 1237248 | tf_op jit(solution)/shard_map/dot_general | solution.py:544
  91.4 0.8 copy.102
  (140 shorter events, 18.8 us)
Async XLA Ops:
  0.6 4.1 %copy-start = (f32[14,8,8,128]{3,2,1,0:T(8,128)S(1)}, f32[14,8,8,128]{3,2,1,0:T(8,128)}, u32[]{:S(2)}) copy-start(f32[14,8,8,128]{3,2,1,0:T(8,128)} %param.6) | copy-start | bytes 1376260
  4.9 3.1 %copy-start.5 = (f32[8,2048]{1,0:T(8,128)S(1)}, f32[8,2048]{1,0:T(8,128)}, u32[]{:S(2)}) copy-start(f32[8,2048]{1,0:T(8,128)} %param.8) | copy-start | bytes 196612
  7.3 0.6 copy-start.11
  38.3 2.1 %copy-start.1 = (f32[3,8,8,128]{3,2,1,0:T(8,128)}, f32[3,8,8,128]{3,2,1,0:T(8,128)S(1)}, u32[]{:S(2)}) copy-start(f32[3,8,8,128]{3,2,1,0:T(8,128)S(1)} %slice.584) | copy-start | bytes 294916
  45.2 32.5 %copy-start.20 = (f32[14,64]{1,0:T(8,128)S(1)}, f32[14,64]{1,0:T(8,128)}, u32[]{:S(2)}) copy-start(f32[14,64]{1,0:T(8,128)} %get-tuple-element.42) | copy-start | bytes 10756
  45.3 32.6 %copy-start.19 = (f32[14,64]{1,0:T(8,128)S(1)}, f32[14,64]{1,0:T(8,128)}, u32[]{:S(2)}) copy-start(f32[14,64]{1,0:T(8,128)} %get-tuple-element.43) | copy-start | bytes 10756
  45.9 32.1 %copy-start.18 = (f32[14,64]{1,0:T(8,128)S(1)}, f32[14,64]{1,0:T(8,128)}, u32[]{:S(2)}) copy-start(f32[14,64]{1,0:T(8,128)} %get-tuple-element.44) | copy-start | bytes 10756
  45.9 32.1 %copy-start.17 = (f32[14,64]{1,0:T(8,128)S(1)}, f32[14,64]{1,0:T(8,128)}, u32[]{:S(2)}) copy-start(f32[14,64]{1,0:T(8,128)} %get-tuple-element.45) | copy-start | bytes 10756
  46.5 32.2 %copy-start.6 = (f32[8,2048]{1,0:T(8,128)S(1)}, f32[8,2048]{1,0:T(8,128)}, u32[]{:S(2)}) copy-start(f32[8,2048]{1,0:T(8,128)} %param.8) | copy-start | bytes 196612
  46.5 32.2 %copy-start.12 = (f32[2048,5]{0,1:T(8,128)S(1)}, f32[2048,5]{0,1:T(8,128)}, u32[]{:S(2)}) copy-start(f32[2048,5]{0,1:T(8,128)} %copy-done.11) | copy-start | bytes 122884
  75.5 7.6 %copy-start.16 = (f32[44,128]{1,0:T(8,128)S(1)}, f32[44,128]{1,0:T(8,128)}, u32[]{:S(2)}) copy-start(f32[44,128]{1,0:T(8,128)} %get-tuple-element.38) | copy-start | bytes 67588
  75.5 7.6 %copy-start.15 = (f32[44,128]{1,0:T(8,128)S(1)}, f32[44,128]{1,0:T(8,128)}, u32[]{:S(2)}) copy-start(f32[44,128]{1,0:T(8,128)} %get-tuple-element.40) | copy-start | bytes 67588
  75.5 7.7 %copy-start.10 = (f32[176,128]{1,0:T(8,128)S(1)}, f32[176,128]{1,0:T(8,128)}, u32[]{:S(2)}) copy-start(f32[176,128]{1,0:T(8,128)} %get-tuple-element.39) | copy-start | bytes 270340
  75.5 7.7 %copy-start.14 = (f32[44,128]{1,0:T(8,128)S(1)}, f32[44,128]{1,0:T(8,128)}, u32[]{:S(2)}) copy-start(f32[44,128]{1,0:T(8,128)} %get-tuple-element.33) | copy-start | bytes 67588
  75.5 7.7 %copy-start.13 = (f32[44,128]{1,0:T(8,128)S(1)}, f32[44,128]{1,0:T(8,128)}, u32[]{:S(2)}) copy-start(f32[44,128]{1,0:T(8,128)} %get-tuple-element.35) | copy-start | bytes 67588
  75.5 7.8 %copy-start.9 = (f32[176,128]{1,0:T(8,128)S(1)}, f32[176,128]{1,0:T(8,128)}, u32[]{:S(2)}) copy-start(f32[176,128]{1,0:T(8,128)} %get-tuple-element.34) | copy-start | bytes 270340
  75.5 7.8 %copy-start.2 = (f32[3,8,8,128]{3,2,1,0:T(8,128)S(1)}, f32[3,8,8,128]{3,2,1,0:T(8,128)}, u32[]{:S(2)}) copy-start(f32[3,8,8,128]{3,2,1,0:T(8,128)} %copy-done.1) | copy-start | bytes 294916
  75.5 7.8 %copy-start.3 = (f32[120,128]{1,0:T(8,128)S(1)}, f32[120,128]{1,0:T(8,128)}, u32[]{:S(2)}) copy-start(f32[120,128]{1,0:T(8,128)} %get-tuple-element.29) | copy-start | bytes 184324
  75.5 7.8 %copy-start.4 = (f32[120,128]{1,0:T(8,128)S(1)}, f32[120,128]{1,0:T(8,128)}, u32[]{:S(2)}) copy-start(f32[120,128]{1,0:T(8,128)} %get-tuple-element.28) | copy-start | bytes 184324
  82.2 1.3 %copy-start.7 = (f32[176,128]{1,0:T(8,128)S(1)}, f32[176,128]{1,0:T(8,128)}, u32[]{:S(2)}) copy-start(f32[176,128]{1,0:T(8,128)} %get-tuple-element.37) | copy-start | bytes 270340
  82.2 1.3 %copy-start.8 = (f32[176,128]{1,0:T(8,128)S(1)}, f32[176,128]{1,0:T(8,128)}, u32[]{:S(2)}) copy-start(f32[176,128]{1,0:T(8,128)} %get-tuple-element.36) | copy-start | bytes 270340
  87.4 1.3 %copy-start.21 = (f32[10]{0:T(128)S(1)}, f32[10]{0:T(128)}, u32[]{:S(2)}) copy-start(f32[10]{0:T(128)} %param.7) | copy-start | bytes 124

commit v10 on v8

--- a/solution.py
+++ b/solution.py
@@ -74,7 +74,7 @@
 
 def neighbour_exchange(items):
     offsets = [step for _, step in items]
-    flat = [a.reshape(-1, a.shape[-1]) for a, _ in items]
+    flat = [a for a, _ in items]
     count = len(flat)
     outs = pl.pallas_call(
         lambda *refs: exchange_kernel(offsets, *refs),
@@ -85,7 +85,7 @@
         + [pltpu.SemaphoreType.DMA((count,)), pltpu.SemaphoreType.DMA((count,))],
         compiler_params=pltpu.CompilerParams(collective_id=1, has_side_effects=True),
     )(*flat)
-    return [o.reshape(a.shape) for o, (a, _) in zip(outs, items)]
+    return list(outs)
 
 
 def rim_slab(block, width, step_axial, step_azim):

time: 89.9 us -> 82.7 us (0.920)
  local copies, waits for them, and re-layouts: 18.3 us -> 11.1 us
    reshape x12 -> x0, local copies, waits for them, and re-layouts: 8.56 us -> none  [the longest x6 4.82 us: neighbour_exchange(): return [o.reshape(a.shape) for o, (a, _) in zip(outs, items)]]
    slice x6, local copies, waits for them, and re-layouts: 2.83 us -> 4.18 us  [pick(): return lax.slice_in_dim(values, values.shape[dim] - width, None, axis=dim)]
where the time goes in v10:
time: 82.7 us; the launch traced here: 81.4 us
  Pallas kernels  47.7 us (58%)
  other arithmetic  15.1 us (18%)
  local copies, waits for them, and re-layouts  11.1 us (13%)
  matrix products  4.65 us (6%)
  between operations  2.75 us (3%)
    pallas_call x1, Pallas kernels, pressure_coefficients(): pl.pallas_call(lambda *refs: reduce_kernel(groups, shift, half_width, *re...  30.5 us
    pallas_call x1, Pallas kernels, neighbour_exchange(): pl.pallas_call(lambda *refs: exchange_kernel(offsets, *refs), out_shape=[...  17.2 us
    slice x6, local copies, waits for them, and re-layouts, pick(): return lax.slice_in_dim(values, values.shape[dim] - width, None, axis=dim)  4.18 us
    add x1, other arithmetic, solve_pressure(): padded_pressure = padded_pressure + coefficients[j] * padded_basis[j]  2.77 us
    dot_general x1, matrix products, on_device(): jnp.dot(plane_hot, gas_table, precision=HIGHEST)  2.53 us

profile of v10, /device:TPU:6, one launch (start us, length us, event | category | flops | bytes accessed | tf_op | source)
XLA Modules:
  0.0 81.4 jit_solution(9043600385622001357)
XLA Ops:
  1.3 0.7 broadcast_compare_fusion
  2.1 1.2 %reduce-window.6 = s32[4,16,128]{2,1,0:T(8,128)S(1)} reduce-window(s32[4,16,128]{2,1,0:T(8,128)S(1)} %fusion.130, s32[]{:T(128)} %constant.45.clone.1), window={size=1x1x128 pad=0_0x0_0x127_0}, to_apply=%region_2.3 | reduce-window | flops 1040384 | bytes 65540 | tf_op jit(solution)/shard_map/reduce-window
  3.9 0.7 add_select_fusion.1
  4.9 2.5 %multiply_reduce_fusion = f32[2048,5]{0,1:T(8,128)S(1)} fusion(f32[2048,128]{0,1:T(8,128)S(1)} %fusion.16, s32[2048]{0:T(1024)S(1)} %get-tuple-element.132, f32[8,8,5,128]{3,2,1,0:T(8,128)S(1)} %bitcast.152), kind=kOutput, calls=%fused_computation | convolution fusion | flops 1009375232 | bytes 1261568 | tf_op jit(solution)/shard_map/dot_general | solution.py:464
  7.5 0.8 %fusion.3 = f32[14,256]{1,0:T(8,128)S(1)} fusion(s32[2048]{0:T(1024)S(1)} %bitcast_select_fusion, f32[1,2048]{1,0:T(1,128)S(1)} %fusion.106, f32[5,2048]{1,0:T(8,128)S(1)} %bitcast.154, f32[8,2048]{1,0:T(8,128)S(1)} %copy-done.4), kind=kOutput, calls=%fused_computation.6 | convolution fusion | flops 88662016 | bytes 137216 | tf_op jit(solution)/shard_map/dot_general | solution.py:473
  9.0 0.7 fusion.133
  9.7 0.7 fusion.136
  10.3 0.7 fusion.137
  11.1 0.8 fusion.138
  11.8 0.7 fusion.135
  12.5 0.7 fusion.134
  13.2 17.2 %shard_map.93 = (f32[14,2,2,128]{3,2,1,0:T(2,128)}, f32[14,2,8,128]{3,2,1,0:T(8,128)}, f32[14,2,2,128]{3,2,1,0:T(2,128)}, f32[14,8,2,128]{3,2,1,0:T(2,128)}, f32...) custom-call(f32[14,2,2,128]{3,2,1,0:T(2,128)} %get-tuple-element.86., ...), custom_call_target="tpu_custom_call" | custom-call | tf_op jit(solution)/shard_map/pallas_call | solution.py:79
  30.5 1.3 %maximum_select_fusion = f32[3,18,18,128]{3,2,1,0:T(8,128)S(1)} fusion(f32[3,5,5,128]{3,2,1,0:T(8,128)} %get-tuple-element.39, f32[3,8,5,128]{3,2,1,0:T(8,128)} %get-tuple-element.38, f32[3,5,5,128]{3,2,1,0:T(8,128)} %get-tuple-element.37, f32[3,5,8,128]{3,2,1,0:T(8,128)} %get-tuple-element.36, f32[3,8,8,128]{3,2,1,0:T(8,128)S(1)} %slice.595, ...), kind=kLoop, calls=%fused_computation.22 | loop fusion | flops 1119744 | bytes 995346 | tf_op jit(solution)/shard_map/jit(_where)/select_n | solution.py:146
  32.8 0.7 fusion.86
  34.8 30.5 %shard_map.94 = f32[8,128]{1,0:T(8,128)} custom-call(f32[192,128]{1,0:T(8,128)} %bitcast.151, f32[64,128]{1,0:T(8,128)} %slice_bitcast_fusion.3.refs_1_, f32[64,128]{1,0:T(8,128)} %slice_bitcast_fusion.2.refs_2_, f32[64,128]{1,0:T(8,128)} %get-tuple-element.101.refs_3_, f32[64,128]{1,0:T(8,128)} %get-tuple-element.102.refs_4_, ...), custom_call_target="tpu_custom_call" | custom-call | tf_op jit(solution)/shard_map/pallas_call | solution.py:368
  65.3 1.5 %fusion.140 = (f32[1,1]{1,0:T(1,128)}, f32[1,1]{1,0:T(1,128)}, f32[1,1]{1,0:T(1,128)}, f32[1,1]{1,0:T(1,128)}, f32[1,1]{1,0:T(1,128)}) fusion(f32[8,128]{1,0:T(8,128)} %shard_map.94), kind=kLoop, calls=%fused_computation.287 | loop fusion | bytes 40 | tf_op jit(solution)/shard_map/slice | solution.py:380
  68.5 0.7 fusion.80
  69.2 2.8 %fusion.52 = f32[10,10,130]{2,1,0:T(8,128)S(1)} fusion(f32[10,10,128]{2,1,0:T(8,128)S(1)} %get-tuple-element.98, f32[10,10,128]{2,1,0:T(8,128)S(1)} %get-tuple-element.99, f32[10,10,128]{2,1,0:T(8,128)S(1)} %get-tuple-element.97, f32[10,10,128]{2,1,0:T(8,128)S(1)} %slice.790, f32[]{:T(128)} %bitcast.41, f32[]{:T(128)} %bitcast.40, f32[]{:T(128)} %bitcast.39, ...), kind=kLoop, calls=%fused_computation.90 | loop fusion | flops 91000 | bytes 256816 | tf_op jit(solution)/shard_map/add | solution.py:437
  73.2 1.2 %slice_reduce_fusion = (f32[14,12,12]{2,0,1:T(8,128)S(1)}, f32[14,12,12]{2,0,1:T(8,128)S(1)}) fusion(f32[14,12,12,128]{3,2,0,1:T(8,128)S(1)} %copy_select_fusion), kind=kLoop, calls=%fused_computation.10 | loop fusion | bytes 32256 | tf_op jit(solution)/shard_map/jit(_pad)/slice | solution.py:150
  75.6 1.1 %pad_maximum_fusion = f32[14,12,12,132]{3,2,0,1:T(8,128)S(1)} fusion(f32[14,12,12,2]{3,2,0,1:T(8,128)S(1)} %reshape.580, f32[14,12,12,128]{3,2,0,1:T(8,128)S(1)} %copy_select_fusion, f32[14,12,12,2]{3,2,0,1:T(8,128)S(1)} %reshape.579), kind=kLoop, calls=%fused_computation.1 | loop fusion | flops 532224 | bytes 2128896 | tf_op jit(solution)/shard_map/jit(_pad)/concatenate | solution.py:150
  76.8 1.0 %slice_multiply_fusion.2 = (f32[10,12,12,132]{3,2,0,1:T(8,128)S(1)}, f32[10,12,12,132]{3,2,0,1:T(8,128)S(1)}, f32[10,12,12,132]{3,2,0,1:T(8,128)S(1)}) fusion(f32[14,12,12,132]{3,2,0,1:T(8,128)S(1)} %pad_maximum_fusion, f32[12,12,132]{2,1,0:T(8,128)S(1)} %get-tuple-element.66, f32[12,12,132]{2,1,0:T(8,128)S(1)} %get-tuple-element.65, ...), kind=kLoop, calls=%fused_computation.9 | loop fusion | flops 570240 | bytes 3269376 | tf_op jit(solution)/shard_map/mul | solution.py:160
  77.9 1.4 %fusion.25 = f32[10,8,8,128]{3,2,0,1:T(8,128)S(1)} fusion(f32[14,12,12,128]{3,2,0,1:T(8,128)S(1)} %copy_select_fusion, f32[14,12,12,2]{3,2,0,1:T(8,128)S(1)} %reshape.579, f32[14,12,12,2]{3,2,0,1:T(8,128)S(1)} %reshape.580, f32[10,12,12,132]{3,2,0,1:T(8,128)S(1)} %get-tuple-element.69, f32[10,12,12,132]{3,2,0,1:T(8,128)S(1)} %get-tuple-element.68, ...), kind=kLoop, calls=%fused_computation.32 | loop fusion | flops 4259840 | bytes 10224132 | tf_op jit(solution)/shard_map/add | solution.py:180
  79.3 1.3 %fusion.10 = f32[2,8,8,128]{3,2,0,1:T(8,128)S(1)} fusion(f32[2048,128]{0,1:T(8,128)S(1)} %copy-done.2, f32[2048,2]{0,1:T(2,128)S(1)} %maximum_bitcast_fusion.4, s32[8,8]{1,0:T(8,128)S(1)} %multiply_add_fusion.2, s32[2048]{0:T(1024)S(1)} %get-tuple-element.132, f32[10,8,8,128]{3,2,0,1:T(8,128)S(1)} %fusion.25, f32[8,8,128]{2,1,0:T(8,128)S(1)} %slice_bitcast_fusion.4), kind=kOutput, calls=%fused_computation.16 | convolution fusion | flops 403341312 | bytes 1237248 | tf_op jit(solution)/shard_map/dot_general | solution.py:499
  80.7 0.8 copy.33
  (101 shorter events, 7.2 us)
Async XLA Ops:
  0.6 4.1 %copy-start = (f32[14,8,8,128]{3,2,1,0:T(8,128)S(1)}, f32[14,8,8,128]{3,2,1,0:T(8,128)}, u32[]{:S(2)}) copy-start(f32[14,8,8,128]{3,2,1,0:T(8,128)} %param.6) | copy-start | bytes 1376260
  4.7 2.7 %copy-start.1 = (f32[2048,128]{0,1:T(8,128)}, f32[2048,128]{0,1:T(8,128)S(1)}, u32[]{:S(2)}) copy-start(f32[2048,128]{0,1:T(8,128)S(1)} %fusion.16) | copy-start | bytes 3145732
  4.9 2.6 %copy-start.4 = (f32[8,2048]{1,0:T(8,128)S(1)}, f32[8,2048]{1,0:T(8,128)}, u32[]{:S(2)}) copy-start(f32[8,2048]{1,0:T(8,128)} %param.8) | copy-start | bytes 196612
  30.5 1.5 %copy-start.3 = (f32[3,8,8,128]{3,2,1,0:T(8,128)}, f32[3,8,8,128]{3,2,1,0:T(8,128)S(1)}, u32[]{:S(2)}) copy-start(f32[3,8,8,128]{3,2,1,0:T(8,128)S(1)} %slice.595) | copy-start | bytes 294916
  32.2 35.2 %copy-start.16 = (f32[14,64]{1,0:T(8,128)S(1)}, f32[14,64]{1,0:T(8,128)}, u32[]{:S(2)}) copy-start(f32[14,64]{1,0:T(8,128)} %get-tuple-element.40) | copy-start | bytes 10756
  32.4 35.2 %copy-start.15 = (f32[14,64]{1,0:T(8,128)S(1)}, f32[14,64]{1,0:T(8,128)}, u32[]{:S(2)}) copy-start(f32[14,64]{1,0:T(8,128)} %get-tuple-element.41) | copy-start | bytes 10756
  32.4 35.2 %copy-start.14 = (f32[14,64]{1,0:T(8,128)S(1)}, f32[14,64]{1,0:T(8,128)}, u32[]{:S(2)}) copy-start(f32[14,64]{1,0:T(8,128)} %get-tuple-element.42) | copy-start | bytes 10756
  32.4 35.3 %copy-start.13 = (f32[14,64]{1,0:T(8,128)S(1)}, f32[14,64]{1,0:T(8,128)}, u32[]{:S(2)}) copy-start(f32[14,64]{1,0:T(8,128)} %get-tuple-element.43) | copy-start | bytes 10756
  32.7 40.1 %copy-start.5 = (f32[14,2,8,128]{3,2,1,0:T(8,128)S(1)}, f32[14,2,8,128]{3,2,1,0:T(8,128)}, u32[]{:S(2)}) copy-start(f32[14,2,8,128]{3,2,1,0:T(8,128)} %get-tuple-element.28) | copy-start | bytes 344068
  32.7 40.1 %copy-start.6 = (f32[14,8,2,128]{3,2,1,0:T(2,128)S(1)}, f32[14,8,2,128]{3,2,1,0:T(2,128)}, u32[]{:S(2)}) copy-start(f32[14,8,2,128]{3,2,1,0:T(2,128)} %get-tuple-element.30) | copy-start | bytes 344068
  32.8 40.1 %copy-start.7 = (f32[14,8,2,128]{3,2,1,0:T(2,128)S(1)}, f32[14,8,2,128]{3,2,1,0:T(2,128)}, u32[]{:S(2)}) copy-start(f32[14,8,2,128]{3,2,1,0:T(2,128)} %get-tuple-element.25) | copy-start | bytes 344068
  32.8 40.1 %copy-start.8 = (f32[14,2,8,128]{3,2,1,0:T(8,128)S(1)}, f32[14,2,8,128]{3,2,1,0:T(8,128)}, u32[]{:S(2)}) copy-start(f32[14,2,8,128]{3,2,1,0:T(8,128)} %get-tuple-element.27) | copy-start | bytes 344068
  32.8 40.1 %copy-start.9 = (f32[14,2,2,128]{3,2,1,0:T(2,128)S(1)}, f32[14,2,2,128]{3,2,1,0:T(2,128)}, u32[]{:S(2)}) copy-start(f32[14,2,2,128]{3,2,1,0:T(2,128)} %get-tuple-element.31) | copy-start | bytes 86020
  32.8 40.1 %copy-start.10 = (f32[14,2,2,128]{3,2,1,0:T(2,128)S(1)}, f32[14,2,2,128]{3,2,1,0:T(2,128)}, u32[]{:S(2)}) copy-start(f32[14,2,2,128]{3,2,1,0:T(2,128)} %get-tuple-element.26) | copy-start | bytes 86020
  32.8 40.1 %copy-start.11 = (f32[14,2,2,128]{3,2,1,0:T(2,128)S(1)}, f32[14,2,2,128]{3,2,1,0:T(2,128)}, u32[]{:S(2)}) copy-start(f32[14,2,2,128]{3,2,1,0:T(2,128)} %get-tuple-element.29) | copy-start | bytes 86020
  32.8 40.1 %copy-start.12 = (f32[14,2,2,128]{3,2,1,0:T(2,128)S(1)}, f32[14,2,2,128]{3,2,1,0:T(2,128)}, u32[]{:S(2)}) copy-start(f32[14,2,2,128]{3,2,1,0:T(2,128)} %get-tuple-element.24) | copy-start | bytes 86020
  76.7 1.1 %copy-start.17 = (f32[10]{0:T(128)S(1)}, f32[10]{0:T(128)}, u32[]{:S(2)}) copy-start(f32[10]{0:T(128)} %param.7) | copy-start | bytes 124
  77.9 1.4 %copy-start.2 = (f32[2048,128]{0,1:T(8,128)S(1)}, f32[2048,128]{0,1:T(8,128)}, u32[]{:S(2)}) copy-start(f32[2048,128]{0,1:T(8,128)} %copy-done.1) | copy-start | bytes 3145732

commit v11 on v10

--- a/solution.py
+++ b/solution.py
@@ -103,9 +103,18 @@
 
 
 def assemble(block, received):
+    rim_a = received[(-1, 0)].shape[1]
+    rim_z = received[(0, -1)].shape[2]
     bands = []
     for pz in (-1, 0, 1):
-        row = [block if (pa, pz) == (0, 0) else received[(pa, pz)] for pa in (-1, 0, 1)]
+        row = []
+        for pa in (-1, 0, 1):
+            if (pa, pz) == (0, 0):
+                row.append(block)
+            elif (pa, pz) in received:
+                row.append(received[(pa, pz)])
+            else:
+                row.append(jnp.zeros(block.shape[:1] + (rim_a, rim_z) + block.shape[3:], block.dtype))
         bands.append(jnp.concatenate(row, axis=1))
     return jnp.concatenate(bands, axis=2)
 
@@ -473,14 +482,26 @@
         jnp.dot(raw, select, precision=HIGHEST).reshape(raw.shape[0], 4, CAP), (1, 0, 2)
     )
     parcel_steps = [(-1, 0), (1, 0), (0, -1), (0, 1)]
-    items = [(rim_slab(state, 2, sa, sz), (sa, sz)) for sa, sz in NEIGHBOURS]
-    items += [(rim_slab(velocity, ITERS + 1, sa, sz), (sa, sz)) for sa, sz in NEIGHBOURS]
+    faces = [(sa, sz) for sa, sz in NEIGHBOURS if sa == 0 or sz == 0]
+
+    def outgoing(block, width, sa, sz):
+        slab = rim_slab(block, width, sa, sz)
+        return jnp.swapaxes(slab, 1, 2) if sa == 0 else slab
+
+    def incoming(slab, sa):
+        return jnp.swapaxes(slab, 1, 2) if sa == 0 else slab
+
+    rim = ITERS + 1
+    items = [(outgoing(state, 2, sa, sz), (sa, sz)) for sa, sz in faces]
+    items += [(outgoing(velocity, rim, sa, sz), (sa, sz)) for sa, sz in NEIGHBOURS]
     items += [(leaving[d], parcel_steps[d]) for d in range(4)]
     got = neighbour_exchange(items)
-    count = len(NEIGHBOURS)
-    state_rims = {(-sa, -sz): got[k] for k, (sa, sz) in enumerate(NEIGHBOURS)}
-    velocity_rims = {(-sa, -sz): got[count + k] for k, (sa, sz) in enumerate(NEIGHBOURS)}
-    landed = got[2 * count :]
+    count = len(faces)
+    state_rims = {(-sa, -sz): incoming(got[k], sa) for k, (sa, sz) in enumerate(faces)}
+    velocity_rims = {
+        (-sa, -sz): incoming(got[count + k], sa) for k, (sa, sz) in enumerate(NEIGHBOURS)
+    }
+    landed = got[count + len(NEIGHBOURS) :]
     whole_pad = assemble(state, state_rims)
     whole_pad = radial_pad(clear_ends(whole_pad, 2, 1), 2, "edge")
     moving = whole_pad[1:]
@@ -488,7 +509,7 @@
     density_rim = 2
     vel_pad = moving[0:3]
     wide_velocity = assemble(velocity, velocity_rims)
-    wide_velocity = radial_pad(clear_ends(wide_velocity, ITERS + 1, 1), 1, "edge")
+    wide_velocity = radial_pad(clear_ends(wide_velocity, rim, 1), 1, "edge")
     padded_pressure, fastest = solve_pressure(wide_velocity, velocity)
     step_size = CFL / (fastest + 1e-06)
     transported = transport(

time: 82.7 us -> 87.7 us (1.060)
  local copies, waits for them, and re-layouts: 11.1 us -> 15.9 us
  other arithmetic: 15.1 us -> 16.7 us
  Pallas kernels: 47.7 us -> 46.3 us
    pallas_call x0 -> x4, local copies, waits for them, and re-layouts: none -> 3.42 us  [neighbour_exchange(): pl.pallas_call(lambda *refs: exchange_kernel(offsets, *refs), out_shape=[...]
    slice x6 -> x5, local copies, waits for them, and re-layouts: 4.18 us -> 2.13 us  [pick(): return lax.slice_in_dim(values, values.shape[dim] - width, None, axis=dim)]
    concatenate x0 -> x3, other arithmetic: none -> 1.79 us  [assemble(): bands.append(jnp.concatenate(row, axis=1))]
    pallas_call x1, Pallas kernels: 17.2 us -> 15.8 us  [neighbour_exchange(): pl.pallas_call(lambda *refs: exchange_kernel(offsets, *refs), out_shape=[...]
    transpose x0 -> x2, local copies, waits for them, and re-layouts: none -> 1.4 us  [outgoing(): return jnp.swapaxes(slab, 1, 2) if sa == 0 else slab]
    select_n x2, other arithmetic: 1.57 us -> 0.44 us  [clear_ends(): return jnp.where(dropped, jnp.float32(0.0), padded)]
    reshape x2, local copies, waits for them, and re-layouts: 0.12 us -> 1.07 us  [on_device(): state[1:6].reshape(5, plane_count, cells_z)]
    select_n x3, other arithmetic: 0.47 us -> 1.4 us  [axial_valid(): return jnp.where(inside, values, jnp.float32(0.0))]
where the time goes in v11:
time: 87.7 us; the launch traced here: 86.1 us
  Pallas kernels  46.3 us (53%)
  other arithmetic  16.7 us (19%)
  local copies, waits for them, and re-layouts  15.9 us (18%)
  matrix products  4.53 us (5%)
  between operations  2.67 us (3%)
    pallas_call x1, Pallas kernels, pressure_coefficients(): pl.pallas_call(lambda *refs: reduce_kernel(groups, shift, half_width, *re...  30.5 us
    pallas_call x1, Pallas kernels, neighbour_exchange(): pl.pallas_call(lambda *refs: exchange_kernel(offsets, *refs), out_shape=[...  15.8 us
    pallas_call x4, local copies, waits for them, and re-layouts, neighbour_exchange(): pl.pallas_call(lambda *refs: exchange_kernel(offsets, *refs), out_shape=[...  3.42 us
    add x1, other arithmetic, solve_pressure(): padded_pressure = padded_pressure + coefficients[j] * padded_basis[j]  2.77 us
    dot_general x1, matrix products, on_device(): jnp.dot(plane_hot, gas_table, precision=HIGHEST)  2.42 us
    slice x2, local copies, waits for them, and re-layouts, radial_pad(): jnp.pad(values, [(0, 0)] * (values.ndim - 1) + [(rim_width, rim_width)],...  2.22 us
    slice x5, local copies, waits for them, and re-layouts, pick(): return lax.slice_in_dim(values, values.shape[dim] - width, None, axis=dim)  2.13 us
    concatenate x3, other arithmetic, assemble(): bands.append(jnp.concatenate(row, axis=1))  1.79 us

profile of v11, /device:TPU:6, one launch (start us, length us, event | category | flops | bytes accessed | tf_op | source)
XLA Modules:
  0.0 86.1 jit_solution(8010987511565348606)
XLA Ops:
  2.0 1.2 %reduce-window.6 = s32[4,16,128]{2,1,0:T(8,128)S(1)} reduce-window(s32[4,16,128]{2,1,0:T(8,128)S(1)} %fusion.130, s32[]{:T(128)} %constant.45.clone.1), window={size=1x1x128 pad=0_0x0_0x127_0}, to_apply=%region_2.3 | reduce-window | flops 1040384 | bytes 65540 | tf_op jit(solution)/shard_map/reduce-window
  3.8 0.7 add_select_fusion.1
  4.7 1.0 %slice_bitcast_fusion = f32[5,64,128]{2,1,0:T(8,128)S(1)} fusion(f32[14,8,8,128]{3,2,1,0:T(8,128)} %param.6), kind=kLoop, calls=%fused_computation.100 | loop fusion | bytes 327680 | tf_op jit(solution)/shard_map/reshape | solution.py:463
  5.8 2.4 %multiply_reduce_fusion = f32[2048,5]{0,1:T(8,128)S(1)} fusion(f32[2048,128]{0,1:T(8,128)S(1)} %fusion.16, s32[2048]{0:T(1024)S(1)} %get-tuple-element.122, f32[8,8,5,128]{3,2,1,0:T(8,128)S(1)} %bitcast.164), kind=kOutput, calls=%fused_computation | convolution fusion | flops 1009375232 | bytes 1261568 | tf_op jit(solution)/shard_map/dot_general | solution.py:473
  8.2 0.8 fusion.3
  9.8 0.7 copy_bitcast_fusion
  13.3 15.8 %shard_map.93 = (f32[14,2,8,128]{3,2,1,0:T(8,128)}, f32[14,2,8,128]{3,2,1,0:T(8,128)}, f32[14,2,8,128]{3,2,1,0:T(8,128)}, f32[14,2,8,128]{3,2,1,0:T(8,128)}, f32...) custom-call(f32[14,2,8,128]{3,2,1,0:T(8,128)} %get-tuple-element.76., ...), custom_call_target="tpu_custom_call" | custom-call | tf_op jit(solution)/shard_map/pallas_call | solution.py:79
  29.1 0.9 %copy.57 = f32[3,5,5,128]{3,1,2,0:T(8,128)S(1)} copy(f32[3,5,5,128]{3,2,1,0:T(8,128)} %get-tuple-element.24) | data formatting | bytes 76800 | tf_op jit(solution)/shard_map/pallas_call | solution.py:79
  29.9 0.8 copy.58
  30.8 0.9 pad_maximum_fusion.9
  31.7 0.8 copy.59
  32.6 0.8 copy.60
  33.4 0.9 pad_maximum_fusion.10
  34.5 1.1 %fusion.132 = (f32[3,18,18,1]{3,2,1,0:T(8,128)S(1)}, f32[3,18,18,1]{3,2,1,0:T(8,128)}) fusion(f32[3,18,18,128]{3,2,1,0:T(8,128)S(1)} %maximum_select_fusion.1), kind=kLoop, calls=%fused_computation.289 | loop fusion | bytes 15552 | tf_op jit(solution)/shard_map/jit(_pad)/slice | solution.py:159
  35.6 1.1 %fusion.59 = f32[16,16,128]{2,1,0:T(8,128)S(1)} fusion(f32[3,18,18,128]{3,2,1,0:T(8,128)S(1)} %maximum_select_fusion.1, f32[3,18,18,1]{3,2,1,0:T(8,128)} %get-tuple-element.63, f32[3,18,18,1]{3,2,1,0:T(8,128)S(1)} %get-tuple-element.62, pred[16]{0:T(512)(128)(4,1)S(1)} %compare_and_fusion.4), kind=kLoop, calls=%fused_computation.106 | loop fusion | flops 294912 | bytes 1986864 | tf_op jit(solution)/shard_map/jit(_where)/select_n | solution.py:404
  39.2 30.5 %shard_map.94 = f32[8,128]{1,0:T(8,128)} custom-call(f32[192,128]{1,0:T(8,128)} %bitcast.163, f32[64,128]{1,0:T(8,128)} %slice_bitcast_fusion.3.refs_1_, f32[64,128]{1,0:T(8,128)} %slice_bitcast_fusion.2.refs_2_, f32[64,128]{1,0:T(8,128)} %get-tuple-element.89.refs_3_, f32[64,128]{1,0:T(8,128)} %get-tuple-element.90.refs_4_, f32[64,128]{1,0:T(8,128)} %get-tuple-element.88.refs_5_), custom_call_target="tpu_custom_call" | custom-call | tf_op jit(solution)/shard_map/pallas_call | solution.py:377
  69.7 1.5 %fusion.139 = (f32[1,1]{1,0:T(1,128)}, f32[1,1]{1,0:T(1,128)}, f32[1,1]{1,0:T(1,128)}, f32[1,1]{1,0:T(1,128)}, f32[1,1]{1,0:T(1,128)}) fusion(f32[8,128]{1,0:T(8,128)} %shard_map.94), kind=kLoop, calls=%fused_computation.296 | loop fusion | bytes 40 | tf_op jit(solution)/shard_map/slice | solution.py:389
  73.7 2.8 %fusion.52 = f32[10,10,130]{2,1,0:T(8,128)S(1)} fusion(f32[10,10,128]{2,1,0:T(8,128)S(1)} %get-tuple-element.86, f32[10,10,128]{2,1,0:T(8,128)S(1)} %get-tuple-element.87, f32[10,10,128]{2,1,0:T(8,128)S(1)} %get-tuple-element.85, f32[10,10,128]{2,1,0:T(8,128)S(1)} %slice.766, f32[]{:T(128)} %bitcast.49, f32[]{:T(128)} %bitcast.48, f32[]{:T(128)} %bitcast.47, ...), kind=kLoop, calls=%fused_computation.96 | loop fusion | flops 91000 | bytes 256816 | tf_op jit(solution)/shard_map/add | solution.py:446
  77.9 1.2 %slice_reduce_fusion = (f32[14,12,12]{2,0,1:T(8,128)S(1)}, f32[14,12,12]{2,0,1:T(8,128)S(1)}) fusion(f32[14,12,12,128]{3,2,0,1:T(8,128)S(1)} %maximum_select_fusion), kind=kLoop, calls=%fused_computation.10 | loop fusion | bytes 32256 | tf_op jit(solution)/shard_map/jit(_pad)/slice | solution.py:159
  80.3 1.1 %pad_maximum_fusion = f32[14,12,12,132]{3,2,0,1:T(8,128)S(1)} fusion(f32[14,12,12,2]{3,2,0,1:T(8,128)S(1)} %reshape.580, f32[14,12,12,128]{3,2,0,1:T(8,128)S(1)} %maximum_select_fusion, f32[14,12,12,2]{3,2,0,1:T(8,128)S(1)} %reshape.579), kind=kLoop, calls=%fused_computation.1 | loop fusion | flops 532224 | bytes 2128896 | tf_op jit(solution)/shard_map/jit(_pad)/concatenate | solution.py:159
  81.5 1.0 %slice_multiply_fusion.2 = (f32[10,12,12,132]{3,2,0,1:T(8,128)S(1)}, f32[10,12,12,132]{3,2,0,1:T(8,128)S(1)}, f32[10,12,12,132]{3,2,0,1:T(8,128)S(1)}) fusion(f32[14,12,12,132]{3,2,0,1:T(8,128)S(1)} %pad_maximum_fusion, f32[12,12,132]{2,1,0:T(8,128)S(1)} %get-tuple-element.58, f32[12,12,132]{2,1,0:T(8,128)S(1)} %get-tuple-element.57, ...), kind=kLoop, calls=%fused_computation.9 | loop fusion | flops 570240 | bytes 3269376 | tf_op jit(solution)/shard_map/mul | solution.py:169
  82.6 1.4 %fusion.25 = f32[10,8,8,128]{3,2,0,1:T(8,128)S(1)} fusion(f32[14,12,12,128]{3,2,0,1:T(8,128)S(1)} %maximum_select_fusion, f32[14,12,12,2]{3,2,0,1:T(8,128)S(1)} %reshape.579, f32[14,12,12,2]{3,2,0,1:T(8,128)S(1)} %reshape.580, f32[10,12,12,132]{3,2,0,1:T(8,128)S(1)} %get-tuple-element.61, f32[10,12,12,132]{3,2,0,1:T(8,128)S(1)} %get-tuple-element.60, ...), kind=kLoop, calls=%fused_computation.36 | loop fusion | flops 4259840 | bytes 10224132 | tf_op jit(solution)/shard_map/add | solution.py:189
  84.0 1.3 %fusion.10 = f32[2,8,8,128]{3,2,0,1:T(8,128)S(1)} fusion(f32[2048,128]{0,1:T(8,128)S(1)} %fusion.16, f32[2048,2]{0,1:T(2,128)S(1)} %maximum_bitcast_fusion.4, s32[8,8]{1,0:T(8,128)S(1)} %multiply_add_fusion.2, s32[2048]{0:T(1024)S(1)} %get-tuple-element.122, f32[10,8,8,128]{3,2,0,1:T(8,128)S(1)} %fusion.25, f32[8,8,128]{2,1,0:T(8,128)S(1)} %slice_bitcast_fusion.4), kind=kOutput, calls=%fused_computation.15 | convolution fusion | flops 403341312 | bytes 1237248 | tf_op jit(solution)/shard_map/dot_general | solution.py:520
  85.3 0.8 copy.63
  (106 shorter events, 12.1 us)
Async XLA Ops:
  4.7 3.5 %copy-start.2 = (f32[8,2048]{1,0:T(8,128)S(1)}, f32[8,2048]{1,0:T(8,128)}, u32[]{:S(2)}) copy-start(f32[8,2048]{1,0:T(8,128)} %param.8) | copy-start | bytes 196612
  5.6 4.1 %copy-start = (f32[14,8,8,128]{3,2,1,0:T(8,128)S(1)}, f32[14,8,8,128]{3,2,1,0:T(8,128)}, u32[]{:S(2)}) copy-start(f32[14,8,8,128]{3,2,1,0:T(8,128)} %param.6) | copy-start | bytes 1376260
  29.0 5.3 %copy-start.7 = (f32[3,5,8,128]{3,2,1,0:T(8,128)S(1)}, f32[3,5,8,128]{3,2,1,0:T(8,128)}, u32[]{:S(2)}) copy-start(f32[3,5,8,128]{3,2,1,0:T(8,128)} %get-tuple-element.28) | copy-start | bytes 184324
  29.1 5.3 %copy-start.8 = (f32[3,5,8,128]{3,2,1,0:T(8,128)S(1)}, f32[3,5,8,128]{3,2,1,0:T(8,128)}, u32[]{:S(2)}) copy-start(f32[3,5,8,128]{3,2,1,0:T(8,128)} %get-tuple-element.27) | copy-start | bytes 184324
  34.4 1.2 %copy-start.1 = (f32[3,8,8,128]{3,2,1,0:T(8,128)}, f32[3,8,8,128]{3,2,1,0:T(8,128)S(1)}, u32[]{:S(2)}) copy-start(f32[3,8,8,128]{3,2,1,0:T(8,128)S(1)} %slice.571) | copy-start | bytes 294916
  36.7 35.2 %copy-start.12 = (f32[14,64]{1,0:T(8,128)S(1)}, f32[14,64]{1,0:T(8,128)}, u32[]{:S(2)}) copy-start(f32[14,64]{1,0:T(8,128)} %get-tuple-element.32) | copy-start | bytes 10756
  36.7 35.3 %copy-start.11 = (f32[14,64]{1,0:T(8,128)S(1)}, f32[14,64]{1,0:T(8,128)}, u32[]{:S(2)}) copy-start(f32[14,64]{1,0:T(8,128)} %get-tuple-element.33) | copy-start | bytes 10756
  36.7 35.3 %copy-start.10 = (f32[14,64]{1,0:T(8,128)S(1)}, f32[14,64]{1,0:T(8,128)}, u32[]{:S(2)}) copy-start(f32[14,64]{1,0:T(8,128)} %get-tuple-element.34) | copy-start | bytes 10756
  36.8 35.4 %copy-start.9 = (f32[14,64]{1,0:T(8,128)S(1)}, f32[14,64]{1,0:T(8,128)}, u32[]{:S(2)}) copy-start(f32[14,64]{1,0:T(8,128)} %get-tuple-element.35) | copy-start | bytes 10756
  37.1 40.2 %copy-start.3 = (f32[14,2,8,128]{3,2,1,0:T(8,128)S(1)}, f32[14,2,8,128]{3,2,1,0:T(8,128)}, u32[]{:S(2)}) copy-start(f32[14,2,8,128]{3,2,1,0:T(8,128)} %get-tuple-element.23) | copy-start | bytes 344068
  37.1 40.2 %copy-start.4 = (f32[14,2,8,128]{3,2,1,0:T(8,128)S(1)}, f32[14,2,8,128]{3,2,1,0:T(8,128)}, u32[]{:S(2)}) copy-start(f32[14,2,8,128]{3,2,1,0:T(8,128)} %get-tuple-element.20) | copy-start | bytes 344068
  38.0 39.6 %copy-start.5 = (f32[14,2,8,128]{3,2,1,0:T(8,128)S(1)}, f32[14,2,8,128]{3,2,1,0:T(8,128)}, u32[]{:S(2)}) copy-start(f32[14,2,8,128]{3,2,1,0:T(8,128)} %get-tuple-element.22) | copy-start | bytes 344068
  38.0 39.6 %copy-start.6 = (f32[14,2,8,128]{3,2,1,0:T(8,128)S(1)}, f32[14,2,8,128]{3,2,1,0:T(8,128)}, u32[]{:S(2)}) copy-start(f32[14,2,8,128]{3,2,1,0:T(8,128)} %get-tuple-element.21) | copy-start | bytes 344068
  81.4 1.1 %copy-start.13 = (f32[10]{0:T(128)S(1)}, f32[10]{0:T(128)}, u32[]{:S(2)}) copy-start(f32[10]{0:T(128)} %param.7) | copy-start | bytes 124

commit v12 on v11

--- a/solution.py
+++ b/solution.py
@@ -105,6 +105,7 @@
 def assemble(block, received):
     rim_a = received[(-1, 0)].shape[1]
     rim_z = received[(0, -1)].shape[2]
+    corner = block.shape[:1] + (rim_a, rim_z) + block.shape[3:]
     bands = []
     for pz in (-1, 0, 1):
         row = []
@@ -114,7 +115,7 @@
             elif (pa, pz) in received:
                 row.append(received[(pa, pz)])
             else:
-                row.append(jnp.zeros(block.shape[:1] + (rim_a, rim_z) + block.shape[3:], block.dtype))
+                row.append(jnp.zeros(corner, block.dtype))
         bands.append(jnp.concatenate(row, axis=1))
     return jnp.concatenate(bands, axis=2)
 
@@ -483,23 +484,14 @@
     )
     parcel_steps = [(-1, 0), (1, 0), (0, -1), (0, 1)]
     faces = [(sa, sz) for sa, sz in NEIGHBOURS if sa == 0 or sz == 0]
-
-    def outgoing(block, width, sa, sz):
-        slab = rim_slab(block, width, sa, sz)
-        return jnp.swapaxes(slab, 1, 2) if sa == 0 else slab
-
-    def incoming(slab, sa):
-        return jnp.swapaxes(slab, 1, 2) if sa == 0 else slab
-
-    rim = ITERS + 1
-    items = [(outgoing(state, 2, sa, sz), (sa, sz)) for sa, sz in faces]
-    items += [(outgoing(velocity, rim, sa, sz), (sa, sz)) for sa, sz in NEIGHBOURS]
+    items = [(rim_slab(state, 2, sa, sz), (sa, sz)) for sa, sz in faces]
+    items += [(rim_slab(velocity, ITERS + 1, sa, sz), (sa, sz)) for sa, sz in NEIGHBOURS]
     items += [(leaving[d], parcel_steps[d]) for d in range(4)]
     got = neighbour_exchange(items)
     count = len(faces)
-    state_rims = {(-sa, -sz): incoming(got[k], sa) for k, (sa, sz) in enumerate(faces)}
+    state_rims = {(-sa, -sz): got[k] for k, (sa, sz) in enumerate(faces)}
     velocity_rims = {
-        (-sa, -sz): incoming(got[count + k], sa) for k, (sa, sz) in enumerate(NEIGHBOURS)
+        (-sa, -sz): got[count + k] for k, (sa, sz) in enumerate(NEIGHBOURS)
     }
     landed = got[count + len(NEIGHBOURS) :]
     whole_pad = assemble(state, state_rims)
@@ -509,7 +501,7 @@
     density_rim = 2
     vel_pad = moving[0:3]
     wide_velocity = assemble(velocity, velocity_rims)
-    wide_velocity = radial_pad(clear_ends(wide_velocity, rim, 1), 1, "edge")
+    wide_velocity = radial_pad(clear_ends(wide_velocity, ITERS + 1, 1), 1, "edge")
     padded_pressure, fastest = solve_pressure(wide_velocity, velocity)
     step_size = CFL / (fastest + 1e-06)
     transported = transport(

time: 87.7 us -> 82.1 us (0.936)
  local copies, waits for them, and re-layouts: 15.9 us -> 11.2 us
    pallas_call x4 -> x0, local copies, waits for them, and re-layouts: 3.42 us -> none  [neighbour_exchange(): pl.pallas_call(lambda *refs: exchange_kernel(offsets, *refs), out_shape=[...]
    concatenate x3 -> x0, other arithmetic: 1.79 us -> none  [assemble(): bands.append(jnp.concatenate(row, axis=1))]
    transpose x2 -> x0, local copies, waits for them, and re-layouts: 1.4 us -> none  [outgoing(): return jnp.swapaxes(slab, 1, 2) if sa == 0 else slab]
    slice x5, local copies, waits for them, and re-layouts: 2.13 us -> 3.5 us  [pick(): return lax.slice_in_dim(values, values.shape[dim] - width, None, axis=dim)]
    select_n x2, other arithmetic: 0.44 us -> 1.55 us  [clear_ends(): return jnp.where(dropped, jnp.float32(0.0), padded)]
    reshape x2, local copies, waits for them, and re-layouts: 1.07 us -> 0.12 us  [on_device(): state[1:6].reshape(5, plane_count, cells_z)]
where the time goes in v12:
time: 82.1 us; the launch traced here: 80.7 us
  Pallas kernels  46.4 us (57%)
  other arithmetic  16 us (19%)
  local copies, waits for them, and re-layouts  11.2 us (14%)
  matrix products  4.53 us (6%)
  between operations  2.65 us (3%)
    pallas_call x1, Pallas kernels, pressure_coefficients(): pl.pallas_call(lambda *refs: reduce_kernel(groups, shift, half_width, *re...  30.5 us
    pallas_call x1, Pallas kernels, neighbour_exchange(): pl.pallas_call(lambda *refs: exchange_kernel(offsets, *refs), out_shape=[...  15.9 us
    slice x5, local copies, waits for them, and re-layouts, pick(): return lax.slice_in_dim(values, values.shape[dim] - width, None, axis=dim)  3.5 us
    add x1, other arithmetic, solve_pressure(): padded_pressure = padded_pressure + coefficients[j] * padded_basis[j]  2.71 us
    dot_general x1, matrix products, on_device(): jnp.dot(plane_hot, gas_table, precision=HIGHEST)  2.42 us
    slice x2, local copies, waits for them, and re-layouts, radial_pad(): jnp.pad(values, [(0, 0)] * (values.ndim - 1) + [(rim_width, rim_width)],...  2.21 us

profile of v12, /device:TPU:6, one launch (start us, length us, event | category | flops | bytes accessed | tf_op | source)
XLA Modules:
  0.0 80.7 jit_solution(16124788461762434769)
XLA Ops:
  1.3 0.7 broadcast_compare_fusion
  2.1 1.2 %reduce-window.6 = s32[4,16,128]{2,1,0:T(8,128)S(1)} reduce-window(s32[4,16,128]{2,1,0:T(8,128)S(1)} %fusion.130, s32[]{:T(128)} %constant.45.clone.1), window={size=1x1x128 pad=0_0x0_0x127_0}, to_apply=%region_2.3 | reduce-window | flops 1040384 | bytes 65540 | tf_op jit(solution)/shard_map/reduce-window
  3.9 0.7 add_select_fusion.1
  4.9 2.4 %multiply_reduce_fusion = f32[2048,5]{0,1:T(8,128)S(1)} fusion(f32[2048,128]{0,1:T(8,128)S(1)} %fusion.16, s32[2048]{0:T(1024)S(1)} %get-tuple-element.120, f32[8,8,5,128]{3,2,1,0:T(8,128)S(1)} %bitcast.152), kind=kOutput, calls=%fused_computation | convolution fusion | flops 1009375232 | bytes 1261568 | tf_op jit(solution)/shard_map/dot_general | solution.py:474
  7.3 0.8 %fusion.3 = f32[14,256]{1,0:T(8,128)S(1)} fusion(s32[2048]{0:T(1024)S(1)} %bitcast_select_fusion, f32[1,2048]{1,0:T(1,128)S(1)} %fusion.106, f32[5,2048]{1,0:T(8,128)S(1)} %bitcast.154, f32[8,2048]{1,0:T(8,128)S(1)} %copy-done.2), kind=kOutput, calls=%fused_computation.6 | convolution fusion | flops 88662016 | bytes 137216 | tf_op jit(solution)/shard_map/dot_general | solution.py:483
  8.9 0.7 fusion.133
  9.5 0.7 fusion.136
  10.3 0.8 fusion.137
  11.0 0.7 fusion.135
  12.4 15.9 %shard_map.93 = (f32[14,2,8,128]{3,2,1,0:T(8,128)}, f32[14,8,2,128]{3,2,1,0:T(2,128)}, f32[14,8,2,128]{3,2,1,0:T(2,128)}, f32[14,2,8,128]{3,2,1,0:T(8,128)}, f32...) custom-call(f32[14,2,8,128]{3,2,1,0:T(8,128)} %get-tuple-element.76., ...), custom_call_target="tpu_custom_call" | custom-call | tf_op jit(solution)/shard_map/pallas_call | solution.py:79
  28.3 1.3 %maximum_select_fusion = f32[3,18,18,128]{3,2,1,0:T(8,128)S(1)} fusion(f32[3,5,5,128]{3,2,1,0:T(8,128)} %get-tuple-element.31, f32[3,8,5,128]{3,2,1,0:T(8,128)} %get-tuple-element.30, f32[3,5,5,128]{3,2,1,0:T(8,128)} %get-tuple-element.29, f32[3,5,8,128]{3,2,1,0:T(8,128)} %get-tuple-element.28, f32[3,8,8,128]{3,2,1,0:T(8,128)S(1)} %slice.571, ...), kind=kLoop, calls=%fused_computation.22 | loop fusion | flops 1119744 | bytes 995346 | tf_op jit(solution)/shard_map/jit(_where)/select_n | solution.py:156
  29.6 1.0 %fusion.132 = (f32[3,18,18,1]{3,2,1,0:T(8,128)S(1)}, f32[3,18,18,1]{3,2,1,0:T(8,128)}) fusion(f32[3,18,18,128]{3,2,1,0:T(8,128)S(1)} %maximum_select_fusion), kind=kLoop, calls=%fused_computation.279 | loop fusion | bytes 15552 | tf_op jit(solution)/shard_map/jit(_pad)/slice | solution.py:160
  30.6 1.1 %fusion.59 = f32[16,16,128]{2,1,0:T(8,128)S(1)} fusion(f32[3,18,18,128]{3,2,1,0:T(8,128)S(1)} %maximum_select_fusion, f32[3,18,18,1]{3,2,1,0:T(8,128)} %get-tuple-element.63, f32[3,18,18,1]{3,2,1,0:T(8,128)S(1)} %get-tuple-element.62, pred[16]{0:T(512)(128)(4,1)S(1)} %compare_and_fusion.4), kind=kLoop, calls=%fused_computation.100 | loop fusion | flops 294912 | bytes 1986864 | tf_op jit(solution)/shard_map/jit(_where)/select_n | solution.py:405
  32.3 0.7 fusion.86
  34.3 30.5 %shard_map.94 = f32[8,128]{1,0:T(8,128)} custom-call(f32[192,128]{1,0:T(8,128)} %bitcast.151, f32[64,128]{1,0:T(8,128)} %slice_bitcast_fusion.3.refs_1_, f32[64,128]{1,0:T(8,128)} %slice_bitcast_fusion.2.refs_2_, f32[64,128]{1,0:T(8,128)} %get-tuple-element.89.refs_3_, f32[64,128]{1,0:T(8,128)} %get-tuple-element.90.refs_4_, f32[64,128]{1,0:T(8,128)} %get-tuple-element.88.refs_5_), custom_call_target="tpu_custom_call" | custom-call | tf_op jit(solution)/shard_map/pallas_call | solution.py:378
  64.8 1.5 %fusion.139 = (f32[1,1]{1,0:T(1,128)}, f32[1,1]{1,0:T(1,128)}, f32[1,1]{1,0:T(1,128)}, f32[1,1]{1,0:T(1,128)}, f32[1,1]{1,0:T(1,128)}) fusion(f32[8,128]{1,0:T(8,128)} %shard_map.94), kind=kLoop, calls=%fused_computation.286 | loop fusion | bytes 40 | tf_op jit(solution)/shard_map/slice | solution.py:390
  68.0 0.7 fusion.80
  68.7 2.7 %fusion.52 = f32[10,10,130]{2,1,0:T(8,128)S(1)} fusion(f32[10,10,128]{2,1,0:T(8,128)S(1)} %get-tuple-element.86, f32[10,10,128]{2,1,0:T(8,128)S(1)} %get-tuple-element.87, f32[10,10,128]{2,1,0:T(8,128)S(1)} %get-tuple-element.85, f32[10,10,128]{2,1,0:T(8,128)S(1)} %slice.766, f32[]{:T(128)} %bitcast.41, f32[]{:T(128)} %bitcast.40, f32[]{:T(128)} %bitcast.39, ...), kind=kLoop, calls=%fused_computation.90 | loop fusion | flops 91000 | bytes 256816 | tf_op jit(solution)/shard_map/add | solution.py:447
  72.6 1.2 %slice_reduce_fusion = (f32[14,12,12]{2,0,1:T(8,128)S(1)}, f32[14,12,12]{2,0,1:T(8,128)S(1)}) fusion(f32[14,12,12,128]{3,2,0,1:T(8,128)S(1)} %copy_select_fusion), kind=kLoop, calls=%fused_computation.10 | loop fusion | bytes 32256 | tf_op jit(solution)/shard_map/jit(_pad)/slice | solution.py:160
  75.0 1.1 %pad_maximum_fusion = f32[14,12,12,132]{3,2,0,1:T(8,128)S(1)} fusion(f32[14,12,12,2]{3,2,0,1:T(8,128)S(1)} %reshape.580, f32[14,12,12,128]{3,2,0,1:T(8,128)S(1)} %copy_select_fusion, f32[14,12,12,2]{3,2,0,1:T(8,128)S(1)} %reshape.579), kind=kLoop, calls=%fused_computation.1 | loop fusion | flops 532224 | bytes 2128896 | tf_op jit(solution)/shard_map/jit(_pad)/concatenate | solution.py:160
  76.1 1.0 %slice_multiply_fusion.2 = (f32[10,12,12,132]{3,2,0,1:T(8,128)S(1)}, f32[10,12,12,132]{3,2,0,1:T(8,128)S(1)}, f32[10,12,12,132]{3,2,0,1:T(8,128)S(1)}) fusion(f32[14,12,12,132]{3,2,0,1:T(8,128)S(1)} %pad_maximum_fusion, f32[12,12,132]{2,1,0:T(8,128)S(1)} %get-tuple-element.58, f32[12,12,132]{2,1,0:T(8,128)S(1)} %get-tuple-element.57, ...), kind=kLoop, calls=%fused_computation.9 | loop fusion | flops 570240 | bytes 3269376 | tf_op jit(solution)/shard_map/mul | solution.py:170
  77.2 1.4 %fusion.25 = f32[10,8,8,128]{3,2,0,1:T(8,128)S(1)} fusion(f32[14,12,12,128]{3,2,0,1:T(8,128)S(1)} %copy_select_fusion, f32[14,12,12,2]{3,2,0,1:T(8,128)S(1)} %reshape.579, f32[14,12,12,2]{3,2,0,1:T(8,128)S(1)} %reshape.580, f32[10,12,12,132]{3,2,0,1:T(8,128)S(1)} %get-tuple-element.61, f32[10,12,12,132]{3,2,0,1:T(8,128)S(1)} %get-tuple-element.60, ...), kind=kLoop, calls=%fused_computation.32 | loop fusion | flops 4259840 | bytes 10224132 | tf_op jit(solution)/shard_map/add | solution.py:190
  78.6 1.3 %fusion.10 = f32[2,8,8,128]{3,2,0,1:T(8,128)S(1)} fusion(f32[2048,128]{0,1:T(8,128)S(1)} %fusion.16, f32[2048,2]{0,1:T(2,128)S(1)} %maximum_bitcast_fusion.4, s32[8,8]{1,0:T(8,128)S(1)} %multiply_add_fusion.2, s32[2048]{0:T(1024)S(1)} %get-tuple-element.120, f32[10,8,8,128]{3,2,0,1:T(8,128)S(1)} %fusion.25, f32[8,8,128]{2,1,0:T(8,128)S(1)} %slice_bitcast_fusion.4), kind=kOutput, calls=%fused_computation.16 | convolution fusion | flops 403341312 | bytes 1237248 | tf_op jit(solution)/shard_map/dot_general | solution.py:512
  80.0 0.8 copy.33
  (89 shorter events, 7.4 us)
Async XLA Ops:
  0.6 4.1 %copy-start = (f32[14,8,8,128]{3,2,1,0:T(8,128)S(1)}, f32[14,8,8,128]{3,2,1,0:T(8,128)}, u32[]{:S(2)}) copy-start(f32[14,8,8,128]{3,2,1,0:T(8,128)} %param.6) | copy-start | bytes 1376260
  4.9 2.5 %copy-start.2 = (f32[8,2048]{1,0:T(8,128)S(1)}, f32[8,2048]{1,0:T(8,128)}, u32[]{:S(2)}) copy-start(f32[8,2048]{1,0:T(8,128)} %param.8) | copy-start | bytes 196612
  28.3 2.3 %copy-start.1 = (f32[3,8,8,128]{3,2,1,0:T(8,128)}, f32[3,8,8,128]{3,2,1,0:T(8,128)S(1)}, u32[]{:S(2)}) copy-start(f32[3,8,8,128]{3,2,1,0:T(8,128)S(1)} %slice.571) | copy-start | bytes 294916
  31.8 35.2 %copy-start.10 = (f32[14,64]{1,0:T(8,128)S(1)}, f32[14,64]{1,0:T(8,128)}, u32[]{:S(2)}) copy-start(f32[14,64]{1,0:T(8,128)} %get-tuple-element.32) | copy-start | bytes 10756
  31.9 35.1 %copy-start.9 = (f32[14,64]{1,0:T(8,128)S(1)}, f32[14,64]{1,0:T(8,128)}, u32[]{:S(2)}) copy-start(f32[14,64]{1,0:T(8,128)} %get-tuple-element.33) | copy-start | bytes 10756
  31.9 35.2 %copy-start.8 = (f32[14,64]{1,0:T(8,128)S(1)}, f32[14,64]{1,0:T(8,128)}, u32[]{:S(2)}) copy-start(f32[14,64]{1,0:T(8,128)} %get-tuple-element.34) | copy-start | bytes 10756
  32.0 35.2 %copy-start.7 = (f32[14,64]{1,0:T(8,128)S(1)}, f32[14,64]{1,0:T(8,128)}, u32[]{:S(2)}) copy-start(f32[14,64]{1,0:T(8,128)} %get-tuple-element.35) | copy-start | bytes 10756
  32.3 40.0 %copy-start.3 = (f32[14,2,8,128]{3,2,1,0:T(8,128)S(1)}, f32[14,2,8,128]{3,2,1,0:T(8,128)}, u32[]{:S(2)}) copy-start(f32[14,2,8,128]{3,2,1,0:T(8,128)} %get-tuple-element.22) | copy-start | bytes 344068
  32.3 40.0 %copy-start.4 = (f32[14,8,2,128]{3,2,1,0:T(2,128)S(1)}, f32[14,8,2,128]{3,2,1,0:T(2,128)}, u32[]{:S(2)}) copy-start(f32[14,8,2,128]{3,2,1,0:T(2,128)} %get-tuple-element.23) | copy-start | bytes 344068
  32.3 40.0 %copy-start.5 = (f32[14,8,2,128]{3,2,1,0:T(2,128)S(1)}, f32[14,8,2,128]{3,2,1,0:T(2,128)}, u32[]{:S(2)}) copy-start(f32[14,8,2,128]{3,2,1,0:T(2,128)} %get-tuple-element.20) | copy-start | bytes 344068
  32.3 40.0 %copy-start.6 = (f32[14,2,8,128]{3,2,1,0:T(8,128)S(1)}, f32[14,2,8,128]{3,2,1,0:T(8,128)}, u32[]{:S(2)}) copy-start(f32[14,2,8,128]{3,2,1,0:T(8,128)} %get-tuple-element.21) | copy-start | bytes 344068
  76.1 1.1 %copy-start.11 = (f32[10]{0:T(128)S(1)}, f32[10]{0:T(128)}, u32[]{:S(2)}) copy-start(f32[10]{0:T(128)} %param.7) | copy-start | bytes 124

commit v13 on v12

--- a/solution.py
+++ b/solution.py
@@ -37,8 +37,7 @@
     count = len(offsets)
     sources = refs[:count]
     outs = refs[count : 2 * count]
-    landing = refs[2 * count : 3 * count]
-    send_sems, recv_sems = refs[3 * count :]
+    send_sems, recv_sems = refs[2 * count :]
     axial = lax.axis_index("axial")
     azim = lax.axis_index("azim")
 
@@ -59,7 +58,7 @@
     for k, step in enumerate(offsets):
         copy = pltpu.make_async_remote_copy(
             src_ref=sources[k],
-            dst_ref=landing[k],
+            dst_ref=outs[k],
             send_sem=send_sems.at[k],
             recv_sem=recv_sems.at[k],
             device_id=device(*step),
@@ -67,9 +66,8 @@
         )
         copy.start()
         copies.append(copy)
-    for k, copy in enumerate(copies):
+    for copy in copies:
         copy.wait()
-        outs[k][...] = landing[k][...]
 
 
 def neighbour_exchange(items):
@@ -79,10 +77,9 @@
     outs = pl.pallas_call(
         lambda *refs: exchange_kernel(offsets, *refs),
         out_shape=[jax.ShapeDtypeStruct(f.shape, f.dtype) for f in flat],
-        in_specs=[pl.BlockSpec(memory_space=pltpu.VMEM)] * count,
-        out_specs=[pl.BlockSpec(memory_space=pltpu.VMEM)] * count,
-        scratch_shapes=[pltpu.VMEM(f.shape, f.dtype) for f in flat]
-        + [pltpu.SemaphoreType.DMA((count,)), pltpu.SemaphoreType.DMA((count,))],
+        in_specs=[pl.BlockSpec(memory_space=pl.ANY)] * count,
+        out_specs=[pl.BlockSpec(memory_space=pl.ANY)] * count,
+        scratch_shapes=[pltpu.SemaphoreType.DMA((count,)), pltpu.SemaphoreType.DMA((count,))],
         compiler_params=pltpu.CompilerParams(collective_id=1, has_side_effects=True),
     )(*flat)
     return list(outs)

time: 82.1 us -> 80.2 us (0.977)
  Pallas kernels: 46.4 us -> 44.5 us
    pallas_call x1, Pallas kernels: 15.9 us -> 13.9 us  [neighbour_exchange(): pl.pallas_call(lambda *refs: exchange_kernel(offsets, *refs), out_shape=[...]
where the time goes in v13:
time: 80.2 us; the launch traced here: 78.8 us
  Pallas kernels  44.5 us (55%)
  other arithmetic  16 us (20%)
  local copies, waits for them, and re-layouts  11.2 us (14%)
  matrix products  4.53 us (6%)
  between operations  2.65 us (3%)
    pallas_call x1, Pallas kernels, pressure_coefficients(): pl.pallas_call(lambda *refs: reduce_kernel(groups, shift, half_width, *re...  30.5 us
    pallas_call x1, Pallas kernels, neighbour_exchange(): pl.pallas_call(lambda *refs: exchange_kernel(offsets, *refs), out_shape=[...  13.9 us
    slice x5, local copies, waits for them, and re-layouts, pick(): return lax.slice_in_dim(values, values.shape[dim] - width, None, axis=dim)  3.5 us
    add x1, other arithmetic, solve_pressure(): padded_pressure = padded_pressure + coefficients[j] * padded_basis[j]  2.71 us
    dot_general x1, matrix products, on_device(): jnp.dot(plane_hot, gas_table, precision=HIGHEST)  2.42 us
    slice x2, local copies, waits for them, and re-layouts, radial_pad(): jnp.pad(values, [(0, 0)] * (values.ndim - 1) + [(rim_width, rim_width)],...  2.21 us

profile of v13, /device:TPU:6, one launch (start us, length us, event | category | flops | bytes accessed | tf_op | source)
XLA Modules:
  0.0 78.8 jit_solution(10850386438118584658)
XLA Ops:
  1.3 0.7 broadcast_compare_fusion
  2.1 1.2 %reduce-window.6 = s32[4,16,128]{2,1,0:T(8,128)S(1)} reduce-window(s32[4,16,128]{2,1,0:T(8,128)S(1)} %fusion.130, s32[]{:T(128)} %constant.45.clone.1), window={size=1x1x128 pad=0_0x0_0x127_0}, to_apply=%region_2.3 | reduce-window | flops 1040384 | bytes 65540 | tf_op jit(solution)/shard_map/reduce-window
  3.9 0.7 add_select_fusion.1
  4.9 2.4 %multiply_reduce_fusion = f32[2048,5]{0,1:T(8,128)S(1)} fusion(f32[2048,128]{0,1:T(8,128)S(1)} %fusion.16, s32[2048]{0:T(1024)S(1)} %get-tuple-element.120, f32[8,8,5,128]{3,2,1,0:T(8,128)S(1)} %bitcast.152), kind=kOutput, calls=%fused_computation | convolution fusion | flops 1009375232 | bytes 1261568 | tf_op jit(solution)/shard_map/dot_general | solution.py:471
  7.3 0.8 %fusion.3 = f32[14,256]{1,0:T(8,128)S(1)} fusion(s32[2048]{0:T(1024)S(1)} %bitcast_select_fusion, f32[1,2048]{1,0:T(1,128)S(1)} %fusion.106, f32[5,2048]{1,0:T(8,128)S(1)} %bitcast.154, f32[8,2048]{1,0:T(8,128)S(1)} %copy-done.2), kind=kOutput, calls=%fused_computation.6 | convolution fusion | flops 88662016 | bytes 137216 | tf_op jit(solution)/shard_map/dot_general | solution.py:480
  8.9 0.7 fusion.133
  9.5 0.7 fusion.136
  10.3 0.8 fusion.137
  11.0 0.7 fusion.135
  12.4 13.9 %shard_map.93 = (f32[14,2,8,128]{3,2,1,0:T(8,128)}, f32[14,8,2,128]{3,2,1,0:T(2,128)}, f32[14,8,2,128]{3,2,1,0:T(2,128)}, f32[14,2,8,128]{3,2,1,0:T(8,128)}, f32...) custom-call(f32[14,2,8,128]{3,2,1,0:T(8,128)} %get-tuple-element.76., ...), custom_call_target="tpu_custom_call" | custom-call | tf_op jit(solution)/shard_map/pallas_call | solution.py:77
  26.3 1.3 %maximum_select_fusion = f32[3,18,18,128]{3,2,1,0:T(8,128)S(1)} fusion(f32[3,5,5,128]{3,2,1,0:T(8,128)} %get-tuple-element.31, f32[3,8,5,128]{3,2,1,0:T(8,128)} %get-tuple-element.30, f32[3,5,5,128]{3,2,1,0:T(8,128)} %get-tuple-element.29, f32[3,5,8,128]{3,2,1,0:T(8,128)} %get-tuple-element.28, f32[3,8,8,128]{3,2,1,0:T(8,128)S(1)} %slice.571, ...), kind=kLoop, calls=%fused_computation.22 | loop fusion | flops 1119744 | bytes 995346 | tf_op jit(solution)/shard_map/jit(_where)/select_n | solution.py:153
  27.6 1.0 %fusion.132 = (f32[3,18,18,1]{3,2,1,0:T(8,128)S(1)}, f32[3,18,18,1]{3,2,1,0:T(8,128)}) fusion(f32[3,18,18,128]{3,2,1,0:T(8,128)S(1)} %maximum_select_fusion), kind=kLoop, calls=%fused_computation.279 | loop fusion | bytes 15552 | tf_op jit(solution)/shard_map/jit(_pad)/slice | solution.py:157
  28.7 1.1 %fusion.59 = f32[16,16,128]{2,1,0:T(8,128)S(1)} fusion(f32[3,18,18,128]{3,2,1,0:T(8,128)S(1)} %maximum_select_fusion, f32[3,18,18,1]{3,2,1,0:T(8,128)} %get-tuple-element.63, f32[3,18,18,1]{3,2,1,0:T(8,128)S(1)} %get-tuple-element.62, pred[16]{0:T(512)(128)(4,1)S(1)} %compare_and_fusion.4), kind=kLoop, calls=%fused_computation.100 | loop fusion | flops 294912 | bytes 1986864 | tf_op jit(solution)/shard_map/jit(_where)/select_n | solution.py:402
  30.3 0.7 fusion.86
  32.3 30.5 %shard_map.94 = f32[8,128]{1,0:T(8,128)} custom-call(f32[192,128]{1,0:T(8,128)} %bitcast.151, f32[64,128]{1,0:T(8,128)} %slice_bitcast_fusion.3.refs_1_, f32[64,128]{1,0:T(8,128)} %slice_bitcast_fusion.2.refs_2_, f32[64,128]{1,0:T(8,128)} %get-tuple-element.89.refs_3_, f32[64,128]{1,0:T(8,128)} %get-tuple-element.90.refs_4_, f32[64,128]{1,0:T(8,128)} %get-tuple-element.88.refs_5_), custom_call_target="tpu_custom_call" | custom-call | tf_op jit(solution)/shard_map/pallas_call | solution.py:375
  62.8 1.5 %fusion.139 = (f32[1,1]{1,0:T(1,128)}, f32[1,1]{1,0:T(1,128)}, f32[1,1]{1,0:T(1,128)}, f32[1,1]{1,0:T(1,128)}, f32[1,1]{1,0:T(1,128)}) fusion(f32[8,128]{1,0:T(8,128)} %shard_map.94), kind=kLoop, calls=%fused_computation.286 | loop fusion | bytes 40 | tf_op jit(solution)/shard_map/slice | solution.py:387
  66.1 0.7 fusion.80
  66.7 2.7 %fusion.52 = f32[10,10,130]{2,1,0:T(8,128)S(1)} fusion(f32[10,10,128]{2,1,0:T(8,128)S(1)} %get-tuple-element.86, f32[10,10,128]{2,1,0:T(8,128)S(1)} %get-tuple-element.87, f32[10,10,128]{2,1,0:T(8,128)S(1)} %get-tuple-element.85, f32[10,10,128]{2,1,0:T(8,128)S(1)} %slice.766, f32[]{:T(128)} %bitcast.41, f32[]{:T(128)} %bitcast.40, f32[]{:T(128)} %bitcast.39, ...), kind=kLoop, calls=%fused_computation.90 | loop fusion | flops 91000 | bytes 256816 | tf_op jit(solution)/shard_map/add | solution.py:444
  70.6 1.2 %slice_reduce_fusion = (f32[14,12,12]{2,0,1:T(8,128)S(1)}, f32[14,12,12]{2,0,1:T(8,128)S(1)}) fusion(f32[14,12,12,128]{3,2,0,1:T(8,128)S(1)} %copy_select_fusion), kind=kLoop, calls=%fused_computation.10 | loop fusion | bytes 32256 | tf_op jit(solution)/shard_map/jit(_pad)/slice | solution.py:157
  73.0 1.1 %pad_maximum_fusion = f32[14,12,12,132]{3,2,0,1:T(8,128)S(1)} fusion(f32[14,12,12,2]{3,2,0,1:T(8,128)S(1)} %reshape.580, f32[14,12,12,128]{3,2,0,1:T(8,128)S(1)} %copy_select_fusion, f32[14,12,12,2]{3,2,0,1:T(8,128)S(1)} %reshape.579), kind=kLoop, calls=%fused_computation.1 | loop fusion | flops 532224 | bytes 2128896 | tf_op jit(solution)/shard_map/jit(_pad)/concatenate | solution.py:157
  74.2 1.0 %slice_multiply_fusion.2 = (f32[10,12,12,132]{3,2,0,1:T(8,128)S(1)}, f32[10,12,12,132]{3,2,0,1:T(8,128)S(1)}, f32[10,12,12,132]{3,2,0,1:T(8,128)S(1)}) fusion(f32[14,12,12,132]{3,2,0,1:T(8,128)S(1)} %pad_maximum_fusion, f32[12,12,132]{2,1,0:T(8,128)S(1)} %get-tuple-element.58, f32[12,12,132]{2,1,0:T(8,128)S(1)} %get-tuple-element.57, ...), kind=kLoop, calls=%fused_computation.9 | loop fusion | flops 570240 | bytes 3269376 | tf_op jit(solution)/shard_map/mul | solution.py:167
  75.3 1.4 %fusion.25 = f32[10,8,8,128]{3,2,0,1:T(8,128)S(1)} fusion(f32[14,12,12,128]{3,2,0,1:T(8,128)S(1)} %copy_select_fusion, f32[14,12,12,2]{3,2,0,1:T(8,128)S(1)} %reshape.579, f32[14,12,12,2]{3,2,0,1:T(8,128)S(1)} %reshape.580, f32[10,12,12,132]{3,2,0,1:T(8,128)S(1)} %get-tuple-element.61, f32[10,12,12,132]{3,2,0,1:T(8,128)S(1)} %get-tuple-element.60, ...), kind=kLoop, calls=%fused_computation.32 | loop fusion | flops 4259840 | bytes 10224132 | tf_op jit(solution)/shard_map/add | solution.py:187
  76.7 1.3 %fusion.10 = f32[2,8,8,128]{3,2,0,1:T(8,128)S(1)} fusion(f32[2048,128]{0,1:T(8,128)S(1)} %fusion.16, f32[2048,2]{0,1:T(2,128)S(1)} %maximum_bitcast_fusion.4, s32[8,8]{1,0:T(8,128)S(1)} %multiply_add_fusion.2, s32[2048]{0:T(1024)S(1)} %get-tuple-element.120, f32[10,8,8,128]{3,2,0,1:T(8,128)S(1)} %fusion.25, f32[8,8,128]{2,1,0:T(8,128)S(1)} %slice_bitcast_fusion.4), kind=kOutput, calls=%fused_computation.16 | convolution fusion | flops 403341312 | bytes 1237248 | tf_op jit(solution)/shard_map/dot_general | solution.py:509
  78.1 0.8 copy.33
  (89 shorter events, 7.4 us)
Async XLA Ops:
  0.6 4.1 %copy-start = (f32[14,8,8,128]{3,2,1,0:T(8,128)S(1)}, f32[14,8,8,128]{3,2,1,0:T(8,128)}, u32[]{:S(2)}) copy-start(f32[14,8,8,128]{3,2,1,0:T(8,128)} %param.6) | copy-start | bytes 1376260
  4.9 2.5 %copy-start.2 = (f32[8,2048]{1,0:T(8,128)S(1)}, f32[8,2048]{1,0:T(8,128)}, u32[]{:S(2)}) copy-start(f32[8,2048]{1,0:T(8,128)} %param.8) | copy-start | bytes 196612
  26.3 2.3 %copy-start.1 = (f32[3,8,8,128]{3,2,1,0:T(8,128)}, f32[3,8,8,128]{3,2,1,0:T(8,128)S(1)}, u32[]{:S(2)}) copy-start(f32[3,8,8,128]{3,2,1,0:T(8,128)S(1)} %slice.571) | copy-start | bytes 294916
  29.8 35.2 %copy-start.10 = (f32[14,64]{1,0:T(8,128)S(1)}, f32[14,64]{1,0:T(8,128)}, u32[]{:S(2)}) copy-start(f32[14,64]{1,0:T(8,128)} %get-tuple-element.32) | copy-start | bytes 10756
  30.0 35.1 %copy-start.9 = (f32[14,64]{1,0:T(8,128)S(1)}, f32[14,64]{1,0:T(8,128)}, u32[]{:S(2)}) copy-start(f32[14,64]{1,0:T(8,128)} %get-tuple-element.33) | copy-start | bytes 10756
  30.0 35.2 %copy-start.8 = (f32[14,64]{1,0:T(8,128)S(1)}, f32[14,64]{1,0:T(8,128)}, u32[]{:S(2)}) copy-start(f32[14,64]{1,0:T(8,128)} %get-tuple-element.34) | copy-start | bytes 10756
  30.0 35.3 %copy-start.7 = (f32[14,64]{1,0:T(8,128)S(1)}, f32[14,64]{1,0:T(8,128)}, u32[]{:S(2)}) copy-start(f32[14,64]{1,0:T(8,128)} %get-tuple-element.35) | copy-start | bytes 10756
  30.3 40.0 %copy-start.3 = (f32[14,2,8,128]{3,2,1,0:T(8,128)S(1)}, f32[14,2,8,128]{3,2,1,0:T(8,128)}, u32[]{:S(2)}) copy-start(f32[14,2,8,128]{3,2,1,0:T(8,128)} %get-tuple-element.22) | copy-start | bytes 344068
  30.3 40.0 %copy-start.4 = (f32[14,8,2,128]{3,2,1,0:T(2,128)S(1)}, f32[14,8,2,128]{3,2,1,0:T(2,128)}, u32[]{:S(2)}) copy-start(f32[14,8,2,128]{3,2,1,0:T(2,128)} %get-tuple-element.23) | copy-start | bytes 344068
  30.3 40.0 %copy-start.5 = (f32[14,8,2,128]{3,2,1,0:T(2,128)S(1)}, f32[14,8,2,128]{3,2,1,0:T(2,128)}, u32[]{:S(2)}) copy-start(f32[14,8,2,128]{3,2,1,0:T(2,128)} %get-tuple-element.20) | copy-start | bytes 344068
  30.3 40.0 %copy-start.6 = (f32[14,2,8,128]{3,2,1,0:T(8,128)S(1)}, f32[14,2,8,128]{3,2,1,0:T(8,128)}, u32[]{:S(2)}) copy-start(f32[14,2,8,128]{3,2,1,0:T(8,128)} %get-tuple-element.21) | copy-start | bytes 344068
  74.2 1.1 %copy-start.11 = (f32[10]{0:T(128)S(1)}, f32[10]{0:T(128)}, u32[]{:S(2)}) copy-start(f32[10]{0:T(128)} %param.7) | copy-start | bytes 124

commit v14 on v13

--- a/solution.py
+++ b/solution.py
@@ -47,13 +47,36 @@
             (azim + step_azim + lax.axis_size("azim")) % lax.axis_size("azim"),
         )
 
+    has_low = axial > 0
+    has_high = axial < lax.axis_size("axial") - 1
+
+    def reachable(step_axial):
+        if step_axial < 0:
+            return has_low
+        if step_axial > 0:
+            return has_high
+        return None
+
+    def guarded(condition, action):
+        if condition is None:
+            action()
+        else:
+            pl.when(condition)(action)
+
     neighbours = sorted(set(offsets))
     barrier = pltpu.get_barrier_semaphore()
+    expected = 0
     for step in neighbours:
-        pl.semaphore_signal(
-            barrier, inc=1, device_id=device(*step), device_id_type=pl.DeviceIdType.MESH
-        )
-    pl.semaphore_wait(barrier, len(neighbours))
+
+        def greet(step=step):
+            pl.semaphore_signal(
+                barrier, inc=1, device_id=device(*step), device_id_type=pl.DeviceIdType.MESH
+            )
+
+        guarded(reachable(step[0]), greet)
+        condition = reachable(-step[0])
+        expected = expected + (1 if condition is None else condition.astype(jnp.int32))
+    pl.semaphore_wait(barrier, expected)
     copies = []
     for k, step in enumerate(offsets):
         copy = pltpu.make_async_remote_copy(
@@ -64,10 +87,11 @@
             device_id=device(*step),
             device_id_type=pl.DeviceIdType.MESH,
         )
-        copy.start()
-        copies.append(copy)
-    for copy in copies:
-        copy.wait()
+        guarded(reachable(step[0]), copy.start)
+        copies.append((copy, step))
+    for copy, step in copies:
+        guarded(reachable(step[0]), copy.wait_send)
+        guarded(reachable(-step[0]), copy.wait_recv)
 
 
 def neighbour_exchange(items):

time: 80.2 us -> 79.2 us (0.988)
  Pallas kernels: 44.5 us -> 43.3 us
    pallas_call x1, Pallas kernels: 30.5 us -> 29.4 us  [pressure_coefficients(): pl.pallas_call(lambda *refs: reduce_kernel(groups, shift, half_width, *re...]
where the time goes in v14:
time: 79.2 us; the launch traced here: 77.7 us
  Pallas kernels  43.3 us (55%)
  other arithmetic  16 us (20%)
  local copies, waits for them, and re-layouts  11.2 us (14%)
  matrix products  4.53 us (6%)
  between operations  2.65 us (3%)
    pallas_call x1, Pallas kernels, pressure_coefficients(): pl.pallas_call(lambda *refs: reduce_kernel(groups, shift, half_width, *re...  29.4 us
    pallas_call x1, Pallas kernels, neighbour_exchange(): pl.pallas_call(lambda *refs: exchange_kernel(offsets, *refs), out_shape=[...  13.9 us
    slice x5, local copies, waits for them, and re-layouts, pick(): return lax.slice_in_dim(values, values.shape[dim] - width, None, axis=dim)  3.5 us
    add x1, other arithmetic, solve_pressure(): padded_pressure = padded_pressure + coefficients[j] * padded_basis[j]  2.71 us
    dot_general x1, matrix products, on_device(): jnp.dot(plane_hot, gas_table, precision=HIGHEST)  2.42 us
    slice x2, local copies, waits for them, and re-layouts, radial_pad(): jnp.pad(values, [(0, 0)] * (values.ndim - 1) + [(rim_width, rim_width)],...  2.21 us

profile of v14, /device:TPU:6, one launch (start us, length us, event | category | flops | bytes accessed | tf_op | source)
XLA Modules:
  0.0 77.7 jit_solution(10380644657569204218)
XLA Ops:
  1.3 0.7 broadcast_compare_fusion
  2.1 1.2 %reduce-window.6 = s32[4,16,128]{2,1,0:T(8,128)S(1)} reduce-window(s32[4,16,128]{2,1,0:T(8,128)S(1)} %fusion.130, s32[]{:T(128)} %constant.45.clone.1), window={size=1x1x128 pad=0_0x0_0x127_0}, to_apply=%region_2.3 | reduce-window | flops 1040384 | bytes 65540 | tf_op jit(solution)/shard_map/reduce-window
  3.9 0.7 add_select_fusion.1
  4.9 2.4 %multiply_reduce_fusion = f32[2048,5]{0,1:T(8,128)S(1)} fusion(f32[2048,128]{0,1:T(8,128)S(1)} %fusion.16, s32[2048]{0:T(1024)S(1)} %get-tuple-element.120, f32[8,8,5,128]{3,2,1,0:T(8,128)S(1)} %bitcast.152), kind=kOutput, calls=%fused_computation | convolution fusion | flops 1009375232 | bytes 1261568 | tf_op jit(solution)/shard_map/dot_general | solution.py:495
  7.3 0.8 %fusion.3 = f32[14,256]{1,0:T(8,128)S(1)} fusion(s32[2048]{0:T(1024)S(1)} %bitcast_select_fusion, f32[1,2048]{1,0:T(1,128)S(1)} %fusion.106, f32[5,2048]{1,0:T(8,128)S(1)} %bitcast.154, f32[8,2048]{1,0:T(8,128)S(1)} %copy-done.2), kind=kOutput, calls=%fused_computation.6 | convolution fusion | flops 88662016 | bytes 137216 | tf_op jit(solution)/shard_map/dot_general | solution.py:504
  8.9 0.7 fusion.133
  9.5 0.7 fusion.136
  10.3 0.8 fusion.137
  11.0 0.7 fusion.135
  12.4 13.9 %shard_map.93 = (f32[14,2,8,128]{3,2,1,0:T(8,128)}, f32[14,8,2,128]{3,2,1,0:T(2,128)}, f32[14,8,2,128]{3,2,1,0:T(2,128)}, f32[14,2,8,128]{3,2,1,0:T(8,128)}, f32...) custom-call(f32[14,2,8,128]{3,2,1,0:T(8,128)} %get-tuple-element.76., ...), custom_call_target="tpu_custom_call" | custom-call | tf_op jit(solution)/shard_map/pallas_call | solution.py:101
  26.3 1.3 %maximum_select_fusion = f32[3,18,18,128]{3,2,1,0:T(8,128)S(1)} fusion(f32[3,5,5,128]{3,2,1,0:T(8,128)} %get-tuple-element.31, f32[3,8,5,128]{3,2,1,0:T(8,128)} %get-tuple-element.30, f32[3,5,5,128]{3,2,1,0:T(8,128)} %get-tuple-element.29, f32[3,5,8,128]{3,2,1,0:T(8,128)} %get-tuple-element.28, f32[3,8,8,128]{3,2,1,0:T(8,128)S(1)} %slice.571, ...), kind=kLoop, calls=%fused_computation.22 | loop fusion | flops 1119744 | bytes 995346 | tf_op jit(solution)/shard_map/jit(_where)/select_n | solution.py:177
  27.6 1.0 %fusion.132 = (f32[3,18,18,1]{3,2,1,0:T(8,128)S(1)}, f32[3,18,18,1]{3,2,1,0:T(8,128)}) fusion(f32[3,18,18,128]{3,2,1,0:T(8,128)S(1)} %maximum_select_fusion), kind=kLoop, calls=%fused_computation.279 | loop fusion | bytes 15552 | tf_op jit(solution)/shard_map/jit(_pad)/slice | solution.py:181
  28.7 1.1 %fusion.59 = f32[16,16,128]{2,1,0:T(8,128)S(1)} fusion(f32[3,18,18,128]{3,2,1,0:T(8,128)S(1)} %maximum_select_fusion, f32[3,18,18,1]{3,2,1,0:T(8,128)} %get-tuple-element.63, f32[3,18,18,1]{3,2,1,0:T(8,128)S(1)} %get-tuple-element.62, pred[16]{0:T(512)(128)(4,1)S(1)} %compare_and_fusion.4), kind=kLoop, calls=%fused_computation.100 | loop fusion | flops 294912 | bytes 1986864 | tf_op jit(solution)/shard_map/jit(_where)/select_n | solution.py:426
  30.4 0.7 fusion.86
  32.3 29.4 %shard_map.94 = f32[8,128]{1,0:T(8,128)} custom-call(f32[192,128]{1,0:T(8,128)} %bitcast.151, f32[64,128]{1,0:T(8,128)} %slice_bitcast_fusion.3.refs_1_, f32[64,128]{1,0:T(8,128)} %slice_bitcast_fusion.2.refs_2_, f32[64,128]{1,0:T(8,128)} %get-tuple-element.89.refs_3_, f32[64,128]{1,0:T(8,128)} %get-tuple-element.90.refs_4_, f32[64,128]{1,0:T(8,128)} %get-tuple-element.88.refs_5_), custom_call_target="tpu_custom_call" | custom-call | tf_op jit(solution)/shard_map/pallas_call | solution.py:399
  61.7 1.5 %fusion.139 = (f32[1,1]{1,0:T(1,128)}, f32[1,1]{1,0:T(1,128)}, f32[1,1]{1,0:T(1,128)}, f32[1,1]{1,0:T(1,128)}, f32[1,1]{1,0:T(1,128)}) fusion(f32[8,128]{1,0:T(8,128)} %shard_map.94), kind=kLoop, calls=%fused_computation.286 | loop fusion | bytes 40 | tf_op jit(solution)/shard_map/slice | solution.py:411
  64.9 0.7 fusion.80
  65.6 2.7 %fusion.52 = f32[10,10,130]{2,1,0:T(8,128)S(1)} fusion(f32[10,10,128]{2,1,0:T(8,128)S(1)} %get-tuple-element.86, f32[10,10,128]{2,1,0:T(8,128)S(1)} %get-tuple-element.87, f32[10,10,128]{2,1,0:T(8,128)S(1)} %get-tuple-element.85, f32[10,10,128]{2,1,0:T(8,128)S(1)} %slice.766, f32[]{:T(128)} %bitcast.41, f32[]{:T(128)} %bitcast.40, f32[]{:T(128)} %bitcast.39, ...), kind=kLoop, calls=%fused_computation.90 | loop fusion | flops 91000 | bytes 256816 | tf_op jit(solution)/shard_map/add | solution.py:468
  69.5 1.2 %slice_reduce_fusion = (f32[14,12,12]{2,0,1:T(8,128)S(1)}, f32[14,12,12]{2,0,1:T(8,128)S(1)}) fusion(f32[14,12,12,128]{3,2,0,1:T(8,128)S(1)} %copy_select_fusion), kind=kLoop, calls=%fused_computation.10 | loop fusion | bytes 32256 | tf_op jit(solution)/shard_map/jit(_pad)/slice | solution.py:181
  71.9 1.1 %pad_maximum_fusion = f32[14,12,12,132]{3,2,0,1:T(8,128)S(1)} fusion(f32[14,12,12,2]{3,2,0,1:T(8,128)S(1)} %reshape.580, f32[14,12,12,128]{3,2,0,1:T(8,128)S(1)} %copy_select_fusion, f32[14,12,12,2]{3,2,0,1:T(8,128)S(1)} %reshape.579), kind=kLoop, calls=%fused_computation.1 | loop fusion | flops 532224 | bytes 2128896 | tf_op jit(solution)/shard_map/jit(_pad)/concatenate | solution.py:181
  73.1 1.0 %slice_multiply_fusion.2 = (f32[10,12,12,132]{3,2,0,1:T(8,128)S(1)}, f32[10,12,12,132]{3,2,0,1:T(8,128)S(1)}, f32[10,12,12,132]{3,2,0,1:T(8,128)S(1)}) fusion(f32[14,12,12,132]{3,2,0,1:T(8,128)S(1)} %pad_maximum_fusion, f32[12,12,132]{2,1,0:T(8,128)S(1)} %get-tuple-element.58, f32[12,12,132]{2,1,0:T(8,128)S(1)} %get-tuple-element.57, ...), kind=kLoop, calls=%fused_computation.9 | loop fusion | flops 570240 | bytes 3269376 | tf_op jit(solution)/shard_map/mul | solution.py:191
  74.2 1.4 %fusion.25 = f32[10,8,8,128]{3,2,0,1:T(8,128)S(1)} fusion(f32[14,12,12,128]{3,2,0,1:T(8,128)S(1)} %copy_select_fusion, f32[14,12,12,2]{3,2,0,1:T(8,128)S(1)} %reshape.579, f32[14,12,12,2]{3,2,0,1:T(8,128)S(1)} %reshape.580, f32[10,12,12,132]{3,2,0,1:T(8,128)S(1)} %get-tuple-element.61, f32[10,12,12,132]{3,2,0,1:T(8,128)S(1)} %get-tuple-element.60, ...), kind=kLoop, calls=%fused_computation.32 | loop fusion | flops 4259840 | bytes 10224132 | tf_op jit(solution)/shard_map/add | solution.py:211
  75.6 1.3 %fusion.10 = f32[2,8,8,128]{3,2,0,1:T(8,128)S(1)} fusion(f32[2048,128]{0,1:T(8,128)S(1)} %fusion.16, f32[2048,2]{0,1:T(2,128)S(1)} %maximum_bitcast_fusion.4, s32[8,8]{1,0:T(8,128)S(1)} %multiply_add_fusion.2, s32[2048]{0:T(1024)S(1)} %get-tuple-element.120, f32[10,8,8,128]{3,2,0,1:T(8,128)S(1)} %fusion.25, f32[8,8,128]{2,1,0:T(8,128)S(1)} %slice_bitcast_fusion.4), kind=kOutput, calls=%fused_computation.16 | convolution fusion | flops 403341312 | bytes 1237248 | tf_op jit(solution)/shard_map/dot_general | solution.py:533
  76.9 0.8 copy.33
  (89 shorter events, 7.4 us)
Async XLA Ops:
  0.6 4.1 %copy-start = (f32[14,8,8,128]{3,2,1,0:T(8,128)S(1)}, f32[14,8,8,128]{3,2,1,0:T(8,128)}, u32[]{:S(2)}) copy-start(f32[14,8,8,128]{3,2,1,0:T(8,128)} %param.6) | copy-start | bytes 1376260
  4.9 2.5 %copy-start.2 = (f32[8,2048]{1,0:T(8,128)S(1)}, f32[8,2048]{1,0:T(8,128)}, u32[]{:S(2)}) copy-start(f32[8,2048]{1,0:T(8,128)} %param.8) | copy-start | bytes 196612
  26.3 2.3 %copy-start.1 = (f32[3,8,8,128]{3,2,1,0:T(8,128)}, f32[3,8,8,128]{3,2,1,0:T(8,128)S(1)}, u32[]{:S(2)}) copy-start(f32[3,8,8,128]{3,2,1,0:T(8,128)S(1)} %slice.571) | copy-start | bytes 294916
  29.8 34.1 %copy-start.10 = (f32[14,64]{1,0:T(8,128)S(1)}, f32[14,64]{1,0:T(8,128)}, u32[]{:S(2)}) copy-start(f32[14,64]{1,0:T(8,128)} %get-tuple-element.32) | copy-start | bytes 10756
  30.0 34.0 %copy-start.9 = (f32[14,64]{1,0:T(8,128)S(1)}, f32[14,64]{1,0:T(8,128)}, u32[]{:S(2)}) copy-start(f32[14,64]{1,0:T(8,128)} %get-tuple-element.33) | copy-start | bytes 10756
  30.0 34.1 %copy-start.8 = (f32[14,64]{1,0:T(8,128)S(1)}, f32[14,64]{1,0:T(8,128)}, u32[]{:S(2)}) copy-start(f32[14,64]{1,0:T(8,128)} %get-tuple-element.34) | copy-start | bytes 10756
  30.0 34.1 %copy-start.7 = (f32[14,64]{1,0:T(8,128)S(1)}, f32[14,64]{1,0:T(8,128)}, u32[]{:S(2)}) copy-start(f32[14,64]{1,0:T(8,128)} %get-tuple-element.35) | copy-start | bytes 10756
  30.3 38.9 %copy-start.3 = (f32[14,2,8,128]{3,2,1,0:T(8,128)S(1)}, f32[14,2,8,128]{3,2,1,0:T(8,128)}, u32[]{:S(2)}) copy-start(f32[14,2,8,128]{3,2,1,0:T(8,128)} %get-tuple-element.22) | copy-start | bytes 344068
  30.3 38.9 %copy-start.4 = (f32[14,8,2,128]{3,2,1,0:T(2,128)S(1)}, f32[14,8,2,128]{3,2,1,0:T(2,128)}, u32[]{:S(2)}) copy-start(f32[14,8,2,128]{3,2,1,0:T(2,128)} %get-tuple-element.23) | copy-start | bytes 344068
  30.3 38.9 %copy-start.5 = (f32[14,8,2,128]{3,2,1,0:T(2,128)S(1)}, f32[14,8,2,128]{3,2,1,0:T(2,128)}, u32[]{:S(2)}) copy-start(f32[14,8,2,128]{3,2,1,0:T(2,128)} %get-tuple-element.20) | copy-start | bytes 344068
  30.4 38.9 %copy-start.6 = (f32[14,2,8,128]{3,2,1,0:T(8,128)S(1)}, f32[14,2,8,128]{3,2,1,0:T(8,128)}, u32[]{:S(2)}) copy-start(f32[14,2,8,128]{3,2,1,0:T(8,128)} %get-tuple-element.21) | copy-start | bytes 344068
  73.0 1.1 %copy-start.11 = (f32[10]{0:T(128)S(1)}, f32[10]{0:T(128)}, u32[]{:S(2)}) copy-start(f32[10]{0:T(128)} %param.7) | copy-start | bytes 124

commit v15 on v14

--- a/solution.py
+++ b/solution.py
@@ -249,8 +249,18 @@
 def reduce_groups():
     axial = lax.axis_size("axial")
     along_x = 4 if axial % 4 == 0 else 1
-    groups = [("azim", 1, lax.axis_size("azim")), ("axial", 1, along_x), ("axial", along_x, axial // along_x)]
-    return [group for group in groups if group[2] > 1]
+    groups = [
+        (("azim", 1, lax.axis_size("azim")), ("axial", 1, along_x)),
+        (("axial", along_x, axial // along_x),),
+    ]
+    return [tuple(d for d in g if d[2] > 1) for g in groups if any(d[2] > 1 for d in g)]
+
+
+def group_size(group):
+    size = 1
+    for _, _, count in group:
+        size *= count
+    return size
 
 
 def coefficient_cg(gram, size, shift, half_width):
@@ -299,25 +309,33 @@
     o_ref, slots, send_sems, recv_sems = refs[size:]
     here = {"axial": lax.axis_index("axial"), "azim": lax.axis_index("azim")}
 
-    def member(axis, stride, count, m):
-        index = here[axis]
-        base = index - ((index // stride) % count) * stride
+    def member(group, m):
         coords = dict(here)
-        coords[axis] = base + m * stride
+        for axis, stride, count in group:
+            index = here[axis]
+            base = index - ((index // stride) % count) * stride
+            coords[axis] = base + (m % count) * stride
+            m = m // count
         return (coords["axial"], coords["azim"])
 
-    def position(axis, stride, count):
-        return (here[axis] // stride) % count
+    def position(group):
+        place = 0
+        weight = 1
+        for axis, stride, count in group:
+            place = place + ((here[axis] // stride) % count) * weight
+            weight *= count
+        return place
 
     barrier = pltpu.get_barrier_semaphore()
     greeted = 0
-    for axis, stride, count in groups:
-        mine = position(axis, stride, count)
+    for group in groups:
+        count = group_size(group)
+        mine = position(group)
         for m in range(1, count):
             pl.semaphore_signal(
                 barrier,
                 inc=1,
-                device_id=member(axis, stride, count, (mine + m) % count),
+                device_id=member(group, (mine + m) % count),
                 device_id_type=pl.DeviceIdType.MESH,
             )
             greeted += 1
@@ -337,8 +355,9 @@
     for n, entry in enumerate(entries):
         acc = jnp.where((row == 0) & (lane == n), entry, acc)
     offset = 0
-    for axis, stride, count in groups:
-        mine = position(axis, stride, count)
+    for group in groups:
+        count = group_size(group)
+        mine = position(group)
         slots[offset + mine] = acc
         copies = []
         for m in range(1, count):
@@ -348,7 +367,7 @@
                 dst_ref=slots.at[offset + mine],
                 send_sem=send_sems.at[offset + target],
                 recv_sem=recv_sems.at[offset + mine],
-                device_id=member(axis, stride, count, target),
+                device_id=member(group, target),
                 device_id_type=pl.DeviceIdType.MESH,
             )
             copy.start()
@@ -361,7 +380,7 @@
                 dst_ref=slots.at[offset + m],
                 send_sem=send_sems.at[offset + m],
                 recv_sem=recv_sems.at[offset + m],
-                device_id=member(axis, stride, count, m),
+                device_id=member(group, m),
                 device_id_type=pl.DeviceIdType.MESH,
             )
 
@@ -394,7 +413,7 @@
 
 def pressure_coefficients(velocity, basis, shift, half_width):
     groups = reduce_groups()
-    slot_count = sum(count for _, _, count in groups)
+    slot_count = sum(group_size(group) for group in groups)
     flat = [v.reshape(-1, v.shape[-1]) for v in basis]
     out = pl.pallas_call(
         lambda *refs: reduce_kernel(groups, shift, half_width, *refs),

time: 79.2 us -> 79.5 us (level)
  the two profiles are of different devices: /device:TPU:6 before, /device:TPU:1 now
where the time goes in v15:
time: 79.5 us; the launch traced here: 79.1 us
  Pallas kernels  44.8 us (56%)
  other arithmetic  16 us (20%)
  local copies, waits for them, and re-layouts  11.2 us (14%)
  matrix products  4.53 us (6%)
  between operations  2.65 us (3%)
    pallas_call x1, Pallas kernels, pressure_coefficients(): pl.pallas_call(lambda *refs: reduce_kernel(groups, shift, half_width, *re...  28.7 us
    pallas_call x1, Pallas kernels, neighbour_exchange(): pl.pallas_call(lambda *refs: exchange_kernel(offsets, *refs), out_shape=[...  16.1 us
    slice x5, local copies, waits for them, and re-layouts, pick(): return lax.slice_in_dim(values, values.shape[dim] - width, None, axis=dim)  3.5 us
    add x1, other arithmetic, solve_pressure(): padded_pressure = padded_pressure + coefficients[j] * padded_basis[j]  2.71 us
    dot_general x1, matrix products, on_device(): jnp.dot(plane_hot, gas_table, precision=HIGHEST)  2.42 us
    slice x2, local copies, waits for them, and re-layouts, radial_pad(): jnp.pad(values, [(0, 0)] * (values.ndim - 1) + [(rim_width, rim_width)],...  2.21 us

profile of v15, /device:TPU:1, one launch (start us, length us, event | category | flops | bytes accessed | tf_op | source)
XLA Modules:
  0.0 79.1 jit_solution(8640460448479265714)
XLA Ops:
  1.3 0.7 broadcast_compare_fusion
  2.1 1.2 %reduce-window.6 = s32[4,16,128]{2,1,0:T(8,128)S(1)} reduce-window(s32[4,16,128]{2,1,0:T(8,128)S(1)} %fusion.130, s32[]{:T(128)} %constant.45.clone.1), window={size=1x1x128 pad=0_0x0_0x127_0}, to_apply=%region_2.3 | reduce-window | flops 1040384 | bytes 65540 | tf_op jit(solution)/shard_map/reduce-window
  3.9 0.7 add_select_fusion.1
  4.9 2.4 %multiply_reduce_fusion = f32[2048,5]{0,1:T(8,128)S(1)} fusion(f32[2048,128]{0,1:T(8,128)S(1)} %fusion.16, s32[2048]{0:T(1024)S(1)} %get-tuple-element.120, f32[8,8,5,128]{3,2,1,0:T(8,128)S(1)} %bitcast.152), kind=kOutput, calls=%fused_computation | convolution fusion | flops 1009375232 | bytes 1261568 | tf_op jit(solution)/shard_map/dot_general | solution.py:514
  7.3 0.8 %fusion.3 = f32[14,256]{1,0:T(8,128)S(1)} fusion(s32[2048]{0:T(1024)S(1)} %bitcast_select_fusion, f32[1,2048]{1,0:T(1,128)S(1)} %fusion.106, f32[5,2048]{1,0:T(8,128)S(1)} %bitcast.154, f32[8,2048]{1,0:T(8,128)S(1)} %copy-done.2), kind=kOutput, calls=%fused_computation.6 | convolution fusion | flops 88662016 | bytes 137216 | tf_op jit(solution)/shard_map/dot_general | solution.py:523
  8.9 0.7 fusion.133
  9.5 0.7 fusion.136
  10.3 0.8 fusion.137
  11.0 0.7 fusion.135
  12.4 16.1 %shard_map.93 = (f32[14,2,8,128]{3,2,1,0:T(8,128)}, f32[14,8,2,128]{3,2,1,0:T(2,128)}, f32[14,8,2,128]{3,2,1,0:T(2,128)}, f32[14,2,8,128]{3,2,1,0:T(8,128)}, f32...) custom-call(f32[14,2,8,128]{3,2,1,0:T(8,128)} %get-tuple-element.76., ...), custom_call_target="tpu_custom_call" | custom-call | tf_op jit(solution)/shard_map/pallas_call | solution.py:101
  28.5 1.3 %maximum_select_fusion = f32[3,18,18,128]{3,2,1,0:T(8,128)S(1)} fusion(f32[3,5,5,128]{3,2,1,0:T(8,128)} %get-tuple-element.31, f32[3,8,5,128]{3,2,1,0:T(8,128)} %get-tuple-element.30, f32[3,5,5,128]{3,2,1,0:T(8,128)} %get-tuple-element.29, f32[3,5,8,128]{3,2,1,0:T(8,128)} %get-tuple-element.28, f32[3,8,8,128]{3,2,1,0:T(8,128)S(1)} %slice.571, ...), kind=kLoop, calls=%fused_computation.22 | loop fusion | flops 1119744 | bytes 995346 | tf_op jit(solution)/shard_map/jit(_where)/select_n | solution.py:177
  29.8 1.0 %fusion.132 = (f32[3,18,18,1]{3,2,1,0:T(8,128)S(1)}, f32[3,18,18,1]{3,2,1,0:T(8,128)}) fusion(f32[3,18,18,128]{3,2,1,0:T(8,128)S(1)} %maximum_select_fusion), kind=kLoop, calls=%fused_computation.279 | loop fusion | bytes 15552 | tf_op jit(solution)/shard_map/jit(_pad)/slice | solution.py:181
  30.8 1.1 %fusion.59 = f32[16,16,128]{2,1,0:T(8,128)S(1)} fusion(f32[3,18,18,128]{3,2,1,0:T(8,128)S(1)} %maximum_select_fusion, f32[3,18,18,1]{3,2,1,0:T(8,128)} %get-tuple-element.63, f32[3,18,18,1]{3,2,1,0:T(8,128)S(1)} %get-tuple-element.62, pred[16]{0:T(512)(128)(4,1)S(1)} %compare_and_fusion.4), kind=kLoop, calls=%fused_computation.100 | loop fusion | flops 294912 | bytes 1986864 | tf_op jit(solution)/shard_map/jit(_where)/select_n | solution.py:445
  32.5 0.7 fusion.86
  34.5 28.7 %shard_map.94 = f32[8,128]{1,0:T(8,128)} custom-call(f32[192,128]{1,0:T(8,128)} %bitcast.151, f32[64,128]{1,0:T(8,128)} %slice_bitcast_fusion.3.refs_1_, f32[64,128]{1,0:T(8,128)} %slice_bitcast_fusion.2.refs_2_, f32[64,128]{1,0:T(8,128)} %get-tuple-element.89.refs_3_, f32[64,128]{1,0:T(8,128)} %get-tuple-element.90.refs_4_, f32[64,128]{1,0:T(8,128)} %get-tuple-element.88.refs_5_), custom_call_target="tpu_custom_call" | custom-call | tf_op jit(solution)/shard_map/pallas_call | solution.py:418
  63.1 1.5 %fusion.139 = (f32[1,1]{1,0:T(1,128)}, f32[1,1]{1,0:T(1,128)}, f32[1,1]{1,0:T(1,128)}, f32[1,1]{1,0:T(1,128)}, f32[1,1]{1,0:T(1,128)}) fusion(f32[8,128]{1,0:T(8,128)} %shard_map.94), kind=kLoop, calls=%fused_computation.286 | loop fusion | bytes 40 | tf_op jit(solution)/shard_map/slice | solution.py:430
  66.4 0.7 fusion.80
  67.0 2.7 %fusion.52 = f32[10,10,130]{2,1,0:T(8,128)S(1)} fusion(f32[10,10,128]{2,1,0:T(8,128)S(1)} %get-tuple-element.86, f32[10,10,128]{2,1,0:T(8,128)S(1)} %get-tuple-element.87, f32[10,10,128]{2,1,0:T(8,128)S(1)} %get-tuple-element.85, f32[10,10,128]{2,1,0:T(8,128)S(1)} %slice.766, f32[]{:T(128)} %bitcast.41, f32[]{:T(128)} %bitcast.40, f32[]{:T(128)} %bitcast.39, ...), kind=kLoop, calls=%fused_computation.90 | loop fusion | flops 91000 | bytes 256816 | tf_op jit(solution)/shard_map/add | solution.py:487
  70.9 1.2 %slice_reduce_fusion = (f32[14,12,12]{2,0,1:T(8,128)S(1)}, f32[14,12,12]{2,0,1:T(8,128)S(1)}) fusion(f32[14,12,12,128]{3,2,0,1:T(8,128)S(1)} %copy_select_fusion), kind=kLoop, calls=%fused_computation.10 | loop fusion | bytes 32256 | tf_op jit(solution)/shard_map/jit(_pad)/slice | solution.py:181
  73.3 1.1 %pad_maximum_fusion = f32[14,12,12,132]{3,2,0,1:T(8,128)S(1)} fusion(f32[14,12,12,2]{3,2,0,1:T(8,128)S(1)} %reshape.580, f32[14,12,12,128]{3,2,0,1:T(8,128)S(1)} %copy_select_fusion, f32[14,12,12,2]{3,2,0,1:T(8,128)S(1)} %reshape.579), kind=kLoop, calls=%fused_computation.1 | loop fusion | flops 532224 | bytes 2128896 | tf_op jit(solution)/shard_map/jit(_pad)/concatenate | solution.py:181
  74.5 1.0 %slice_multiply_fusion.2 = (f32[10,12,12,132]{3,2,0,1:T(8,128)S(1)}, f32[10,12,12,132]{3,2,0,1:T(8,128)S(1)}, f32[10,12,12,132]{3,2,0,1:T(8,128)S(1)}) fusion(f32[14,12,12,132]{3,2,0,1:T(8,128)S(1)} %pad_maximum_fusion, f32[12,12,132]{2,1,0:T(8,128)S(1)} %get-tuple-element.58, f32[12,12,132]{2,1,0:T(8,128)S(1)} %get-tuple-element.57, ...), kind=kLoop, calls=%fused_computation.9 | loop fusion | flops 570240 | bytes 3269376 | tf_op jit(solution)/shard_map/mul | solution.py:191
  75.6 1.4 %fusion.25 = f32[10,8,8,128]{3,2,0,1:T(8,128)S(1)} fusion(f32[14,12,12,128]{3,2,0,1:T(8,128)S(1)} %copy_select_fusion, f32[14,12,12,2]{3,2,0,1:T(8,128)S(1)} %reshape.579, f32[14,12,12,2]{3,2,0,1:T(8,128)S(1)} %reshape.580, f32[10,12,12,132]{3,2,0,1:T(8,128)S(1)} %get-tuple-element.61, f32[10,12,12,132]{3,2,0,1:T(8,128)S(1)} %get-tuple-element.60, ...), kind=kLoop, calls=%fused_computation.32 | loop fusion | flops 4259840 | bytes 10224132 | tf_op jit(solution)/shard_map/add | solution.py:211
  77.0 1.3 %fusion.10 = f32[2,8,8,128]{3,2,0,1:T(8,128)S(1)} fusion(f32[2048,128]{0,1:T(8,128)S(1)} %fusion.16, f32[2048,2]{0,1:T(2,128)S(1)} %maximum_bitcast_fusion.4, s32[8,8]{1,0:T(8,128)S(1)} %multiply_add_fusion.2, s32[2048]{0:T(1024)S(1)} %get-tuple-element.120, f32[10,8,8,128]{3,2,0,1:T(8,128)S(1)} %fusion.25, f32[8,8,128]{2,1,0:T(8,128)S(1)} %slice_bitcast_fusion.4), kind=kOutput, calls=%fused_computation.16 | convolution fusion | flops 403341312 | bytes 1237248 | tf_op jit(solution)/shard_map/dot_general | solution.py:552
  78.4 0.8 copy.33
  (89 shorter events, 7.4 us)
Async XLA Ops:
  0.6 4.1 %copy-start = (f32[14,8,8,128]{3,2,1,0:T(8,128)S(1)}, f32[14,8,8,128]{3,2,1,0:T(8,128)}, u32[]{:S(2)}) copy-start(f32[14,8,8,128]{3,2,1,0:T(8,128)} %param.6) | copy-start | bytes 1376260
  4.9 2.5 %copy-start.2 = (f32[8,2048]{1,0:T(8,128)S(1)}, f32[8,2048]{1,0:T(8,128)}, u32[]{:S(2)}) copy-start(f32[8,2048]{1,0:T(8,128)} %param.8) | copy-start | bytes 196612
  28.5 2.3 %copy-start.1 = (f32[3,8,8,128]{3,2,1,0:T(8,128)}, f32[3,8,8,128]{3,2,1,0:T(8,128)S(1)}, u32[]{:S(2)}) copy-start(f32[3,8,8,128]{3,2,1,0:T(8,128)S(1)} %slice.571) | copy-start | bytes 294916
  32.0 33.3 %copy-start.10 = (f32[14,64]{1,0:T(8,128)S(1)}, f32[14,64]{1,0:T(8,128)}, u32[]{:S(2)}) copy-start(f32[14,64]{1,0:T(8,128)} %get-tuple-element.32) | copy-start | bytes 10756
  32.1 33.3 %copy-start.9 = (f32[14,64]{1,0:T(8,128)S(1)}, f32[14,64]{1,0:T(8,128)}, u32[]{:S(2)}) copy-start(f32[14,64]{1,0:T(8,128)} %get-tuple-element.33) | copy-start | bytes 10756
  32.1 33.3 %copy-start.8 = (f32[14,64]{1,0:T(8,128)S(1)}, f32[14,64]{1,0:T(8,128)}, u32[]{:S(2)}) copy-start(f32[14,64]{1,0:T(8,128)} %get-tuple-element.34) | copy-start | bytes 10756
  32.1 33.4 %copy-start.7 = (f32[14,64]{1,0:T(8,128)S(1)}, f32[14,64]{1,0:T(8,128)}, u32[]{:S(2)}) copy-start(f32[14,64]{1,0:T(8,128)} %get-tuple-element.35) | copy-start | bytes 10756
  32.5 38.1 %copy-start.3 = (f32[14,2,8,128]{3,2,1,0:T(8,128)S(1)}, f32[14,2,8,128]{3,2,1,0:T(8,128)}, u32[]{:S(2)}) copy-start(f32[14,2,8,128]{3,2,1,0:T(8,128)} %get-tuple-element.22) | copy-start | bytes 344068
  32.5 38.1 %copy-start.4 = (f32[14,8,2,128]{3,2,1,0:T(2,128)S(1)}, f32[14,8,2,128]{3,2,1,0:T(2,128)}, u32[]{:S(2)}) copy-start(f32[14,8,2,128]{3,2,1,0:T(2,128)} %get-tuple-element.23) | copy-start | bytes 344068
  32.5 38.1 %copy-start.5 = (f32[14,8,2,128]{3,2,1,0:T(2,128)S(1)}, f32[14,8,2,128]{3,2,1,0:T(2,128)}, u32[]{:S(2)}) copy-start(f32[14,8,2,128]{3,2,1,0:T(2,128)} %get-tuple-element.20) | copy-start | bytes 344068
  32.5 38.1 %copy-start.6 = (f32[14,2,8,128]{3,2,1,0:T(8,128)S(1)}, f32[14,2,8,128]{3,2,1,0:T(8,128)}, u32[]{:S(2)}) copy-start(f32[14,2,8,128]{3,2,1,0:T(8,128)} %get-tuple-element.21) | copy-start | bytes 344068
  74.5 1.1 %copy-start.11 = (f32[10]{0:T(128)S(1)}, f32[10]{0:T(128)}, u32[]{:S(2)}) copy-start(f32[10]{0:T(128)} %param.7) | copy-start | bytes 124

commit v16 on v14

--- a/solution.py
+++ b/solution.py
@@ -293,11 +293,36 @@
     return solution_c
 
 
-def reduce_kernel(groups, shift, half_width, vel_ref, *refs):
+def reduce_kernel(groups, extra_steps, shift, half_width, vel_ref, *refs):
     size = ITERS + 1
+    extras = len(extra_steps)
     basis_refs = refs[:size]
-    o_ref, slots, send_sems, recv_sems = refs[size:]
+    extra_sources = refs[size : size + extras]
+    o_ref = refs[size + extras]
+    extra_outs = refs[size + extras + 1 : size + 2 * extras + 1]
+    slots, send_sems, recv_sems, extra_send, extra_recv = refs[size + 2 * extras + 1 :]
     here = {"axial": lax.axis_index("axial"), "azim": lax.axis_index("azim")}
+    has_low = here["axial"] > 0
+    has_high = here["axial"] < lax.axis_size("axial") - 1
+
+    def reachable(step_axial):
+        if step_axial < 0:
+            return has_low
+        if step_axial > 0:
+            return has_high
+        return None
+
+    def guarded(condition, action):
+        if condition is None:
+            action()
+        else:
+            pl.when(condition)(action)
+
+    def neighbour(step_axial, step_azim):
+        return (
+            (here["axial"] + step_axial + lax.axis_size("axial")) % lax.axis_size("axial"),
+            (here["azim"] + step_azim + lax.axis_size("azim")) % lax.axis_size("azim"),
+        )
 
     def member(axis, stride, count, m):
         index = here[axis]
@@ -321,7 +346,29 @@
                 device_id_type=pl.DeviceIdType.MESH,
             )
             greeted += 1
+    for step in sorted(set(extra_steps)):
+
+        def greet(step=step):
+            pl.semaphore_signal(
+                barrier, inc=1, device_id=neighbour(*step), device_id_type=pl.DeviceIdType.MESH
+            )
+
+        guarded(reachable(step[0]), greet)
+        condition = reachable(-step[0])
+        greeted = greeted + (1 if condition is None else condition.astype(jnp.int32))
     pl.semaphore_wait(barrier, greeted)
+    extra_copies = []
+    for k, step in enumerate(extra_steps):
+        copy = pltpu.make_async_remote_copy(
+            src_ref=extra_sources[k],
+            dst_ref=extra_outs[k],
+            send_sem=extra_send.at[k],
+            recv_sem=extra_recv.at[k],
+            device_id=neighbour(*step),
+            device_id_type=pl.DeviceIdType.MESH,
+        )
+        guarded(reachable(step[0]), copy.start)
+        extra_copies.append((copy, step))
     row = lax.broadcasted_iota(jnp.int32, o_ref.shape, 0)
     lane = lax.broadcasted_iota(jnp.int32, o_ref.shape, 1)
     is_max = (row == 0) & (lane == 0)
@@ -390,25 +437,37 @@
     for j in range(ITERS):
         out = jnp.where((lane == j), coefficients[j], out)
     o_ref[...] = out
-
-
-def pressure_coefficients(velocity, basis, shift, half_width):
+    for copy, step in extra_copies:
+        guarded(reachable(step[0]), copy.wait_send)
+        guarded(reachable(-step[0]), copy.wait_recv)
+
+
+def pressure_coefficients(velocity, basis, shift, half_width, extra_items):
     groups = reduce_groups()
     slot_count = sum(count for _, _, count in groups)
     flat = [v.reshape(-1, v.shape[-1]) for v in basis]
-    out = pl.pallas_call(
-        lambda *refs: reduce_kernel(groups, shift, half_width, *refs),
-        out_shape=jax.ShapeDtypeStruct((8, 128), jnp.float32),
-        in_specs=[pl.BlockSpec(memory_space=pltpu.VMEM)] * (1 + len(flat)),
-        out_specs=pl.BlockSpec(memory_space=pltpu.VMEM),
+    extra_steps = [step for _, step in extra_items]
+    extra_arrays = [a for a, _ in extra_items]
+    extras = len(extra_arrays)
+    vmem = pl.BlockSpec(memory_space=pltpu.VMEM)
+    anywhere = pl.BlockSpec(memory_space=pl.ANY)
+    outs = pl.pallas_call(
+        lambda *refs: reduce_kernel(groups, extra_steps, shift, half_width, *refs),
+        out_shape=[jax.ShapeDtypeStruct((8, 128), jnp.float32)]
+        + [jax.ShapeDtypeStruct(a.shape, a.dtype) for a in extra_arrays],
+        in_specs=[vmem] * (1 + len(flat)) + [anywhere] * extras,
+        out_specs=[vmem] + [anywhere] * extras,
         scratch_shapes=[
             pltpu.VMEM((slot_count, 8, 128), jnp.float32),
             pltpu.SemaphoreType.DMA((slot_count,)),
             pltpu.SemaphoreType.DMA((slot_count,)),
+            pltpu.SemaphoreType.DMA((extras,)),
+            pltpu.SemaphoreType.DMA((extras,)),
         ],
         compiler_params=pltpu.CompilerParams(collective_id=0, has_side_effects=True),
-    )(velocity.reshape(-1, velocity.shape[-1]), *flat)
-    return [out[0, j] for j in range(ITERS)], out[0, ITERS]
+    )(velocity.reshape(-1, velocity.shape[-1]), *flat, *extra_arrays)
+    out = outs[0]
+    return [out[0, j] for j in range(ITERS)], out[0, ITERS], list(outs[1:])
 
 
 def neighbour_sum(padded):
@@ -444,7 +503,7 @@
     return beside + at(0, 0, 1) + at(0, 0, -1)
 
 
-def solve_pressure(wide_velocity, velocity):
+def solve_pressure(wide_velocity, velocity, extra_items):
     half_width = 6.0
     u = wide_velocity
     divergence = 0.5 * (u[0, 2:, 1:-1, 1:-1] - u[0, :-2, 1:-1, 1:-1])
@@ -459,14 +518,14 @@
             fresh = 2.0 * scaled - crop(basis[j - 1], 2)
         basis.append(axial_valid(fresh, ITERS - 1 - j))
     interior = [crop(basis[j], ITERS - j) for j in range(ITERS + 1)]
-    coefficients, fastest = pressure_coefficients(
-        velocity, interior, 6.0 + SHIFT_PRESSURE, half_width
+    coefficients, fastest, received = pressure_coefficients(
+        velocity, interior, 6.0 + SHIFT_PRESSURE, half_width, extra_items
     )
     padded_basis = [radial_pad(crop(basis[j], ITERS - j - 1), 1, "constant") for j in range(ITERS)]
     padded_pressure = coefficients[0] * padded_basis[0]
     for j in range(1, ITERS):
         padded_pressure = padded_pressure + coefficients[j] * padded_basis[j]
-    return padded_pressure, fastest
+    return padded_pressure, fastest, received
 
 
 def along_axial(buffer, step_by):
@@ -507,14 +566,12 @@
     faces = [(sa, sz) for sa, sz in NEIGHBOURS if sa == 0 or sz == 0]
     items = [(rim_slab(state, 2, sa, sz), (sa, sz)) for sa, sz in faces]
     items += [(rim_slab(velocity, ITERS + 1, sa, sz), (sa, sz)) for sa, sz in NEIGHBOURS]
-    items += [(leaving[d], parcel_steps[d]) for d in range(4)]
     got = neighbour_exchange(items)
     count = len(faces)
     state_rims = {(-sa, -sz): got[k] for k, (sa, sz) in enumerate(faces)}
     velocity_rims = {
         (-sa, -sz): got[count + k] for k, (sa, sz) in enumerate(NEIGHBOURS)
     }
-    landed = got[count + len(NEIGHBOURS) :]
     whole_pad = assemble(state, state_rims)
     whole_pad = radial_pad(clear_ends(whole_pad, 2, 1), 2, "edge")
     moving = whole_pad[1:]
@@ -523,7 +580,8 @@
     vel_pad = moving[0:3]
     wide_velocity = assemble(velocity, velocity_rims)
     wide_velocity = radial_pad(clear_ends(wide_velocity, ITERS + 1, 1), 1, "edge")
-    padded_pressure, fastest = solve_pressure(wide_velocity, velocity)
+    parcel_items = [(leaving[d], parcel_steps[d]) for d in range(4)]
+    padded_pressure, fastest, landed = solve_pressure(wide_velocity, velocity, parcel_items)
     step_size = CFL / (fastest + 1e-06)
     transported = transport(
         moving[3:], vel_pad, density_pad, density_rim, diff_coef[:, None, None, None], step_size

time: 79.2 us -> 102 us (1.29)
  other arithmetic: 16 us -> 30.3 us
  local copies, waits for them, and re-layouts: 11.2 us -> 17.6 us
  matrix products: 4.53 us -> 5.91 us
    add x1, other arithmetic: 1.36 us -> 7.56 us  [transport(): return center + step_size * change]
    slice x5, local copies, waits for them, and re-layouts: 3.5 us -> 6.77 us  [pick(): return lax.slice_in_dim(values, values.shape[dim] - width, None, axis=dim)]
    unnamed x25 -> x65, local copies, waits for them, and re-layouts: 0.81 us -> 2.85 us
    mul x2, other arithmetic: 0.12 us -> 1.93 us  [evaporate(): sources = jnp.stack([heat_source * alive_mask, lost_mass * alive_mask])]
    slice x1, other arithmetic: 0.12 us -> 1.9 us  [crop(): return values[by:-by, by:-by]]
    mul x1, other arithmetic: 0.97 us -> 2.72 us  [transport(): carried = vel_pad[direction] * scalar_pad]
    reshape x2, local copies, waits for them, and re-layouts: 0.09 us -> 1.45 us  [on_device(): jnp.dot(raw, select, precision=HIGHEST).reshape(raw.shape[0], 4, CAP)]
    dot_general x1, matrix products: 1.3 us -> 2.56 us  [on_device(): lax.dot_general(plane_hot, spread, (((0,), (0,)), ((), ())), precision=HI...]
where the time goes in v16:
time: 102 us; the launch traced here: 99.6 us
  Pallas kernels  43.1 us (42%)
  other arithmetic  30.3 us (30%)
  local copies, waits for them, and re-layouts  17.6 us (17%)
  matrix products  5.91 us (6%)
  between operations  2.74 us (3%)
    pallas_call x1, Pallas kernels, pressure_coefficients(): pl.pallas_call(lambda *refs: reduce_kernel(groups, extra_steps, shift, ha...  29.3 us
    pallas_call x1, Pallas kernels, neighbour_exchange(): pl.pallas_call(lambda *refs: exchange_kernel(offsets, *refs), out_shape=[...  13.9 us
    add x1, other arithmetic, transport(): return center + step_size * change  7.56 us
    slice x5, local copies, waits for them, and re-layouts, pick(): return lax.slice_in_dim(values, values.shape[dim] - width, None, axis=dim)  6.77 us
    add x1, other arithmetic, solve_pressure(): padded_pressure = padded_pressure + coefficients[j] * padded_basis[j]  2.87 us
    unnamed x65, local copies, waits for them, and re-layouts  2.85 us
    mul x1, other arithmetic, transport(): carried = vel_pad[direction] * scalar_pad  2.72 us
    dot_general x1, matrix products, on_device(): lax.dot_general(plane_hot, spread, (((0,), (0,)), ((), ())), precision=HI...  2.56 us

profile of v16, /device:TPU:6, one launch (start us, length us, event | category | flops | bytes accessed | tf_op | source)
XLA Modules:
  0.0 99.6 jit_solution(14882798582679612671)
XLA Ops:
  0.7 1.7 %fusion.136 = (f32[14,2,8,128]{3,2,1,0:T(8,128)}, f32[14,2,8,128]{3,2,1,0:T(8,128)}) fusion(f32[14,8,8,128]{3,2,1,0:T(8,128)} %param.6), kind=kLoop, calls=%fused_computation.283 | loop fusion | bytes 458752 | tf_op jit(solution)/shard_map/slice | solution.py:115
  2.4 2.0 %fusion.137 = (f32[14,8,2,128]{3,2,1,0:T(2,128)}, f32[14,8,2,128]{3,2,1,0:T(2,128)}) fusion(f32[14,8,8,128]{3,2,1,0:T(8,128)} %param.6), kind=kLoop, calls=%fused_computation.284 | loop fusion | bytes 458752 | tf_op jit(solution)/shard_map/slice | solution.py:115
  4.3 1.7 %fusion.133 = (f32[3,5,5,128]{3,2,1,0:T(8,128)}, f32[3,5,5,128]{3,2,1,0:T(8,128)}, f32[3,5,5,128]{3,2,1,0:T(8,128)}, f32[3,5,5,128]{3,2,1,0:T(8,128)}) fusion(f32[14,8,8,128]{3,2,1,0:T(8,128)} %param.6), kind=kLoop, calls=%fused_computation.280 | loop fusion | bytes 307200 | tf_op jit(solution)/shard_map/slice | solution.py:115
  7.4 13.9 %shard_map.93 = (f32[14,2,8,128]{3,2,1,0:T(8,128)}, f32[14,8,2,128]{3,2,1,0:T(2,128)}, f32[14,8,2,128]{3,2,1,0:T(2,128)}, f32[14,2,8,128]{3,2,1,0:T(8,128)}, f32...) custom-call(f32[14,2,8,128]{3,2,1,0:T(8,128)} %get-tuple-element.78., ...), custom_call_target="tpu_custom_call" | custom-call | tf_op jit(solution)/shard_map/pallas_call | solution.py:101
  21.3 1.4 %copy_select_fusion = f32[14,12,12,128]{3,2,0,1:T(8,128)S(1)} fusion(pred[12]{0:T(512)(128)(4,1)S(1)} %and_or_fusion.1, f32[14,2,2,128]{3,2,1,0:T(2,128)S(1)} %broadcast.428, f32[14,8,2,128]{3,2,1,0:T(2,128)} %get-tuple-element.24, f32[14,2,8,128]{3,2,1,0:T(8,128)} %get-tuple-element.23, f32[14,8,8,128]{3,2,1,0:T(8,128)S(1)} %copy-done.1, ...), kind=kLoop, calls=%fused_computation.13 | loop fusion | flops 2322432 | bytes 1978380 | tf_op jit(solution)/shard_map/jit(_where)/select_n | solution.py:177
  22.7 1.2 %slice_reduce_fusion = (f32[14,12,12]{2,0,1:T(8,128)S(1)}, f32[14,12,12]{2,0,1:T(8,128)S(1)}) fusion(f32[14,12,12,128]{3,2,0,1:T(8,128)S(1)} %copy_select_fusion), kind=kLoop, calls=%fused_computation.10 | loop fusion | bytes 32256 | tf_op jit(solution)/shard_map/jit(_pad)/slice | solution.py:181
  24.7 1.1 %pad_maximum_fusion = f32[14,12,12,132]{3,2,0,1:T(8,128)S(1)} fusion(f32[14,12,12,2]{3,2,0,1:T(8,128)S(1)} %reshape.580, f32[14,12,12,128]{3,2,0,1:T(8,128)S(1)} %copy_select_fusion, f32[14,12,12,2]{3,2,0,1:T(8,128)S(1)} %reshape.579), kind=kLoop, calls=%fused_computation.1 | loop fusion | flops 532224 | bytes 2128896 | tf_op jit(solution)/shard_map/jit(_pad)/concatenate | solution.py:181
  26.3 2.7 %slice_multiply_fusion.2 = (f32[10,12,12,132]{3,2,0,1:T(8,128)}, f32[10,12,12,132]{3,2,0,1:T(8,128)}, f32[10,12,12,132]{3,2,0,1:T(8,128)}) fusion(f32[14,12,12,132]{3,2,0,1:T(8,128)S(1)} %pad_maximum_fusion, f32[12,12,132]{2,1,0:T(8,128)S(1)} %get-tuple-element.60, f32[12,12,132]{2,1,0:T(8,128)S(1)} %get-tuple-element.59, f32[12,12,132]{2,1,0:T(8,128)S(1)} %get-tuple-element.58), kind=kLoop, calls=%fused_computation.9 | loop fusion | flops 570240 | bytes 3269376 | tf_op jit(solution)/shard_map/mul | solution.py:191
  29.1 0.8 slice_add_fusion.17
  31.2 1.3 %fusion.132 = (f32[3,18,18,1]{3,2,1,0:T(8,128)}, f32[3,18,18,1]{3,2,1,0:T(8,128)}) fusion(f32[3,18,18,128]{3,2,1,0:T(8,128)S(1)} %maximum_select_fusion), kind=kLoop, calls=%fused_computation.279 | loop fusion | bytes 15552 | tf_op jit(solution)/shard_map/jit(_pad)/slice | solution.py:181
  32.6 1.2 %fusion.59 = f32[16,16,128]{2,1,0:T(8,128)S(1)} fusion(f32[3,18,18,128]{3,2,1,0:T(8,128)S(1)} %maximum_select_fusion, f32[3,18,18,1]{3,2,1,0:T(8,128)} %get-tuple-element.65, f32[3,18,18,1]{3,2,1,0:T(8,128)} %get-tuple-element.64, pred[16]{0:T(512)(128)(4,1)S(1)} %compare_and_fusion.4), kind=kLoop, calls=%fused_computation.100 | loop fusion | flops 294912 | bytes 1327200 | tf_op jit(solution)/shard_map/jit(_where)/select_n | solution.py:485
  34.6 0.8 fusion.74
  35.4 1.9 %fusion.138 = (f32[10,10,128]{2,1,0:T(8,128)}, f32[10,10,128]{2,1,0:T(8,128)S(1)}, f32[10,10,128]{2,1,0:T(8,128)}) fusion(f32[14,14,128]{2,1,0:T(8,128)S(1)} %fusion.69, f32[12,12,128]{2,1,0:T(8,128)} %fusion.74, pred[10]{0:T(512)(128)(4,1)S(1)} %compare_and_fusion.1), kind=kLoop, calls=%fused_computation.285 | loop fusion | flops 102400 | bytes 712714 | tf_op jit(solution)/shard_map/slice | solution.py:491
  37.3 1.5 %fusion.86 = (f32[64,128]{1,0:T(8,128)}, f32[64,128]{1,0:T(8,128)}, f32[64,128]{1,0:T(8,128)}, f32[64,128]{1,0:T(8,128)}) fusion(f32[10,10,128]{2,1,0:T(8,128)S(1)} %get-tuple-element.88, f32[12,12,128]{2,1,0:T(8,128)} %fusion.74, pred[8]{0:T(512)(128)(4,1)S(1)} %compare_and_fusion, f32[14,14,128]{2,1,0:T(8,128)S(1)} %fusion.69), kind=kLoop, calls=%fused_computation.142 | loop fusion | flops 65536 | bytes 442880 | tf_op jit(solution)/shard_map/reshape | solution.py:448
  40.1 1.1 %reduce-window.6 = s32[4,16,128]{2,1,0:T(8,128)S(1)} reduce-window(s32[4,16,128]{2,1,0:T(8,128)S(1)} %fusion.130, s32[]{:T(128)} %constant.45.clone.1), window={size=1x1x128 pad=0_0x0_0x127_0}, to_apply=%region_2.3 | reduce-window | flops 1040384 | bytes 65540 | tf_op jit(solution)/shard_map/reduce-window
  43.0 2.5 %multiply_reduce_fusion = f32[2048,5]{0,1:T(8,128)S(1)} fusion(f32[2048,128]{0,1:T(8,128)S(1)} %fusion.16, s32[2048]{0:T(1024)S(1)} %get-tuple-element.122, f32[8,8,5,128]{3,2,1,0:T(8,128)S(1)} %bitcast.152), kind=kOutput, calls=%fused_computation | convolution fusion | flops 1009375232 | bytes 1261568 | tf_op jit(solution)/shard_map/dot_general | solution.py:554
  46.1 0.8 fusion.3
  49.0 29.3 %shard_map.94 = (f32[8,128]{1,0:T(8,128)}, f32[14,64]{1,0:T(8,128)}, f32[14,64]{1,0:T(8,128)}, f32[14,64]{1,0:T(8,128)}, f32[14,64]{1,0:T(8,128)}) custom-call(f32[192,128]{1,0:T(8,128)} %bitcast.151, f32[64,128]{1,0:T(8,128)} %slice_bitcast_fusion.3.refs_1_, f32[64,128]{1,0:T(8,128)} %get-tuple-element.130.refs_2_, f32[64,128]{1,0:T(8,128)} %get-tuple-element.91.refs_3_, ...), custom_call_target="tpu_custom_call" | custom-call | tf_op jit(solution)/shard_map/pallas_call | solution.py:454
  78.3 1.5 %fusion.139 = (f32[1,1]{1,0:T(1,128)}, f32[1,1]{1,0:T(1,128)}, f32[1,1]{1,0:T(1,128)}, f32[1,1]{1,0:T(1,128)}, f32[1,1]{1,0:T(1,128)}) fusion(f32[8,128]{1,0:T(8,128)} %get-tuple-element.33), kind=kLoop, calls=%fused_computation.286 | loop fusion | bytes 40 | tf_op jit(solution)/shard_map/slice | solution.py:470
  80.6 7.6 %fusion.25 = f32[10,8,8,128]{3,2,0,1:T(8,128)S(1)} fusion(f32[14,12,12,128]{3,2,0,1:T(8,128)S(1)} %copy_select_fusion, f32[14,12,12,2]{3,2,0,1:T(8,128)S(1)} %reshape.579, f32[14,12,12,2]{3,2,0,1:T(8,128)} %copy-done, f32[10,12,12,132]{3,2,0,1:T(8,128)} %get-tuple-element.63, f32[10,12,12,132]{3,2,0,1:T(8,128)} %get-tuple-element.62, ...), kind=kLoop, calls=%fused_computation.32 | loop fusion | flops 4259840 | bytes 8864004 | tf_op jit(solution)/shard_map/add | solution.py:211
  88.9 1.1 %subtract_select_fusion = (f32[1,2048]{1,0:T(1,128)S(1)}, f32[1,2048]{1,0:T(1,128)S(1)}, f32[1,2048]{1,0:T(1,128)S(1)}) fusion(s32[]{:T(128)} %bitcast.148, f32[8,2048]{1,0:T(8,128)} %param.8, f32[5,2048]{1,0:T(8,128)} %bitcast.155, f32[]{:T(128)S(6)} %mul.613, f32[]{:T(128)S(6)} %neg.43), kind=kLoop, calls=%fused_computation.194 | loop fusion | flops 45056 | bytes 57356 | tf_op jit(solution)/shard_map/mul | solution.py:232
  89.9 0.9 fusion.105
  90.9 2.6 %fusion.10 = f32[2,8,8,128]{3,2,0,1:T(8,128)S(1)} fusion(f32[2048,128]{0,1:T(8,128)} %copy-done.3, f32[2048,2]{0,1:T(2,128)S(1)} %maximum_bitcast_fusion.4, s32[8,8]{1,0:T(8,128)S(1)} %multiply_add_fusion.2, s32[2048]{0:T(1024)S(1)} %get-tuple-element.122, f32[10,8,8,128]{3,2,0,1:T(8,128)} %copy-done.4, f32[8,8,128]{2,1,0:T(8,128)S(1)} %slice_bitcast_fusion.4), kind=kOutput, calls=%fused_computation.16 | convolution fusion | flops 403341312 | bytes 1237248 | tf_op jit(solution)/shard_map/dot_general | solution.py:591
  94.3 2.9 %fusion.52 = f32[10,10,130]{2,1,0:T(8,128)S(1)} fusion(f32[10,10,128]{2,1,0:T(8,128)S(1)} %get-tuple-element.88, f32[10,10,128]{2,1,0:T(8,128)S(1)} %copy-done.7, f32[10,10,128]{2,1,0:T(8,128)S(1)} %copy-done.6, f32[10,10,128]{2,1,0:T(8,128)S(1)} %slice.766, f32[]{:T(128)} %bitcast.41, f32[]{:T(128)} %bitcast.40, f32[]{:T(128)} %bitcast.39, f32[]{:T(128)} %bitcast.38), kind=kLoop, calls=%fused_computation.90 | loop fusion | flops 91000 | bytes 256816 | tf_op jit(solution)/shard_map/add | solution.py:527
  (129 shorter events, 13.5 us)
Async XLA Ops:
  0.6 5.5 %copy-start.1 = (f32[14,8,8,128]{3,2,1,0:T(8,128)S(1)}, f32[14,8,8,128]{3,2,1,0:T(8,128)}, u32[]{:S(2)}) copy-start(f32[14,8,8,128]{3,2,1,0:T(8,128)} %param.6) | copy-start | bytes 1376260
  26.2 4.8 %copy-start.13 = (f32[3,8,5,128]{3,2,1,0:T(8,128)S(1)}, f32[3,8,5,128]{3,2,1,0:T(8,128)}, u32[]{:S(2)}) copy-start(f32[3,8,5,128]{3,2,1,0:T(8,128)} %get-tuple-element.31) | copy-start | bytes 184324
  26.3 4.8 %copy-start.14 = (f32[3,8,5,128]{3,2,1,0:T(8,128)S(1)}, f32[3,8,5,128]{3,2,1,0:T(8,128)}, u32[]{:S(2)}) copy-start(f32[3,8,5,128]{3,2,1,0:T(8,128)} %get-tuple-element.26) | copy-start | bytes 184324
  26.3 4.8 %copy-start.15 = (f32[3,5,5,128]{3,2,1,0:T(8,128)S(1)}, f32[3,5,5,128]{3,2,1,0:T(8,128)}, u32[]{:S(2)}) copy-start(f32[3,5,5,128]{3,2,1,0:T(8,128)} %get-tuple-element.32) | copy-start | bytes 115204
  26.3 4.8 %copy-start.16 = (f32[3,5,8,128]{3,2,1,0:T(8,128)S(1)}, f32[3,5,8,128]{3,2,1,0:T(8,128)}, u32[]{:S(2)}) copy-start(f32[3,5,8,128]{3,2,1,0:T(8,128)} %get-tuple-element.29) | copy-start | bytes 184324
  26.3 4.8 %copy-start.17 = (f32[3,5,5,128]{3,2,1,0:T(8,128)S(1)}, f32[3,5,5,128]{3,2,1,0:T(8,128)}, u32[]{:S(2)}) copy-start(f32[3,5,5,128]{3,2,1,0:T(8,128)} %get-tuple-element.27) | copy-start | bytes 115204
  26.3 4.8 %copy-start.18 = (f32[3,5,5,128]{3,2,1,0:T(8,128)S(1)}, f32[3,5,5,128]{3,2,1,0:T(8,128)}, u32[]{:S(2)}) copy-start(f32[3,5,5,128]{3,2,1,0:T(8,128)} %get-tuple-element.30) | copy-start | bytes 115204
  26.3 4.8 %copy-start.19 = (f32[3,5,8,128]{3,2,1,0:T(8,128)S(1)}, f32[3,5,8,128]{3,2,1,0:T(8,128)}, u32[]{:S(2)}) copy-start(f32[3,5,8,128]{3,2,1,0:T(8,128)} %get-tuple-element.28) | copy-start | bytes 184324
  26.3 4.8 %copy-start.20 = (f32[3,5,5,128]{3,2,1,0:T(8,128)S(1)}, f32[3,5,5,128]{3,2,1,0:T(8,128)}, u32[]{:S(2)}) copy-start(f32[3,5,5,128]{3,2,1,0:T(8,128)} %get-tuple-element.25) | copy-start | bytes 115204
  33.8 5.7 %copy-start.27 = (s32[2048]{0:T(1024)S(1)}, s32[2048]{0:T(1024)}, u32[]{:S(2)}) copy-start(s32[2048]{0:T(1024)} %param.10) | copy-start | bytes 24580
  35.3 7.4 %copy-start.2 = (f32[14,8,8,128]{3,2,1,0:T(8,128)S(1)}, f32[14,8,8,128]{3,2,1,0:T(8,128)}, u32[]{:S(2)}) copy-start(f32[14,8,8,128]{3,2,1,0:T(8,128)} %param.6) | copy-start | bytes 1376260
  42.9 37.6 %copy-start.8 = (f32[8,8,128]{2,1,0:T(8,128)S(1)}, f32[8,8,128]{2,1,0:T(8,128)}, u32[]{:S(2)}) copy-start(f32[8,8,128]{2,1,0:T(8,128)} %get-tuple-element.81) | copy-start | bytes 98308
  42.9 37.6 %copy-start.9 = (f32[8,8,128]{2,1,0:T(8,128)S(1)}, f32[8,8,128]{2,1,0:T(8,128)}, u32[]{:S(2)}) copy-start(f32[8,8,128]{2,1,0:T(8,128)} %get-tuple-element.82) | copy-start | bytes 98308
  42.9 37.6 %copy-start.10 = (f32[8,8,128]{2,1,0:T(8,128)S(1)}, f32[8,8,128]{2,1,0:T(8,128)}, u32[]{:S(2)}) copy-start(f32[8,8,128]{2,1,0:T(8,128)} %get-tuple-element.83) | copy-start | bytes 98308
  42.9 37.6 %copy-start.30 = (f32[10]{0:T(128)S(1)}, f32[10]{0:T(128)}, u32[]{:S(2)}) copy-start(f32[10]{0:T(128)} %broadcast_multiply_fusion) | copy-start | bytes 124
  88.9 4.6 %slice-start = ((f32[10,8,8,128]{3,2,0,1:T(8,128)}), f32[8,8,8,128]{3,2,0,1:T(8,128)S(1)}, s32[]{:S(2)}) async-start(f32[10,8,8,128]{3,2,0,1:T(8,128)} %copy-done.4), calls=%async_computation | async-start | bytes 524288 | tf_op jit(solution)/shard_map/slice | solution.py:594
  93.4 4.5 %copy-start.12 = (f32[8,2048]{1,0:T(8,128)S(1)}, f32[8,2048]{1,0:T(8,128)}, u32[]{:S(2)}) copy-start(f32[8,2048]{1,0:T(8,128)} %param.8) | copy-start | bytes 196612
  93.4 4.5 %copy-start.22 = (f32[2048,5]{0,1:T(8,128)S(1)}, f32[2048,5]{0,1:T(8,128)}, u32[]{:S(2)}) copy-start(f32[2048,5]{0,1:T(8,128)} %copy-done.21) | copy-start | bytes 122884
  93.5 4.6 %copy-start.23 = (f32[2048]{0:T(1024)S(1)}, f32[2048]{0:T(1024)}, u32[]{:S(2)}) copy-start(f32[2048]{0:T(1024)} %get-tuple-element.129) | copy-start | bytes 24580
  93.5 4.6 %copy-start.26 = (pred[2048]{0:T(1024)(128)(4,1)S(1)}, pred[2048]{0:T(1024)(128)(4,1)}, u32[]{:S(2)}) copy-start(pred[2048]{0:T(1024)(128)(4,1)} %get-tuple-element.117) | copy-start | bytes 6148
  93.5 5.2 %copy-start.25 = (f32[14,64]{1,0:T(8,128)S(1)}, f32[14,64]{1,0:T(8,128)}, u32[]{:S(2)}) copy-start(f32[14,64]{1,0:T(8,128)} %get-tuple-element.37) | copy-start | bytes 10756
  93.5 5.3 %copy-start.24 = (f32[14,64]{1,0:T(8,128)S(1)}, f32[14,64]{1,0:T(8,128)}, u32[]{:S(2)}) copy-start(f32[14,64]{1,0:T(8,128)} %get-tuple-element.36) | copy-start | bytes 10756
  93.5 5.3 %copy-start.29 = (f32[14,64]{1,0:T(8,128)S(1)}, f32[14,64]{1,0:T(8,128)}, u32[]{:S(2)}) copy-start(f32[14,64]{1,0:T(8,128)} %get-tuple-element.35) | copy-start | bytes 10756
  93.5 5.4 %copy-start.28 = (f32[14,64]{1,0:T(8,128)S(1)}, f32[14,64]{1,0:T(8,128)}, u32[]{:S(2)}) copy-start(f32[14,64]{1,0:T(8,128)} %get-tuple-element.34) | copy-start | bytes 10756
  (9 other events, 19.7 us)

commit v17 on v15

--- a/solution.py
+++ b/solution.py
@@ -78,7 +78,9 @@
         expected = expected + (1 if condition is None else condition.astype(jnp.int32))
     pl.semaphore_wait(barrier, expected)
     copies = []
-    for k, step in enumerate(offsets):
+    order = sorted(range(count), key=lambda k: -abs(offsets[k][0]) - abs(offsets[k][1]))
+    for k in order:
+        step = offsets[k]
         copy = pltpu.make_async_remote_copy(
             src_ref=sources[k],
             dst_ref=outs[k],

time: 79.5 us -> 79.4 us (level)
  no operation moved by 1% of the time
where the time goes in v17:
time: 79.4 us; the launch traced here: 79 us
  Pallas kernels  44.6 us (56%)
  other arithmetic  16 us (20%)
  local copies, waits for them, and re-layouts  11.2 us (14%)
  matrix products  4.53 us (6%)
  between operations  2.65 us (3%)
    pallas_call x1, Pallas kernels, pressure_coefficients(): pl.pallas_call(lambda *refs: reduce_kernel(groups, shift, half_width, *re...  28.6 us
    pallas_call x1, Pallas kernels, neighbour_exchange(): pl.pallas_call(lambda *refs: exchange_kernel(offsets, *refs), out_shape=[...  16 us
    slice x5, local copies, waits for them, and re-layouts, pick(): return lax.slice_in_dim(values, values.shape[dim] - width, None, axis=dim)  3.5 us
    add x1, other arithmetic, solve_pressure(): padded_pressure = padded_pressure + coefficients[j] * padded_basis[j]  2.71 us
    dot_general x1, matrix products, on_device(): jnp.dot(plane_hot, gas_table, precision=HIGHEST)  2.42 us
    slice x2, local copies, waits for them, and re-layouts, radial_pad(): jnp.pad(values, [(0, 0)] * (values.ndim - 1) + [(rim_width, rim_width)],...  2.21 us

profile of v17, /device:TPU:1, one launch (start us, length us, event | category | flops | bytes accessed | tf_op | source)
XLA Modules:
  0.0 79.0 jit_solution(2655065688876125286)
XLA Ops:
  1.3 0.7 broadcast_compare_fusion
  2.1 1.2 %reduce-window.6 = s32[4,16,128]{2,1,0:T(8,128)S(1)} reduce-window(s32[4,16,128]{2,1,0:T(8,128)S(1)} %fusion.130, s32[]{:T(128)} %constant.45.clone.1), window={size=1x1x128 pad=0_0x0_0x127_0}, to_apply=%region_2.3 | reduce-window | flops 1040384 | bytes 65540 | tf_op jit(solution)/shard_map/reduce-window
  3.9 0.7 add_select_fusion.1
  4.9 2.4 %multiply_reduce_fusion = f32[2048,5]{0,1:T(8,128)S(1)} fusion(f32[2048,128]{0,1:T(8,128)S(1)} %fusion.16, s32[2048]{0:T(1024)S(1)} %get-tuple-element.120, f32[8,8,5,128]{3,2,1,0:T(8,128)S(1)} %bitcast.152), kind=kOutput, calls=%fused_computation | convolution fusion | flops 1009375232 | bytes 1261568 | tf_op jit(solution)/shard_map/dot_general | solution.py:516
  7.3 0.8 %fusion.3 = f32[14,256]{1,0:T(8,128)S(1)} fusion(s32[2048]{0:T(1024)S(1)} %bitcast_select_fusion, f32[1,2048]{1,0:T(1,128)S(1)} %fusion.106, f32[5,2048]{1,0:T(8,128)S(1)} %bitcast.154, f32[8,2048]{1,0:T(8,128)S(1)} %copy-done.2), kind=kOutput, calls=%fused_computation.6 | convolution fusion | flops 88662016 | bytes 137216 | tf_op jit(solution)/shard_map/dot_general | solution.py:525
  8.9 0.7 fusion.133
  9.5 0.7 fusion.136
  10.3 0.8 fusion.137
  11.0 0.7 fusion.135
  12.4 16.0 %shard_map.93 = (f32[14,2,8,128]{3,2,1,0:T(8,128)}, f32[14,8,2,128]{3,2,1,0:T(2,128)}, f32[14,8,2,128]{3,2,1,0:T(2,128)}, f32[14,2,8,128]{3,2,1,0:T(8,128)}, f32...) custom-call(f32[14,2,8,128]{3,2,1,0:T(8,128)} %get-tuple-element.76., ...), custom_call_target="tpu_custom_call" | custom-call | tf_op jit(solution)/shard_map/pallas_call | solution.py:103
  28.4 1.3 %maximum_select_fusion = f32[3,18,18,128]{3,2,1,0:T(8,128)S(1)} fusion(f32[3,5,5,128]{3,2,1,0:T(8,128)} %get-tuple-element.31, f32[3,8,5,128]{3,2,1,0:T(8,128)} %get-tuple-element.30, f32[3,5,5,128]{3,2,1,0:T(8,128)} %get-tuple-element.29, f32[3,5,8,128]{3,2,1,0:T(8,128)} %get-tuple-element.28, f32[3,8,8,128]{3,2,1,0:T(8,128)S(1)} %slice.571, ...), kind=kLoop, calls=%fused_computation.22 | loop fusion | flops 1119744 | bytes 995346 | tf_op jit(solution)/shard_map/jit(_where)/select_n | solution.py:179
  29.7 1.0 %fusion.132 = (f32[3,18,18,1]{3,2,1,0:T(8,128)S(1)}, f32[3,18,18,1]{3,2,1,0:T(8,128)}) fusion(f32[3,18,18,128]{3,2,1,0:T(8,128)S(1)} %maximum_select_fusion), kind=kLoop, calls=%fused_computation.279 | loop fusion | bytes 15552 | tf_op jit(solution)/shard_map/jit(_pad)/slice | solution.py:183
  30.7 1.1 %fusion.59 = f32[16,16,128]{2,1,0:T(8,128)S(1)} fusion(f32[3,18,18,128]{3,2,1,0:T(8,128)S(1)} %maximum_select_fusion, f32[3,18,18,1]{3,2,1,0:T(8,128)} %get-tuple-element.63, f32[3,18,18,1]{3,2,1,0:T(8,128)S(1)} %get-tuple-element.62, pred[16]{0:T(512)(128)(4,1)S(1)} %compare_and_fusion.4), kind=kLoop, calls=%fused_computation.100 | loop fusion | flops 294912 | bytes 1986864 | tf_op jit(solution)/shard_map/jit(_where)/select_n | solution.py:447
  32.4 0.7 fusion.86
  34.3 28.6 %shard_map.94 = f32[8,128]{1,0:T(8,128)} custom-call(f32[192,128]{1,0:T(8,128)} %bitcast.151, f32[64,128]{1,0:T(8,128)} %slice_bitcast_fusion.3.refs_1_, f32[64,128]{1,0:T(8,128)} %slice_bitcast_fusion.2.refs_2_, f32[64,128]{1,0:T(8,128)} %get-tuple-element.89.refs_3_, f32[64,128]{1,0:T(8,128)} %get-tuple-element.90.refs_4_, f32[64,128]{1,0:T(8,128)} %get-tuple-element.88.refs_5_), custom_call_target="tpu_custom_call" | custom-call | tf_op jit(solution)/shard_map/pallas_call | solution.py:420
  63.0 1.5 %fusion.139 = (f32[1,1]{1,0:T(1,128)}, f32[1,1]{1,0:T(1,128)}, f32[1,1]{1,0:T(1,128)}, f32[1,1]{1,0:T(1,128)}, f32[1,1]{1,0:T(1,128)}) fusion(f32[8,128]{1,0:T(8,128)} %shard_map.94), kind=kLoop, calls=%fused_computation.286 | loop fusion | bytes 40 | tf_op jit(solution)/shard_map/slice | solution.py:432
  66.2 0.7 fusion.80
  66.9 2.7 %fusion.52 = f32[10,10,130]{2,1,0:T(8,128)S(1)} fusion(f32[10,10,128]{2,1,0:T(8,128)S(1)} %get-tuple-element.86, f32[10,10,128]{2,1,0:T(8,128)S(1)} %get-tuple-element.87, f32[10,10,128]{2,1,0:T(8,128)S(1)} %get-tuple-element.85, f32[10,10,128]{2,1,0:T(8,128)S(1)} %slice.766, f32[]{:T(128)} %bitcast.41, f32[]{:T(128)} %bitcast.40, f32[]{:T(128)} %bitcast.39, ...), kind=kLoop, calls=%fused_computation.90 | loop fusion | flops 91000 | bytes 256816 | tf_op jit(solution)/shard_map/add | solution.py:489
  70.8 1.2 %slice_reduce_fusion = (f32[14,12,12]{2,0,1:T(8,128)S(1)}, f32[14,12,12]{2,0,1:T(8,128)S(1)}) fusion(f32[14,12,12,128]{3,2,0,1:T(8,128)S(1)} %copy_select_fusion), kind=kLoop, calls=%fused_computation.10 | loop fusion | bytes 32256 | tf_op jit(solution)/shard_map/jit(_pad)/slice | solution.py:183
  73.2 1.1 %pad_maximum_fusion = f32[14,12,12,132]{3,2,0,1:T(8,128)S(1)} fusion(f32[14,12,12,2]{3,2,0,1:T(8,128)S(1)} %reshape.580, f32[14,12,12,128]{3,2,0,1:T(8,128)S(1)} %copy_select_fusion, f32[14,12,12,2]{3,2,0,1:T(8,128)S(1)} %reshape.579), kind=kLoop, calls=%fused_computation.1 | loop fusion | flops 532224 | bytes 2128896 | tf_op jit(solution)/shard_map/jit(_pad)/concatenate | solution.py:183
  74.3 1.0 %slice_multiply_fusion.2 = (f32[10,12,12,132]{3,2,0,1:T(8,128)S(1)}, f32[10,12,12,132]{3,2,0,1:T(8,128)S(1)}, f32[10,12,12,132]{3,2,0,1:T(8,128)S(1)}) fusion(f32[14,12,12,132]{3,2,0,1:T(8,128)S(1)} %pad_maximum_fusion, f32[12,12,132]{2,1,0:T(8,128)S(1)} %get-tuple-element.58, f32[12,12,132]{2,1,0:T(8,128)S(1)} %get-tuple-element.57, ...), kind=kLoop, calls=%fused_computation.9 | loop fusion | flops 570240 | bytes 3269376 | tf_op jit(solution)/shard_map/mul | solution.py:193
  75.5 1.4 %fusion.25 = f32[10,8,8,128]{3,2,0,1:T(8,128)S(1)} fusion(f32[14,12,12,128]{3,2,0,1:T(8,128)S(1)} %copy_select_fusion, f32[14,12,12,2]{3,2,0,1:T(8,128)S(1)} %reshape.579, f32[14,12,12,2]{3,2,0,1:T(8,128)S(1)} %reshape.580, f32[10,12,12,132]{3,2,0,1:T(8,128)S(1)} %get-tuple-element.61, f32[10,12,12,132]{3,2,0,1:T(8,128)S(1)} %get-tuple-element.60, ...), kind=kLoop, calls=%fused_computation.32 | loop fusion | flops 4259840 | bytes 10224132 | tf_op jit(solution)/shard_map/add | solution.py:213
  76.9 1.3 %fusion.10 = f32[2,8,8,128]{3,2,0,1:T(8,128)S(1)} fusion(f32[2048,128]{0,1:T(8,128)S(1)} %fusion.16, f32[2048,2]{0,1:T(2,128)S(1)} %maximum_bitcast_fusion.4, s32[8,8]{1,0:T(8,128)S(1)} %multiply_add_fusion.2, s32[2048]{0:T(1024)S(1)} %get-tuple-element.120, f32[10,8,8,128]{3,2,0,1:T(8,128)S(1)} %fusion.25, f32[8,8,128]{2,1,0:T(8,128)S(1)} %slice_bitcast_fusion.4), kind=kOutput, calls=%fused_computation.16 | convolution fusion | flops 403341312 | bytes 1237248 | tf_op jit(solution)/shard_map/dot_general | solution.py:554
  78.2 0.8 copy.33
  (89 shorter events, 7.4 us)
Async XLA Ops:
  0.6 4.1 %copy-start = (f32[14,8,8,128]{3,2,1,0:T(8,128)S(1)}, f32[14,8,8,128]{3,2,1,0:T(8,128)}, u32[]{:S(2)}) copy-start(f32[14,8,8,128]{3,2,1,0:T(8,128)} %param.6) | copy-start | bytes 1376260
  4.9 2.5 %copy-start.2 = (f32[8,2048]{1,0:T(8,128)S(1)}, f32[8,2048]{1,0:T(8,128)}, u32[]{:S(2)}) copy-start(f32[8,2048]{1,0:T(8,128)} %param.8) | copy-start | bytes 196612
  28.4 2.3 %copy-start.1 = (f32[3,8,8,128]{3,2,1,0:T(8,128)}, f32[3,8,8,128]{3,2,1,0:T(8,128)S(1)}, u32[]{:S(2)}) copy-start(f32[3,8,8,128]{3,2,1,0:T(8,128)S(1)} %slice.571) | copy-start | bytes 294916
  31.9 33.3 %copy-start.10 = (f32[14,64]{1,0:T(8,128)S(1)}, f32[14,64]{1,0:T(8,128)}, u32[]{:S(2)}) copy-start(f32[14,64]{1,0:T(8,128)} %get-tuple-element.32) | copy-start | bytes 10756
  32.0 33.2 %copy-start.9 = (f32[14,64]{1,0:T(8,128)S(1)}, f32[14,64]{1,0:T(8,128)}, u32[]{:S(2)}) copy-start(f32[14,64]{1,0:T(8,128)} %get-tuple-element.33) | copy-start | bytes 10756
  32.0 33.3 %copy-start.8 = (f32[14,64]{1,0:T(8,128)S(1)}, f32[14,64]{1,0:T(8,128)}, u32[]{:S(2)}) copy-start(f32[14,64]{1,0:T(8,128)} %get-tuple-element.34) | copy-start | bytes 10756
  32.0 33.4 %copy-start.7 = (f32[14,64]{1,0:T(8,128)S(1)}, f32[14,64]{1,0:T(8,128)}, u32[]{:S(2)}) copy-start(f32[14,64]{1,0:T(8,128)} %get-tuple-element.35) | copy-start | bytes 10756
  32.4 38.1 %copy-start.3 = (f32[14,2,8,128]{3,2,1,0:T(8,128)S(1)}, f32[14,2,8,128]{3,2,1,0:T(8,128)}, u32[]{:S(2)}) copy-start(f32[14,2,8,128]{3,2,1,0:T(8,128)} %get-tuple-element.22) | copy-start | bytes 344068
  32.4 38.1 %copy-start.4 = (f32[14,8,2,128]{3,2,1,0:T(2,128)S(1)}, f32[14,8,2,128]{3,2,1,0:T(2,128)}, u32[]{:S(2)}) copy-start(f32[14,8,2,128]{3,2,1,0:T(2,128)} %get-tuple-element.23) | copy-start | bytes 344068
  32.4 38.1 %copy-start.5 = (f32[14,8,2,128]{3,2,1,0:T(2,128)S(1)}, f32[14,8,2,128]{3,2,1,0:T(2,128)}, u32[]{:S(2)}) copy-start(f32[14,8,2,128]{3,2,1,0:T(2,128)} %get-tuple-element.20) | copy-start | bytes 344068
  32.4 38.1 %copy-start.6 = (f32[14,2,8,128]{3,2,1,0:T(8,128)S(1)}, f32[14,2,8,128]{3,2,1,0:T(8,128)}, u32[]{:S(2)}) copy-start(f32[14,2,8,128]{3,2,1,0:T(8,128)} %get-tuple-element.21) | copy-start | bytes 344068
  74.3 1.1 %copy-start.11 = (f32[10]{0:T(128)S(1)}, f32[10]{0:T(128)}, u32[]{:S(2)}) copy-start(f32[10]{0:T(128)} %param.7) | copy-start | bytes 124

commit v18 on v17

--- a/solution.py
+++ b/solution.py
@@ -341,7 +341,6 @@
                 device_id_type=pl.DeviceIdType.MESH,
             )
             greeted += 1
-    pl.semaphore_wait(barrier, greeted)
     row = lax.broadcasted_iota(jnp.int32, o_ref.shape, 0)
     lane = lax.broadcasted_iota(jnp.int32, o_ref.shape, 1)
     is_max = (row == 0) & (lane == 0)
@@ -356,6 +355,7 @@
     acc = jnp.zeros(o_ref.shape, jnp.float32)
     for n, entry in enumerate(entries):
         acc = jnp.where((row == 0) & (lane == n), entry, acc)
+    pl.semaphore_wait(barrier, greeted)
     offset = 0
     for group in groups:
         count = group_size(group)

time: 79.4 us -> 79.2 us (level)
  no operation moved by 1% of the time
where the time goes in v18:
time: 79.2 us; the launch traced here: 78.8 us
  Pallas kernels  44.5 us (56%)
  other arithmetic  16 us (20%)
  local copies, waits for them, and re-layouts  11.2 us (14%)
  matrix products  4.53 us (6%)
  between operations  2.65 us (3%)
    pallas_call x1, Pallas kernels, pressure_coefficients(): pl.pallas_call(lambda *refs: reduce_kernel(groups, shift, half_width, *re...  28.5 us
    pallas_call x1, Pallas kernels, neighbour_exchange(): pl.pallas_call(lambda *refs: exchange_kernel(offsets, *refs), out_shape=[...  16 us
    slice x5, local copies, waits for them, and re-layouts, pick(): return lax.slice_in_dim(values, values.shape[dim] - width, None, axis=dim)  3.5 us
    add x1, other arithmetic, solve_pressure(): padded_pressure = padded_pressure + coefficients[j] * padded_basis[j]  2.71 us
    dot_general x1, matrix products, on_device(): jnp.dot(plane_hot, gas_table, precision=HIGHEST)  2.42 us
    slice x2, local copies, waits for them, and re-layouts, radial_pad(): jnp.pad(values, [(0, 0)] * (values.ndim - 1) + [(rim_width, rim_width)],...  2.21 us

profile of v18, /device:TPU:1, one launch (start us, length us, event | category | flops | bytes accessed | tf_op | source)
XLA Modules:
  0.0 78.8 jit_solution(1586538649639428600)
XLA Ops:
  1.3 0.7 broadcast_compare_fusion
  2.1 1.2 %reduce-window.6 = s32[4,16,128]{2,1,0:T(8,128)S(1)} reduce-window(s32[4,16,128]{2,1,0:T(8,128)S(1)} %fusion.130, s32[]{:T(128)} %constant.45.clone.1), window={size=1x1x128 pad=0_0x0_0x127_0}, to_apply=%region_2.3 | reduce-window | flops 1040384 | bytes 65540 | tf_op jit(solution)/shard_map/reduce-window
  3.9 0.7 add_select_fusion.1
  4.9 2.4 %multiply_reduce_fusion = f32[2048,5]{0,1:T(8,128)S(1)} fusion(f32[2048,128]{0,1:T(8,128)S(1)} %fusion.16, s32[2048]{0:T(1024)S(1)} %get-tuple-element.120, f32[8,8,5,128]{3,2,1,0:T(8,128)S(1)} %bitcast.152), kind=kOutput, calls=%fused_computation | convolution fusion | flops 1009375232 | bytes 1261568 | tf_op jit(solution)/shard_map/dot_general | solution.py:516
  7.3 0.8 %fusion.3 = f32[14,256]{1,0:T(8,128)S(1)} fusion(s32[2048]{0:T(1024)S(1)} %bitcast_select_fusion, f32[1,2048]{1,0:T(1,128)S(1)} %fusion.106, f32[5,2048]{1,0:T(8,128)S(1)} %bitcast.154, f32[8,2048]{1,0:T(8,128)S(1)} %copy-done.2), kind=kOutput, calls=%fused_computation.6 | convolution fusion | flops 88662016 | bytes 137216 | tf_op jit(solution)/shard_map/dot_general | solution.py:525
  8.9 0.7 fusion.133
  9.5 0.7 fusion.136
  10.3 0.8 fusion.137
  11.0 0.7 fusion.135
  12.4 16.0 %shard_map.93 = (f32[14,2,8,128]{3,2,1,0:T(8,128)}, f32[14,8,2,128]{3,2,1,0:T(2,128)}, f32[14,8,2,128]{3,2,1,0:T(2,128)}, f32[14,2,8,128]{3,2,1,0:T(8,128)}, f32...) custom-call(f32[14,2,8,128]{3,2,1,0:T(8,128)} %get-tuple-element.76., ...), custom_call_target="tpu_custom_call" | custom-call | tf_op jit(solution)/shard_map/pallas_call | solution.py:103
  28.4 1.3 %maximum_select_fusion = f32[3,18,18,128]{3,2,1,0:T(8,128)S(1)} fusion(f32[3,5,5,128]{3,2,1,0:T(8,128)} %get-tuple-element.31, f32[3,8,5,128]{3,2,1,0:T(8,128)} %get-tuple-element.30, f32[3,5,5,128]{3,2,1,0:T(8,128)} %get-tuple-element.29, f32[3,5,8,128]{3,2,1,0:T(8,128)} %get-tuple-element.28, f32[3,8,8,128]{3,2,1,0:T(8,128)S(1)} %slice.571, ...), kind=kLoop, calls=%fused_computation.22 | loop fusion | flops 1119744 | bytes 995346 | tf_op jit(solution)/shard_map/jit(_where)/select_n | solution.py:179
  29.7 1.0 %fusion.132 = (f32[3,18,18,1]{3,2,1,0:T(8,128)S(1)}, f32[3,18,18,1]{3,2,1,0:T(8,128)}) fusion(f32[3,18,18,128]{3,2,1,0:T(8,128)S(1)} %maximum_select_fusion), kind=kLoop, calls=%fused_computation.279 | loop fusion | bytes 15552 | tf_op jit(solution)/shard_map/jit(_pad)/slice | solution.py:183
  30.7 1.1 %fusion.59 = f32[16,16,128]{2,1,0:T(8,128)S(1)} fusion(f32[3,18,18,128]{3,2,1,0:T(8,128)S(1)} %maximum_select_fusion, f32[3,18,18,1]{3,2,1,0:T(8,128)} %get-tuple-element.63, f32[3,18,18,1]{3,2,1,0:T(8,128)S(1)} %get-tuple-element.62, pred[16]{0:T(512)(128)(4,1)S(1)} %compare_and_fusion.4), kind=kLoop, calls=%fused_computation.100 | loop fusion | flops 294912 | bytes 1986864 | tf_op jit(solution)/shard_map/jit(_where)/select_n | solution.py:447
  32.4 0.7 fusion.86
  34.3 28.5 %shard_map.94 = f32[8,128]{1,0:T(8,128)} custom-call(f32[192,128]{1,0:T(8,128)} %bitcast.151, f32[64,128]{1,0:T(8,128)} %slice_bitcast_fusion.3.refs_1_, f32[64,128]{1,0:T(8,128)} %slice_bitcast_fusion.2.refs_2_, f32[64,128]{1,0:T(8,128)} %get-tuple-element.89.refs_3_, f32[64,128]{1,0:T(8,128)} %get-tuple-element.90.refs_4_, f32[64,128]{1,0:T(8,128)} %get-tuple-element.88.refs_5_), custom_call_target="tpu_custom_call" | custom-call | tf_op jit(solution)/shard_map/pallas_call | solution.py:420
  62.9 1.5 %fusion.139 = (f32[1,1]{1,0:T(1,128)}, f32[1,1]{1,0:T(1,128)}, f32[1,1]{1,0:T(1,128)}, f32[1,1]{1,0:T(1,128)}, f32[1,1]{1,0:T(1,128)}) fusion(f32[8,128]{1,0:T(8,128)} %shard_map.94), kind=kLoop, calls=%fused_computation.286 | loop fusion | bytes 40 | tf_op jit(solution)/shard_map/slice | solution.py:432
  66.1 0.7 fusion.80
  66.8 2.7 %fusion.52 = f32[10,10,130]{2,1,0:T(8,128)S(1)} fusion(f32[10,10,128]{2,1,0:T(8,128)S(1)} %get-tuple-element.86, f32[10,10,128]{2,1,0:T(8,128)S(1)} %get-tuple-element.87, f32[10,10,128]{2,1,0:T(8,128)S(1)} %get-tuple-element.85, f32[10,10,128]{2,1,0:T(8,128)S(1)} %slice.766, f32[]{:T(128)} %bitcast.41, f32[]{:T(128)} %bitcast.40, f32[]{:T(128)} %bitcast.39, ...), kind=kLoop, calls=%fused_computation.90 | loop fusion | flops 91000 | bytes 256816 | tf_op jit(solution)/shard_map/add | solution.py:489
  70.7 1.2 %slice_reduce_fusion = (f32[14,12,12]{2,0,1:T(8,128)S(1)}, f32[14,12,12]{2,0,1:T(8,128)S(1)}) fusion(f32[14,12,12,128]{3,2,0,1:T(8,128)S(1)} %copy_select_fusion), kind=kLoop, calls=%fused_computation.10 | loop fusion | bytes 32256 | tf_op jit(solution)/shard_map/jit(_pad)/slice | solution.py:183
  73.0 1.1 %pad_maximum_fusion = f32[14,12,12,132]{3,2,0,1:T(8,128)S(1)} fusion(f32[14,12,12,2]{3,2,0,1:T(8,128)S(1)} %reshape.580, f32[14,12,12,128]{3,2,0,1:T(8,128)S(1)} %copy_select_fusion, f32[14,12,12,2]{3,2,0,1:T(8,128)S(1)} %reshape.579), kind=kLoop, calls=%fused_computation.1 | loop fusion | flops 532224 | bytes 2128896 | tf_op jit(solution)/shard_map/jit(_pad)/concatenate | solution.py:183
  74.2 1.0 %slice_multiply_fusion.2 = (f32[10,12,12,132]{3,2,0,1:T(8,128)S(1)}, f32[10,12,12,132]{3,2,0,1:T(8,128)S(1)}, f32[10,12,12,132]{3,2,0,1:T(8,128)S(1)}) fusion(f32[14,12,12,132]{3,2,0,1:T(8,128)S(1)} %pad_maximum_fusion, f32[12,12,132]{2,1,0:T(8,128)S(1)} %get-tuple-element.58, f32[12,12,132]{2,1,0:T(8,128)S(1)} %get-tuple-element.57, ...), kind=kLoop, calls=%fused_computation.9 | loop fusion | flops 570240 | bytes 3269376 | tf_op jit(solution)/shard_map/mul | solution.py:193
  75.3 1.4 %fusion.25 = f32[10,8,8,128]{3,2,0,1:T(8,128)S(1)} fusion(f32[14,12,12,128]{3,2,0,1:T(8,128)S(1)} %copy_select_fusion, f32[14,12,12,2]{3,2,0,1:T(8,128)S(1)} %reshape.579, f32[14,12,12,2]{3,2,0,1:T(8,128)S(1)} %reshape.580, f32[10,12,12,132]{3,2,0,1:T(8,128)S(1)} %get-tuple-element.61, f32[10,12,12,132]{3,2,0,1:T(8,128)S(1)} %get-tuple-element.60, ...), kind=kLoop, calls=%fused_computation.32 | loop fusion | flops 4259840 | bytes 10224132 | tf_op jit(solution)/shard_map/add | solution.py:213
  76.7 1.3 %fusion.10 = f32[2,8,8,128]{3,2,0,1:T(8,128)S(1)} fusion(f32[2048,128]{0,1:T(8,128)S(1)} %fusion.16, f32[2048,2]{0,1:T(2,128)S(1)} %maximum_bitcast_fusion.4, s32[8,8]{1,0:T(8,128)S(1)} %multiply_add_fusion.2, s32[2048]{0:T(1024)S(1)} %get-tuple-element.120, f32[10,8,8,128]{3,2,0,1:T(8,128)S(1)} %fusion.25, f32[8,8,128]{2,1,0:T(8,128)S(1)} %slice_bitcast_fusion.4), kind=kOutput, calls=%fused_computation.16 | convolution fusion | flops 403341312 | bytes 1237248 | tf_op jit(solution)/shard_map/dot_general | solution.py:554
  78.1 0.8 copy.33
  (89 shorter events, 7.4 us)
Async XLA Ops:
  0.6 4.1 %copy-start = (f32[14,8,8,128]{3,2,1,0:T(8,128)S(1)}, f32[14,8,8,128]{3,2,1,0:T(8,128)}, u32[]{:S(2)}) copy-start(f32[14,8,8,128]{3,2,1,0:T(8,128)} %param.6) | copy-start | bytes 1376260
  4.9 2.5 %copy-start.2 = (f32[8,2048]{1,0:T(8,128)S(1)}, f32[8,2048]{1,0:T(8,128)}, u32[]{:S(2)}) copy-start(f32[8,2048]{1,0:T(8,128)} %param.8) | copy-start | bytes 196612
  28.4 2.3 %copy-start.1 = (f32[3,8,8,128]{3,2,1,0:T(8,128)}, f32[3,8,8,128]{3,2,1,0:T(8,128)S(1)}, u32[]{:S(2)}) copy-start(f32[3,8,8,128]{3,2,1,0:T(8,128)S(1)} %slice.571) | copy-start | bytes 294916
  31.9 33.2 %copy-start.10 = (f32[14,64]{1,0:T(8,128)S(1)}, f32[14,64]{1,0:T(8,128)}, u32[]{:S(2)}) copy-start(f32[14,64]{1,0:T(8,128)} %get-tuple-element.32) | copy-start | bytes 10756
  32.0 33.1 %copy-start.9 = (f32[14,64]{1,0:T(8,128)S(1)}, f32[14,64]{1,0:T(8,128)}, u32[]{:S(2)}) copy-start(f32[14,64]{1,0:T(8,128)} %get-tuple-element.33) | copy-start | bytes 10756
  32.0 33.2 %copy-start.8 = (f32[14,64]{1,0:T(8,128)S(1)}, f32[14,64]{1,0:T(8,128)}, u32[]{:S(2)}) copy-start(f32[14,64]{1,0:T(8,128)} %get-tuple-element.34) | copy-start | bytes 10756
  32.0 33.2 %copy-start.7 = (f32[14,64]{1,0:T(8,128)S(1)}, f32[14,64]{1,0:T(8,128)}, u32[]{:S(2)}) copy-start(f32[14,64]{1,0:T(8,128)} %get-tuple-element.35) | copy-start | bytes 10756
  32.4 38.0 %copy-start.3 = (f32[14,2,8,128]{3,2,1,0:T(8,128)S(1)}, f32[14,2,8,128]{3,2,1,0:T(8,128)}, u32[]{:S(2)}) copy-start(f32[14,2,8,128]{3,2,1,0:T(8,128)} %get-tuple-element.22) | copy-start | bytes 344068
  32.4 38.0 %copy-start.4 = (f32[14,8,2,128]{3,2,1,0:T(2,128)S(1)}, f32[14,8,2,128]{3,2,1,0:T(2,128)}, u32[]{:S(2)}) copy-start(f32[14,8,2,128]{3,2,1,0:T(2,128)} %get-tuple-element.23) | copy-start | bytes 344068
  32.4 38.0 %copy-start.5 = (f32[14,8,2,128]{3,2,1,0:T(2,128)S(1)}, f32[14,8,2,128]{3,2,1,0:T(2,128)}, u32[]{:S(2)}) copy-start(f32[14,8,2,128]{3,2,1,0:T(2,128)} %get-tuple-element.20) | copy-start | bytes 344068
  32.4 38.0 %copy-start.6 = (f32[14,2,8,128]{3,2,1,0:T(8,128)S(1)}, f32[14,2,8,128]{3,2,1,0:T(8,128)}, u32[]{:S(2)}) copy-start(f32[14,2,8,128]{3,2,1,0:T(8,128)} %get-tuple-element.21) | copy-start | bytes 344068
  74.2 1.1 %copy-start.11 = (f32[10]{0:T(128)S(1)}, f32[10]{0:T(128)}, u32[]{:S(2)}) copy-start(f32[10]{0:T(128)} %param.7) | copy-start | bytes 124
